TPU v7x, 32 devices: a whole 2x2x4 slice. The times are simulated.
32 devices in a mesh: clip: 2 (over y), rows: 8 (over z, x), section: 2 (over core).
Axes of the slice: x: 2, y: 2, z: 4, core: 2. Of those that a mesh axis runs over, the one named last changes fastest.
Arguments:
- codes: int32 [8, 32, 24], P('clip', 'rows'), parts along dimension 0, may hold values from 0 to 262143
- in_proj: bfloat16 [18, 512], replicated, may hold values from -1.5 to 1.5
- gain_up: float32 [512], replicated, may hold values from 0.5 to 2
- up_kernel: bfloat16 [27, 512, 256], P(None, None, 'section'), may hold values from -0.0546875 to 0.0546875
- gain_res: float32 [256], replicated, may hold values from 0.5 to 2
- out_kernel: bfloat16 [27, 128, 256], P(None, 'section'), may hold values from -0.078125 to 0.078125
Outputs:
- decoded: bfloat16 [8, 64, 48, 128], P('clip', 'rows', None, 'section'), parts along dimension 0
There are 2 independent parts, one for each index of `clip`. A program takes and returns all parts, laid end to end along the dimension named above; an argument that names none is the same for every part. Nothing has to cross between parts.
All inputs are finite; a program needn't handle non-finite values.
Results may differ from a plain program's by a relative error of at most 0.0058.
Values may be sent and summed in bfloat16 or wider, within the bound.
No kernel may reach another device: no remote copies, remote signals or barrier semaphores. Data moves between devices by JAX's collectives and lax.ppermute only.
A program may use at most 128 MiB of HBM per device.

v0:
```python
import jax
import jax.numpy as jnp
from jax import lax
from jax.sharding import PartitionSpec as P

C_HID = 256
CODE_BITS = 18


def extended(block, sides, width):
    for axis, dim in sides:
        count = lax.axis_size(axis)
        forward = [(i, i + 1) for i in range(count - 1)]
        backward = [(target, source) for source, target in forward]
        low = lax.ppermute(
            lax.slice_in_dim(block, block.shape[dim] - width, None, axis=dim), axis, forward
        )
        high = lax.ppermute(lax.slice_in_dim(block, 0, width, axis=dim), axis, backward)
        block = jnp.concatenate([low, block, high], axis=dim)
    return block


def norm_act(values, gain_vec):
    mean_square = jnp.mean(values * values, axis=-1, keepdims=True)
    return jax.nn.silu(values * lax.rsqrt(mean_square + 1e-06) * gain_vec)


def enlarge(source):
    return jnp.repeat(jnp.repeat(source, 2, axis=1), 2, axis=2)


def pad_window(source):
    return jnp.pad(source, ((2, 0), (0, 0), (1, 1), (0, 0)))


def up_conv(padded, kernel):
    frame_count = padded.shape[0] - 2
    height = padded.shape[1] - 2
    breadth = padded.shape[2] - 2
    in_width = kernel.shape[1]
    out_width = kernel.shape[2]
    stacked = kernel.reshape(9, 3 * in_width, out_width)
    total = jnp.zeros((frame_count * height * breadth, out_width), jnp.float32)
    for tap_time in range(3):
        for tap_row in range(3):
            pieces = [
                padded[
                    tap_time : tap_time + frame_count,
                    tap_row : tap_row + height,
                    tap_col : tap_col + breadth,
                ]
                for tap_col in range(3)
            ]
            joined = jnp.concatenate(pieces, axis=-1).reshape(-1, 3 * in_width)
            total = total + jnp.dot(
                joined, stacked[3 * tap_time + tap_row], preferred_element_type=jnp.float32
            )
    return total.reshape(frame_count, height, breadth, out_width)


def out_conv(padded, kernel):
    frame_count = padded.shape[0] - 2
    height = padded.shape[1] - 2
    breadth = padded.shape[2] - 2
    in_width = padded.shape[3]
    total = jnp.zeros((frame_count * height * breadth, kernel.shape[1]), jnp.float32)
    for tap_time in range(3):
        for tap_row in range(3):
            for tap_col in range(3):
                piece = padded[
                    tap_time : tap_time + frame_count,
                    tap_row : tap_row + height,
                    tap_col : tap_col + breadth,
                ].reshape(-1, in_width)
                total = total + lax.dot_general(
                    piece,
                    kernel[9 * tap_time + 3 * tap_row + tap_col],
                    (((1,), (1,)), ((), ())),
                    preferred_element_type=jnp.float32,
                )
    return total


def full_channels(normed, out_kernel):
    window = extended(normed, (("rows", 1),), 1)
    return out_conv(pad_window(window), out_kernel)


def body(codes, in_proj, gain_up, up_kernel, gain_res, out_kernel):
    frame_count = codes.shape[0]
    bit_shifts = jnp.arange(CODE_BITS, dtype=jnp.int32)
    bits = ((jnp.right_shift(codes[..., None], bit_shifts) & 1) * 2 - 1).astype(jnp.bfloat16)
    latent = jnp.dot(bits.reshape(-1, CODE_BITS), in_proj, preferred_element_type=jnp.float32)
    latent = latent.reshape(codes.shape[0], codes.shape[1], codes.shape[2], -1)
    active = norm_act(latent, gain_up).astype(jnp.bfloat16)
    window = extended(enlarge(active), (("rows", 1),), 1)
    hidden_share = up_conv(pad_window(window), up_kernel)
    share_width = hidden_share.shape[3]
    partial_sum = jnp.sum(hidden_share * hidden_share, axis=-1, keepdims=True)
    total_sum = lax.psum(partial_sum, "section")
    gain_share = lax.dynamic_slice_in_dim(
        gain_res, lax.axis_index("section") * share_width, share_width, 0
    )
    scaled = hidden_share * lax.rsqrt(total_sum / C_HID + 1e-06) * gain_share
    normed_share = jax.nn.silu(scaled).astype(jnp.bfloat16)
    normed = lax.all_gather(normed_share, "section", axis=3, tiled=True)
    result = full_channels(normed, out_kernel)
    shaped = result.reshape(
        frame_count, hidden_share.shape[1], hidden_share.shape[2], out_kernel.shape[1]
    )
    return shaped.astype(jnp.bfloat16)


def solution(mesh):
    in_specs = (
        P("clip", "rows", None),
        P(),
        P(),
        P(None, None, "section"),
        P(),
        P(None, "section", None),
    )
    out_specs = P("clip", "rows", None, "section")
    return jax.shard_map(body, mesh=mesh, in_specs=in_specs, out_specs=out_specs, check_vma=False)
```

profile of v0, /device:TPU:0, one launch (start us, length us, event | category | flops | bytes accessed | tf_op | source)
XLA Modules:
  0.0 99.7 jit_solution(2404875357311606745)
XLA Ops:
  0.7 1.1 %multiply_reduce_fusion.1 = (f32[4,4,24]{2,1,0:T(4,128)S(1)}, f32[4,4,24,512]{3,2,1,0:T(8,128)S(1)}) fusion(bf16[18,512]{1,0:T(8,128)(2,1)S(1)} %copy-done, s32[4,4,24]{2,1,0:T(4,128)} %param.6), kind=kOutput, calls=%fused_computation.84 | convolution fusion | flops 7505280 | bytes 807936 | tf_op jit(solution)/shard_map/dot_general | solution.py:93
  1.8 1.0 multiply_convert_fusion.1
  2.9 1.4 %broadcast_in_dim.7 = bf16[4,8,24,2,512]{4,3,2,1,0:T(2,128)(2,1)S(1)} broadcast(bf16[4,8,24,512]{3,2,1,0:T(8,128)(2,1)S(1)} %bitcast.194), dimensions={0,1,2,4} | broadcast | bytes 2359296 | tf_op jit(solution)/shard_map/broadcast_in_dim | solution.py:29
  5.8 5.5 %collective-permute-start = (bf16[4,1,48,512]{3,2,1,0:T(8,128)(2,1)}, bf16[4,1,48,512]{3,2,1,0:T(8,128)(2,1)}, u32[]{:S(2)}, u32[]{:S(2)}) collective-permute-start(bf16[4,1,48,512]{3,2,1,0:T(8,128)(2,1)} %get-tuple-element.64), channel_id=1, source_target_pairs={{0,2},{2,4},{4,6},{6,8},{8,10},{10,12},{12,14},{1,3},{3,5},{5,7},{... | collective-permute-start | bytes 589832 | tf_op jit(solution)/shard_map/ppermute | solution.py:15
  11.3 1.3 %collective-permute-start.1 = (bf16[4,1,48,512]{3,2,1,0:T(8,128)(2,1)}, bf16[4,1,48,512]{3,2,1,0:T(8,128)(2,1)}, u32[]{:S(2)}, u32[]{:S(2)}) collective-permute-start(bf16[4,1,48,512]{3,2,1,0:T(8,128)(2,1)} %get-tuple-element.65), channel_id=1, source_target_pairs={{2,0},{4,2},{6,4},{8,6},{10,8},{12,10},{14,12},{3,1},{5,3},{7,5},{... | collective-permute-start | bytes 589832 | tf_op jit(solution)/shard_map/ppermute | solution.py:18
  12.6 2.0 %concatenate.62 = bf16[1536,512]{1,0:T(8,128)(2,1)} reshape(bf16[4,8,24,2,512]{4,3,2,1,0:T(2,128)(2,1)S(1)} %broadcast_in_dim.7) | data formatting | bytes 3145728 | tf_op jit(solution)/shard_map/concatenate | solution.py:54
  14.7 3.5 %fusion.102 = (bf16[3,512,128]{2,1,0:T(8,128)(2,1)S(1)}, bf16[3,512,128]{2,1,0:T(8,128)(2,1)}, bf16[3,512,128]{2,1,0:T(8,128)(2,1)}, bf16[3,512,128]{2,1,0:T(8,1...) fusion(bf16[27,512,128]{2,1,0:T(8,128)(2,1)} %param.9), kind=kLoop, calls=%fused_computation.155 | loop fusion | bytes 7077888 | tf_op jit(solution)/shard_map/slice | solution.py:56
  18.2 1.7 %collective-permute-done.1 = bf16[4,1,48,512]{3,2,1,0:T(8,128)(2,1)} collective-permute-done((bf16[4,1,48,512]{3,2,1,0:T(8,128)(2,1)}, bf16[4,1,48,512]{3,2,1,0:T(8,128)(2,1)}, u32[]{:S(2)}, u32[]{:S(2)}) %collective-permute-start.1) | collective-permute-done | bytes 196640 | tf_op jit(solution)/shard_map/ppermute | solution.py:18
  19.8 4.2 %fusion.17 = bf16[6,10,50,512]{3,2,1,0:T(8,128)(2,1)S(1)} fusion(bf16[4,1,48,512]{3,2,1,0:T(8,128)(2,1)} %collective-permute-done.1, bf16[4,8,48,512]{3,2,1,0:T(8,128)(2,1)S(1)} %reshape.167, bf16[4,1,48,512]{3,2,1,0:T(8,128)(2,1)} %collective-permute-done), kind=kLoop, calls=%fused_computation.30 | loop fusion | flops 26112000 | bytes 5038080 | tf_op jit(solution)/shard_map/concatenate | solution.py:19
  24.0 3.2 %fusion.104 = (bf16[4,8,48,512]{3,2,1,0:T(8,128)(2,1)S(1)}, bf16[4,8,48,512]{3,2,1,0:T(8,128)(2,1)}, bf16[4,8,48,512]{3,2,1,0:T(8,128)(2,1)S(1)}, bf16[4,8,48,512]{3,2,1,0:T(8,128)(2,1)S(1)}, bf16[4,8,48,512]{3,2,1,0:T(8,128)(2,1)}) fusion(bf16[6,10,50,512]{3,2,1,0:T(8,128)(2,1)S(1)} %fusion.17), kind=kLoop, calls=%fused_computation.157 | loop fusion | bytes 15728640 | tf_op jit(solution)/shard_map/slice | solution.py:47
  27.2 9.5 %fusion.103 = (bf16[4,8,48,512]{3,2,1,0:T(8,128)(2,1)}, bf16[4,8,48,512]{3,2,1,0:T(8,128)(2,1)}, bf16[4,8,48,512]{3,2,1,0:T(8,128)(2,1)}, bf16[4,8,48,512]{3,2,1...) fusion(bf16[6,10,50,512]{3,2,1,0:T(8,128)(2,1)S(1)} %fusion.17), kind=kLoop, calls=%fused_computation.156 | loop fusion | bytes 59768832 | tf_op jit(solution)/shard_map/slice | solution.py:47
  36.7 3.9 %fusion.8 = (bf16[4,8,48,1536]{3,2,1,0:T(8,128)(2,1)S(1)}, bf16[4,8,48,1536]{3,2,1,0:T(8,128)(2,1)S(1)}) fusion(bf16[4,8,48,512]{3,2,1,0:T(8,128)(2,1)S(1)} %reshape.167, bf16[4,1,48,512]{3,2,1,0:T(8,128)(2,1)} %collective-permute-done, bf16[4,8,48,512]{3,2,1,0:T(8,128)(2,1)} %get-tuple-element.18, bf16[4,8,48,512]{3,2,1,0:T(8,128)(2,1)} %get-tuple-element.14, ...), kind=kLoop, calls=%fused_computation.15 | loop fusion | flops 37748736 | bytes 17694720 | tf_op jit(solution)/shard_map/concatenate | solution.py:54
  40.6 2.3 %fusion.110 = f32[1536,128]{1,0:T(8,128)} fusion(bf16[1536,1536]{1,0:T(8,128)(2,1)S(1)} %bitcast.188, bf16[1536,128]{1,0:T(8,128)(2,1)S(1)} %bitcast.227), kind=kOutput, calls=%fused_computation.163 | convolution fusion | flops 603979776 | bytes 5898240 | tf_op jit(solution)/shard_map/dot_general | solution.py:55
  42.9 3.8 %pad_maximum_fusion.3 = (bf16[4,8,48,1536]{3,2,1,0:T(8,128)(2,1)S(1)}, bf16[4,8,48,1536]{3,2,1,0:T(8,128)(2,1)S(1)}) fusion(bf16[4,8,48,512]{3,2,1,0:T(8,128)(2,1)} %get-tuple-element.31, bf16[4,8,48,512]{3,2,1,0:T(8,128)(2,1)} %get-tuple-element.32, bf16[4,8,48,512]{3,2,1,0:T(8,128)(2,1)S(1)} %copy-done.3, bf16[4,8,48,512]{3,2,1,0:T(8,128)(2,1)S(1)} %copy-done.4, ...), kind=kLoop, calls=%fused_computation.17 | loop fusion | flops 28311552 | bytes 18874368 | tf_op jit(solution)/shard_map/concatenate | solution.py:54
  46.7 3.3 %fusion.109 = f32[1536,128]{1,0:T(8,128)} fusion(bf16[1536,1536]{1,0:T(8,128)(2,1)S(1)} %bitcast.190, bf16[1536,128]{1,0:T(8,128)(2,1)} %bitcast.226), kind=kOutput, calls=%fused_computation.162 | convolution fusion | flops 603979776 | bytes 5898240 | tf_op jit(solution)/shard_map/dot_general | solution.py:55
  50.3 1.0 %copy-done.2 = bf16[4,8,48,512]{3,2,1,0:T(8,128)(2,1)S(1)} copy-done((bf16[4,8,48,512]{3,2,1,0:T(8,128)(2,1)S(1)}, bf16[4,8,48,512]{3,2,1,0:T(8,128)(2,1)}, u32[]{:S(2)}) %copy-start.2) | copy-done | bytes 1572888
  52.6 1.4 %convolution_add_fusion.5 = f32[1536,128]{1,0:T(8,128)S(1)} fusion(f32[1536,128]{1,0:T(8,128)S(1)} %copy-done.6, bf16[1536,1536]{1,0:T(8,128)(2,1)S(1)} %bitcast.185, bf16[1536,128]{1,0:T(8,128)(2,1)S(1)} %bitcast.225), kind=kOutput, calls=%fused_computation.45 | convolution fusion | flops 604176384 | bytes 6684672 | tf_op jit(solution)/shard_map/dot_general | solution.py:55
  54.0 1.4 %convolution_add_fusion.4 = f32[1536,128]{1,0:T(8,128)S(1)} fusion(f32[1536,128]{1,0:T(8,128)S(1)} %convolution_add_fusion.5, bf16[1536,1536]{1,0:T(8,128)(2,1)S(1)} %bitcast.186, bf16[1536,128]{1,0:T(8,128)(2,1)S(1)} %bitcast.224), kind=kOutput, calls=%fused_computation.44 | convolution fusion | flops 604176384 | bytes 6684672 | tf_op jit(solution)/shard_map/dot_general | solution.py:55
  55.4 1.1 %pad_maximum_fusion.5 = (bf16[4,8,48,1536]{3,2,1,0:T(8,128)(2,1)S(1)}, bf16[4,8,48,1536]{3,2,1,0:T(8,128)(2,1)S(1)}) fusion(bf16[4,8,48,512]{3,2,1,0:T(8,128)(2,1)S(1)} %get-tuple-element.25, bf16[4,8,48,512]{3,2,1,0:T(8,128)(2,1)S(1)} %get-tuple-element.26, bf16[4,8,48,512]{3,2,1,0:T(8,128)(2,1)S(1)} %get-tuple-element.27, ...), kind=kLoop, calls=%fused_computation.19 | loop fusion | flops 28311552 | bytes 18874368 | tf_op jit(solution)/shard_map/concatenate | solution.py:54
  56.6 1.4 %convolution_add_fusion.3 = f32[1536,128]{1,0:T(8,128)S(1)} fusion(f32[1536,128]{1,0:T(8,128)S(1)} %convolution_add_fusion.4, bf16[1536,1536]{1,0:T(8,128)(2,1)S(1)} %bitcast.189, bf16[1536,128]{1,0:T(8,128)(2,1)S(1)} %bitcast.223), kind=kOutput, calls=%fused_computation.43 | convolution fusion | flops 604176384 | bytes 6684672 | tf_op jit(solution)/shard_map/dot_general | solution.py:55
  58.1 1.4 %convolution_add_fusion.2 = f32[1536,128]{1,0:T(8,128)S(1)} fusion(f32[1536,128]{1,0:T(8,128)S(1)} %convolution_add_fusion.3, bf16[1536,1536]{1,0:T(8,128)(2,1)S(1)} %bitcast.187, bf16[1536,128]{1,0:T(8,128)(2,1)S(1)} %bitcast.222), kind=kOutput, calls=%fused_computation.42 | convolution fusion | flops 604176384 | bytes 6684672 | tf_op jit(solution)/shard_map/dot_general | solution.py:55
  59.5 1.4 %convolution_add_fusion.1 = f32[1536,128]{1,0:T(8,128)S(1)} fusion(f32[1536,128]{1,0:T(8,128)S(1)} %convolution_add_fusion.2, bf16[1536,1536]{1,0:T(8,128)(2,1)S(1)} %bitcast.184, bf16[1536,128]{1,0:T(8,128)(2,1)S(1)} %bitcast.221), kind=kOutput, calls=%fused_computation.41 | convolution fusion | flops 604176384 | bytes 6684672 | tf_op jit(solution)/shard_map/dot_general | solution.py:55
  61.9 1.7 %fusion.9 = f32[1536,128]{1,0:T(8,128)S(1)} fusion(bf16[1536,128]{1,0:T(8,128)(2,1)S(1)} %bitcast.230, bf16[1536,512]{1,0:T(8,128)(2,1)S(1)} %bitcast.228, bf16[1536,512]{1,0:T(8,128)(2,1)S(1)} %copy-done.7, bf16[1536,512]{1,0:T(8,128)(2,1)S(1)} %bitcast.229), kind=kOutput, calls=%fused_computation.22 | convolution fusion | flops 618135552 | bytes 5898240 | tf_op jit(solution)/shard_map/dot_general | solution.py:55
  63.6 1.5 %multiply_reduce_fusion = (f32[1536]{0:T(1024)S(1)}, f32[1536,128]{1,0:T(8,128)S(1)}) fusion(f32[1536,128]{1,0:T(8,128)S(1)} %copy-done.5, f32[1536,128]{1,0:T(8,128)S(1)} %fusion.9, f32[1536,128]{1,0:T(8,128)S(1)} %convolution_add_fusion.1, bf16[1536,1536]{1,0:T(8,128)(2,1)S(1)} %bitcast.183, bf16[1536,128]{1,0:T(8,128)(2,1)S(1)} %bitcast.220), kind=kOutput, calls=%fused_computation.82 | convolution fusion | flops 604961280 | bytes 8263680 | tf_op jit(solution)/shard_map/dot_general | solution.py:55
  65.3 3.4 %psum.7 = f32[4,8,48,1]{2,1,0,3:T(8,128)S(1)} all-reduce(f32[4,8,48,1]{2,1,0,3:T(8,128)S(1)} %broadcast_in_dim.16), channel_id=1, replica_groups=mesh['clip'=2,'rows'=8,'section'=2] {'section'}, use_global_device_ids=true, to_apply=%region_2.3 | all-reduce | flops 1536 | bytes 12288 | tf_op jit(solution)/shard_map/psum | solution.py:100
  68.9 2.4 %all_gather.3 = bf16[4,8,48,256]{3,2,1,0:T(8,128)(2,1)S(1)} all-gather(bf16[4,8,48,128]{3,2,1,0:T(8,128)(2,1)S(1)} %multiply_convert_fusion), channel_id=1, replica_groups=mesh['clip'=2,'rows'=8,'section'=2] {'section'}, dimensions={3}, use_global_device_ids=true | all-gather | bytes 1179648 | tf_op jit(solution)/shard_map/all_gather | solution.py:106
  71.3 3.8 %collective-permute-start.2 = (bf16[4,1,48,256]{3,2,1,0:T(8,128)(2,1)S(1)}, bf16[4,1,48,256]{3,2,1,0:T(8,128)(2,1)S(1)}, u32[]{:S(2)}, u32[]{:S(2)}) collective-permute-start(bf16[4,1,48,256]{3,2,1,0:T(8,128)(2,1)S(1)} %get-tuple-element.68), channel_id=1, source_target_pairs={{0,2},{2,4},{4,6},{6,8},{8,10},{10,12},{12,14},{1,3},{3,5},{5,7},{... | collective-permute-start | bytes 294920 | tf_op jit(solution)/shard_map/ppermute | solution.py:15
  75.2 1.3 %collective-permute-start.3 = (bf16[4,1,48,256]{3,2,1,0:T(8,128)(2,1)S(1)}, bf16[4,1,48,256]{3,2,1,0:T(8,128)(2,1)S(1)}, u32[]{:S(2)}, u32[]{:S(2)}) collective-permute-start(bf16[4,1,48,256]{3,2,1,0:T(8,128)(2,1)S(1)} %get-tuple-element.69), channel_id=1, source_target_pairs={{2,0},{4,2},{6,4},{8,6},{10,8},{12,10},{14,12},{3,1},{5,3},{7,5},{... | collective-permute-start | bytes 294920 | tf_op jit(solution)/shard_map/ppermute | solution.py:18
  76.5 1.2 %collective-permute-done.2 = bf16[4,1,48,256]{3,2,1,0:T(8,128)(2,1)S(1)} collective-permute-done((bf16[4,1,48,256]{3,2,1,0:T(8,128)(2,1)S(1)}, bf16[4,1,48,256]{3,2,1,0:T(8,128)(2,1)S(1)}, u32[]{:S(2)}, u32[]{:S(2)}) %collective-permute-start.2) | collective-permute-done | bytes 98336 | tf_op jit(solution)/shard_map/ppermute | solution.py:15
  77.7 4.8 %collective-permute-done.3 = bf16[4,1,48,256]{3,2,1,0:T(8,128)(2,1)S(1)} collective-permute-done((bf16[4,1,48,256]{3,2,1,0:T(8,128)(2,1)S(1)}, bf16[4,1,48,256]{3,2,1,0:T(8,128)(2,1)S(1)}, u32[]{:S(2)}, u32[]{:S(2)}) %collective-permute-start.3) | collective-permute-done | bytes 98336 | tf_op jit(solution)/shard_map/ppermute | solution.py:18
  82.5 1.5 %fusion.32 = bf16[6,10,50,256]{3,2,1,0:T(8,128)(2,1)S(1)} fusion(bf16[4,1,48,256]{3,2,1,0:T(8,128)(2,1)S(1)} %collective-permute-done.3, bf16[4,8,48,256]{3,2,1,0:T(8,128)(2,1)S(1)} %all_gather.3, bf16[4,1,48,256]{3,2,1,0:T(8,128)(2,1)S(1)} %collective-permute-done.2), kind=kLoop, calls=%fused_computation.76 | loop fusion | flops 13056000 | bytes 2519040 | tf_op jit(solution)/shard_map/concatenate | solution.py:19
  84.9 3.8 %fusion.105 = (bf16[4,8,48,256]{3,2,1,0:T(8,128)(2,1)S(1)}, bf16[4,8,48,256]{3,2,1,0:T(8,128)(2,1)S(1)}, bf16[4,8,48,256]{3,2,1,0:T(8,128)(2,1)S(1)}, bf16[4,8,4...) fusion(bf16[6,10,50,256]{3,2,1,0:T(8,128)(2,1)S(1)} %fusion.32), kind=kLoop, calls=%fused_computation.158 | loop fusion | bytes 29884416 | tf_op jit(solution)/shard_map/slice | solution.py:70
  (77 shorter events, 17.0 us)
Async XLA Ops:
  0.0 0.7 copy-start
  2.9 11.7 %copy-start.17 = (f32[256]{0:T(256)S(1)}, f32[256]{0:T(256)}, u32[]{:S(2)}) copy-start(f32[256]{0:T(256)} %param.10) | copy-start | bytes 3076
  5.8 12.4 %collective-permute-start = (bf16[4,1,48,512]{3,2,1,0:T(8,128)(2,1)}, bf16[4,1,48,512]{3,2,1,0:T(8,128)(2,1)}, u32[]{:S(2)}, u32[]{:S(2)}) collective-permute-start(bf16[4,1,48,512]{3,2,1,0:T(8,128)(2,1)} %get-tuple-element.64), channel_id=1, source_target_pairs={{0,2},{2,4},{4,6},{6,8},{8,10},{10,12},{12,14},{1,3},{3,5},{5,7},{... | collective-permute-start | bytes 589832 | tf_op jit(solution)/shard_map/ppermute | solution.py:15
  11.3 8.6 %collective-permute-start.1 = (bf16[4,1,48,512]{3,2,1,0:T(8,128)(2,1)}, bf16[4,1,48,512]{3,2,1,0:T(8,128)(2,1)}, u32[]{:S(2)}, u32[]{:S(2)}) collective-permute-start(bf16[4,1,48,512]{3,2,1,0:T(8,128)(2,1)} %get-tuple-element.65), channel_id=1, source_target_pairs={{2,0},{4,2},{6,4},{8,6},{10,8},{12,10},{14,12},{3,1},{5,3},{7,5},{... | collective-permute-start | bytes 589832 | tf_op jit(solution)/shard_map/ppermute | solution.py:18
  40.6 2.3 %copy-start.3 = (bf16[4,8,48,512]{3,2,1,0:T(8,128)(2,1)S(1)}, bf16[4,8,48,512]{3,2,1,0:T(8,128)(2,1)}, u32[]{:S(2)}) copy-start(bf16[4,8,48,512]{3,2,1,0:T(8,128)(2,1)} %get-tuple-element.34) | copy-start | bytes 4718596
  40.6 2.3 %copy-start.4 = (bf16[4,8,48,512]{3,2,1,0:T(8,128)(2,1)S(1)}, bf16[4,8,48,512]{3,2,1,0:T(8,128)(2,1)}, u32[]{:S(2)}) copy-start(bf16[4,8,48,512]{3,2,1,0:T(8,128)(2,1)} %get-tuple-element.28) | copy-start | bytes 4718596
  50.0 1.4 %copy-start.2 = (bf16[4,8,48,512]{3,2,1,0:T(8,128)(2,1)S(1)}, bf16[4,8,48,512]{3,2,1,0:T(8,128)(2,1)}, u32[]{:S(2)}) copy-start(bf16[4,8,48,512]{3,2,1,0:T(8,128)(2,1)} %get-tuple-element.21) | copy-start | bytes 4718596
  51.4 1.1 %copy-start.6 = (f32[1536,128]{1,0:T(8,128)S(1)}, f32[1536,128]{1,0:T(8,128)}, u32[]{:S(2)}) copy-start(f32[1536,128]{1,0:T(8,128)} %fusion.109) | copy-start | bytes 2359300
  51.4 1.2 %copy-start.12 = (bf16[3,512,128]{2,1,0:T(8,128)(2,1)S(1)}, bf16[3,512,128]{2,1,0:T(8,128)(2,1)}, u32[]{:S(2)}) copy-start(bf16[3,512,128]{2,1,0:T(8,128)(2,1)} %get-tuple-element.11) | copy-start | bytes 1179652
  51.8 2.2 %copy-start.11 = (bf16[3,512,128]{2,1,0:T(8,128)(2,1)S(1)}, bf16[3,512,128]{2,1,0:T(8,128)(2,1)}, u32[]{:S(2)}) copy-start(bf16[3,512,128]{2,1,0:T(8,128)(2,1)} %get-tuple-element.9) | copy-start | bytes 1179652
  55.4 1.2 %copy-start.10 = (bf16[3,512,128]{2,1,0:T(8,128)(2,1)S(1)}, bf16[3,512,128]{2,1,0:T(8,128)(2,1)}, u32[]{:S(2)}) copy-start(bf16[3,512,128]{2,1,0:T(8,128)(2,1)} %get-tuple-element.8) | copy-start | bytes 1179652
  56.6 1.5 %copy-start.9 = (bf16[3,512,128]{2,1,0:T(8,128)(2,1)S(1)}, bf16[3,512,128]{2,1,0:T(8,128)(2,1)}, u32[]{:S(2)}) copy-start(bf16[3,512,128]{2,1,0:T(8,128)(2,1)} %get-tuple-element.7) | copy-start | bytes 1179652
  58.0 1.5 %copy-start.8 = (bf16[3,512,128]{2,1,0:T(8,128)(2,1)S(1)}, bf16[3,512,128]{2,1,0:T(8,128)(2,1)}, u32[]{:S(2)}) copy-start(bf16[3,512,128]{2,1,0:T(8,128)(2,1)} %get-tuple-element.6) | copy-start | bytes 1179652
  59.5 1.5 %copy-start.7 = (bf16[1536,512]{1,0:T(8,128)(2,1)S(1)}, bf16[1536,512]{1,0:T(8,128)(2,1)}, u32[]{:S(2)}) copy-start(bf16[1536,512]{1,0:T(8,128)(2,1)} %concatenate.62) | copy-start | bytes 4718596
  59.5 1.9 %copy-start.13 = (bf16[4,8,48,512]{3,2,1,0:T(8,128)(2,1)S(1)}, bf16[4,8,48,512]{3,2,1,0:T(8,128)(2,1)}, u32[]{:S(2)}) copy-start(bf16[4,8,48,512]{3,2,1,0:T(8,128)(2,1)} %get-tuple-element.16) | copy-start | bytes 4718596
  59.5 2.3 %copy-start.14 = (bf16[4,8,48,512]{3,2,1,0:T(8,128)(2,1)S(1)}, bf16[4,8,48,512]{3,2,1,0:T(8,128)(2,1)}, u32[]{:S(2)}) copy-start(bf16[4,8,48,512]{3,2,1,0:T(8,128)(2,1)} %get-tuple-element.17) | copy-start | bytes 4718596
  59.5 2.4 %copy-start.16 = (bf16[3,512,128]{2,1,0:T(8,128)(2,1)S(1)}, bf16[3,512,128]{2,1,0:T(8,128)(2,1)}, u32[]{:S(2)}) copy-start(bf16[3,512,128]{2,1,0:T(8,128)(2,1)} %get-tuple-element.13) | copy-start | bytes 1179652
  61.9 1.7 %copy-start.5 = (f32[1536,128]{1,0:T(8,128)S(1)}, f32[1536,128]{1,0:T(8,128)}, u32[]{:S(2)}) copy-start(f32[1536,128]{1,0:T(8,128)} %fusion.110) | copy-start | bytes 2359300
  71.3 6.4 %collective-permute-start.2 = (bf16[4,1,48,256]{3,2,1,0:T(8,128)(2,1)S(1)}, bf16[4,1,48,256]{3,2,1,0:T(8,128)(2,1)S(1)}, u32[]{:S(2)}, u32[]{:S(2)}) collective-permute-start(bf16[4,1,48,256]{3,2,1,0:T(8,128)(2,1)S(1)} %get-tuple-element.68), channel_id=1, source_target_pairs={{0,2},{2,4},{4,6},{6,8},{8,10},{10,12},{12,14},{1,3},{3,5},{5,7},{... | collective-permute-start | bytes 294920 | tf_op jit(solution)/shard_map/ppermute | solution.py:15
  75.2 7.4 %collective-permute-start.3 = (bf16[4,1,48,256]{3,2,1,0:T(8,128)(2,1)S(1)}, bf16[4,1,48,256]{3,2,1,0:T(8,128)(2,1)S(1)}, u32[]{:S(2)}, u32[]{:S(2)}) collective-permute-start(bf16[4,1,48,256]{3,2,1,0:T(8,128)(2,1)S(1)} %get-tuple-element.69), channel_id=1, source_target_pairs={{2,0},{4,2},{6,4},{8,6},{10,8},{12,10},{14,12},{3,1},{5,3},{7,5},{... | collective-permute-start | bytes 294920 | tf_op jit(solution)/shard_map/ppermute | solution.py:18
  84.9 3.8 %copy-start.15 = (bf16[27,64,256]{2,1,0:T(8,128)(2,1)S(1)}, bf16[27,64,256]{2,1,0:T(8,128)(2,1)}, u32[]{:S(2)}) copy-start(bf16[27,64,256]{2,1,0:T(8,128)(2,1)} %param.11) | copy-start | bytes 2654212
  96.5 3.1 %copy-start.1 = (bf16[18,512]{1,0:T(8,128)(2,1)S(1)}, bf16[18,512]{1,0:T(8,128)(2,1)}, u32[]{:S(2)}) copy-start(bf16[18,512]{1,0:T(8,128)(2,1)} %param.7) | copy-start | bytes 55300
where the time goes:
time: 100 us; the launch traced here: 99.7 us
  local copies, waits for them, and re-layouts  30.4 us (30%)
  matrix products  26.8 us (27%)
  other arithmetic  16.6 us (17%)
  starting transfers between devices  11.9 us (12%)
  waiting for transfers between devices  7.72 us (8%)
  blocking collectives  5.73 us (6%)
    dot_general x9, matrix products, up_conv(): jnp.dot(joined, stacked[3 * tap_time + tap_row], preferred_element_type=j...  15.9 us
    slice x2, local copies, waits for them, and re-layouts, up_conv(): padded[tap_time:tap_time + frame_count, tap_row:tap_row + height, tap_col...  12.7 us
    dot_general x27, matrix products, out_conv(): lax.dot_general(piece, kernel[9 * tap_time + 3 * tap_row + tap_col], (((1...  9.83 us
    concatenate x5, other arithmetic, up_conv(): joined = jnp.concatenate(pieces, axis=-1).reshape(-1, 3 * in_width)  9.56 us
    ppermute x2, starting transfers between devices, extended(): lax.ppermute(lax.slice_in_dim(block, block.shape[dim] - width, None, axis...  9.35 us
    ppermute x2, waiting for transfers between devices, extended(): lax.ppermute(lax.slice_in_dim(block, 0, width, axis=dim), axis, backward)  6.48 us
    concatenate x3, other arithmetic, extended(): block = jnp.concatenate([low, block, high], axis=dim)  5.8 us
    slice x2, local copies, waits for them, and re-layouts, out_conv(): padded[tap_time:tap_time + frame_count, tap_row:tap_row + height, tap_col...  4.64 us
  transfers between devices with their start and end apart: 4, of which 3 were waited for; matrix products, arithmetic and copies ran while one was open for 6% of the time, Pallas kernels for 0%

commit v1 on v0

v1 whole, which is shorter than its diff:
```python
import functools

import jax
import jax.numpy as jnp
from jax import lax
from jax.experimental import pallas as pl
from jax.experimental.pallas import tpu as pltpu
from jax.sharding import PartitionSpec as P

BITS = 18
EPS = 1e-06
F32 = jnp.float32
BF16 = jnp.bfloat16
VMEM_LIMIT = 48 * 1024 * 1024


def silu(v):
    return 0.5 * v * (1.0 + jnp.tanh(0.5 * v))


def latent_rows(rows, in_proj, gain):
    cols = rows[0].shape[1]
    count = len(rows)
    wide = jnp.concatenate([jnp.broadcast_to(row, (cols, cols)) for row in rows], axis=0)
    sub = lax.broadcasted_iota(jnp.int32, (count, cols, cols), 1).reshape(count * cols, cols)
    lane = lax.broadcasted_iota(jnp.int32, (count * cols, cols), 1)
    picked = jnp.where(sub == lane, wide, 0).astype(F32)
    column = jnp.sum(picked, axis=1, keepdims=True).astype(jnp.int32)
    spread = jnp.broadcast_to(column, (count * cols, BITS))
    shift = lax.broadcasted_iota(jnp.int32, (count * cols, BITS), 1)
    bits = ((jnp.right_shift(spread, shift) & 1) * 2 - 1).astype(F32).astype(BF16)
    latent = jnp.dot(bits, in_proj, preferred_element_type=F32)
    mean = jnp.mean(latent * latent, axis=1, keepdims=True)
    return silu(latent * lax.rsqrt(mean + EPS) * gain)


def prep_kernel(codes_ref, proj_ref, gain_ref, up_hbm, out_hbm, w1_ref, w2_ref, act_ref, up_ref, tap_ref, sems):
    copies = [
        pltpu.make_async_copy(up_hbm.at[pl.ds(9 * a, 9)], up_ref.at[pl.ds(9 * a, 9)], sems.at[a])
        for a in range(3)
    ]
    copies.append(pltpu.make_async_copy(out_hbm, tap_ref, sems.at[3]))
    for copy in copies:
        copy.start()

    frames, rows, cols = codes_ref.shape
    size = frames * cols
    for r in range(rows):
        act = latent_rows([codes_ref[t, r : r + 1, :] for t in range(frames)], proj_ref[...], gain_ref[...])
        act_ref[r] = act.astype(BF16)

    width = up_ref.shape[1]
    out_w = up_ref.shape[2]
    step = 32
    for a in range(3):
        copies[a].wait()

        @pl.loop(0, width // step)
        def _(i, a=a):
            k = pl.multiple_of(i * step, step)
            tap = [[up_ref[9 * a + 3 * b + c, pl.ds(k, step), :].astype(F32) for c in range(3)] for b in range(3)]
            row_sets = (
                ([tap[0][c] + tap[1][c] for c in range(3)], tap[0]),
                (tap[2], [tap[1][c] + tap[2][c] for c in range(3)]),
            )
            for half in range(2):
                for py in range(2):
                    x = row_sets[half][py]
                    parts = (x[0], x[1] + x[2], x[0] + x[1], x[2])
                    for v in range(4):
                        w1_ref[a, pl.ds(half * width + k, step), pl.ds((4 * py + v) * out_w, out_w)] = parts[v].astype(BF16)

    copies[3].wait()
    ow, ch = tap_ref.shape[1], tap_ref.shape[2]
    zero = jnp.zeros((ow, ch), BF16)
    for ab in range(9):
        w = [tap_ref[3 * ab + c] for c in range(3)]
        table = ((w[1], w[2]), (w[0], w[1]), (zero, w[0]), (w[2], zero))
        for n in range(4):
            for k in range(2):
                w2_ref[ab, pl.ds(n * ow, ow), pl.ds(k * ch, ch)] = table[n][k]


def shifted(x, cols, amount):
    rows, lanes = x.shape
    place = lax.broadcasted_iota(jnp.int32, (rows // cols, cols, lanes), 1).reshape(rows, lanes)
    moved = pltpu.roll(x, amount % rows, 0)
    return jnp.where(place == (0 if amount == 1 else cols - 1), 0.0, moved)


def reach(frames, cols, a):
    need = (frames - 2 + a) * cols
    return -(-need // 16) * 16


def hidden_kernel(axis, lo_ref, hi_ref, proj_ref, gain_ref, own_ref, w1_ref, h_ref, act_ref, acc_ref):
    frames, rows, cols = lo_ref.shape
    size = frames * cols
    width = own_ref.shape[2]
    place = lax.axis_index(axis)
    last = lax.axis_size(axis) - 1
    for edge, (src, row, ok) in enumerate(((lo_ref, rows - 1, place > 0), (hi_ref, 0, place < last))):
        act = latent_rows([src[t, row : row + 1, :] for t in range(frames)], proj_ref[...], gain_ref[...])
        act_ref[edge * (rows + 1)] = jnp.where(ok, act, 0.0).astype(BF16)
    act_ref[pl.ds(1, rows)] = own_ref[...]

    pairs = rows + 1

    @pl.loop(0, 4)
    def _(n):
        lanes = pl.ds(pl.multiple_of(n * 256, 256), 256)
        for a in (2, 1, 0):
            m = reach(frames, cols, a)
            total = None
            for half in range(2):
                part = jnp.dot(
                    act_ref[pl.ds(half, pairs), pl.ds(0, m), :].reshape(pairs * m, width),
                    w1_ref[a, pl.ds(half * width, width), lanes],
                    preferred_element_type=F32,
                )
                total = part if total is None else total + part
            total = total.reshape(pairs, m, 256)
            if a == 2:
                acc_ref[...] = total
            else:
                skip = (2 - a) * cols
                acc_ref[:, pl.ds(skip, size - skip), :] += total[:, : size - skip, :]
        full = acc_ref[...].reshape(pairs * size, 256)
        left, right = full[:, :128], full[:, 128:]
        px = n % 2

        @pl.when(px == 0)
        def _():
            h_ref[:, pl.ds(pl.multiple_of(n * 128, 128), 128)] = (right + shifted(left, cols, 1)).astype(BF16)

        @pl.when(px == 1)
        def _():
            h_ref[:, pl.ds(pl.multiple_of(n * 128, 128), 128)] = (left + shifted(right, cols, -1)).astype(BF16)


def out_kernel_body(axis, frames, cols, g_ref, gain_ref, w2_ref, o_ref, norm_ref, acc_ref, mix_ref):
    size = frames * cols
    pairs = g_ref.shape[1] // size
    half_ch = g_ref.shape[2] // 4
    place = lax.axis_index(axis)
    last = lax.axis_size(axis) - 1
    for q in range(pairs):
        for py in range(2):
            for px in range(2):
                n = 2 * py + px
                x = [g_ref[s, pl.ds(q * size, size), pl.ds(n * half_ch, half_ch)].astype(F32) for s in range(2)]
                mean = jnp.sum(x[0] * x[0] + x[1] * x[1], axis=1, keepdims=True) / (2 * half_ch)
                scale = lax.rsqrt(mean + EPS)
                if q == 0 and py == 0:
                    scale = jnp.where(place > 0, scale, 0.0)
                if q == pairs - 1 and py == 1:
                    scale = jnp.where(place < last, scale, 0.0)
                for s in range(2):
                    value = silu(x[s] * scale * gain_ref[:, pl.ds(s * half_ch, half_ch)])
                    norm_ref[2 * q + py, :, pl.ds((2 * px + s) * half_ch, half_ch)] = value.astype(BF16)

    height = 2 * (pairs - 1)
    depth = norm_ref.shape[2]
    for a in (2, 1, 0):
        m = reach(frames, cols, a)
        total = None
        for b in range(3):
            part = lax.dot_general(
                norm_ref[pl.ds(b, height), pl.ds(0, m), :].reshape(height * m, depth),
                w2_ref[3 * a + b],
                (((1,), (1,)), ((), ())),
                preferred_element_type=F32,
            )
            total = part if total is None else total + part
        total = total.reshape(height, m, 256)
        if a == 2:
            acc_ref[...] = total
        else:
            skip = (2 - a) * cols
            acc_ref[:, pl.ds(skip, size - skip), :] += total[:, : size - skip, :]

    ow = o_ref.shape[3]
    for y in range(height):
        full = acc_ref[y]
        side = full[:, 128:]
        lane = lax.broadcasted_iota(jnp.int32, side.shape, 1)
        both = full[:, :128] + jnp.where(lane < ow, shifted(side, cols, 1), shifted(side, cols, -1))
        mix_ref[pl.ds(0, size, stride=2), :] = both
        mix_ref[pl.ds(1, size, stride=2), :] = pltpu.roll(both, ow, 1)
        result = mix_ref[...][:, :ow].astype(BF16)
        for t in range(frames):
            o_ref[t, y] = result[2 * cols * t : 2 * cols * (t + 1)]


def params():
    return pltpu.CompilerParams(vmem_limit_bytes=VMEM_LIMIT)


def vmem():
    return pl.BlockSpec(memory_space=pltpu.VMEM)


def body(codes, in_proj, gain_up, up_kernel, gain_res, out_kernel):
    frames, rows, cols = codes.shape
    size = frames * cols
    taps, width, share = up_kernel.shape
    ow, ch = out_kernel.shape[1:]
    count = lax.axis_size("rows")
    forward = [(i, i + 1) for i in range(count - 1)]
    backward = [(i + 1, i) for i in range(count - 1)]
    low = lax.ppermute(codes, "rows", forward)
    high = lax.ppermute(codes, "rows", backward)
    gain_up = gain_up.reshape(1, -1)
    gain_res = gain_res.reshape(1, -1)

    hbm = pl.BlockSpec(memory_space=pl.ANY)
    w1, w2, act = pl.pallas_call(
        prep_kernel,
        out_shape=(
            pltpu.VMEM((3, 2 * width, 8 * share), BF16),
            pltpu.VMEM((9, 4 * ow, 2 * ch), BF16),
            pltpu.VMEM((rows, size, width), BF16),
        ),
        in_specs=[vmem(), vmem(), vmem(), hbm, hbm],
        out_specs=(vmem(), vmem(), vmem()),
        scratch_shapes=[
            pltpu.VMEM(up_kernel.shape, BF16),
            pltpu.VMEM(out_kernel.shape, BF16),
            pltpu.SemaphoreType.DMA((4,)),
        ],
        compiler_params=params(),
        cost_estimate=pl.CostEstimate(flops=10**9, bytes_accessed=2 * 10**7, transcendentals=0),
        name="prep",
    )(codes, in_proj, gain_up, up_kernel, out_kernel)

    pairs = rows + 1
    hidden = pl.pallas_call(
        functools.partial(hidden_kernel, "rows"),
        out_shape=jax.ShapeDtypeStruct((pairs * size, 4 * share), BF16),
        in_specs=[vmem()] * 6,
        out_specs=vmem(),
        scratch_shapes=[
            pltpu.VMEM((rows + 2, size, width), BF16),
            pltpu.VMEM((pairs, size, 256), F32),
        ],
        compiler_params=params(),
        name="hidden",
    )(low, high, in_proj, gain_up, act, w1)

    gathered = lax.all_gather(hidden, "section", axis=0)

    return pl.pallas_call(
        functools.partial(out_kernel_body, "rows", frames, cols),
        out_shape=jax.ShapeDtypeStruct((frames, 2 * rows, 2 * cols, ow), BF16),
        in_specs=[vmem()] * 3,
        out_specs=vmem(),
        scratch_shapes=[
            pltpu.VMEM((2 * pairs, size, 2 * ch), BF16),
            pltpu.VMEM((2 * rows, size, 256), F32),
            pltpu.VMEM((2 * size, 128), F32),
        ],
        compiler_params=params(),
        name="decode",
    )(gathered, gain_res, w2)


def solution(mesh):
    in_specs = (
        P("clip", "rows", None),
        P(),
        P(),
        P(None, None, "section"),
        P(),
        P(None, "section", None),
    )
    out_specs = P("clip", "rows", None, "section")
    return jax.shard_map(body, mesh=mesh, in_specs=in_specs, out_specs=out_specs, check_vma=False)
```

time: 100 us -> 25.9 us (0.26)
  the two profiles are of different devices: /device:TPU:0 before, /device:TPU:9 now
where the time goes in v1:
time: 25.9 us; the launch traced here: 25.6 us
  Pallas kernels  13.2 us (51%)
  starting transfers between devices  6.3 us (24%)
  blocking collectives  3.37 us (13%)
  local copies, waits for them, and re-layouts  2.67 us (10%)
    pallas_call x1, Pallas kernels, body(): pl.pallas_call(functools.partial(hidden_kernel, 'rows'), out_shape=jax.Sh...  6.51 us
    pallas_call x1, Pallas kernels, body(): pl.pallas_call(prep_kernel, out_shape=(pltpu.VMEM((3, 2 * width, 8 * shar...  3.72 us
    all_gather x1, blocking collectives, body(): gathered = lax.all_gather(hidden, 'section', axis=0)  3.37 us
    ppermute x1, starting transfers between devices, body(): low = lax.ppermute(codes, 'rows', forward)  3.24 us
    ppermute x1, starting transfers between devices, body(): high = lax.ppermute(codes, 'rows', backward)  3.06 us
    pallas_call x1, Pallas kernels, body(): pl.pallas_call(functools.partial(out_kernel_body, 'rows', frames, cols),...  3 us
    unnamed x8, local copies, waits for them, and re-layouts  2.67 us
  transfers between devices with their start and end apart: 2, of which 0 were waited for; matrix products, arithmetic and copies ran while one was open for 0% of the time, Pallas kernels for 15%

profile of v1, /device:TPU:9, one launch (start us, length us, event | category | flops | bytes accessed | tf_op | source)
XLA Modules:
  0.0 25.6 jit_solution(17133547108743353569)
XLA Ops:
  0.0 0.0 copy-start.1
  0.0 0.0 copy-start.2
  0.0 3.2 %collective-permute-start = (s32[4,4,24]{2,1,0:T(4,128)}, s32[4,4,24]{2,1,0:T(4,128)S(1)}, u32[]{:S(2)}, u32[]{:S(2)}) collective-permute-start(s32[4,4,24]{2,1,0:T(4,128)} %codes_ref.1), channel_id=1, source_target_pairs={{0,2},{2,4},{4,6},{6,8},{8,10},{10,12},{12,14},{1,3},{3,5},{5,7},{... | collective-permute-start | bytes 4616 | tf_op jit(solution)/shard_map/ppermute | solution.py:211
  3.3 3.1 %collective-permute-start.1 = (s32[4,4,24]{2,1,0:T(4,128)}, s32[4,4,24]{2,1,0:T(4,128)S(1)}, u32[]{:S(2)}, u32[]{:S(2)}) collective-permute-start(s32[4,4,24]{2,1,0:T(4,128)} %codes_ref.1), channel_id=1, source_target_pairs={{2,0},{4,2},{6,4},{8,6},{10,8},{12,10},{14,12},{3,1},{5,3},{7,5},{... | collective-permute-start | bytes 4616 | tf_op jit(solution)/shard_map/ppermute | solution.py:212
  6.3 3.7 %prep.1 = (bf16[3,1024,1024]{2,1,0:T(8,128)(2,1)S(1)}, bf16[9,256,512]{2,1,0:T(8,128)(2,1)S(1)}, bf16[4,96,512]{2,1,0:T(8,128)(2,1)S(1)}) custom-call(s32[4,4,24]{2,1,0:T(4,128)} %codes_ref.1, bf16[18,512]{1,0:T(8,128)(2,1)} %proj_ref.3, f32[1,512]{1,0:T(1,128)} %bitcast.4, bf16[27,512,128]{2,1,0:T(8,128)(2,1)} %up_hbm.1, bf16[27,64,256]{2,1,0:T(8,128)(2,1)} %out_hbm.1), custom_call_target="tpu_custom_call" | custom-call | flops 1000000000 | bytes 20000000 | tf_op jit(solution)/shard_map/prep/pallas_call | solution.py:217
  10.0 0.0 copy-start
  10.1 2.7 %copy-done = bf16[3,1024,1024]{2,1,0:T(8,128)(2,1)} copy-done((bf16[3,1024,1024]{2,1,0:T(8,128)(2,1)}, bf16[3,1024,1024]{2,1,0:T(8,128)(2,1)S(1)}, u32[]{:S(2)}) %copy-start) | copy-done | bytes 6291480
  12.7 0.0 collective-permute-done.lo_ref
  12.7 0.0 collective-permute-done.1.hi_ref
  12.7 0.0 copy-done.1
  12.7 0.0 copy-done.2
  12.7 0.0 copy-start.3
  12.7 6.5 %hidden.1 = bf16[480,512]{1,0:T(8,128)(2,1)S(1)} custom-call(s32[4,4,24]{2,1,0:T(4,128)S(1)} %collective-permute-done.lo_ref, s32[4,4,24]{2,1,0:T(4,128)S(1)} %collective-permute-done.1.hi_ref, bf16[18,512]{1,0:T(8,128)(2,1)S(1)} %copy-done.1, f32[1,512]{1,0:T(1,128)S(1)} %bitcast.5, bf16[4,96,512]{2,1,0:T(8,128)(2,1)S(1)} %get-tuple-element.8.own_ref, ...), custom_call_target="tpu_custom_call" | custom-call | tf_op jit(solution)/shard_map/hidden/pallas_call | solution.py:237
  19.3 3.4 %all-gather = bf16[960,512]{1,0:T(8,128)(2,1)S(1)} all-gather(bf16[480,512]{1,0:T(8,128)(2,1)S(1)} %hidden.1), channel_id=2, replica_groups=mesh['clip'=2,'rows'=8,'section'=2] {'section'}, dimensions={0}, use_global_device_ids=true | all-gather | bytes 1474560 | tf_op jit(solution)/shard_map/all_gather | solution.py:250
  22.6 0.0 copy-done.3
  22.6 3.0 %decode.1 = bf16[4,8,48,64]{3,2,1,0:T(8,128)(2,1)} custom-call(bf16[2,480,512]{2,1,0:T(8,128)(2,1)S(1)} %bitcast.3, f32[1,256]{1,0:T(1,128)S(1)} %bitcast.6, bf16[9,256,512]{2,1,0:T(8,128)(2,1)S(1)} %get-tuple-element.10.w2_ref), custom_call_target="tpu_custom_call" | custom-call | tf_op jit(solution)/shard_map/decode/pallas_call | solution.py:252
Async XLA Ops:
  0.0 12.7 %copy-start.1 = (bf16[18,512]{1,0:T(8,128)(2,1)S(1)}, bf16[18,512]{1,0:T(8,128)(2,1)}, u32[]{:S(2)}) copy-start(bf16[18,512]{1,0:T(8,128)(2,1)} %proj_ref.3) | copy-start | bytes 55300
  0.0 12.7 %copy-start.2 = (f32[512]{0:T(512)S(1)}, f32[512]{0:T(512)}, u32[]{:S(2)}) copy-start(f32[512]{0:T(512)} %param.8) | copy-start | bytes 6148
  0.0 12.7 %collective-permute-start = (s32[4,4,24]{2,1,0:T(4,128)}, s32[4,4,24]{2,1,0:T(4,128)S(1)}, u32[]{:S(2)}, u32[]{:S(2)}) collective-permute-start(s32[4,4,24]{2,1,0:T(4,128)} %codes_ref.1), channel_id=1, source_target_pairs={{0,2},{2,4},{4,6},{6,8},{8,10},{10,12},{12,14},{1,3},{3,5},{5,7},{... | collective-permute-start | bytes 4616 | tf_op jit(solution)/shard_map/ppermute | solution.py:211
  3.3 9.5 %collective-permute-start.1 = (s32[4,4,24]{2,1,0:T(4,128)}, s32[4,4,24]{2,1,0:T(4,128)S(1)}, u32[]{:S(2)}, u32[]{:S(2)}) collective-permute-start(s32[4,4,24]{2,1,0:T(4,128)} %codes_ref.1), channel_id=1, source_target_pairs={{2,0},{4,2},{6,4},{8,6},{10,8},{12,10},{14,12},{3,1},{5,3},{7,5},{... | collective-permute-start | bytes 4616 | tf_op jit(solution)/shard_map/ppermute | solution.py:212
  10.0 2.7 %copy-start = (bf16[3,1024,1024]{2,1,0:T(8,128)(2,1)}, bf16[3,1024,1024]{2,1,0:T(8,128)(2,1)S(1)}, u32[]{:S(2)}) copy-start(bf16[3,1024,1024]{2,1,0:T(8,128)(2,1)S(1)} %get-tuple-element.9.w1_ref) | copy-start | bytes 18874372
  12.7 9.9 %copy-start.3 = (f32[256]{0:T(256)S(1)}, f32[256]{0:T(256)}, u32[]{:S(2)}) copy-start(f32[256]{0:T(256)} %param.10) | copy-start | bytes 3076

commit v2 on v1

--- a/solution.py
+++ b/solution.py
@@ -11,7 +11,7 @@
 EPS = 1e-06
 F32 = jnp.float32
 BF16 = jnp.bfloat16
-VMEM_LIMIT = 48 * 1024 * 1024
+MIB = 1024 * 1024
 
 
 def silu(v):
@@ -71,14 +71,17 @@
                         w1_ref[a, pl.ds(half * width + k, step), pl.ds((4 * py + v) * out_w, out_w)] = parts[v].astype(BF16)
 
     copies[3].wait()
-    ow, ch = tap_ref.shape[1], tap_ref.shape[2]
-    zero = jnp.zeros((ow, ch), BF16)
-    for ab in range(9):
-        w = [tap_ref[3 * ab + c] for c in range(3)]
-        table = ((w[1], w[2]), (w[0], w[1]), (zero, w[0]), (w[2], zero))
-        for n in range(4):
-            for k in range(2):
-                w2_ref[ab, pl.ds(n * ow, ow), pl.ds(k * ch, ch)] = table[n][k]
+    ow, half_ch = tap_ref.shape[1], tap_ref.shape[2] // 2
+    zero = jnp.zeros((ow, half_ch), BF16)
+    section = lax.axis_index("section")
+    for slot, part in enumerate((section, 1 - section)):
+        lanes = pl.ds(pl.multiple_of(part * half_ch, half_ch), half_ch)
+        for ab in range(9):
+            w = [tap_ref[3 * ab + c, :, lanes] for c in range(3)]
+            table = ((w[1], w[2]), (w[0], w[1]), (zero, w[0]), (w[2], zero))
+            for n in range(4):
+                for px in range(2):
+                    w2_ref[ab, pl.ds(n * ow, ow), pl.ds((2 * px + slot) * half_ch, half_ch)] = table[n][px]
 
 
 def shifted(x, cols, amount):
@@ -138,17 +141,19 @@
             h_ref[:, pl.ds(pl.multiple_of(n * 128, 128), 128)] = (left + shifted(right, cols, -1)).astype(BF16)
 
 
-def out_kernel_body(axis, frames, cols, g_ref, gain_ref, w2_ref, o_ref, norm_ref, acc_ref, mix_ref):
-    size = frames * cols
-    pairs = g_ref.shape[1] // size
-    half_ch = g_ref.shape[2] // 4
+def out_kernel_body(axis, frames, cols, own_ref, other_ref, gain_ref, w2_ref, o_ref, norm_ref, acc_ref, mix_ref):
+    size = frames * cols
+    pairs = own_ref.shape[0] // size
+    half_ch = own_ref.shape[1] // 4
+    section = lax.axis_index("section")
+    gains = [gain_ref[:, pl.ds(pl.multiple_of(k * half_ch, half_ch), half_ch)] for k in (section, 1 - section)]
     place = lax.axis_index(axis)
     last = lax.axis_size(axis) - 1
     for q in range(pairs):
         for py in range(2):
             for px in range(2):
                 n = 2 * py + px
-                x = [g_ref[s, pl.ds(q * size, size), pl.ds(n * half_ch, half_ch)].astype(F32) for s in range(2)]
+                x = [r[pl.ds(q * size, size), pl.ds(n * half_ch, half_ch)].astype(F32) for r in (own_ref, other_ref)]
                 mean = jnp.sum(x[0] * x[0] + x[1] * x[1], axis=1, keepdims=True) / (2 * half_ch)
                 scale = lax.rsqrt(mean + EPS)
                 if q == 0 and py == 0:
@@ -156,7 +161,7 @@
                 if q == pairs - 1 and py == 1:
                     scale = jnp.where(place < last, scale, 0.0)
                 for s in range(2):
-                    value = silu(x[s] * scale * gain_ref[:, pl.ds(s * half_ch, half_ch)])
+                    value = silu(x[s] * scale * gains[s])
                     norm_ref[2 * q + py, :, pl.ds((2 * px + s) * half_ch, half_ch)] = value.astype(BF16)
 
     height = 2 * (pairs - 1)
@@ -192,8 +197,12 @@
             o_ref[t, y] = result[2 * cols * t : 2 * cols * (t + 1)]
 
 
-def params():
-    return pltpu.CompilerParams(vmem_limit_bytes=VMEM_LIMIT)
+def params(mib):
+    return pltpu.CompilerParams(vmem_limit_bytes=mib * MIB)
+
+
+def in_vmem(*arrays):
+    return tuple(pltpu.with_memory_space_constraint(x, pltpu.VMEM) for x in arrays)
 
 
 def vmem():
@@ -228,40 +237,41 @@
             pltpu.VMEM(out_kernel.shape, BF16),
             pltpu.SemaphoreType.DMA((4,)),
         ],
-        compiler_params=params(),
+        compiler_params=params(12),
         cost_estimate=pl.CostEstimate(flops=10**9, bytes_accessed=2 * 10**7, transcendentals=0),
         name="prep",
     )(codes, in_proj, gain_up, up_kernel, out_kernel)
 
     pairs = rows + 1
+    w1, w2, act, low, high = in_vmem(w1, w2, act, low, high)
     hidden = pl.pallas_call(
         functools.partial(hidden_kernel, "rows"),
-        out_shape=jax.ShapeDtypeStruct((pairs * size, 4 * share), BF16),
+        out_shape=pltpu.VMEM((pairs * size, 4 * share), BF16),
         in_specs=[vmem()] * 6,
         out_specs=vmem(),
         scratch_shapes=[
             pltpu.VMEM((rows + 2, size, width), BF16),
             pltpu.VMEM((pairs, size, 256), F32),
         ],
-        compiler_params=params(),
+        compiler_params=params(8),
         name="hidden",
     )(low, high, in_proj, gain_up, act, w1)
 
-    gathered = lax.all_gather(hidden, "section", axis=0)
+    other = lax.ppermute(hidden, "section", [(0, 1), (1, 0)])
 
     return pl.pallas_call(
         functools.partial(out_kernel_body, "rows", frames, cols),
         out_shape=jax.ShapeDtypeStruct((frames, 2 * rows, 2 * cols, ow), BF16),
-        in_specs=[vmem()] * 3,
+        in_specs=[vmem()] * 4,
         out_specs=vmem(),
         scratch_shapes=[
             pltpu.VMEM((2 * pairs, size, 2 * ch), BF16),
             pltpu.VMEM((2 * rows, size, 256), F32),
             pltpu.VMEM((2 * size, 128), F32),
         ],
-        compiler_params=params(),
+        compiler_params=params(12),
         name="decode",
-    )(gathered, gain_res, w2)
+    )(*in_vmem(hidden, other), gain_res, w2)
 
 
 def solution(mesh):

time: 25.9 us -> 24.7 us (0.954)
  the two profiles are of different devices: /device:TPU:9 before, /device:TPU:13 now
where the time goes in v2:
time: 24.7 us; the launch traced here: 24.3 us
  Pallas kernels  10 us (40%)
  starting transfers between devices  7.47 us (30%)
  local copies, waits for them, and re-layouts  5.28 us (21%)
  waiting for transfers between devices  1.5 us (6%)
    unnamed x12, local copies, waits for them, and re-layouts  5.28 us
    pallas_call x1, Pallas kernels, body(): pl.pallas_call(functools.partial(hidden_kernel, 'rows'), out_shape=pltpu....  3.7 us
    pallas_call x1, Pallas kernels, body(): pl.pallas_call(prep_kernel, out_shape=(pltpu.VMEM((3, 2 * width, 8 * shar...  3.27 us
    ppermute x1, starting transfers between devices, body(): low = lax.ppermute(codes, 'rows', forward)  3.11 us
    ppermute x1, starting transfers between devices, body(): high = lax.ppermute(codes, 'rows', backward)  3.06 us
    pallas_call x1, Pallas kernels, body(): pl.pallas_call(functools.partial(out_kernel_body, 'rows', frames, cols),...  3.04 us
    ppermute x1, waiting for transfers between devices, body(): other = lax.ppermute(hidden, 'section', [(0, 1), (1, 0)])  1.49 us
    ppermute x1, starting transfers between devices, body(): other = lax.ppermute(hidden, 'section', [(0, 1), (1, 0)])  1.3 us
  transfers between devices with their start and end apart: 3, of which 1 were waited for; matrix products, arithmetic and copies ran while one was open for 0% of the time, Pallas kernels for 13%

profile of v2, /device:TPU:13, one launch (start us, length us, event | category | flops | bytes accessed | tf_op | source)
XLA Modules:
  0.0 24.3 jit_solution(1817534326397896756)
XLA Ops:
  0.0 3.1 %collective-permute-start = (s32[4,4,24]{2,1,0:T(4,128)}, s32[4,4,24]{2,1,0:T(4,128)S(1)}, u32[]{:S(2)}, u32[]{:S(2)}) collective-permute-start(s32[4,4,24]{2,1,0:T(4,128)} %codes_ref.1), channel_id=1, source_target_pairs={{0,2},{2,4},{4,6},{6,8},{8,10},{10,12},{12,14},{1,3},{3,5},{5,7},{... | collective-permute-start | bytes 4616 | tf_op jit(solution)/shard_map/ppermute | solution.py:220
  3.1 3.1 %collective-permute-start.1 = (s32[4,4,24]{2,1,0:T(4,128)}, s32[4,4,24]{2,1,0:T(4,128)S(1)}, u32[]{:S(2)}, u32[]{:S(2)}) collective-permute-start(s32[4,4,24]{2,1,0:T(4,128)} %codes_ref.1), channel_id=1, source_target_pairs={{2,0},{4,2},{6,4},{8,6},{10,8},{12,10},{14,12},{3,1},{5,3},{7,5},{... | collective-permute-start | bytes 4616 | tf_op jit(solution)/shard_map/ppermute | solution.py:221
  6.2 0.0 copy-start
  6.2 2.0 %copy-done = bf16[27,512,128]{2,1,0:T(8,128)(2,1)S(1)} copy-done((bf16[27,512,128]{2,1,0:T(8,128)(2,1)S(1)}, bf16[27,512,128]{2,1,0:T(8,128)(2,1)}, u32[]{:S(2)}) %copy-start) | copy-done | bytes 3538968
  8.2 0.0 copy-start.1
  8.2 1.2 %copy-done.1 = bf16[27,64,256]{2,1,0:T(8,128)(2,1)S(1)} copy-done((bf16[27,64,256]{2,1,0:T(8,128)(2,1)S(1)}, bf16[27,64,256]{2,1,0:T(8,128)(2,1)}, u32[]{:S(2)}) %copy-start.1) | copy-done | bytes 884760
  9.4 0.0 copy-start.2
  9.4 0.7 %copy-done.2 = bf16[18,512]{1,0:T(8,128)(2,1)S(1)} copy-done((bf16[18,512]{1,0:T(8,128)(2,1)S(1)}, bf16[18,512]{1,0:T(8,128)(2,1)}, u32[]{:S(2)}) %copy-start.2) | copy-done | bytes 18456
  10.1 0.0 copy-start.3
  10.1 0.7 %copy-done.3 = s32[4,4,24]{2,1,0:T(4,128)S(1)} copy-done((s32[4,4,24]{2,1,0:T(4,128)S(1)}, s32[4,4,24]{2,1,0:T(4,128)}, u32[]{:S(2)}) %copy-start.3) | copy-done | bytes 1560
  10.8 0.0 copy-start.4
  10.8 0.7 %copy-done.4 = f32[512]{0:T(512)S(1)} copy-done((f32[512]{0:T(512)S(1)}, f32[512]{0:T(512)}, u32[]{:S(2)}) %copy-start.4) | copy-done | bytes 2072
  11.5 3.3 %prep.1 = (bf16[3,1024,1024]{2,1,0:T(8,128)(2,1)S(1)}, bf16[9,256,512]{2,1,0:T(8,128)(2,1)S(1)}, bf16[4,96,512]{2,1,0:T(8,128)(2,1)S(1)}) custom-call(s32[4,4,24]{2,1,0:T(4,128)S(1)} %copy-done.3, bf16[18,512]{1,0:T(8,128)(2,1)S(1)} %copy-done.2, f32[1,512]{1,0:T(1,128)S(1)} %bitcast.2, bf16[27,512,128]{2,1,0:T(8,128)(2,1)S(1)} %copy-done, ...), custom_call_target="tpu_custom_call" | custom-call | flops 1000000000 | bytes 20000000 | tf_op jit(solution)/shard_map/prep/pallas_call | solution.py:226
  14.8 0.0 collective-permute-done.lo_ref
  14.8 0.0 collective-permute-done.1.hi_ref
  14.8 0.0 copy-start.5
  14.8 3.7 %hidden.1.own_ref = bf16[480,512]{1,0:T(8,128)(2,1)S(1)} custom-call(s32[4,4,24]{2,1,0:T(4,128)S(1)} %collective-permute-done.lo_ref, s32[4,4,24]{2,1,0:T(4,128)S(1)} %collective-permute-done.1.hi_ref, bf16[18,512]{1,0:T(8,128)(2,1)S(1)} %copy-done.2, f32[1,512]{1,0:T(1,128)S(1)} %bitcast.3, bf16[4,96,512]{2,1,0:T(8,128)(2,1)S(1)} %get-tuple-element.8.own_ref, ...), custom_call_target="tpu_custom_call" | custom-call | tf_op jit(solution)/shard_map/hidden/pallas_call | solution.py:247
  18.5 1.3 %collective-permute-start.2 = (bf16[480,512]{1,0:T(8,128)(2,1)S(1)}, bf16[480,512]{1,0:T(8,128)(2,1)S(1)}, u32[]{:S(2)}, u32[]{:S(2)}) collective-permute-start(bf16[480,512]{1,0:T(8,128)(2,1)S(1)} %hidden.1.own_ref), channel_id=1, source_target_pairs={{0,1},{1,0},{2,3},{3,2},{4,5},{5,4},{6,7},{7,6},{8,9},{9,8},{10,11... | collective-permute-start | bytes 1474568 | tf_op jit(solution)/shard_map/ppermute | solution.py:260
  19.8 1.5 %collective-permute-done.2.other_ref = bf16[480,512]{1,0:T(8,128)(2,1)S(1)} collective-permute-done((bf16[480,512]{1,0:T(8,128)(2,1)S(1)}, bf16[480,512]{1,0:T(8,128)(2,1)S(1)}, u32[]{:S(2)}, u32[]{:S(2)}) %collective-permute-start.2) | collective-permute-done | bytes 491552 | tf_op jit(solution)/shard_map/ppermute | solution.py:260
  21.3 0.0 copy-done.5
  21.3 3.0 %decode.1 = bf16[4,8,48,64]{3,2,1,0:T(8,128)(2,1)} custom-call(bf16[480,512]{1,0:T(8,128)(2,1)S(1)} %hidden.1.own_ref, bf16[480,512]{1,0:T(8,128)(2,1)S(1)} %collective-permute-done.2.other_ref, f32[1,256]{1,0:T(1,128)S(1)} %bitcast.4, bf16[9,256,512]{2,1,0:T(8,128)(2,1)S(1)} %get-tuple-element.10.w2_ref), custom_call_target="tpu_custom_call" | custom-call | tf_op jit(solution)/shard_map/decode/pallas_call | solution.py:262
Async XLA Ops:
  0.0 14.8 %collective-permute-start = (s32[4,4,24]{2,1,0:T(4,128)}, s32[4,4,24]{2,1,0:T(4,128)S(1)}, u32[]{:S(2)}, u32[]{:S(2)}) collective-permute-start(s32[4,4,24]{2,1,0:T(4,128)} %codes_ref.1), channel_id=1, source_target_pairs={{0,2},{2,4},{4,6},{6,8},{8,10},{10,12},{12,14},{1,3},{3,5},{5,7},{... | collective-permute-start | bytes 4616 | tf_op jit(solution)/shard_map/ppermute | solution.py:220
  3.1 11.6 %collective-permute-start.1 = (s32[4,4,24]{2,1,0:T(4,128)}, s32[4,4,24]{2,1,0:T(4,128)S(1)}, u32[]{:S(2)}, u32[]{:S(2)}) collective-permute-start(s32[4,4,24]{2,1,0:T(4,128)} %codes_ref.1), channel_id=1, source_target_pairs={{2,0},{4,2},{6,4},{8,6},{10,8},{12,10},{14,12},{3,1},{5,3},{7,5},{... | collective-permute-start | bytes 4616 | tf_op jit(solution)/shard_map/ppermute | solution.py:221
  6.2 2.0 %copy-start = (bf16[27,512,128]{2,1,0:T(8,128)(2,1)S(1)}, bf16[27,512,128]{2,1,0:T(8,128)(2,1)}, u32[]{:S(2)}) copy-start(bf16[27,512,128]{2,1,0:T(8,128)(2,1)} %up_hbm.1) | copy-start | bytes 10616836
  8.2 1.2 %copy-start.1 = (bf16[27,64,256]{2,1,0:T(8,128)(2,1)S(1)}, bf16[27,64,256]{2,1,0:T(8,128)(2,1)}, u32[]{:S(2)}) copy-start(bf16[27,64,256]{2,1,0:T(8,128)(2,1)} %out_hbm.1) | copy-start | bytes 2654212
  9.4 0.7 %copy-start.2 = (bf16[18,512]{1,0:T(8,128)(2,1)S(1)}, bf16[18,512]{1,0:T(8,128)(2,1)}, u32[]{:S(2)}) copy-start(bf16[18,512]{1,0:T(8,128)(2,1)} %proj_ref.3) | copy-start | bytes 55300
  10.1 0.7 %copy-start.3 = (s32[4,4,24]{2,1,0:T(4,128)S(1)}, s32[4,4,24]{2,1,0:T(4,128)}, u32[]{:S(2)}) copy-start(s32[4,4,24]{2,1,0:T(4,128)} %codes_ref.1) | copy-start | bytes 4612
  10.8 0.7 %copy-start.4 = (f32[512]{0:T(512)S(1)}, f32[512]{0:T(512)}, u32[]{:S(2)}) copy-start(f32[512]{0:T(512)} %param.8) | copy-start | bytes 6148
  14.8 6.5 %copy-start.5 = (f32[256]{0:T(256)S(1)}, f32[256]{0:T(256)}, u32[]{:S(2)}) copy-start(f32[256]{0:T(256)} %param.10) | copy-start | bytes 3076
  18.5 2.8 %collective-permute-start.2 = (bf16[480,512]{1,0:T(8,128)(2,1)S(1)}, bf16[480,512]{1,0:T(8,128)(2,1)S(1)}, u32[]{:S(2)}, u32[]{:S(2)}) collective-permute-start(bf16[480,512]{1,0:T(8,128)(2,1)S(1)} %hidden.1.own_ref), channel_id=1, source_target_pairs={{0,1},{1,0},{2,3},{3,2},{4,5},{5,4},{6,7},{7,6},{8,9},{9,8},{10,11... | collective-permute-start | bytes 1474568 | tf_op jit(solution)/shard_map/ppermute | solution.py:260

commit v3 on v2

--- a/solution.py
+++ b/solution.py
@@ -34,20 +34,13 @@
     return silu(latent * lax.rsqrt(mean + EPS) * gain)
 
 
-def prep_kernel(codes_ref, proj_ref, gain_ref, up_hbm, out_hbm, w1_ref, w2_ref, act_ref, up_ref, tap_ref, sems):
+def up_prep_kernel(up_hbm, w1_ref, up_ref, sems):
     copies = [
         pltpu.make_async_copy(up_hbm.at[pl.ds(9 * a, 9)], up_ref.at[pl.ds(9 * a, 9)], sems.at[a])
         for a in range(3)
     ]
-    copies.append(pltpu.make_async_copy(out_hbm, tap_ref, sems.at[3]))
     for copy in copies:
         copy.start()
-
-    frames, rows, cols = codes_ref.shape
-    size = frames * cols
-    for r in range(rows):
-        act = latent_rows([codes_ref[t, r : r + 1, :] for t in range(frames)], proj_ref[...], gain_ref[...])
-        act_ref[r] = act.astype(BF16)
 
     width = up_ref.shape[1]
     out_w = up_ref.shape[2]
@@ -70,6 +63,20 @@
                     for v in range(4):
                         w1_ref[a, pl.ds(half * width + k, step), pl.ds((4 * py + v) * out_w, out_w)] = parts[v].astype(BF16)
 
+
+def own_prep_kernel(codes_hbm, proj_hbm, gain_hbm, out_hbm, after_ref, w2_ref, act_ref, proj_ref, gain_ref, codes_ref, tap_ref, sems):
+    pairs = ((codes_hbm, codes_ref), (proj_hbm, proj_ref), (gain_hbm, gain_ref), (out_hbm, tap_ref))
+    copies = [pltpu.make_async_copy(src, dst, sems.at[n]) for n, (src, dst) in enumerate(pairs)]
+    for copy in copies:
+        copy.start()
+    for copy in copies[:3]:
+        copy.wait()
+
+    frames, rows, cols = codes_ref.shape
+    for r in range(rows):
+        act = latent_rows([codes_ref[t, r : r + 1, :] for t in range(frames)], proj_ref[...], gain_ref[...])
+        act_ref[r] = act.astype(BF16)
+
     copies[3].wait()
     ow, half_ch = tap_ref.shape[1], tap_ref.shape[2] // 2
     zero = jnp.zeros((ow, half_ch), BF16)
@@ -96,14 +103,17 @@
     return -(-need // 16) * 16
 
 
-def hidden_kernel(axis, lo_ref, hi_ref, proj_ref, gain_ref, own_ref, w1_ref, h_ref, act_ref, acc_ref):
-    frames, rows, cols = lo_ref.shape
+def hidden_kernel(axis, near_ref, far_ref, proj_ref, gain_ref, own_ref, w1_ref, h_ref, act_ref, acc_ref):
+    frames, rows, cols = near_ref.shape
     size = frames * cols
     width = own_ref.shape[2]
+    first = lax.axis_index("section") == 0
     place = lax.axis_index(axis)
     last = lax.axis_size(axis) - 1
-    for edge, (src, row, ok) in enumerate(((lo_ref, rows - 1, place > 0), (hi_ref, 0, place < last))):
-        act = latent_rows([src[t, row : row + 1, :] for t in range(frames)], proj_ref[...], gain_ref[...])
+    for edge, (row, ok) in enumerate(((rows - 1, place > 0), (0, place < last))):
+        one, two = (near_ref, far_ref) if edge == 0 else (far_ref, near_ref)
+        codes = [jnp.where(first, one[t, row : row + 1, :], two[t, row : row + 1, :]) for t in range(frames)]
+        act = latent_rows(codes, proj_ref[...], gain_ref[...])
         act_ref[edge * (rows + 1)] = jnp.where(ok, act, 0.0).astype(BF16)
     act_ref[pl.ds(1, rows)] = own_ref[...]
 
@@ -201,49 +211,63 @@
     return pltpu.CompilerParams(vmem_limit_bytes=mib * MIB)
 
 
-def in_vmem(*arrays):
-    return tuple(pltpu.with_memory_space_constraint(x, pltpu.VMEM) for x in arrays)
-
-
 def vmem():
     return pl.BlockSpec(memory_space=pltpu.VMEM)
+
+
+def in_space(space, *arrays):
+    return tuple(pltpu.with_memory_space_constraint(x, space) for x in arrays)
 
 
 def body(codes, in_proj, gain_up, up_kernel, gain_res, out_kernel):
     frames, rows, cols = codes.shape
     size = frames * cols
-    taps, width, share = up_kernel.shape
+    width, share = up_kernel.shape[1:]
     ow, ch = out_kernel.shape[1:]
+    pairs = rows + 1
     count = lax.axis_size("rows")
-    forward = [(i, i + 1) for i in range(count - 1)]
-    backward = [(i + 1, i) for i in range(count - 1)]
-    low = lax.ppermute(codes, "rows", forward)
-    high = lax.ppermute(codes, "rows", backward)
-    gain_up = gain_up.reshape(1, -1)
+    joint = [(2 * i, 2 * i + 2) for i in range(count - 1)] + [(2 * i + 3, 2 * i + 1) for i in range(count - 1)]
+    swap = [(0, 1), (1, 0)]
+    near = lax.ppermute(codes, ("rows", "section"), joint)
+    far = lax.ppermute(near, "section", swap)
     gain_res = gain_res.reshape(1, -1)
-
-    hbm = pl.BlockSpec(memory_space=pl.ANY)
-    w1, w2, act = pl.pallas_call(
-        prep_kernel,
+    up_kernel, out_kernel, codes, in_proj, gain_up = in_space(
+        pltpu.HBM, up_kernel, out_kernel, codes, in_proj, gain_up.reshape(1, -1)
+    )
+
+    hbm = pl.BlockSpec(memory_space=pltpu.HBM)
+    w1 = pl.pallas_call(
+        up_prep_kernel,
+        out_shape=pltpu.VMEM((3, 2 * width, 8 * share), BF16),
+        in_specs=[hbm],
+        out_specs=vmem(),
+        scratch_shapes=[pltpu.VMEM(up_kernel.shape, BF16), pltpu.SemaphoreType.DMA((3,))],
+        compiler_params=params(8),
+        cost_estimate=pl.CostEstimate(flops=10**9, bytes_accessed=2 * 10**7, transcendentals=0),
+        name="up_prep",
+    )(up_kernel)
+    near, far = in_space(pltpu.VMEM, near, far)
+    w2, act, proj, gain = pl.pallas_call(
+        own_prep_kernel,
         out_shape=(
-            pltpu.VMEM((3, 2 * width, 8 * share), BF16),
             pltpu.VMEM((9, 4 * ow, 2 * ch), BF16),
             pltpu.VMEM((rows, size, width), BF16),
+            pltpu.VMEM(in_proj.shape, BF16),
+            pltpu.VMEM(gain_up.shape, F32),
         ),
-        in_specs=[vmem(), vmem(), vmem(), hbm, hbm],
-        out_specs=(vmem(), vmem(), vmem()),
+        in_specs=[hbm] * 4 + [vmem()],
+        out_specs=(vmem(),) * 4,
         scratch_shapes=[
-            pltpu.VMEM(up_kernel.shape, BF16),
+            pltpu.VMEM(codes.shape, jnp.int32),
             pltpu.VMEM(out_kernel.shape, BF16),
             pltpu.SemaphoreType.DMA((4,)),
         ],
-        compiler_params=params(12),
-        cost_estimate=pl.CostEstimate(flops=10**9, bytes_accessed=2 * 10**7, transcendentals=0),
-        name="prep",
-    )(codes, in_proj, gain_up, up_kernel, out_kernel)
-
-    pairs = rows + 1
-    w1, w2, act, low, high = in_vmem(w1, w2, act, low, high)
+        compiler_params=params(8),
+        cost_estimate=pl.CostEstimate(flops=10**8, bytes_accessed=10**7, transcendentals=0),
+        name="own_prep",
+    )(codes, in_proj, gain_up, out_kernel, near)
+
+    w1, w2, act, proj, gain = in_space(pltpu.VMEM, w1, w2, act, proj, gain)
     hidden = pl.pallas_call(
         functools.partial(hidden_kernel, "rows"),
         out_shape=pltpu.VMEM((pairs * size, 4 * share), BF16),
@@ -255,9 +279,9 @@
         ],
         compiler_params=params(8),
         name="hidden",
-    )(low, high, in_proj, gain_up, act, w1)
-
-    other = lax.ppermute(hidden, "section", [(0, 1), (1, 0)])
+    )(near, far, proj, gain, act, w1)
+
+    other = lax.ppermute(hidden, "section", swap)
 
     return pl.pallas_call(
         functools.partial(out_kernel_body, "rows", frames, cols),
@@ -271,7 +295,7 @@
         ],
         compiler_params=params(12),
         name="decode",
-    )(*in_vmem(hidden, other), gain_res, w2)
+    )(*in_space(pltpu.VMEM, hidden, other), gain_res, w2)
 
 
 def solution(mesh):

time: 24.7 us -> 18.4 us (0.74)
  the two profiles are of different devices: /device:TPU:13 before, /device:TPU:0 now
where the time goes in v3:
time: 18.4 us; the launch traced here: 18.2 us
  Pallas kernels  11.2 us (61%)
  starting transfers between devices  5.46 us (30%)
  waiting for transfers between devices  1.5 us (8%)
    ppermute x1, starting transfers between devices, body(): near = lax.ppermute(codes, ('rows', 'section'), joint)  4.83 us
    pallas_call x1, Pallas kernels, body(): pl.pallas_call(functools.partial(hidden_kernel, 'rows'), out_shape=pltpu....  3.71 us
    pallas_call x1, Pallas kernels, body(): pl.pallas_call(functools.partial(out_kernel_body, 'rows', frames, cols),...  3.01 us
    pallas_call x1, Pallas kernels, body(): pl.pallas_call(up_prep_kernel, out_shape=pltpu.VMEM((3, 2 * width, 8 * sh...  2.81 us
    pallas_call x1, Pallas kernels, body(): pl.pallas_call(own_prep_kernel, out_shape=(pltpu.VMEM((9, 4 * ow, 2 * ch)...  1.62 us
    ppermute x1, waiting for transfers between devices, body(): other = lax.ppermute(hidden, 'section', swap)  1.49 us
    ppermute x1, starting transfers between devices, body(): other = lax.ppermute(hidden, 'section', swap)  0.56 us
  transfers between devices with their start and end apart: 3, of which 1 were waited for; matrix products, arithmetic and copies ran while one was open for 0% of the time, Pallas kernels for 24%

profile of v3, /device:TPU:0, one launch (start us, length us, event | category | flops | bytes accessed | tf_op | source)
XLA Modules:
  0.0 18.2 jit_solution(13304525638457013801)
XLA Ops:
  0.0 4.8 %collective-permute-start = (s32[4,4,24]{2,1,0:T(4,128)}, s32[4,4,24]{2,1,0:T(4,128)S(1)}, u32[]{:S(2)}, u32[]{:S(2)}) collective-permute-start(s32[4,4,24]{2,1,0:T(4,128)} %codes_hbm.1), channel_id=1, source_target_pairs={{0,2},{2,4},{4,6},{6,8},{8,10},{10,12},{12,14},{3,1},{5,3},{7,5},{... | collective-permute-start | bytes 4616 | tf_op jit(solution)/shard_map/ppermute | solution.py:231
  4.8 2.8 %up_prep.1.w1_ref = bf16[3,1024,1024]{2,1,0:T(8,128)(2,1)S(1)} custom-call(bf16[27,512,128]{2,1,0:T(8,128)(2,1)} %up_hbm.1), custom_call_target="tpu_custom_call" | custom-call | flops 1000000000 | bytes 20000000 | tf_op jit(solution)/shard_map/up_prep/pallas_call | solution.py:239
  7.7 0.0 collective-permute-done.after_ref.near_ref
  7.7 0.1 collective-permute-start.1
  7.7 1.6 %own_prep.1 = (bf16[9,256,512]{2,1,0:T(8,128)(2,1)S(1)}, bf16[4,96,512]{2,1,0:T(8,128)(2,1)S(1)}, bf16[18,512]{1,0:T(8,128)(2,1)S(1)}, f32[1,512]{1,0:T(1,128)S(1)}) custom-call(s32[4,4,24]{2,1,0:T(4,128)} %codes_hbm.1, bf16[18,512]{1,0:T(8,128)(2,1)} %proj_hbm.1, f32[1,512]{1,0:T(1,128)} %bitcast.3, bf16[27,64,256]{2,1,0:T(8,128)(2,1)} %out_hbm.1, ...), custom_call_target="tpu_custom_call" | custom-call | flops 100000000 | bytes 10000000 | tf_op jit(solution)/shard_map/own_prep/pallas_call | solution.py:250
  9.4 0.0 collective-permute-done.1.far_ref
  9.4 0.0 copy-start
  9.4 3.7 %hidden.1.own_ref = bf16[480,512]{1,0:T(8,128)(2,1)S(1)} custom-call(s32[4,4,24]{2,1,0:T(4,128)S(1)} %collective-permute-done.after_ref.near_ref, s32[4,4,24]{2,1,0:T(4,128)S(1)} %collective-permute-done.1.far_ref, bf16[18,512]{1,0:T(8,128)(2,1)S(1)} %get-tuple-element.9.proj_ref, f32[1,512]{1,0:T(1,128)S(1)} %get-tuple-element.10.gain_ref, ...), custom_call_target="tpu_custom_call" | custom-call | tf_op jit(solution)/shard_map/hidden/pallas_call | solution.py:271
  13.1 0.6 %collective-permute-start.2 = (bf16[480,512]{1,0:T(8,128)(2,1)S(1)}, bf16[480,512]{1,0:T(8,128)(2,1)S(1)}, u32[]{:S(2)}, u32[]{:S(2)}) collective-permute-start(bf16[480,512]{1,0:T(8,128)(2,1)S(1)} %hidden.1.own_ref), channel_id=1, source_target_pairs={{0,1},{1,0},{2,3},{3,2},{4,5},{5,4},{6,7},{7,6},{8,9},{9,8},{10,11... | collective-permute-start | bytes 1474568 | tf_op jit(solution)/shard_map/ppermute | solution.py:284
  13.7 1.5 %collective-permute-done.2.other_ref = bf16[480,512]{1,0:T(8,128)(2,1)S(1)} collective-permute-done((bf16[480,512]{1,0:T(8,128)(2,1)S(1)}, bf16[480,512]{1,0:T(8,128)(2,1)S(1)}, u32[]{:S(2)}, u32[]{:S(2)}) %collective-permute-start.2) | collective-permute-done | bytes 491552 | tf_op jit(solution)/shard_map/ppermute | solution.py:284
  15.2 0.0 copy-done
  15.2 3.0 %decode.1 = bf16[4,8,48,64]{3,2,1,0:T(8,128)(2,1)} custom-call(bf16[480,512]{1,0:T(8,128)(2,1)S(1)} %hidden.1.own_ref, bf16[480,512]{1,0:T(8,128)(2,1)S(1)} %collective-permute-done.2.other_ref, f32[1,256]{1,0:T(1,128)S(1)} %bitcast.2, bf16[9,256,512]{2,1,0:T(8,128)(2,1)S(1)} %get-tuple-element.12.w2_ref), custom_call_target="tpu_custom_call" | custom-call | tf_op jit(solution)/shard_map/decode/pallas_call | solution.py:286
Async XLA Ops:
  0.0 7.7 %collective-permute-start = (s32[4,4,24]{2,1,0:T(4,128)}, s32[4,4,24]{2,1,0:T(4,128)S(1)}, u32[]{:S(2)}, u32[]{:S(2)}) collective-permute-start(s32[4,4,24]{2,1,0:T(4,128)} %codes_hbm.1), channel_id=1, source_target_pairs={{0,2},{2,4},{4,6},{6,8},{8,10},{10,12},{12,14},{3,1},{5,3},{7,5},{... | collective-permute-start | bytes 4616 | tf_op jit(solution)/shard_map/ppermute | solution.py:231
  7.7 1.7 %collective-permute-start.1 = (s32[4,4,24]{2,1,0:T(4,128)S(1)}, s32[4,4,24]{2,1,0:T(4,128)S(1)}, u32[]{:S(2)}, u32[]{:S(2)}) collective-permute-start(s32[4,4,24]{2,1,0:T(4,128)S(1)} %collective-permute-done.after_ref.near_ref), channel_id=1, source_target_pairs={{0,1},{1,0},{2,3},{3,2},{4,5},{5,4},{6,7},{7,6},{8,9},{9,8},{10,11... | collective-permute-start | bytes 4616 | tf_op jit(solution)/shard_map/ppermute | solution.py:232
  9.4 5.8 %copy-start = (f32[256]{0:T(256)S(1)}, f32[256]{0:T(256)}, u32[]{:S(2)}) copy-start(f32[256]{0:T(256)} %param.10) | copy-start | bytes 3076
  13.1 2.0 %collective-permute-start.2 = (bf16[480,512]{1,0:T(8,128)(2,1)S(1)}, bf16[480,512]{1,0:T(8,128)(2,1)S(1)}, u32[]{:S(2)}, u32[]{:S(2)}) collective-permute-start(bf16[480,512]{1,0:T(8,128)(2,1)S(1)} %hidden.1.own_ref), channel_id=1, source_target_pairs={{0,1},{1,0},{2,3},{3,2},{4,5},{5,4},{6,7},{7,6},{8,9},{9,8},{10,11... | collective-permute-start | bytes 1474568 | tf_op jit(solution)/shard_map/ppermute | solution.py:284

commit v4 on v3

--- a/solution.py
+++ b/solution.py
@@ -11,6 +11,7 @@
 EPS = 1e-06
 F32 = jnp.float32
 BF16 = jnp.bfloat16
+SPLIT = 6
 MIB = 1024 * 1024
 
 
@@ -34,50 +35,54 @@
     return silu(latent * lax.rsqrt(mean + EPS) * gain)
 
 
-def up_prep_kernel(up_hbm, w1_ref, up_ref, sems):
-    copies = [
-        pltpu.make_async_copy(up_hbm.at[pl.ds(9 * a, 9)], up_ref.at[pl.ds(9 * a, 9)], sems.at[a])
-        for a in range(3)
-    ]
-    for copy in copies:
-        copy.start()
-
-    width = up_ref.shape[1]
-    out_w = up_ref.shape[2]
-    step = 32
-    for a in range(3):
-        copies[a].wait()
-
-        @pl.loop(0, width // step)
-        def _(i, a=a):
-            k = pl.multiple_of(i * step, step)
-            tap = [[up_ref[9 * a + 3 * b + c, pl.ds(k, step), :].astype(F32) for c in range(3)] for b in range(3)]
-            row_sets = (
-                ([tap[0][c] + tap[1][c] for c in range(3)], tap[0]),
-                (tap[2], [tap[1][c] + tap[2][c] for c in range(3)]),
-            )
-            for half in range(2):
-                for py in range(2):
-                    x = row_sets[half][py]
-                    parts = (x[0], x[1] + x[2], x[0] + x[1], x[2])
-                    for v in range(4):
-                        w1_ref[a, pl.ds(half * width + k, step), pl.ds((4 * py + v) * out_w, out_w)] = parts[v].astype(BF16)
-
-
-def own_prep_kernel(codes_hbm, proj_hbm, gain_hbm, out_hbm, after_ref, w2_ref, act_ref, proj_ref, gain_ref, codes_ref, tap_ref, sems):
-    pairs = ((codes_hbm, codes_ref), (proj_hbm, proj_ref), (gain_hbm, gain_ref), (out_hbm, tap_ref))
+def products(act, frame_rows, w_ref, acc_ref, start, stop):
+    n = frame_rows
+    share = w_ref.shape[2]
+
+    def taps(a, first, count):
+        return jnp.concatenate([w_ref[9 * a + first + k] for k in range(count)], axis=1)
+
+    def dot(frames, weights):
+        return jnp.dot(act[pl.ds(0, frames * n), :], weights, preferred_element_type=F32)
+
+    def put(first, lanes, p2, p1, p0):
+        lanes = pl.ds((first - start) * share, lanes)
+        acc_ref[pl.ds(0, n), lanes] = p2[:n]
+        acc_ref[pl.ds(n, n), lanes] = p2[n : 2 * n] + p1[:n]
+        acc_ref[pl.ds(2 * n, 2 * n), lanes] = p2[2 * n :] + p1[n : 3 * n] + p0
+
+    for first in range(start, stop - 1, 2):
+        put(first, 2 * share, dot(4, taps(2, first, 2)), dot(3, taps(1, first, 2)), dot(2, taps(0, first, 2)))
+    if (stop - start) % 2:
+        k = stop - 1
+        both = dot(4, jnp.concatenate([w_ref[18 + k], w_ref[9 + k]], axis=1))
+        put(k, share, both[:, :share], both[:, share:], dot(2, w_ref[k]))
+
+
+def own_kernel(codes_hbm, proj_hbm, gain_hbm, up_hbm, acc_ref, act_ref, w_ref, proj_ref, gain_ref, codes_ref, sems):
+    pairs = [(codes_hbm, codes_ref), (proj_hbm, proj_ref), (gain_hbm, gain_ref)]
+    pairs += [(up_hbm.at[pl.ds(9 * a, 9)], w_ref.at[pl.ds(9 * a, 9)]) for a in range(3)]
     copies = [pltpu.make_async_copy(src, dst, sems.at[n]) for n, (src, dst) in enumerate(pairs)]
     for copy in copies:
         copy.start()
     for copy in copies[:3]:
         copy.wait()
-
     frames, rows, cols = codes_ref.shape
-    for r in range(rows):
-        act = latent_rows([codes_ref[t, r : r + 1, :] for t in range(frames)], proj_ref[...], gain_ref[...])
-        act_ref[r] = act.astype(BF16)
-
-    copies[3].wait()
+    codes = [codes_ref[t, r : r + 1, :] for t in range(frames) for r in range(rows)]
+    act_ref[...] = latent_rows(codes, proj_ref[...], gain_ref[...]).astype(BF16)
+    for copy in copies[3:]:
+        copy.wait()
+    products(act_ref, rows * cols, w_ref, acc_ref, 0, SPLIT)
+
+
+def rest_kernel(frame_rows, act_ref, w_ref, after_ref, acc_ref):
+    products(act_ref, frame_rows, w_ref, acc_ref, SPLIT, 9)
+
+
+def tap_kernel(out_hbm, w2_ref, tap_ref, sem):
+    copy = pltpu.make_async_copy(out_hbm, tap_ref, sem)
+    copy.start()
+    copy.wait()
     ow, half_ch = tap_ref.shape[1], tap_ref.shape[2] // 2
     zero = jnp.zeros((ow, half_ch), BF16)
     section = lax.axis_index("section")
@@ -103,52 +108,48 @@
     return -(-need // 16) * 16
 
 
-def hidden_kernel(axis, near_ref, far_ref, proj_ref, gain_ref, own_ref, w1_ref, h_ref, act_ref, acc_ref):
+def hidden_kernel(near_ref, far_ref, proj_ref, gain_ref, w_ref, own_ref, rest_ref, h_ref, act_ref, halo_ref):
     frames, rows, cols = near_ref.shape
+    share = w_ref.shape[2]
     size = frames * cols
-    width = own_ref.shape[2]
     first = lax.axis_index("section") == 0
-    place = lax.axis_index(axis)
-    last = lax.axis_size(axis) - 1
-    for edge, (row, ok) in enumerate(((rows - 1, place > 0), (0, place < last))):
-        one, two = (near_ref, far_ref) if edge == 0 else (far_ref, near_ref)
-        codes = [jnp.where(first, one[t, row : row + 1, :], two[t, row : row + 1, :]) for t in range(frames)]
-        act = latent_rows(codes, proj_ref[...], gain_ref[...])
-        act_ref[edge * (rows + 1)] = jnp.where(ok, act, 0.0).astype(BF16)
-    act_ref[pl.ds(1, rows)] = own_ref[...]
-
-    pairs = rows + 1
-
-    @pl.loop(0, 4)
-    def _(n):
-        lanes = pl.ds(pl.multiple_of(n * 256, 256), 256)
-        for a in (2, 1, 0):
-            m = reach(frames, cols, a)
-            total = None
-            for half in range(2):
-                part = jnp.dot(
-                    act_ref[pl.ds(half, pairs), pl.ds(0, m), :].reshape(pairs * m, width),
-                    w1_ref[a, pl.ds(half * width, width), lanes],
-                    preferred_element_type=F32,
-                )
-                total = part if total is None else total + part
-            total = total.reshape(pairs, m, 256)
-            if a == 2:
-                acc_ref[...] = total
-            else:
-                skip = (2 - a) * cols
-                acc_ref[:, pl.ds(skip, size - skip), :] += total[:, : size - skip, :]
-        full = acc_ref[...].reshape(pairs * size, 256)
-        left, right = full[:, :128], full[:, 128:]
-        px = n % 2
-
-        @pl.when(px == 0)
-        def _():
-            h_ref[:, pl.ds(pl.multiple_of(n * 128, 128), 128)] = (right + shifted(left, cols, 1)).astype(BF16)
-
-        @pl.when(px == 1)
-        def _():
-            h_ref[:, pl.ds(pl.multiple_of(n * 128, 128), 128)] = (left + shifted(right, cols, -1)).astype(BF16)
+    place = lax.axis_index("rows")
+    last = lax.axis_size("rows") - 1
+    codes = []
+    for t in range(frames):
+        low = [ref[t, rows - 1 : rows, :] for ref in (near_ref, far_ref)]
+        high = [ref[t, 0:1, :] for ref in (near_ref, far_ref)]
+        codes += [jnp.where(first, low[0], low[1]), jnp.where(first, high[1], high[0])]
+    act = latent_rows(codes, proj_ref[...], gain_ref[...])
+    edge = lax.broadcasted_iota(jnp.int32, (frames, 2, cols, act.shape[1]), 1).reshape(act.shape)
+    keep = jnp.where(edge == 0, (place > 0).astype(F32), (place < last).astype(F32))
+    act_ref[...] = (act * keep).astype(BF16)
+    products(act_ref, 2 * cols, w_ref, halo_ref, 0, 9)
+
+    def taken(slot, pair, tap):
+        ref = own_ref
+        if slot in (0, rows + 1):
+            ref, span, row = halo_ref, 2 * cols, 0 if slot == 0 else 1
+        else:
+            span, row = rows * cols, slot - 1
+            if tap >= SPLIT:
+                ref, tap = rest_ref, tap - SPLIT
+        lanes = pl.ds(tap * share, share)
+        return jnp.concatenate([ref[pl.ds(t * span + row * cols, cols), lanes] for t in (2 * pair, 2 * pair + 1)], axis=0)
+
+    for pair in range(frames // 2):
+        for q in range(rows + 1):
+            sums = [[], []]
+            for c in range(3):
+                x = taken(q, pair, c) + taken(q + 1, pair, 6 + c)
+                sums[0].append(x + taken(q, pair, 3 + c))
+                sums[1].append(x + taken(q + 1, pair, 3 + c))
+            out = pl.ds(q * size + pair * 2 * cols, 2 * cols)
+            for py, (left, mid, right) in enumerate(sums):
+                even = shifted(left, cols, 1) + (mid + right)
+                odd = (left + mid) + shifted(right, cols, -1)
+                h_ref[out, pl.ds(2 * py * share, share)] = even.astype(BF16)
+                h_ref[out, pl.ds((2 * py + 1) * share, share)] = odd.astype(BF16)
 
 
 def out_kernel_body(axis, frames, cols, own_ref, other_ref, gain_ref, w2_ref, o_ref, norm_ref, acc_ref, mix_ref):
@@ -229,57 +230,68 @@
     joint = [(2 * i, 2 * i + 2) for i in range(count - 1)] + [(2 * i + 3, 2 * i + 1) for i in range(count - 1)]
     swap = [(0, 1), (1, 0)]
     near = lax.ppermute(codes, ("rows", "section"), joint)
-    far = lax.ppermute(near, "section", swap)
     gain_res = gain_res.reshape(1, -1)
     up_kernel, out_kernel, codes, in_proj, gain_up = in_space(
         pltpu.HBM, up_kernel, out_kernel, codes, in_proj, gain_up.reshape(1, -1)
     )
 
     hbm = pl.BlockSpec(memory_space=pltpu.HBM)
-    w1 = pl.pallas_call(
-        up_prep_kernel,
-        out_shape=pltpu.VMEM((3, 2 * width, 8 * share), BF16),
-        in_specs=[hbm],
-        out_specs=vmem(),
-        scratch_shapes=[pltpu.VMEM(up_kernel.shape, BF16), pltpu.SemaphoreType.DMA((3,))],
-        compiler_params=params(8),
-        cost_estimate=pl.CostEstimate(flops=10**9, bytes_accessed=2 * 10**7, transcendentals=0),
-        name="up_prep",
-    )(up_kernel)
-    near, far = in_space(pltpu.VMEM, near, far)
-    w2, act, proj, gain = pl.pallas_call(
-        own_prep_kernel,
+    own, act, w1, proj, gain = pl.pallas_call(
+        own_kernel,
         out_shape=(
-            pltpu.VMEM((9, 4 * ow, 2 * ch), BF16),
-            pltpu.VMEM((rows, size, width), BF16),
+            pltpu.VMEM((rows * size, SPLIT * share), F32),
+            pltpu.VMEM((rows * size, width), BF16),
+            pltpu.VMEM(up_kernel.shape, BF16),
             pltpu.VMEM(in_proj.shape, BF16),
             pltpu.VMEM(gain_up.shape, F32),
         ),
-        in_specs=[hbm] * 4 + [vmem()],
-        out_specs=(vmem(),) * 4,
+        in_specs=[hbm] * 4,
+        out_specs=(vmem(),) * 5,
         scratch_shapes=[
             pltpu.VMEM(codes.shape, jnp.int32),
-            pltpu.VMEM(out_kernel.shape, BF16),
-            pltpu.SemaphoreType.DMA((4,)),
+            pltpu.SemaphoreType.DMA((6,)),
         ],
         compiler_params=params(8),
+        cost_estimate=pl.CostEstimate(flops=10**9, bytes_accessed=2 * 10**7, transcendentals=0),
+        name="own",
+    )(codes, in_proj, gain_up, up_kernel)
+    own, act, w1, proj, gain = in_space(pltpu.VMEM, own, act, w1, proj, gain)
+    near, proj = lax.optimization_barrier((near, proj))
+    far = lax.ppermute(near, "section", swap)
+    near, far = in_space(pltpu.VMEM, near, far)
+    rest = pl.pallas_call(
+        functools.partial(rest_kernel, rows * cols),
+        out_shape=pltpu.VMEM((rows * size, (9 - SPLIT) * share), F32),
+        in_specs=[vmem()] * 3,
+        out_specs=vmem(),
+        compiler_params=params(4),
+        cost_estimate=pl.CostEstimate(flops=10**9, bytes_accessed=10**7, transcendentals=0),
+        name="rest",
+    )(act, w1, near)
+    w2 = pl.pallas_call(
+        tap_kernel,
+        out_shape=pltpu.VMEM((9, 4 * ow, 2 * ch), BF16),
+        in_specs=[hbm],
+        out_specs=vmem(),
+        scratch_shapes=[pltpu.VMEM(out_kernel.shape, BF16), pltpu.SemaphoreType.DMA],
+        compiler_params=params(4),
         cost_estimate=pl.CostEstimate(flops=10**8, bytes_accessed=10**7, transcendentals=0),
-        name="own_prep",
-    )(codes, in_proj, gain_up, out_kernel, near)
-
-    w1, w2, act, proj, gain = in_space(pltpu.VMEM, w1, w2, act, proj, gain)
+        name="taps",
+    )(out_kernel)
+
+    rest, w2 = in_space(pltpu.VMEM, rest, w2)
     hidden = pl.pallas_call(
-        functools.partial(hidden_kernel, "rows"),
+        hidden_kernel,
         out_shape=pltpu.VMEM((pairs * size, 4 * share), BF16),
-        in_specs=[vmem()] * 6,
+        in_specs=[vmem()] * 7,
         out_specs=vmem(),
         scratch_shapes=[
-            pltpu.VMEM((rows + 2, size, width), BF16),
-            pltpu.VMEM((pairs, size, 256), F32),
+            pltpu.VMEM((2 * size, width), BF16),
+            pltpu.VMEM((2 * size, 9 * share), F32),
         ],
         compiler_params=params(8),
         name="hidden",
-    )(near, far, proj, gain, act, w1)
+    )(near, far, proj, gain, w1, own, rest)
 
     other = lax.ppermute(hidden, "section", swap)
 

time: 18.4 us -> 15.5 us (0.84)
  Pallas kernels: 11.2 us -> 9.29 us
  waiting for transfers between devices: 1.5 us -> 0.81 us
  starting transfers between devices: 5.46 us -> 5.13 us
    pallas_call x3 -> x4, Pallas kernels: 8.14 us -> 6.27 us  [the longest x1 2.97 us: body(): pl.pallas_call(own_kernel, out_shape=(pltpu.VMEM((rows * size, SPLIT * sh...]
    ppermute x1, waiting for transfers between devices: 1.49 us -> 0.21 us  [body(): other = lax.ppermute(hidden, 'section', swap)]
    ppermute x1, waiting for transfers between devices: 0.01 us -> 0.6 us  [body(): far = lax.ppermute(near, 'section', swap)]
    ppermute x1, starting transfers between devices: 0.56 us -> 0.23 us  [body(): other = lax.ppermute(hidden, 'section', swap)]
  transfers between devices with their start and end apart: 3 -> 3, of which waited for: 1 -> 2; matrix products, arithmetic and copies ran while one was open for 0% -> 0% of each run, Pallas kernels for 24% -> 33%
where the time goes in v4:
time: 15.5 us; the launch traced here: 15.3 us
  Pallas kernels  9.29 us (60%)
  starting transfers between devices  5.13 us (33%)
  waiting for transfers between devices  0.81 us (5%)
    ppermute x1, starting transfers between devices, body(): near = lax.ppermute(codes, ('rows', 'section'), joint)  4.83 us
    pallas_call x1, Pallas kernels, body(): pl.pallas_call(functools.partial(out_kernel_body, 'rows', frames, cols),...  3.02 us
    pallas_call x1, Pallas kernels, body(): pl.pallas_call(own_kernel, out_shape=(pltpu.VMEM((rows * size, SPLIT * sh...  2.97 us
    pallas_call x1, Pallas kernels, body(): pl.pallas_call(tap_kernel, out_shape=pltpu.VMEM((9, 4 * ow, 2 * ch), BF16...  1.48 us
    pallas_call x1, Pallas kernels, body(): pl.pallas_call(hidden_kernel, out_shape=pltpu.VMEM((pairs * size, 4 * sha...  1.27 us
    ppermute x1, waiting for transfers between devices, body(): far = lax.ppermute(near, 'section', swap)  0.6 us
    pallas_call x1, Pallas kernels, body(): pl.pallas_call(functools.partial(rest_kernel, rows * cols), out_shape=plt...  0.55 us
  transfers between devices with their start and end apart: 3, of which 2 were waited for; matrix products, arithmetic and copies ran while one was open for 0% of the time, Pallas kernels for 33%

profile of v4, /device:TPU:0, one launch (start us, length us, event | category | flops | bytes accessed | tf_op | source)
XLA Modules:
  0.0 15.3 jit_solution(15181765685235490854)
XLA Ops:
  0.0 4.8 %collective-permute-start = (s32[4,4,24]{2,1,0:T(4,128)}, s32[4,4,24]{2,1,0:T(4,128)S(1)}, u32[]{:S(2)}, u32[]{:S(2)}) collective-permute-start(s32[4,4,24]{2,1,0:T(4,128)} %codes_hbm.1), channel_id=1, source_target_pairs={{0,2},{2,4},{4,6},{6,8},{8,10},{10,12},{12,14},{3,1},{5,3},{7,5},{... | collective-permute-start | bytes 4616 | tf_op jit(solution)/shard_map/ppermute | solution.py:232
  4.8 3.0 %own.1 = (f32[384,768]{1,0:T(8,128)S(1)}, bf16[384,512]{1,0:T(8,128)(2,1)S(1)}, bf16[27,512,128]{2,1,0:T(8,128)(2,1)S(1)}, bf16[18,512]{1,0:T(8,128)(2,1)S(1)}, f32[1,512]{1,0:T(1,128)S(1)}) custom-call(s32[4,4,24]{2,1,0:T(4,128)} %codes_hbm.1, bf16[18,512]{1,0:T(8,128)(2,1)} %proj_hbm.1, f32[1,512]{1,0:T(1,128)} %bitcast.3, bf16[27,512,128]{2,1,0:T(8,128)(2,1)} %up_hbm.1), custom_call_target="tpu_custom_call" | custom-call | flops 1000000000 | bytes 20000000 | tf_op jit(solution)/shard_map/own/pallas_call | solution.py:239
  7.8 0.0 collective-permute-done.after_ref.near_ref
  7.8 0.1 collective-permute-start.1
  7.9 0.6 %rest.1.rest_ref = f32[384,384]{1,0:T(8,128)S(1)} custom-call(bf16[384,512]{1,0:T(8,128)(2,1)S(1)} %get-tuple-element.18.act_ref, bf16[27,512,128]{2,1,0:T(8,128)(2,1)S(1)} %get-tuple-element.16.w_ref, s32[4,4,24]{2,1,0:T(4,128)S(1)} %collective-permute-done.after_ref.near_ref), custom_call_target="tpu_custom_call" | custom-call | flops 1000000000 | bytes 10000000 | tf_op jit(solution)/shard_map/rest/pallas_call | solution.py:262
  8.5 0.6 %collective-permute-done.1.far_ref = s32[4,4,24]{2,1,0:T(4,128)S(1)} collective-permute-done((s32[4,4,24]{2,1,0:T(4,128)S(1)}, s32[4,4,24]{2,1,0:T(4,128)S(1)}, u32[]{:S(2)}, u32[]{:S(2)}) %collective-permute-start.1) | collective-permute-done | bytes 1568 | tf_op jit(solution)/shard_map/ppermute | solution.py:260
  9.1 0.0 copy-start
  9.1 1.3 %hidden.1.own_ref = bf16[480,512]{1,0:T(8,128)(2,1)S(1)} custom-call(s32[4,4,24]{2,1,0:T(4,128)S(1)} %collective-permute-done.after_ref.near_ref, s32[4,4,24]{2,1,0:T(4,128)S(1)} %collective-permute-done.1.far_ref, bf16[18,512]{1,0:T(8,128)(2,1)S(1)} %get-tuple-element.14.proj_ref, f32[1,512]{1,0:T(1,128)S(1)} %get-tuple-element.15.gain_ref, ...), custom_call_target="tpu_custom_call" | custom-call | tf_op jit(solution)/shard_map/hidden/pallas_call | solution.py:283
  10.3 0.2 %collective-permute-start.2 = (bf16[480,512]{1,0:T(8,128)(2,1)S(1)}, bf16[480,512]{1,0:T(8,128)(2,1)S(1)}, u32[]{:S(2)}, u32[]{:S(2)}) collective-permute-start(bf16[480,512]{1,0:T(8,128)(2,1)S(1)} %hidden.1.own_ref), channel_id=1, source_target_pairs={{0,1},{1,0},{2,3},{3,2},{4,5},{5,4},{6,7},{7,6},{8,9},{9,8},{10,11... | collective-permute-start | bytes 1474568 | tf_op jit(solution)/shard_map/ppermute | solution.py:296
  10.6 1.5 %taps.1.w2_ref = bf16[9,256,512]{2,1,0:T(8,128)(2,1)S(1)} custom-call(bf16[27,64,256]{2,1,0:T(8,128)(2,1)} %out_hbm.1), custom_call_target="tpu_custom_call" | custom-call | flops 100000000 | bytes 10000000 | tf_op jit(solution)/shard_map/taps/pallas_call | solution.py:271
  12.1 0.2 %collective-permute-done.2.other_ref = bf16[480,512]{1,0:T(8,128)(2,1)S(1)} collective-permute-done((bf16[480,512]{1,0:T(8,128)(2,1)S(1)}, bf16[480,512]{1,0:T(8,128)(2,1)S(1)}, u32[]{:S(2)}, u32[]{:S(2)}) %collective-permute-start.2) | collective-permute-done | bytes 491552 | tf_op jit(solution)/shard_map/ppermute | solution.py:296
  12.3 0.0 copy-done
  12.3 3.0 %decode.1 = bf16[4,8,48,64]{3,2,1,0:T(8,128)(2,1)} custom-call(bf16[480,512]{1,0:T(8,128)(2,1)S(1)} %hidden.1.own_ref, bf16[480,512]{1,0:T(8,128)(2,1)S(1)} %collective-permute-done.2.other_ref, f32[1,256]{1,0:T(1,128)S(1)} %bitcast.2, bf16[9,256,512]{2,1,0:T(8,128)(2,1)S(1)} %taps.1.w2_ref), custom_call_target="tpu_custom_call" | custom-call | tf_op jit(solution)/shard_map/decode/pallas_call | solution.py:298
Async XLA Ops:
  0.0 7.8 %collective-permute-start = (s32[4,4,24]{2,1,0:T(4,128)}, s32[4,4,24]{2,1,0:T(4,128)S(1)}, u32[]{:S(2)}, u32[]{:S(2)}) collective-permute-start(s32[4,4,24]{2,1,0:T(4,128)} %codes_hbm.1), channel_id=1, source_target_pairs={{0,2},{2,4},{4,6},{6,8},{8,10},{10,12},{12,14},{3,1},{5,3},{7,5},{... | collective-permute-start | bytes 4616 | tf_op jit(solution)/shard_map/ppermute | solution.py:232
  7.8 1.2 %collective-permute-start.1 = (s32[4,4,24]{2,1,0:T(4,128)S(1)}, s32[4,4,24]{2,1,0:T(4,128)S(1)}, u32[]{:S(2)}, u32[]{:S(2)}) collective-permute-start(s32[4,4,24]{2,1,0:T(4,128)S(1)} %collective-permute-done.after_ref.near_ref), channel_id=1, source_target_pairs={{0,1},{1,0},{2,3},{3,2},{4,5},{5,4},{6,7},{7,6},{8,9},{9,8},{10,11... | collective-permute-start | bytes 4616 | tf_op jit(solution)/shard_map/ppermute | solution.py:260
  9.1 3.2 %copy-start = (f32[256]{0:T(256)S(1)}, f32[256]{0:T(256)}, u32[]{:S(2)}) copy-start(f32[256]{0:T(256)} %param.10) | copy-start | bytes 3076
  10.3 1.9 %collective-permute-start.2 = (bf16[480,512]{1,0:T(8,128)(2,1)S(1)}, bf16[480,512]{1,0:T(8,128)(2,1)S(1)}, u32[]{:S(2)}, u32[]{:S(2)}) collective-permute-start(bf16[480,512]{1,0:T(8,128)(2,1)S(1)} %hidden.1.own_ref), channel_id=1, source_target_pairs={{0,1},{1,0},{2,3},{3,2},{4,5},{5,4},{6,7},{7,6},{8,9},{9,8},{10,11... | collective-permute-start | bytes 1474568 | tf_op jit(solution)/shard_map/ppermute | solution.py:296

commit v5 on v4

v5 whole, which is shorter than its diff:
```python
import functools

import jax
import jax.numpy as jnp
from jax import lax
from jax.experimental import pallas as pl
from jax.experimental.pallas import tpu as pltpu
from jax.sharding import PartitionSpec as P

BITS = 18
EPS = 1e-06
F32 = jnp.float32
BF16 = jnp.bfloat16
MIB = 1024 * 1024
GROUPS = ((0, 2), (2, 2), (4, 2), (6, 2), (8, 1))


def silu(v):
    return 0.5 * v * (1.0 + jnp.tanh(0.5 * v))


def latent_rows(rows, in_proj, gain):
    cols = rows[0].shape[1]
    count = len(rows)
    wide = jnp.concatenate([jnp.broadcast_to(row, (cols, cols)) for row in rows], axis=0)
    sub = lax.broadcasted_iota(jnp.int32, (count, cols, cols), 1).reshape(count * cols, cols)
    lane = lax.broadcasted_iota(jnp.int32, (count * cols, cols), 1)
    picked = jnp.where(sub == lane, wide, 0).astype(F32)
    column = jnp.sum(picked, axis=1, keepdims=True).astype(jnp.int32)
    spread = jnp.broadcast_to(column, (count * cols, BITS))
    shift = lax.broadcasted_iota(jnp.int32, (count * cols, BITS), 1)
    bits = ((jnp.right_shift(spread, shift) & 1) * 2 - 1).astype(F32).astype(BF16)
    latent = jnp.dot(bits, in_proj, preferred_element_type=F32)
    mean = jnp.mean(latent * latent, axis=1, keepdims=True)
    return silu(latent * lax.rsqrt(mean + EPS) * gain)


def shifted(x, cols, amount):
    rows, lanes = x.shape
    place = lax.broadcasted_iota(jnp.int32, (rows // cols, cols, lanes), 1).reshape(rows, lanes)
    moved = pltpu.roll(x, amount % rows, 0)
    return jnp.where(place == (0 if amount == 1 else cols - 1), 0.0, moved)


def weights(w_ref, a, group):
    return jnp.concatenate([w_ref[9 * a + group[0] + k] for k in range(group[1])], axis=1)


def early_products(act, n, w_ref, acc_ref, group):
    lanes = pl.ds(group[0] * w_ref.shape[2], group[1] * w_ref.shape[2])
    if group[1] == 1:
        both = jnp.concatenate([weights(w_ref, 2, group), weights(w_ref, 1, group)], axis=1)
        now = jnp.dot(act[pl.ds(0, 2 * n), :], both, preferred_element_type=F32)
        half = w_ref.shape[2]
        now, back = now[:, :half], now[:n, half:]
    else:
        now = jnp.dot(act[pl.ds(0, 2 * n), :], weights(w_ref, 2, group), preferred_element_type=F32)
        back = jnp.dot(act[pl.ds(0, n), :], weights(w_ref, 1, group), preferred_element_type=F32)
    acc_ref[pl.ds(0, n), lanes] = now[:n]
    acc_ref[pl.ds(n, n), lanes] = now[n:] + back


def late_products(act, n, w_ref, acc_ref, group):
    lanes = pl.ds(group[0] * w_ref.shape[2], group[1] * w_ref.shape[2])
    left = jnp.concatenate([act[pl.ds(a * n, 2 * n), :] for a in range(3)], axis=1)
    right = jnp.concatenate([weights(w_ref, a, group) for a in range(3)], axis=0)
    acc_ref[:, lanes] = jnp.dot(left, right, preferred_element_type=F32)


def own_kernel(codes_hbm, proj_hbm, gain_hbm, up_hbm, out_hbm, acc_ref, act_ref, w_ref, tap_ref, proj_ref, gain_ref, codes_ref, sems):
    pairs = [(codes_hbm, codes_ref), (proj_hbm, proj_ref), (gain_hbm, gain_ref)]
    for first, count in GROUPS:
        for a in range(3):
            part = pl.ds(9 * a + first, count)
            pairs.append((up_hbm.at[part], w_ref.at[part]))
    pairs.append((out_hbm, tap_ref))
    copies = [pltpu.make_async_copy(src, dst, sems.at[n]) for n, (src, dst) in enumerate(pairs)]
    for copy in copies:
        copy.start()
    for copy in copies[:3]:
        copy.wait()
    frames, rows, cols = codes_ref.shape
    codes = [codes_ref[t, r : r + 1, :] for t in range(frames) for r in range(rows)]
    act_ref[...] = latent_rows(codes, proj_ref[...], gain_ref[...]).astype(BF16)
    for g, group in enumerate(GROUPS):
        for copy in copies[3 + 3 * g : 6 + 3 * g]:
            copy.wait()
        early_products(act_ref, rows * cols, w_ref, acc_ref, group)
    copies[-1].wait()


def late_kernel(n, act_ref, w_ref, after_ref, acc_ref):
    for group in GROUPS:
        late_products(act_ref, n, w_ref, acc_ref, group)


def combine(rows, cols, share, own_ref, halo_ref, h_ref):
    def taken(slot, tap):
        if slot in (0, rows + 1):
            ref, span, row = halo_ref, 2 * cols, 0 if slot == 0 else 1
        else:
            ref, span, row = own_ref, rows * cols, slot - 1
        lanes = pl.ds(tap * share, share)
        return jnp.concatenate([ref[pl.ds(t * span + row * cols, cols), lanes] for t in range(2)], axis=0)

    for q in range(rows + 1):
        sums = [[], []]
        for c in range(3):
            x = taken(q, c) + taken(q + 1, 6 + c)
            sums[0].append(x + taken(q, 3 + c))
            sums[1].append(x + taken(q + 1, 3 + c))
        out = pl.ds(q * 2 * cols, 2 * cols)
        for py, (left, mid, right) in enumerate(sums):
            even = shifted(left, cols, 1) + (mid + right)
            odd = (left + mid) + shifted(right, cols, -1)
            h_ref[out, pl.ds(2 * py * share, share)] = even.astype(BF16)
            h_ref[out, pl.ds((2 * py + 1) * share, share)] = odd.astype(BF16)


def early_hidden_kernel(near_ref, far_ref, proj_ref, gain_ref, w_ref, own_ref, h_ref, act_ref, halo_ref):
    frames, rows, cols = near_ref.shape
    first = lax.axis_index("section") == 0
    place = lax.axis_index("rows")
    last = lax.axis_size("rows") - 1
    codes = []
    for t in range(frames):
        low = [ref[t, rows - 1 : rows, :] for ref in (near_ref, far_ref)]
        high = [ref[t, 0:1, :] for ref in (near_ref, far_ref)]
        codes += [jnp.where(first, low[0], low[1]), jnp.where(first, high[1], high[0])]
    act = latent_rows(codes, proj_ref[...], gain_ref[...])
    edge = lax.broadcasted_iota(jnp.int32, (frames, 2, cols, act.shape[1]), 1).reshape(act.shape)
    keep = jnp.where(edge == 0, (place > 0).astype(F32), (place < last).astype(F32))
    act_ref[...] = (act * keep).astype(BF16)
    for group in GROUPS:
        early_products(act_ref, 2 * cols, w_ref, halo_ref, group)
    combine(rows, cols, w_ref.shape[2], own_ref, halo_ref, h_ref)


def late_hidden_kernel(rows, cols, act_ref, w_ref, own_ref, h_ref, halo_ref):
    for group in GROUPS:
        late_products(act_ref, 2 * cols, w_ref, halo_ref, group)
    combine(rows, cols, w_ref.shape[2], own_ref, halo_ref, h_ref)


def normalise(size, own_ref, other_ref, gain_ref, norm_ref):
    pairs = own_ref.shape[0] // size
    part = own_ref.shape[1] // 4
    section = lax.axis_index("section")
    starts = [pl.multiple_of(k * part, part) for k in (section, 1 - section)]
    gains = [gain_ref[:, pl.ds(start, part)] for start in starts]
    place = lax.axis_index("rows")
    last = lax.axis_size("rows") - 1
    for q in range(pairs):
        for py in range(2):
            for px in range(2):
                lanes = pl.ds((2 * py + px) * part, part)
                x = [ref[pl.ds(q * size, size), lanes].astype(F32) for ref in (own_ref, other_ref)]
                mean = jnp.sum(x[0] * x[0] + x[1] * x[1], axis=1, keepdims=True) / (2 * part)
                scale = lax.rsqrt(mean + EPS)
                if q == 0 and py == 0:
                    scale = jnp.where(place > 0, scale, 0.0)
                if q == pairs - 1 and py == 1:
                    scale = jnp.where(place < last, scale, 0.0)
                for s in range(2):
                    value = silu(x[s] * scale * gains[s])
                    norm_ref[2 * q + py, :, pl.ds(starts[s] + 2 * px * part, part)] = value.astype(BF16)


def out_products(norm_ref, tap_ref, a, m):
    height = norm_ref.shape[0] - 2
    depth = norm_ref.shape[2]
    left = [norm_ref[pl.ds(b, height), pl.ds(0, m), :].reshape(height * m, depth) for b in range(3)]
    lines = [[], [], [], []]
    for b in range(3):
        w = [tap_ref[9 * a + 3 * b + c] for c in range(3)]
        zero = jnp.zeros_like(w[0])
        for line, cells in zip(lines, ((w[1], w[2]), (w[0], w[1]), (zero, w[0]), (w[2], zero))):
            line += cells
    right = jnp.concatenate([jnp.concatenate(line, axis=1) for line in lines], axis=0)
    total = lax.dot_general(
        jnp.concatenate(left, axis=1), right, (((1,), (1,)), ((), ())), preferred_element_type=F32
    )
    return total.reshape(height, m, right.shape[0])


def finish(y, full, cols, o_ref, mix_ref):
    rows = full.shape[0]
    ow = o_ref.shape[3]
    side = full[:, 2 * ow :]
    lane = lax.broadcasted_iota(jnp.int32, side.shape, 1)
    both = full[:, : 2 * ow] + jnp.where(lane < ow, shifted(side, cols, 1), shifted(side, cols, -1))
    mix_ref[y, pl.ds(0, rows, stride=2), :] = both
    mix_ref[y, pl.ds(1, rows, stride=2), :] = pltpu.roll(both, ow, 1)
    result = mix_ref[y][:, :ow].astype(BF16)
    for t in range(2):
        o_ref[t, y] = result[rows * t : rows * (t + 1)]


def early_out_kernel(cols, own_ref, other_ref, gain_ref, tap_ref, o_ref, acc_ref, norm_ref, mix_ref):
    size = 2 * cols
    normalise(size, own_ref, other_ref, gain_ref, norm_ref)
    now = out_products(norm_ref, tap_ref, 2, size)
    back = out_products(norm_ref, tap_ref, 1, size)
    acc_ref[...] = out_products(norm_ref, tap_ref, 0, size)
    acc_ref[:, pl.ds(0, cols), :] += back[:, cols:]
    for y in range(now.shape[0]):
        full = jnp.concatenate([now[y, :cols], now[y, cols:] + back[y, :cols]], axis=0)
        finish(y, full, cols, o_ref, mix_ref)


def late_out_kernel(cols, own_ref, other_ref, gain_ref, tap_ref, early_ref, acc_ref, o_hbm, o_ref, norm_ref, mix_ref, sems):
    size = 2 * cols
    first = pltpu.make_async_copy(early_ref, o_hbm.at[pl.ds(0, 2)], sems.at[0])
    first.start()
    normalise(size, own_ref, other_ref, gain_ref, norm_ref)
    now = out_products(norm_ref, tap_ref, 2, size)
    back = out_products(norm_ref, tap_ref, 1, -(-cols // 16) * 16)
    for y in range(now.shape[0]):
        held = acc_ref[y]
        full = jnp.concatenate([held[:cols] + now[y, :cols], held[cols:] + now[y, cols:] + back[y, :cols]], axis=0)
        finish(y, full, cols, o_ref, mix_ref)
    second = pltpu.make_async_copy(o_ref, o_hbm.at[pl.ds(2, 2)], sems.at[1])
    second.start()
    first.wait()
    second.wait()


def params(mib):
    return pltpu.CompilerParams(vmem_limit_bytes=mib * MIB)


def cost(mflops):
    return pl.CostEstimate(flops=mflops * 10**6, bytes_accessed=10**7, transcendentals=0)


def vmem():
    return pl.BlockSpec(memory_space=pltpu.VMEM)


def in_space(space, *arrays):
    return tuple(pltpu.with_memory_space_constraint(x, space) for x in arrays)


def body(codes, in_proj, gain_up, up_kernel, gain_res, out_kernel):
    frames, rows, cols = codes.shape
    size = 2 * cols
    width, share = up_kernel.shape[1:]
    ow, ch = out_kernel.shape[1:]
    pairs = rows + 1
    height = 2 * rows
    count = lax.axis_size("rows")
    joint = [(2 * i, 2 * i + 2) for i in range(count - 1)] + [(2 * i + 3, 2 * i + 1) for i in range(count - 1)]
    swap = [(0, 1), (1, 0)]
    near = lax.ppermute(codes, ("rows", "section"), joint)
    gain_res = gain_res.reshape(1, -1)
    up_kernel, out_kernel, codes, in_proj, gain_up = in_space(
        pltpu.HBM, up_kernel, out_kernel, codes, in_proj, gain_up.reshape(1, -1)
    )
    hbm = pl.BlockSpec(memory_space=pltpu.HBM)
    hidden_shape = pltpu.VMEM((pairs * size, 4 * share), BF16)

    own_early, act, w, tap, proj, gain = pl.pallas_call(
        own_kernel,
        out_shape=(
            pltpu.VMEM((2 * rows * cols, 9 * share), F32),
            pltpu.VMEM((frames * rows * cols, width), BF16),
            pltpu.VMEM(up_kernel.shape, BF16),
            pltpu.VMEM(out_kernel.shape, BF16),
            pltpu.VMEM(in_proj.shape, BF16),
            pltpu.VMEM(gain_up.shape, F32),
        ),
        in_specs=[hbm] * 5,
        out_specs=(vmem(),) * 6,
        scratch_shapes=[pltpu.VMEM(codes.shape, jnp.int32), pltpu.SemaphoreType.DMA((4 + 3 * len(GROUPS),))],
        compiler_params=params(6),
        cost_estimate=cost(2000),
        name="own_early",
    )(codes, in_proj, gain_up, up_kernel, out_kernel)
    own_early, act, w, tap, proj, gain = in_space(pltpu.VMEM, own_early, act, w, tap, proj, gain)

    near, proj = lax.optimization_barrier((near, proj))
    far = lax.ppermute(near, "section", swap)
    near, far = in_space(pltpu.VMEM, near, far)
    (own_late,) = in_space(
        pltpu.VMEM,
        pl.pallas_call(
            functools.partial(late_kernel, rows * cols),
            out_shape=pltpu.VMEM(own_early.shape, F32),
            in_specs=[vmem()] * 3,
            out_specs=vmem(),
            compiler_params=params(4),
            cost_estimate=cost(1000),
            name="own_late",
        )(act, w, near),
    )
    far, own_late = lax.optimization_barrier((far, own_late))

    early, halo = pl.pallas_call(
        early_hidden_kernel,
        out_shape=(hidden_shape, pltpu.VMEM((2 * frames * cols, width), BF16)),
        in_specs=[vmem()] * 6,
        out_specs=(vmem(),) * 2,
        scratch_shapes=[pltpu.VMEM((4 * cols, 9 * share), F32)],
        compiler_params=params(6),
        cost_estimate=cost(1000),
        name="hidden_early",
    )(near, far, proj, gain, w, own_early)
    early, halo = in_space(pltpu.VMEM, early, halo)
    early_other = lax.ppermute(early, "section", swap)

    (late,) = in_space(
        pltpu.VMEM,
        pl.pallas_call(
            functools.partial(late_hidden_kernel, rows, cols),
            out_shape=hidden_shape,
            in_specs=[vmem()] * 3,
            out_specs=vmem(),
            scratch_shapes=[pltpu.VMEM((4 * cols, 9 * share), F32)],
            compiler_params=params(6),
            cost_estimate=cost(1000),
            name="hidden_late",
        )(halo, w, own_late),
    )
    late_other = lax.ppermute(late, "section", swap)

    work = [pltpu.VMEM((2 * pairs, size, 2 * ch), BF16), pltpu.VMEM((height, 2 * size, 2 * ow), F32)]
    out_early, held = pl.pallas_call(
        functools.partial(early_out_kernel, cols),
        out_shape=(pltpu.VMEM((2, height, 2 * cols, ow), BF16), pltpu.VMEM((height, size, 4 * ow), F32)),
        in_specs=[vmem()] * 4,
        out_specs=(vmem(),) * 2,
        scratch_shapes=work,
        compiler_params=params(8),
        cost_estimate=cost(2000),
        name="out_early",
    )(early, *in_space(pltpu.VMEM, early_other), gain_res, tap)
    out_early, held = in_space(pltpu.VMEM, out_early, held)

    return pl.pallas_call(
        functools.partial(late_out_kernel, cols),
        out_shape=jax.ShapeDtypeStruct((frames, height, 2 * cols, ow), BF16),
        in_specs=[vmem()] * 6,
        out_specs=hbm,
        scratch_shapes=[pltpu.VMEM((2, height, 2 * cols, ow), BF16)] + work + [pltpu.SemaphoreType.DMA((2,))],
        compiler_params=params(8),
        cost_estimate=cost(1000),
        name="out_late",
    )(late, *in_space(pltpu.VMEM, late_other), gain_res, tap, out_early, held)


def solution(mesh):
    in_specs = (
        P("clip", "rows", None),
        P(),
        P(),
        P(None, None, "section"),
        P(),
        P(None, "section", None),
    )
    out_specs = P("clip", "rows", None, "section")
    return jax.shard_map(body, mesh=mesh, in_specs=in_specs, out_specs=out_specs, check_vma=False)
```

time: 15.5 us -> 15.3 us (0.987)
  waiting for transfers between devices: 0.81 us -> 0.35 us
  starting transfers between devices: 5.13 us -> 5.54 us
  Pallas kernels: 9.29 us -> 9.04 us
    ppermute x1, waiting for transfers between devices: 0.6 us -> 0.19 us  [body(): far = lax.ppermute(near, 'section', swap)]
    ppermute x1 -> x2, starting transfers between devices: 0.23 us -> 0.64 us  [the longest x1 0.38 us: body(): early_other = lax.ppermute(early, 'section', swap)]
    pallas_call x5 -> x6, Pallas kernels: 9.29 us -> 9.04 us  [the longest x1 3.02 us: body(): pl.pallas_call(own_kernel, out_shape=(pltpu.VMEM((2 * rows * cols, 9 * sh...]
  transfers between devices with their start and end apart: 3 -> 4, of which waited for: 2 -> 2; matrix products, arithmetic and copies ran while one was open for 0% -> 0% of each run, Pallas kernels for 33% -> 42%
where the time goes in v5:
time: 15.3 us; the launch traced here: 15 us
  Pallas kernels  9.04 us (59%)
  starting transfers between devices  5.54 us (36%)
  waiting for transfers between devices  0.35 us (2%)
    ppermute x1, starting transfers between devices, body(): near = lax.ppermute(codes, ('rows', 'section'), joint)  4.83 us
    pallas_call x1, Pallas kernels, body(): pl.pallas_call(own_kernel, out_shape=(pltpu.VMEM((2 * rows * cols, 9 * sh...  3.02 us
    pallas_call x1, Pallas kernels, body(): pl.pallas_call(functools.partial(late_out_kernel, cols), out_shape=jax.Sh...  1.88 us
    pallas_call x1, Pallas kernels, body(): pl.pallas_call(functools.partial(early_out_kernel, cols), out_shape=(pltp...  1.52 us
    pallas_call x1, Pallas kernels, body(): pl.pallas_call(functools.partial(late_kernel, rows * cols), out_shape=plt...  0.97 us
    pallas_call x1, Pallas kernels, body(): pl.pallas_call(early_hidden_kernel, out_shape=(hidden_shape, pltpu.VMEM((...  0.9 us
    pallas_call x1, Pallas kernels, body(): pl.pallas_call(functools.partial(late_hidden_kernel, rows, cols), out_sha...  0.77 us
    ppermute x1, starting transfers between devices, body(): early_other = lax.ppermute(early, 'section', swap)  0.38 us
  transfers between devices with their start and end apart: 4, of which 2 were waited for; matrix products, arithmetic and copies ran while one was open for 0% of the time, Pallas kernels for 42%

profile of v5, /device:TPU:0, one launch (start us, length us, event | category | flops | bytes accessed | tf_op | source)
XLA Modules:
  0.0 15.0 jit_solution(10553169088877088630)
XLA Ops:
  0.0 4.8 %collective-permute-start = (s32[4,4,24]{2,1,0:T(4,128)}, s32[4,4,24]{2,1,0:T(4,128)S(1)}, u32[]{:S(2)}, u32[]{:S(2)}) collective-permute-start(s32[4,4,24]{2,1,0:T(4,128)} %codes_hbm.1), channel_id=1, source_target_pairs={{0,2},{2,4},{4,6},{6,8},{8,10},{10,12},{12,14},{3,1},{5,3},{7,5},{... | collective-permute-start | bytes 4616 | tf_op jit(solution)/shard_map/ppermute | solution.py:254
  4.8 3.0 %own_early.1 = (f32[192,1152]{1,0:T(8,128)S(1)}, bf16[384,512]{1,0:T(8,128)(2,1)S(1)}, bf16[27,512,128]{2,1,0:T(8,128)(2,1)S(1)}, bf16[27,64,256]{2,1,0:T(8,128)...) custom-call(s32[4,4,24]{2,1,0:T(4,128)} %codes_hbm.1, bf16[18,512]{1,0:T(8,128)(2,1)} %proj_hbm.1, ...), custom_call_target="tpu_custom_call" | custom-call | flops 2000000000 | bytes 10000000 | tf_op jit(solution)/shard_map/own_early/pallas_call | solution.py:262
  7.9 0.0 collective-permute-done.after_ref.near_ref
  7.9 0.1 collective-permute-start.1
  8.0 1.0 %own_late.1.own_ref = f32[192,1152]{1,0:T(8,128)S(1)} custom-call(bf16[384,512]{1,0:T(8,128)(2,1)S(1)} %get-tuple-element.21.act_ref, bf16[27,512,128]{2,1,0:T(8,128)(2,1)S(1)} %get-tuple-element.22.w_ref, s32[4,4,24]{2,1,0:T(4,128)S(1)} %collective-permute-done.after_ref.near_ref), custom_call_target="tpu_custom_call" | custom-call | flops 1000000000 | bytes 10000000 | tf_op jit(solution)/shard_map/own_late/pallas_call | solution.py:286
  8.9 0.2 %collective-permute-done.1.far_ref = s32[4,4,24]{2,1,0:T(4,128)S(1)} collective-permute-done((s32[4,4,24]{2,1,0:T(4,128)S(1)}, s32[4,4,24]{2,1,0:T(4,128)S(1)}, u32[]{:S(2)}, u32[]{:S(2)}) %collective-permute-start.1) | collective-permute-done | bytes 1568 | tf_op jit(solution)/shard_map/ppermute | solution.py:282
  9.1 0.9 %hidden_early.1 = (bf16[240,512]{1,0:T(8,128)(2,1)S(1)}, bf16[192,512]{1,0:T(8,128)(2,1)S(1)}) custom-call(s32[4,4,24]{2,1,0:T(4,128)S(1)} %collective-permute-done.after_ref.near_ref, s32[4,4,24]{2,1,0:T(4,128)S(1)} %collective-permute-done.1.far_ref, bf16[18,512]{1,0:T(8,128)(2,1)S(1)} %get-tuple-element.24.proj_ref, ...), custom_call_target="tpu_custom_call" | custom-call | flops 1000000000 | bytes 10000000 | tf_op jit(solution)/shard_map/hidden_early/pallas_call | solution.py:298
  10.0 0.0 copy-start
  10.0 0.4 %collective-permute-start.3 = (bf16[240,512]{1,0:T(8,128)(2,1)S(1)}, bf16[240,512]{1,0:T(8,128)(2,1)S(1)}, u32[]{:S(2)}, u32[]{:S(2)}) collective-permute-start(bf16[240,512]{1,0:T(8,128)(2,1)S(1)} %get-tuple-element.30.own_ref), channel_id=1, source_target_pairs={{0,1},{1,0},{2,3},{3,2},{4,5},{5,4},{6,7},{7,6},{8,9},{9,8},{10,11... | collective-permute-start | bytes 737288 | tf_op jit(solution)/shard_map/ppermute | solution.py:309
  10.4 0.8 %hidden_late.1.own_ref = bf16[240,512]{1,0:T(8,128)(2,1)S(1)} custom-call(bf16[192,512]{1,0:T(8,128)(2,1)S(1)} %get-tuple-element.27.act_ref, bf16[27,512,128]{2,1,0:T(8,128)(2,1)S(1)} %get-tuple-element.22.w_ref, f32[192,1152]{1,0:T(8,128)S(1)} %own_late.1.own_ref), custom_call_target="tpu_custom_call" | custom-call | flops 1000000000 | bytes 10000000 | tf_op jit(solution)/shard_map/hidden_late/pallas_call | solution.py:313
  11.2 0.3 %collective-permute-start.2 = (bf16[240,512]{1,0:T(8,128)(2,1)S(1)}, bf16[240,512]{1,0:T(8,128)(2,1)S(1)}, u32[]{:S(2)}, u32[]{:S(2)}) collective-permute-start(bf16[240,512]{1,0:T(8,128)(2,1)S(1)} %hidden_late.1.own_ref), channel_id=1, source_target_pairs={{0,1},{1,0},{2,3},{3,2},{4,5},{5,4},{6,7},{7,6},{8,9},{9,8},{10,11... | collective-permute-start | bytes 737288 | tf_op jit(solution)/shard_map/ppermute | solution.py:324
  11.4 0.2 %collective-permute-done.3.other_ref = bf16[240,512]{1,0:T(8,128)(2,1)S(1)} collective-permute-done((bf16[240,512]{1,0:T(8,128)(2,1)S(1)}, bf16[240,512]{1,0:T(8,128)(2,1)S(1)}, u32[]{:S(2)}, u32[]{:S(2)}) %collective-permute-start.3) | collective-permute-done | bytes 245792 | tf_op jit(solution)/shard_map/ppermute | solution.py:309
  11.6 0.0 copy-done
  11.6 1.5 %out_early.1 = (bf16[2,8,48,64]{3,2,1,0:T(8,128)(2,1)S(1)}, f32[8,48,256]{2,1,0:T(8,128)S(1)}) custom-call(bf16[240,512]{1,0:T(8,128)(2,1)S(1)} %get-tuple-element.30.own_ref, bf16[240,512]{1,0:T(8,128)(2,1)S(1)} %collective-permute-done.3.other_ref, f32[1,256]{1,0:T(1,128)S(1)} %bitcast.2, bf16[27,64,256]{2,1,0:T(8,128)(2,1)S(1)} %get-tuple-element.29.tap_ref), custom_call_target="tpu_custom_call" | custom-call | flops 2000000000 | bytes 10000000 | tf_op jit(solution)/shard_map/out_early/pallas_call | solution.py:327
  13.1 0.0 collective-permute-done.2.other_ref
  13.1 1.9 %out_late.1 = bf16[4,8,48,64]{3,2,1,0:T(8,128)(2,1)} custom-call(bf16[240,512]{1,0:T(8,128)(2,1)S(1)} %hidden_late.1.own_ref, bf16[240,512]{1,0:T(8,128)(2,1)S(1)} %collective-permute-done.2.other_ref, f32[1,256]{1,0:T(1,128)S(1)} %bitcast.3, bf16[27,64,256]{2,1,0:T(8,128)(2,1)S(1)} %get-tuple-element.29.tap_ref, ...), custom_call_target="tpu_custom_call" | custom-call | flops 1000000000 | bytes 10000000 | tf_op jit(solution)/shard_map/out_late/pallas_call | solution.py:339
Async XLA Ops:
  0.0 7.9 %collective-permute-start = (s32[4,4,24]{2,1,0:T(4,128)}, s32[4,4,24]{2,1,0:T(4,128)S(1)}, u32[]{:S(2)}, u32[]{:S(2)}) collective-permute-start(s32[4,4,24]{2,1,0:T(4,128)} %codes_hbm.1), channel_id=1, source_target_pairs={{0,2},{2,4},{4,6},{6,8},{8,10},{10,12},{12,14},{3,1},{5,3},{7,5},{... | collective-permute-start | bytes 4616 | tf_op jit(solution)/shard_map/ppermute | solution.py:254
  7.9 1.2 %collective-permute-start.1 = (s32[4,4,24]{2,1,0:T(4,128)S(1)}, s32[4,4,24]{2,1,0:T(4,128)S(1)}, u32[]{:S(2)}, u32[]{:S(2)}) collective-permute-start(s32[4,4,24]{2,1,0:T(4,128)S(1)} %collective-permute-done.after_ref.near_ref), channel_id=1, source_target_pairs={{0,1},{1,0},{2,3},{3,2},{4,5},{5,4},{6,7},{7,6},{8,9},{9,8},{10,11... | collective-permute-start | bytes 4616 | tf_op jit(solution)/shard_map/ppermute | solution.py:282
  10.0 1.6 %copy-start = (f32[256]{0:T(256)S(1)}, f32[256]{0:T(256)}, u32[]{:S(2)}) copy-start(f32[256]{0:T(256)} %param.10) | copy-start | bytes 3076
  10.0 1.6 %collective-permute-start.3 = (bf16[240,512]{1,0:T(8,128)(2,1)S(1)}, bf16[240,512]{1,0:T(8,128)(2,1)S(1)}, u32[]{:S(2)}, u32[]{:S(2)}) collective-permute-start(bf16[240,512]{1,0:T(8,128)(2,1)S(1)} %get-tuple-element.30.own_ref), channel_id=1, source_target_pairs={{0,1},{1,0},{2,3},{3,2},{4,5},{5,4},{6,7},{7,6},{8,9},{9,8},{10,11... | collective-permute-start | bytes 737288 | tf_op jit(solution)/shard_map/ppermute | solution.py:309
  11.2 2.0 %collective-permute-start.2 = (bf16[240,512]{1,0:T(8,128)(2,1)S(1)}, bf16[240,512]{1,0:T(8,128)(2,1)S(1)}, u32[]{:S(2)}, u32[]{:S(2)}) collective-permute-start(bf16[240,512]{1,0:T(8,128)(2,1)S(1)} %hidden_late.1.own_ref), channel_id=1, source_target_pairs={{0,1},{1,0},{2,3},{3,2},{4,5},{5,4},{6,7},{7,6},{8,9},{9,8},{10,11... | collective-permute-start | bytes 737288 | tf_op jit(solution)/shard_map/ppermute | solution.py:324

commit v6 on v5

--- a/solution.py
+++ b/solution.py
@@ -42,38 +42,38 @@
     return jnp.where(place == (0 if amount == 1 else cols - 1), 0.0, moved)
 
 
-def weights(w_ref, a, group):
-    return jnp.concatenate([w_ref[9 * a + group[0] + k] for k in range(group[1])], axis=1)
-
-
-def early_products(act, n, w_ref, acc_ref, group):
-    lanes = pl.ds(group[0] * w_ref.shape[2], group[1] * w_ref.shape[2])
+def weights(w_refs, a, group):
+    ref, first = (w_refs[0], 0) if a == 0 else (w_refs[1], 9 * (a - 1))
+    return jnp.concatenate([ref[first + group[0] + k] for k in range(group[1])], axis=1)
+
+
+def early_products(act, n, w_refs, acc_ref, group):
+    share = w_refs[1].shape[2]
+    lanes = pl.ds(group[0] * share, group[1] * share)
     if group[1] == 1:
-        both = jnp.concatenate([weights(w_ref, 2, group), weights(w_ref, 1, group)], axis=1)
+        both = jnp.concatenate([weights(w_refs, 2, group), weights(w_refs, 1, group)], axis=1)
         now = jnp.dot(act[pl.ds(0, 2 * n), :], both, preferred_element_type=F32)
-        half = w_ref.shape[2]
-        now, back = now[:, :half], now[:n, half:]
+        now, back = now[:, :share], now[:n, share:]
     else:
-        now = jnp.dot(act[pl.ds(0, 2 * n), :], weights(w_ref, 2, group), preferred_element_type=F32)
-        back = jnp.dot(act[pl.ds(0, n), :], weights(w_ref, 1, group), preferred_element_type=F32)
+        now = jnp.dot(act[pl.ds(0, 2 * n), :], weights(w_refs, 2, group), preferred_element_type=F32)
+        back = jnp.dot(act[pl.ds(0, n), :], weights(w_refs, 1, group), preferred_element_type=F32)
     acc_ref[pl.ds(0, n), lanes] = now[:n]
     acc_ref[pl.ds(n, n), lanes] = now[n:] + back
 
 
-def late_products(act, n, w_ref, acc_ref, group):
-    lanes = pl.ds(group[0] * w_ref.shape[2], group[1] * w_ref.shape[2])
+def late_products(act, n, w_refs, acc_ref, group):
+    share = w_refs[1].shape[2]
+    lanes = pl.ds(group[0] * share, group[1] * share)
     left = jnp.concatenate([act[pl.ds(a * n, 2 * n), :] for a in range(3)], axis=1)
-    right = jnp.concatenate([weights(w_ref, a, group) for a in range(3)], axis=0)
+    right = jnp.concatenate([weights(w_refs, a, group) for a in range(3)], axis=0)
     acc_ref[:, lanes] = jnp.dot(left, right, preferred_element_type=F32)
 
 
-def own_kernel(codes_hbm, proj_hbm, gain_hbm, up_hbm, out_hbm, acc_ref, act_ref, w_ref, tap_ref, proj_ref, gain_ref, codes_ref, sems):
+def own_kernel(codes_hbm, proj_hbm, gain_hbm, up_hbm, acc_ref, act_ref, w_ref, proj_ref, gain_ref, codes_ref, sems):
     pairs = [(codes_hbm, codes_ref), (proj_hbm, proj_ref), (gain_hbm, gain_ref)]
     for first, count in GROUPS:
-        for a in range(3):
-            part = pl.ds(9 * a + first, count)
-            pairs.append((up_hbm.at[part], w_ref.at[part]))
-    pairs.append((out_hbm, tap_ref))
+        for a in (1, 2):
+            pairs.append((up_hbm.at[pl.ds(9 * a + first, count)], w_ref.at[pl.ds(9 * (a - 1) + first, count)]))
     copies = [pltpu.make_async_copy(src, dst, sems.at[n]) for n, (src, dst) in enumerate(pairs)]
     for copy in copies:
         copy.start()
@@ -83,15 +83,21 @@
     codes = [codes_ref[t, r : r + 1, :] for t in range(frames) for r in range(rows)]
     act_ref[...] = latent_rows(codes, proj_ref[...], gain_ref[...]).astype(BF16)
     for g, group in enumerate(GROUPS):
-        for copy in copies[3 + 3 * g : 6 + 3 * g]:
+        for copy in copies[3 + 2 * g : 5 + 2 * g]:
             copy.wait()
-        early_products(act_ref, rows * cols, w_ref, acc_ref, group)
-    copies[-1].wait()
-
-
-def late_kernel(n, act_ref, w_ref, after_ref, acc_ref):
-    for group in GROUPS:
-        late_products(act_ref, n, w_ref, acc_ref, group)
+        early_products(act_ref, rows * cols, (None, w_ref), acc_ref, group)
+
+
+def late_kernel(n, act_ref, w_ref, up_hbm, after_ref, acc_ref, first_ref, sems):
+    copies = []
+    for g, (first, count) in enumerate(GROUPS):
+        part = pl.ds(first, count)
+        copies.append(pltpu.make_async_copy(up_hbm.at[part], first_ref.at[part], sems.at[g]))
+    for copy in copies:
+        copy.start()
+    for copy, group in zip(copies, GROUPS):
+        copy.wait()
+        late_products(act_ref, n, (first_ref, w_ref), acc_ref, group)
 
 
 def combine(rows, cols, share, own_ref, halo_ref, h_ref):
@@ -132,13 +138,13 @@
     keep = jnp.where(edge == 0, (place > 0).astype(F32), (place < last).astype(F32))
     act_ref[...] = (act * keep).astype(BF16)
     for group in GROUPS:
-        early_products(act_ref, 2 * cols, w_ref, halo_ref, group)
+        early_products(act_ref, 2 * cols, (None, w_ref), halo_ref, group)
     combine(rows, cols, w_ref.shape[2], own_ref, halo_ref, h_ref)
 
 
-def late_hidden_kernel(rows, cols, act_ref, w_ref, own_ref, h_ref, halo_ref):
+def late_hidden_kernel(rows, cols, act_ref, first_ref, w_ref, own_ref, h_ref, halo_ref):
     for group in GROUPS:
-        late_products(act_ref, 2 * cols, w_ref, halo_ref, group)
+        late_products(act_ref, 2 * cols, (first_ref, w_ref), halo_ref, group)
     combine(rows, cols, w_ref.shape[2], own_ref, halo_ref, h_ref)
 
 
@@ -253,45 +259,44 @@
     swap = [(0, 1), (1, 0)]
     near = lax.ppermute(codes, ("rows", "section"), joint)
     gain_res = gain_res.reshape(1, -1)
-    up_kernel, out_kernel, codes, in_proj, gain_up = in_space(
-        pltpu.HBM, up_kernel, out_kernel, codes, in_proj, gain_up.reshape(1, -1)
-    )
+    up_kernel, codes, in_proj, gain_up = in_space(pltpu.HBM, up_kernel, codes, in_proj, gain_up.reshape(1, -1))
+    (tap,) = in_space(pltpu.VMEM, out_kernel)
     hbm = pl.BlockSpec(memory_space=pltpu.HBM)
     hidden_shape = pltpu.VMEM((pairs * size, 4 * share), BF16)
 
-    own_early, act, w, tap, proj, gain = pl.pallas_call(
+    own_early, act, w, proj, gain = pl.pallas_call(
         own_kernel,
         out_shape=(
             pltpu.VMEM((2 * rows * cols, 9 * share), F32),
             pltpu.VMEM((frames * rows * cols, width), BF16),
-            pltpu.VMEM(up_kernel.shape, BF16),
-            pltpu.VMEM(out_kernel.shape, BF16),
+            pltpu.VMEM((18, width, share), BF16),
             pltpu.VMEM(in_proj.shape, BF16),
             pltpu.VMEM(gain_up.shape, F32),
         ),
-        in_specs=[hbm] * 5,
-        out_specs=(vmem(),) * 6,
-        scratch_shapes=[pltpu.VMEM(codes.shape, jnp.int32), pltpu.SemaphoreType.DMA((4 + 3 * len(GROUPS),))],
+        in_specs=[hbm] * 4,
+        out_specs=(vmem(),) * 5,
+        scratch_shapes=[pltpu.VMEM(codes.shape, jnp.int32), pltpu.SemaphoreType.DMA((3 + 2 * len(GROUPS),))],
         compiler_params=params(6),
         cost_estimate=cost(2000),
         name="own_early",
-    )(codes, in_proj, gain_up, up_kernel, out_kernel)
-    own_early, act, w, tap, proj, gain = in_space(pltpu.VMEM, own_early, act, w, tap, proj, gain)
+    )(codes, in_proj, gain_up, up_kernel)
+    own_early, act, w, proj, gain = in_space(pltpu.VMEM, own_early, act, w, proj, gain)
 
     near, proj = lax.optimization_barrier((near, proj))
     far = lax.ppermute(near, "section", swap)
     near, far = in_space(pltpu.VMEM, near, far)
-    (own_late,) = in_space(
+    own_late, w_first = in_space(
         pltpu.VMEM,
-        pl.pallas_call(
+        *pl.pallas_call(
             functools.partial(late_kernel, rows * cols),
-            out_shape=pltpu.VMEM(own_early.shape, F32),
-            in_specs=[vmem()] * 3,
-            out_specs=vmem(),
+            out_shape=(pltpu.VMEM(own_early.shape, F32), pltpu.VMEM((9, width, share), BF16)),
+            in_specs=[vmem(), vmem(), hbm, vmem()],
+            out_specs=(vmem(),) * 2,
+            scratch_shapes=[pltpu.SemaphoreType.DMA((len(GROUPS),))],
             compiler_params=params(4),
             cost_estimate=cost(1000),
             name="own_late",
-        )(act, w, near),
+        )(act, w, up_kernel, near),
     )
     far, own_late = lax.optimization_barrier((far, own_late))
 
@@ -313,13 +318,13 @@
         pl.pallas_call(
             functools.partial(late_hidden_kernel, rows, cols),
             out_shape=hidden_shape,
-            in_specs=[vmem()] * 3,
+            in_specs=[vmem()] * 4,
             out_specs=vmem(),
             scratch_shapes=[pltpu.VMEM((4 * cols, 9 * share), F32)],
             compiler_params=params(6),
             cost_estimate=cost(1000),
             name="hidden_late",
-        )(halo, w, own_late),
+        )(halo, w_first, w, own_late),
     )
     late_other = lax.ppermute(late, "section", swap)
 

time: 15.3 us -> 17.3 us (1.13)
  Pallas kernels: 9.04 us -> 11.1 us
    pallas_call x1, Pallas kernels: 0.97 us -> 3.11 us  [body(): pl.pallas_call(functools.partial(late_kernel, rows * cols), out_shape=(pl...]
    ppermute x1, waiting for transfers between devices: 0.19 us -> 0.01 us  [body(): far = lax.ppermute(near, 'section', swap)]
    ppermute x1, starting transfers between devices: 0.38 us -> 0.56 us  [body(): early_other = lax.ppermute(early, 'section', swap)]
  transfers between devices with their start and end apart: 4 -> 4, of which waited for: 2 -> 1; matrix products, arithmetic and copies ran while one was open for 0% -> 0% of each run, Pallas kernels for 42% -> 49%
where the time goes in v6:
time: 17.3 us; the launch traced here: 17.1 us
  Pallas kernels  11.1 us (64%)
  starting transfers between devices  5.56 us (32%)
  waiting for transfers between devices  0.24 us (1%)
    ppermute x1, starting transfers between devices, body(): near = lax.ppermute(codes, ('rows', 'section'), joint)  4.83 us
    pallas_call x1, Pallas kernels, body(): pl.pallas_call(functools.partial(late_kernel, rows * cols), out_shape=(pl...  3.11 us
    pallas_call x1, Pallas kernels, body(): pl.pallas_call(own_kernel, out_shape=(pltpu.VMEM((2 * rows * cols, 9 * sh...  2.93 us
    pallas_call x1, Pallas kernels, body(): pl.pallas_call(functools.partial(late_out_kernel, cols), out_shape=jax.Sh...  1.89 us
    pallas_call x1, Pallas kernels, body(): pl.pallas_call(functools.partial(early_out_kernel, cols), out_shape=(pltp...  1.51 us
    pallas_call x1, Pallas kernels, body(): pl.pallas_call(early_hidden_kernel, out_shape=(hidden_shape, pltpu.VMEM((...  0.9 us
    pallas_call x1, Pallas kernels, body(): pl.pallas_call(functools.partial(late_hidden_kernel, rows, cols), out_sha...  0.79 us
    ppermute x1, starting transfers between devices, body(): early_other = lax.ppermute(early, 'section', swap)  0.56 us
  transfers between devices with their start and end apart: 4, of which 1 were waited for; matrix products, arithmetic and copies ran while one was open for 0% of the time, Pallas kernels for 49%

profile of v6, /device:TPU:0, one launch (start us, length us, event | category | flops | bytes accessed | tf_op | source)
XLA Modules:
  0.0 17.1 jit_solution(8483372889979843854)
XLA Ops:
  0.0 4.8 %collective-permute-start = (s32[4,4,24]{2,1,0:T(4,128)}, s32[4,4,24]{2,1,0:T(4,128)S(1)}, u32[]{:S(2)}, u32[]{:S(2)}) collective-permute-start(s32[4,4,24]{2,1,0:T(4,128)} %codes_hbm.1), channel_id=1, source_target_pairs={{0,2},{2,4},{4,6},{6,8},{8,10},{10,12},{12,14},{3,1},{5,3},{7,5},{... | collective-permute-start | bytes 4616 | tf_op jit(solution)/shard_map/ppermute | solution.py:260
  4.8 2.9 %own_early.1 = (f32[192,1152]{1,0:T(8,128)S(1)}, bf16[384,512]{1,0:T(8,128)(2,1)S(1)}, bf16[18,512,128]{2,1,0:T(8,128)(2,1)S(1)}, bf16[18,512]{1,0:T(8,128)(2,1)S(1)}, f32[1,512]{1,0:T(1,128)S(1)}) custom-call(s32[4,4,24]{2,1,0:T(4,128)} %codes_hbm.1, bf16[18,512]{1,0:T(8,128)(2,1)} %proj_hbm.1, f32[1,512]{1,0:T(1,128)} %bitcast.4, bf16[27,512,128]{2,1,0:T(8,128)(2,1)} %up_hbm.3), custom_call_target="tpu_custom_call" | custom-call | flops 2000000000 | bytes 10000000 | tf_op jit(solution)/shard_map/own_early/pallas_call | solution.py:267
  7.8 0.0 collective-permute-done.after_ref.near_ref
  7.8 0.1 collective-permute-start.1
  7.9 3.1 %own_late.1 = (f32[192,1152]{1,0:T(8,128)S(1)}, bf16[9,512,128]{2,1,0:T(8,128)(2,1)S(1)}) custom-call(bf16[384,512]{1,0:T(8,128)(2,1)S(1)} %get-tuple-element.22.act_ref, bf16[18,512,128]{2,1,0:T(8,128)(2,1)S(1)} %get-tuple-element.23.w_ref, bf16[27,512,128]{2,1,0:T(8,128)(2,1)} %up_hbm.3, s32[4,4,24]{2,1,0:T(4,128)S(1)} %collective-permute-done.after_ref.near_ref), custom_call_target="tpu_custom_call" | custom-call | flops 1000000000 | bytes 10000000 | tf_op jit(solution)/shard_map/own_late/pallas_call | solution.py:290
  11.0 0.0 collective-permute-done.1.far_ref
  11.0 0.9 %hidden_early.1 = (bf16[240,512]{1,0:T(8,128)(2,1)S(1)}, bf16[192,512]{1,0:T(8,128)(2,1)S(1)}) custom-call(s32[4,4,24]{2,1,0:T(4,128)S(1)} %collective-permute-done.after_ref.near_ref, s32[4,4,24]{2,1,0:T(4,128)S(1)} %collective-permute-done.1.far_ref, bf16[18,512]{1,0:T(8,128)(2,1)S(1)} %get-tuple-element.26.proj_ref, ...), custom_call_target="tpu_custom_call" | custom-call | flops 1000000000 | bytes 10000000 | tf_op jit(solution)/shard_map/hidden_early/pallas_call | solution.py:303
  11.9 0.6 %collective-permute-start.3 = (bf16[240,512]{1,0:T(8,128)(2,1)S(1)}, bf16[240,512]{1,0:T(8,128)(2,1)S(1)}, u32[]{:S(2)}, u32[]{:S(2)}) collective-permute-start(bf16[240,512]{1,0:T(8,128)(2,1)S(1)} %get-tuple-element.32.own_ref), channel_id=1, source_target_pairs={{0,1},{1,0},{2,3},{3,2},{4,5},{5,4},{6,7},{7,6},{8,9},{9,8},{10,11... | collective-permute-start | bytes 737288 | tf_op jit(solution)/shard_map/ppermute | solution.py:314
  12.5 0.0 copy-start
  12.5 0.0 copy-start.1
  12.5 0.8 %hidden_late.1.own_ref = bf16[240,512]{1,0:T(8,128)(2,1)S(1)} custom-call(bf16[192,512]{1,0:T(8,128)(2,1)S(1)} %get-tuple-element.29.act_ref, bf16[9,512,128]{2,1,0:T(8,128)(2,1)S(1)} %get-tuple-element.30.first_ref, bf16[18,512,128]{2,1,0:T(8,128)(2,1)S(1)} %get-tuple-element.23.w_ref, f32[192,1152]{1,0:T(8,128)S(1)} %get-tuple-element.31.own_ref), custom_call_target="tpu_custom_call" | custom-call | flops 1000000000 | bytes 10000000 | tf_op jit(solution)/shard_map/hidden_late/pallas_call | solution.py:318
  13.3 0.1 collective-permute-start.2
  13.4 0.2 %collective-permute-done.3.other_ref = bf16[240,512]{1,0:T(8,128)(2,1)S(1)} collective-permute-done((bf16[240,512]{1,0:T(8,128)(2,1)S(1)}, bf16[240,512]{1,0:T(8,128)(2,1)S(1)}, u32[]{:S(2)}, u32[]{:S(2)}) %collective-permute-start.3) | collective-permute-done | bytes 245792 | tf_op jit(solution)/shard_map/ppermute | solution.py:314
  13.6 0.0 copy-done
  13.6 0.0 copy-done.1
  13.6 1.5 %out_early.1 = (bf16[2,8,48,64]{3,2,1,0:T(8,128)(2,1)S(1)}, f32[8,48,256]{2,1,0:T(8,128)S(1)}) custom-call(bf16[240,512]{1,0:T(8,128)(2,1)S(1)} %get-tuple-element.32.own_ref, bf16[240,512]{1,0:T(8,128)(2,1)S(1)} %collective-permute-done.3.other_ref, f32[1,256]{1,0:T(1,128)S(1)} %bitcast.2, bf16[27,64,256]{2,1,0:T(8,128)(2,1)S(1)} %copy-done), custom_call_target="tpu_custom_call" | custom-call | flops 2000000000 | bytes 10000000 | tf_op jit(solution)/shard_map/out_early/pallas_call | solution.py:332
  15.2 0.0 collective-permute-done.2.other_ref
  15.2 1.9 %out_late.1 = bf16[4,8,48,64]{3,2,1,0:T(8,128)(2,1)} custom-call(bf16[240,512]{1,0:T(8,128)(2,1)S(1)} %hidden_late.1.own_ref, bf16[240,512]{1,0:T(8,128)(2,1)S(1)} %collective-permute-done.2.other_ref, f32[1,256]{1,0:T(1,128)S(1)} %bitcast.3, bf16[27,64,256]{2,1,0:T(8,128)(2,1)S(1)} %copy-done, bf16[2,8,48,64]{3,2,1,0:T(8,128)(2,1)S(1)} %get-tuple-element.33.early_ref, ...), custom_call_target="tpu_custom_call" | custom-call | flops 1000000000 | bytes 10000000 | tf_op jit(solution)/shard_map/out_late/pallas_call | solution.py:344
Async XLA Ops:
  0.0 7.8 %collective-permute-start = (s32[4,4,24]{2,1,0:T(4,128)}, s32[4,4,24]{2,1,0:T(4,128)S(1)}, u32[]{:S(2)}, u32[]{:S(2)}) collective-permute-start(s32[4,4,24]{2,1,0:T(4,128)} %codes_hbm.1), channel_id=1, source_target_pairs={{0,2},{2,4},{4,6},{6,8},{8,10},{10,12},{12,14},{3,1},{5,3},{7,5},{... | collective-permute-start | bytes 4616 | tf_op jit(solution)/shard_map/ppermute | solution.py:260
  7.8 3.2 %collective-permute-start.1 = (s32[4,4,24]{2,1,0:T(4,128)S(1)}, s32[4,4,24]{2,1,0:T(4,128)S(1)}, u32[]{:S(2)}, u32[]{:S(2)}) collective-permute-start(s32[4,4,24]{2,1,0:T(4,128)S(1)} %collective-permute-done.after_ref.near_ref), channel_id=1, source_target_pairs={{0,1},{1,0},{2,3},{3,2},{4,5},{5,4},{6,7},{7,6},{8,9},{9,8},{10,11... | collective-permute-start | bytes 4616 | tf_op jit(solution)/shard_map/ppermute | solution.py:286
  11.9 1.7 %collective-permute-start.3 = (bf16[240,512]{1,0:T(8,128)(2,1)S(1)}, bf16[240,512]{1,0:T(8,128)(2,1)S(1)}, u32[]{:S(2)}, u32[]{:S(2)}) collective-permute-start(bf16[240,512]{1,0:T(8,128)(2,1)S(1)} %get-tuple-element.32.own_ref), channel_id=1, source_target_pairs={{0,1},{1,0},{2,3},{3,2},{4,5},{5,4},{6,7},{7,6},{8,9},{9,8},{10,11... | collective-permute-start | bytes 737288 | tf_op jit(solution)/shard_map/ppermute | solution.py:314
  12.5 1.2 %copy-start = (bf16[27,64,256]{2,1,0:T(8,128)(2,1)S(1)}, bf16[27,64,256]{2,1,0:T(8,128)(2,1)}, u32[]{:S(2)}) copy-start(bf16[27,64,256]{2,1,0:T(8,128)(2,1)} %tap_ref.3) | copy-start | bytes 2654212
  12.5 1.2 %copy-start.1 = (f32[256]{0:T(256)S(1)}, f32[256]{0:T(256)}, u32[]{:S(2)}) copy-start(f32[256]{0:T(256)} %param.10) | copy-start | bytes 3076
  13.3 1.9 %collective-permute-start.2 = (bf16[240,512]{1,0:T(8,128)(2,1)S(1)}, bf16[240,512]{1,0:T(8,128)(2,1)S(1)}, u32[]{:S(2)}, u32[]{:S(2)}) collective-permute-start(bf16[240,512]{1,0:T(8,128)(2,1)S(1)} %hidden_late.1.own_ref), channel_id=1, source_target_pairs={{0,1},{1,0},{2,3},{3,2},{4,5},{5,4},{6,7},{7,6},{8,9},{9,8},{10,11... | collective-permute-start | bytes 737288 | tf_op jit(solution)/shard_map/ppermute | solution.py:329

commit v7 on v5

v7 whole, which is shorter than its diff:
```python
import functools

import jax
import jax.numpy as jnp
from jax import lax
from jax.experimental import pallas as pl
from jax.experimental.pallas import tpu as pltpu
from jax.sharding import PartitionSpec as P

BITS = 18
EPS = 1e-06
F32 = jnp.float32
BF16 = jnp.bfloat16
MIB = 1024 * 1024
GROUPS = ((0, 2), (2, 2), (4, 2), (6, 2), (8, 1))
SPLIT = 1


def silu_of_half(h):
    return h + h * jnp.tanh(h)


def latent_rows(rows, in_proj, gain):
    cols = rows[0].shape[1]
    count = len(rows)
    wide = jnp.concatenate([jnp.broadcast_to(row, (cols, cols)) for row in rows], axis=0)
    sub = lax.broadcasted_iota(jnp.int32, (count, cols, cols), 1).reshape(count * cols, cols)
    lane = lax.broadcasted_iota(jnp.int32, (count * cols, cols), 1)
    picked = jnp.where(sub == lane, wide, 0).astype(F32)
    column = jnp.sum(picked, axis=1, keepdims=True).astype(jnp.int32)
    spread = jnp.broadcast_to(column, (count * cols, BITS))
    shift = lax.broadcasted_iota(jnp.int32, (count * cols, BITS), 1)
    bits = ((jnp.right_shift(spread, shift) & 1) * 2 - 1).astype(F32).astype(BF16)
    latent = jnp.dot(bits, in_proj, preferred_element_type=F32)
    mean = jnp.mean(latent * latent, axis=1, keepdims=True)
    return silu_of_half(latent * lax.rsqrt(mean + EPS) * (0.5 * gain))


def shifted(x, cols, amount):
    rows, lanes = x.shape
    place = lax.broadcasted_iota(jnp.int32, (rows // cols, cols, lanes), 1).reshape(rows, lanes)
    moved = pltpu.roll(x, amount % rows, 0)
    return jnp.where(place == (0 if amount == 1 else cols - 1), 0.0, moved)


def weights(w_ref, a, group):
    return jnp.concatenate([w_ref[9 * a + group[0] + k] for k in range(group[1])], axis=1)


def early_products(act, n, w_ref, group):
    share = w_ref.shape[2]
    if group[1] == 1:
        both = jnp.concatenate([weights(w_ref, 2, group), weights(w_ref, 1, group)], axis=1)
        now = jnp.dot(act[: 2 * n], both, preferred_element_type=F32)
        now, back = now[:, :share], now[:n, share:]
    else:
        now = jnp.dot(act[: 2 * n], weights(w_ref, 2, group), preferred_element_type=F32)
        back = jnp.dot(act[:n], weights(w_ref, 1, group), preferred_element_type=F32)
    return jnp.concatenate([now[:n], now[n:] + back], axis=0)


def late_products(act, n, w_ref, group):
    left = jnp.concatenate([act[a * n : (a + 2) * n] for a in range(3)], axis=1)
    right = jnp.concatenate([weights(w_ref, a, group) for a in range(3)], axis=0)
    return jnp.dot(left, right, preferred_element_type=F32)


def load_kernel(codes_hbm, proj_hbm, gain_hbm, up_hbm, act_ref, w_ref, proj_ref, gain_ref, codes_ref, sems):
    pairs = ((codes_hbm, codes_ref), (proj_hbm, proj_ref), (gain_hbm, gain_ref), (up_hbm, w_ref))
    copies = [pltpu.make_async_copy(src, dst, sems.at[n]) for n, (src, dst) in enumerate(pairs)]
    for copy in copies:
        copy.start()
    for copy in copies[:3]:
        copy.wait()
    frames, rows, cols = codes_ref.shape
    codes = [codes_ref[t, r : r + 1, :] for t in range(frames) for r in range(rows)]
    act_ref[...] = latent_rows(codes, proj_ref[...], gain_ref[...]).astype(BF16)
    copies[3].wait()


def lanes_of(group, share, start=0):
    return pl.ds((group[0] - start) * share, group[1] * share)


def own_early_kernel(n, act_ref, w_ref, early_ref, late_ref):
    share = w_ref.shape[2]
    act = act_ref[...]
    for group in GROUPS:
        early_ref[:, lanes_of(group, share)] = early_products(act, n, w_ref, group)
    for group in GROUPS[:SPLIT]:
        late_ref[:, lanes_of(group, share)] = late_products(act, n, w_ref, group)


def own_late_kernel(n, act_ref, w_ref, after_ref, late_ref):
    share = w_ref.shape[2]
    act = act_ref[...]
    for group in GROUPS[SPLIT:]:
        late_ref[:, lanes_of(group, share, GROUPS[SPLIT][0])] = late_products(act, n, w_ref, group)


def combine(rows, cols, share, own, halo, h_ref):
    def taken(slot, tap):
        if slot in (0, rows + 1):
            row = 0 if slot == 0 else 1
            part = halo[:, tap * share : (tap + 1) * share]
            pieces = [part[(2 * t + row) * cols : (2 * t + row + 1) * cols] for t in range(2)]
        else:
            pieces = [own(tap, (t * rows + slot - 1) * cols) for t in range(2)]
        return jnp.concatenate(pieces, axis=0)

    for q in range(rows + 1):
        sums = [[], []]
        for c in range(3):
            x = taken(q, c) + taken(q + 1, 6 + c)
            sums[0].append(x + taken(q, 3 + c))
            sums[1].append(x + taken(q + 1, 3 + c))
        out = pl.ds(q * 2 * cols, 2 * cols)
        for py, (left, mid, right) in enumerate(sums):
            even = shifted(left, cols, 1) + (mid + right)
            odd = (left + mid) + shifted(right, cols, -1)
            h_ref[out, pl.ds(2 * py * share, share)] = even.astype(BF16)
            h_ref[out, pl.ds((2 * py + 1) * share, share)] = odd.astype(BF16)


def early_hidden_kernel(near_ref, far_ref, proj_ref, gain_ref, w_ref, own_ref, h_ref, act_ref):
    frames, rows, cols = near_ref.shape
    share = w_ref.shape[2]
    first = lax.axis_index("section") == 0
    place = lax.axis_index("rows")
    last = lax.axis_size("rows") - 1
    codes = []
    for t in range(frames):
        low = [ref[t, rows - 1 : rows, :] for ref in (near_ref, far_ref)]
        high = [ref[t, 0:1, :] for ref in (near_ref, far_ref)]
        codes += [jnp.where(first, low[0], low[1]), jnp.where(first, high[1], high[0])]
    act = latent_rows(codes, proj_ref[...], gain_ref[...])
    edge = lax.broadcasted_iota(jnp.int32, (frames, 2, cols, act.shape[1]), 1).reshape(act.shape)
    keep = jnp.where(edge == 0, (place > 0).astype(F32), (place < last).astype(F32))
    act = (act * keep).astype(BF16)
    act_ref[...] = act
    halo = jnp.concatenate([early_products(act, 2 * cols, w_ref, group) for group in GROUPS], axis=1)

    def own(tap, start):
        return own_ref[pl.ds(start, cols), pl.ds(tap * share, share)]

    combine(rows, cols, share, own, halo, h_ref)


def late_hidden_kernel(rows, cols, act_ref, w_ref, first_ref, rest_ref, h_ref):
    share = w_ref.shape[2]
    act = act_ref[...]
    halo = jnp.concatenate([late_products(act, 2 * cols, w_ref, group) for group in GROUPS], axis=1)
    cut = GROUPS[SPLIT][0]

    def own(tap, start):
        ref, k = (first_ref, tap) if tap < cut else (rest_ref, tap - cut)
        return ref[pl.ds(start, cols), pl.ds(k * share, share)]

    combine(rows, cols, share, own, halo, h_ref)


def part_starts(part):
    section = lax.axis_index("section")
    return [pl.multiple_of(k * part, part) for k in (section, 1 - section)]


def normalise(size, own_ref, other_ref, gain_ref):
    pairs = own_ref.shape[0] // size
    part = own_ref.shape[1] // 4
    gains = [0.5 * gain_ref[:, pl.ds(start, part)] for start in part_starts(part)]
    place = lax.axis_index("rows")
    last = lax.axis_size("rows") - 1
    rows = []
    for q in range(pairs):
        for py in range(2):
            cells = []
            for px in range(2):
                lanes = pl.ds((2 * py + px) * part, part)
                x = [ref[pl.ds(q * size, size), lanes].astype(F32) for ref in (own_ref, other_ref)]
                mean = jnp.sum(x[0] * x[0] + x[1] * x[1], axis=1, keepdims=True) / (2 * part)
                scale = lax.rsqrt(mean + EPS)
                if q == 0 and py == 0:
                    scale = jnp.where(place > 0, scale, 0.0)
                if q == pairs - 1 and py == 1:
                    scale = jnp.where(place < last, scale, 0.0)
                cells += [silu_of_half(x[s] * scale * gains[s]).astype(BF16) for s in range(2)]
            rows.append(jnp.concatenate(cells, axis=1))
    return rows


def out_products(rows, tap_ref, a, m):
    height = len(rows) - 2
    left = jnp.concatenate(
        [jnp.concatenate([rows[y + b][:m] for b in range(3)], axis=1) for y in range(height)], axis=0
    )
    part = tap_ref.shape[2] // 2
    starts = part_starts(part)
    lines = [[], [], [], []]
    for b in range(3):
        w = [
            jnp.concatenate([tap_ref[9 * a + 3 * b + c, :, pl.ds(start, part)] for start in starts], axis=1)
            for c in range(3)
        ]
        zero = jnp.zeros_like(w[0])
        for line, cells in zip(lines, ((w[1], w[2]), (w[0], w[1]), (zero, w[0]), (w[2], zero))):
            line += cells
    right = jnp.concatenate([jnp.concatenate(line, axis=1) for line in lines], axis=0)
    total = lax.dot_general(left, right, (((1,), (1,)), ((), ())), preferred_element_type=F32)
    return total.reshape(height, m, right.shape[0])


def mix(y, full, cols, ow, mix_ref):
    rows = full.shape[0]
    side = full[:, 2 * ow :]
    lane = lax.broadcasted_iota(jnp.int32, side.shape, 1)
    both = full[:, : 2 * ow] + jnp.where(lane < ow, shifted(side, cols, 1), shifted(side, cols, -1))
    mix_ref[y, pl.ds(0, rows, stride=2), :] = both
    mix_ref[y, pl.ds(1, rows, stride=2), :] = pltpu.roll(both, ow, 1)


def place_row(y, o_ref, mix_ref):
    rows, ow = o_ref.shape[2:]
    result = mix_ref[y][:, :ow].astype(BF16)
    for t in range(2):
        o_ref[t, y] = result[rows * t : rows * (t + 1)]


def early_out_kernel(cols, own_ref, other_ref, gain_ref, tap_ref, o_ref, acc_ref, mix_ref):
    size = 2 * cols
    rows = normalise(size, own_ref, other_ref, gain_ref)
    now, back, held = [out_products(rows, tap_ref, a, size) for a in (2, 1, 0)]
    height = now.shape[0]
    for y in range(height):
        full = jnp.concatenate([now[y, :cols], now[y, cols:] + back[y, :cols]], axis=0)
        mix(y, full, cols, o_ref.shape[3], mix_ref)
        acc_ref[y] = jnp.concatenate([held[y, :cols] + back[y, cols:], held[y, cols:]], axis=0)
    for y in range(height):
        place_row(y, o_ref, mix_ref)


def late_out_kernel(cols, own_ref, other_ref, gain_ref, tap_ref, early_ref, acc_ref, o_hbm, o_ref, mix_ref, sems):
    size = 2 * cols
    copies = [pltpu.make_async_copy(early_ref, o_hbm.at[pl.ds(0, 2)], sems.at[0])]
    copies[0].start()
    rows = normalise(size, own_ref, other_ref, gain_ref)
    now = out_products(rows, tap_ref, 2, size)
    back = out_products(rows, tap_ref, 1, -(-cols // 16) * 16)
    height = now.shape[0]
    for y in range(height):
        held = acc_ref[y]
        full = jnp.concatenate([held[:cols] + now[y, :cols], held[cols:] + now[y, cols:] + back[y, :cols]], axis=0)
        mix(y, full, cols, o_ref.shape[3], mix_ref)
    half = height // 2
    for k in range(2):
        for y in range(k * half, (k + 1) * half):
            place_row(y, o_ref, mix_ref)
        part = pl.ds(k * half, half)
        copies.append(
            pltpu.make_async_copy(o_ref.at[:, part], o_hbm.at[pl.ds(2, 2), part], sems.at[1 + k])
        )
        copies[-1].start()
    for copy in copies:
        copy.wait()


def params(mib):
    return pltpu.CompilerParams(vmem_limit_bytes=mib * MIB)


def cost(mflops):
    return pl.CostEstimate(flops=mflops * 10**6, bytes_accessed=10**7, transcendentals=0)


def vmem():
    return pl.BlockSpec(memory_space=pltpu.VMEM)


def in_space(space, *arrays):
    return tuple(pltpu.with_memory_space_constraint(x, space) for x in arrays)


def call(kernel, name, outs, ins, mib, mflops, scratch=(), in_specs=None, out_specs=None):
    results = pl.pallas_call(
        kernel,
        out_shape=outs,
        in_specs=in_specs or [vmem()] * len(ins),
        out_specs=out_specs or (vmem(),) * len(outs),
        scratch_shapes=list(scratch),
        compiler_params=params(mib),
        cost_estimate=cost(mflops),
        name=name,
    )(*ins)
    return results if out_specs else in_space(pltpu.VMEM, *results)


def body(codes, in_proj, gain_up, up_kernel, gain_res, out_kernel):
    frames, rows, cols = codes.shape
    size = 2 * cols
    width, share = up_kernel.shape[1:]
    ow = out_kernel.shape[1]
    pairs = rows + 1
    height = 2 * rows
    count = lax.axis_size("rows")
    joint = [(2 * i, 2 * i + 2) for i in range(count - 1)] + [(2 * i + 3, 2 * i + 1) for i in range(count - 1)]
    swap = [(0, 1), (1, 0)]
    near = lax.ppermute(codes, ("rows", "section"), joint)
    gain_res = gain_res.reshape(1, -1)
    up_kernel, codes, in_proj, gain_up = in_space(pltpu.HBM, up_kernel, codes, in_proj, gain_up.reshape(1, -1))
    (tap,) = in_space(pltpu.VMEM, out_kernel)
    hbm = pl.BlockSpec(memory_space=pltpu.HBM)
    hidden_shape = pltpu.VMEM((pairs * size, 4 * share), BF16)

    act, w, proj, gain = call(
        load_kernel,
        "load",
        (
            pltpu.VMEM((frames * rows * cols, width), BF16),
            pltpu.VMEM(up_kernel.shape, BF16),
            pltpu.VMEM(in_proj.shape, BF16),
            pltpu.VMEM(gain_up.shape, F32),
        ),
        (codes, in_proj, gain_up, up_kernel),
        6,
        2000,
        [pltpu.VMEM(codes.shape, jnp.int32), pltpu.SemaphoreType.DMA((4,))],
        in_specs=[hbm] * 4,
    )
    cut = GROUPS[SPLIT][0]
    own_early, own_first = call(
        functools.partial(own_early_kernel, rows * cols),
        "own_early",
        (pltpu.VMEM((2 * rows * cols, 9 * share), F32), pltpu.VMEM((2 * rows * cols, cut * share), F32)),
        (act, w),
        4,
        1000,
    )

    near, own_early = lax.optimization_barrier((near, own_early))
    far = lax.ppermute(near, "section", swap)
    near, far = in_space(pltpu.VMEM, near, far)
    (own_rest,) = call(
        functools.partial(own_late_kernel, rows * cols),
        "own_late",
        (pltpu.VMEM((2 * rows * cols, (9 - cut) * share), F32),),
        (act, w, near),
        4,
        1000,
    )
    far, own_rest = lax.optimization_barrier((far, own_rest))

    early, halo = call(
        early_hidden_kernel,
        "hidden_early",
        (hidden_shape, pltpu.VMEM((2 * frames * cols, width), BF16)),
        (near, far, proj, gain, w, own_early),
        8,
        1000,
    )
    early_other = lax.ppermute(early, "section", swap)
    (late,) = call(
        functools.partial(late_hidden_kernel, rows, cols),
        "hidden_late",
        (hidden_shape,),
        (halo, w, own_first, own_rest),
        8,
        1000,
    )
    late_other = lax.ppermute(late, "section", swap)
    early_other, late_other = in_space(pltpu.VMEM, early_other, late_other)

    mixed = pltpu.VMEM((height, 2 * size, 2 * ow), F32)
    out_early, held = call(
        functools.partial(early_out_kernel, cols),
        "out_early",
        (pltpu.VMEM((2, height, 2 * cols, ow), BF16), pltpu.VMEM((height, size, 4 * ow), F32)),
        (early, early_other, gain_res, tap),
        12,
        2000,
        [mixed],
    )
    return call(
        functools.partial(late_out_kernel, cols),
        "out_late",
        jax.ShapeDtypeStruct((frames, height, 2 * cols, ow), BF16),
        (late, late_other, gain_res, tap, out_early, held),
        12,
        1000,
        [pltpu.VMEM((2, height, 2 * cols, ow), BF16), mixed, pltpu.SemaphoreType.DMA((3,))],
        out_specs=hbm,
    )


def solution(mesh):
    in_specs = (
        P("clip", "rows", None),
        P(),
        P(),
        P(None, None, "section"),
        P(),
        P(None, "section", None),
    )
    out_specs = P("clip", "rows", None, "section")
    return jax.shard_map(body, mesh=mesh, in_specs=in_specs, out_specs=out_specs, check_vma=False)
```

time: 15.3 us -> 14.6 us (0.954)
  Pallas kernels: 9.04 us -> 8.22 us
    pallas_call x6 -> x7, Pallas kernels: 9.04 us -> 8.22 us  [call(): pl.pallas_call(kernel, out_shape=outs, in_specs=in_specs or [vmem()] * le...]
    ppermute x1, waiting for transfers between devices: 0.19 us -> 0.35 us  [body(): far = lax.ppermute(near, 'section', swap)]
  transfers between devices with their start and end apart: 4 -> 4, of which waited for: 2 -> 2; matrix products, arithmetic and copies ran while one was open for 0% -> 0% of each run, Pallas kernels for 42% -> 40%
where the time goes in v7:
time: 14.6 us; the launch traced here: 14.4 us
  Pallas kernels  8.22 us (56%)
  starting transfers between devices  5.54 us (38%)
  waiting for transfers between devices  0.48 us (3%)
    pallas_call x7, Pallas kernels, call(): pl.pallas_call(kernel, out_shape=outs, in_specs=in_specs or [vmem()] * le...  8.22 us
    ppermute x1, starting transfers between devices, body(): near = lax.ppermute(codes, ('rows', 'section'), joint)  4.83 us
    ppermute x1, starting transfers between devices, body(): late_other = lax.ppermute(late, 'section', swap)  0.41 us
    ppermute x1, waiting for transfers between devices, body(): far = lax.ppermute(near, 'section', swap)  0.35 us
  transfers between devices with their start and end apart: 4, of which 2 were waited for; matrix products, arithmetic and copies ran while one was open for 0% of the time, Pallas kernels for 40%

profile of v7, /device:TPU:0, one launch (start us, length us, event | category | flops | bytes accessed | tf_op | source)
XLA Modules:
  0.0 14.4 jit_solution(12936373903782119896)
XLA Ops:
  0.0 4.8 %collective-permute-start = (s32[4,4,24]{2,1,0:T(4,128)}, s32[4,4,24]{2,1,0:T(4,128)S(1)}, u32[]{:S(2)}, u32[]{:S(2)}) collective-permute-start(s32[4,4,24]{2,1,0:T(4,128)} %codes_hbm.1), channel_id=1, source_target_pairs={{0,2},{2,4},{4,6},{6,8},{8,10},{10,12},{12,14},{3,1},{5,3},{7,5},{... | collective-permute-start | bytes 4616 | tf_op jit(solution)/shard_map/ppermute | solution.py:306
  4.8 2.1 %load.1 = (bf16[384,512]{1,0:T(8,128)(2,1)S(1)}, bf16[27,512,128]{2,1,0:T(8,128)(2,1)S(1)}, bf16[18,512]{1,0:T(8,128)(2,1)S(1)}, f32[1,512]{1,0:T(1,128)S(1)}) custom-call(s32[4,4,24]{2,1,0:T(4,128)} %codes_hbm.1, bf16[18,512]{1,0:T(8,128)(2,1)} %proj_hbm.1, f32[1,512]{1,0:T(1,128)} %bitcast.4, bf16[27,512,128]{2,1,0:T(8,128)(2,1)} %up_hbm.1), custom_call_target="tpu_custom_call" | custom-call | flops 2000000000 | bytes 10000000 | tf_op jit(solution)/shard_map/load/pallas_call | solution.py:283
  6.9 0.7 %own_early.1 = (f32[192,1152]{1,0:T(8,128)S(1)}, f32[192,256]{1,0:T(8,128)S(1)}) custom-call(bf16[384,512]{1,0:T(8,128)(2,1)S(1)} %get-tuple-element.19.act_ref, bf16[27,512,128]{2,1,0:T(8,128)(2,1)S(1)} %get-tuple-element.20.w_ref), custom_call_target="tpu_custom_call" | custom-call | flops 1000000000 | bytes 10000000 | tf_op jit(solution)/shard_map/own_early/pallas_call | solution.py:283
  7.7 0.0 collective-permute-done.after_ref.near_ref
  7.7 0.1 collective-permute-start.1
  7.8 0.8 %own_late.1.rest_ref = f32[192,896]{1,0:T(8,128)S(1)} custom-call(bf16[384,512]{1,0:T(8,128)(2,1)S(1)} %get-tuple-element.19.act_ref, bf16[27,512,128]{2,1,0:T(8,128)(2,1)S(1)} %get-tuple-element.20.w_ref, s32[4,4,24]{2,1,0:T(4,128)S(1)} %collective-permute-done.after_ref.near_ref), custom_call_target="tpu_custom_call" | custom-call | flops 1000000000 | bytes 10000000 | tf_op jit(solution)/shard_map/own_late/pallas_call | solution.py:283
  8.6 0.3 %collective-permute-done.1.far_ref = s32[4,4,24]{2,1,0:T(4,128)S(1)} collective-permute-done((s32[4,4,24]{2,1,0:T(4,128)S(1)}, s32[4,4,24]{2,1,0:T(4,128)S(1)}, u32[]{:S(2)}, u32[]{:S(2)}) %collective-permute-start.1) | collective-permute-done | bytes 1568 | tf_op jit(solution)/shard_map/ppermute | solution.py:339
  8.9 0.9 %hidden_early.1 = (bf16[240,512]{1,0:T(8,128)(2,1)S(1)}, bf16[192,512]{1,0:T(8,128)(2,1)S(1)}) custom-call(s32[4,4,24]{2,1,0:T(4,128)S(1)} %collective-permute-done.after_ref.near_ref, s32[4,4,24]{2,1,0:T(4,128)S(1)} %collective-permute-done.1.far_ref, bf16[18,512]{1,0:T(8,128)(2,1)S(1)} %get-tuple-element.24.proj_ref, ...), custom_call_target="tpu_custom_call" | custom-call | flops 1000000000 | bytes 10000000 | tf_op jit(solution)/shard_map/hidden_early/pallas_call | solution.py:283
  9.8 0.0 copy-start
  9.8 0.0 copy-start.1
  9.9 0.2 %collective-permute-start.3 = (bf16[240,512]{1,0:T(8,128)(2,1)S(1)}, bf16[240,512]{1,0:T(8,128)(2,1)S(1)}, u32[]{:S(2)}, u32[]{:S(2)}) collective-permute-start(bf16[240,512]{1,0:T(8,128)(2,1)S(1)} %get-tuple-element.30.own_ref), channel_id=1, source_target_pairs={{0,1},{1,0},{2,3},{3,2},{4,5},{5,4},{6,7},{7,6},{8,9},{9,8},{10,11... | collective-permute-start | bytes 737288 | tf_op jit(solution)/shard_map/ppermute | solution.py:359
  10.1 0.8 %hidden_late.1.own_ref = bf16[240,512]{1,0:T(8,128)(2,1)S(1)} custom-call(bf16[192,512]{1,0:T(8,128)(2,1)S(1)} %get-tuple-element.27.act_ref, bf16[27,512,128]{2,1,0:T(8,128)(2,1)S(1)} %get-tuple-element.20.w_ref, f32[192,256]{1,0:T(8,128)S(1)} %get-tuple-element.28.first_ref, f32[192,896]{1,0:T(8,128)S(1)} %own_late.1.rest_ref), custom_call_target="tpu_custom_call" | custom-call | flops 1000000000 | bytes 10000000 | tf_op jit(solution)/shard_map/hidden_late/pallas_call | solution.py:283
  10.9 0.4 %collective-permute-start.2 = (bf16[240,512]{1,0:T(8,128)(2,1)S(1)}, bf16[240,512]{1,0:T(8,128)(2,1)S(1)}, u32[]{:S(2)}, u32[]{:S(2)}) collective-permute-start(bf16[240,512]{1,0:T(8,128)(2,1)S(1)} %hidden_late.1.own_ref), channel_id=1, source_target_pairs={{0,1},{1,0},{2,3},{3,2},{4,5},{5,4},{6,7},{7,6},{8,9},{9,8},{10,11... | collective-permute-start | bytes 737288 | tf_op jit(solution)/shard_map/ppermute | solution.py:368
  11.3 0.1 collective-permute-done.3.other_ref
  11.4 0.0 copy-done
  11.4 0.0 copy-done.1
  11.4 1.3 %out_early.1 = (bf16[2,8,48,64]{3,2,1,0:T(8,128)(2,1)S(1)}, f32[8,48,256]{2,1,0:T(8,128)S(1)}) custom-call(bf16[240,512]{1,0:T(8,128)(2,1)S(1)} %get-tuple-element.30.own_ref, bf16[240,512]{1,0:T(8,128)(2,1)S(1)} %collective-permute-done.3.other_ref, f32[1,256]{1,0:T(1,128)S(1)} %bitcast.2, bf16[27,64,256]{2,1,0:T(8,128)(2,1)S(1)} %copy-done), custom_call_target="tpu_custom_call" | custom-call | flops 2000000000 | bytes 10000000 | tf_op jit(solution)/shard_map/out_early/pallas_call | solution.py:283
  12.7 0.0 collective-permute-done.2.other_ref
  12.7 1.6 %out_late.1 = bf16[4,8,48,64]{3,2,1,0:T(8,128)(2,1)} custom-call(bf16[240,512]{1,0:T(8,128)(2,1)S(1)} %hidden_late.1.own_ref, bf16[240,512]{1,0:T(8,128)(2,1)S(1)} %collective-permute-done.2.other_ref, f32[1,256]{1,0:T(1,128)S(1)} %bitcast.3, bf16[27,64,256]{2,1,0:T(8,128)(2,1)S(1)} %copy-done, bf16[2,8,48,64]{3,2,1,0:T(8,128)(2,1)S(1)} %get-tuple-element.31.early_ref, ...), custom_call_target="tpu_custom_call" | custom-call | flops 1000000000 | bytes 10000000 | tf_op jit(solution)/shard_map/out_late/pallas_call | solution.py:283
Async XLA Ops:
  0.0 7.7 %collective-permute-start = (s32[4,4,24]{2,1,0:T(4,128)}, s32[4,4,24]{2,1,0:T(4,128)S(1)}, u32[]{:S(2)}, u32[]{:S(2)}) collective-permute-start(s32[4,4,24]{2,1,0:T(4,128)} %codes_hbm.1), channel_id=1, source_target_pairs={{0,2},{2,4},{4,6},{6,8},{8,10},{10,12},{12,14},{3,1},{5,3},{7,5},{... | collective-permute-start | bytes 4616 | tf_op jit(solution)/shard_map/ppermute | solution.py:306
  7.7 1.2 %collective-permute-start.1 = (s32[4,4,24]{2,1,0:T(4,128)S(1)}, s32[4,4,24]{2,1,0:T(4,128)S(1)}, u32[]{:S(2)}, u32[]{:S(2)}) collective-permute-start(s32[4,4,24]{2,1,0:T(4,128)S(1)} %collective-permute-done.after_ref.near_ref), channel_id=1, source_target_pairs={{0,1},{1,0},{2,3},{3,2},{4,5},{5,4},{6,7},{7,6},{8,9},{9,8},{10,11... | collective-permute-start | bytes 4616 | tf_op jit(solution)/shard_map/ppermute | solution.py:339
  9.8 1.6 %copy-start = (bf16[27,64,256]{2,1,0:T(8,128)(2,1)S(1)}, bf16[27,64,256]{2,1,0:T(8,128)(2,1)}, u32[]{:S(2)}) copy-start(bf16[27,64,256]{2,1,0:T(8,128)(2,1)} %tap_ref.3) | copy-start | bytes 2654212
  9.8 1.6 %copy-start.1 = (f32[256]{0:T(256)S(1)}, f32[256]{0:T(256)}, u32[]{:S(2)}) copy-start(f32[256]{0:T(256)} %param.10) | copy-start | bytes 3076
  9.9 1.6 %collective-permute-start.3 = (bf16[240,512]{1,0:T(8,128)(2,1)S(1)}, bf16[240,512]{1,0:T(8,128)(2,1)S(1)}, u32[]{:S(2)}, u32[]{:S(2)}) collective-permute-start(bf16[240,512]{1,0:T(8,128)(2,1)S(1)} %get-tuple-element.30.own_ref), channel_id=1, source_target_pairs={{0,1},{1,0},{2,3},{3,2},{4,5},{5,4},{6,7},{7,6},{8,9},{9,8},{10,11... | collective-permute-start | bytes 737288 | tf_op jit(solution)/shard_map/ppermute | solution.py:359
  10.9 1.8 %collective-permute-start.2 = (bf16[240,512]{1,0:T(8,128)(2,1)S(1)}, bf16[240,512]{1,0:T(8,128)(2,1)S(1)}, u32[]{:S(2)}, u32[]{:S(2)}) collective-permute-start(bf16[240,512]{1,0:T(8,128)(2,1)S(1)} %hidden_late.1.own_ref), channel_id=1, source_target_pairs={{0,1},{1,0},{2,3},{3,2},{4,5},{5,4},{6,7},{7,6},{8,9},{9,8},{10,11... | collective-permute-start | bytes 737288 | tf_op jit(solution)/shard_map/ppermute | solution.py:368

commit v8 on v7

--- a/solution.py
+++ b/solution.py
@@ -13,7 +13,7 @@
 BF16 = jnp.bfloat16
 MIB = 1024 * 1024
 GROUPS = ((0, 2), (2, 2), (4, 2), (6, 2), (8, 1))
-SPLIT = 1
+SPLIT = 3
 
 
 def silu_of_half(h):
@@ -65,37 +65,36 @@
     return jnp.dot(left, right, preferred_element_type=F32)
 
 
-def load_kernel(codes_hbm, proj_hbm, gain_hbm, up_hbm, act_ref, w_ref, proj_ref, gain_ref, codes_ref, sems):
-    pairs = ((codes_hbm, codes_ref), (proj_hbm, proj_ref), (gain_hbm, gain_ref), (up_hbm, w_ref))
+def latent_kernel(codes_hbm, proj_hbm, gain_hbm, act_ref, proj_ref, gain_ref, codes_ref, sems):
+    pairs = ((codes_hbm, codes_ref), (proj_hbm, proj_ref), (gain_hbm, gain_ref))
     copies = [pltpu.make_async_copy(src, dst, sems.at[n]) for n, (src, dst) in enumerate(pairs)]
     for copy in copies:
         copy.start()
-    for copy in copies[:3]:
+    for copy in copies:
         copy.wait()
     frames, rows, cols = codes_ref.shape
     codes = [codes_ref[t, r : r + 1, :] for t in range(frames) for r in range(rows)]
     act_ref[...] = latent_rows(codes, proj_ref[...], gain_ref[...]).astype(BF16)
-    copies[3].wait()
 
 
 def lanes_of(group, share, start=0):
     return pl.ds((group[0] - start) * share, group[1] * share)
 
 
-def own_early_kernel(n, act_ref, w_ref, early_ref, late_ref):
+def own_first_kernel(n, act_ref, w_ref, first_ref):
     share = w_ref.shape[2]
     act = act_ref[...]
-    for group in GROUPS:
-        early_ref[:, lanes_of(group, share)] = early_products(act, n, w_ref, group)
     for group in GROUPS[:SPLIT]:
-        late_ref[:, lanes_of(group, share)] = late_products(act, n, w_ref, group)
-
-
-def own_late_kernel(n, act_ref, w_ref, after_ref, late_ref):
+        first_ref[:, lanes_of(group, share)] = early_products(act, n, w_ref, group)
+
+
+def own_rest_kernel(n, act_ref, w_ref, after_ref, rest_ref, late_ref):
     share = w_ref.shape[2]
     act = act_ref[...]
     for group in GROUPS[SPLIT:]:
-        late_ref[:, lanes_of(group, share, GROUPS[SPLIT][0])] = late_products(act, n, w_ref, group)
+        rest_ref[:, lanes_of(group, share, GROUPS[SPLIT][0])] = early_products(act, n, w_ref, group)
+    for group in GROUPS:
+        late_ref[:, lanes_of(group, share)] = late_products(act, n, w_ref, group)
 
 
 def combine(rows, cols, share, own, halo, h_ref):
@@ -122,7 +121,7 @@
             h_ref[out, pl.ds((2 * py + 1) * share, share)] = odd.astype(BF16)
 
 
-def early_hidden_kernel(near_ref, far_ref, proj_ref, gain_ref, w_ref, own_ref, h_ref, act_ref):
+def early_hidden_kernel(near_ref, far_ref, proj_ref, gain_ref, w_ref, first_ref, rest_ref, h_ref, act_ref):
     frames, rows, cols = near_ref.shape
     share = w_ref.shape[2]
     first = lax.axis_index("section") == 0
@@ -140,21 +139,22 @@
     act_ref[...] = act
     halo = jnp.concatenate([early_products(act, 2 * cols, w_ref, group) for group in GROUPS], axis=1)
 
+    cut = GROUPS[SPLIT][0]
+
     def own(tap, start):
-        return own_ref[pl.ds(start, cols), pl.ds(tap * share, share)]
+        ref, k = (first_ref, tap) if tap < cut else (rest_ref, tap - cut)
+        return ref[pl.ds(start, cols), pl.ds(k * share, share)]
 
     combine(rows, cols, share, own, halo, h_ref)
 
 
-def late_hidden_kernel(rows, cols, act_ref, w_ref, first_ref, rest_ref, h_ref):
+def late_hidden_kernel(rows, cols, act_ref, w_ref, own_ref, h_ref):
     share = w_ref.shape[2]
     act = act_ref[...]
     halo = jnp.concatenate([late_products(act, 2 * cols, w_ref, group) for group in GROUPS], axis=1)
-    cut = GROUPS[SPLIT][0]
 
     def own(tap, start):
-        ref, k = (first_ref, tap) if tap < cut else (rest_ref, tap - cut)
-        return ref[pl.ds(start, cols), pl.ds(k * share, share)]
+        return own_ref[pl.ds(start, cols), pl.ds(tap * share, share)]
 
     combine(rows, cols, share, own, halo, h_ref)
 
@@ -305,54 +305,54 @@
     swap = [(0, 1), (1, 0)]
     near = lax.ppermute(codes, ("rows", "section"), joint)
     gain_res = gain_res.reshape(1, -1)
-    up_kernel, codes, in_proj, gain_up = in_space(pltpu.HBM, up_kernel, codes, in_proj, gain_up.reshape(1, -1))
-    (tap,) = in_space(pltpu.VMEM, out_kernel)
+    w, tap = in_space(pltpu.VMEM, up_kernel, out_kernel)
+    codes, in_proj, gain_up = in_space(pltpu.HBM, codes, in_proj, gain_up.reshape(1, -1))
     hbm = pl.BlockSpec(memory_space=pltpu.HBM)
     hidden_shape = pltpu.VMEM((pairs * size, 4 * share), BF16)
 
-    act, w, proj, gain = call(
-        load_kernel,
-        "load",
+    act, proj, gain = call(
+        latent_kernel,
+        "latent",
         (
             pltpu.VMEM((frames * rows * cols, width), BF16),
-            pltpu.VMEM(up_kernel.shape, BF16),
             pltpu.VMEM(in_proj.shape, BF16),
             pltpu.VMEM(gain_up.shape, F32),
         ),
-        (codes, in_proj, gain_up, up_kernel),
-        6,
-        2000,
-        [pltpu.VMEM(codes.shape, jnp.int32), pltpu.SemaphoreType.DMA((4,))],
-        in_specs=[hbm] * 4,
+        (codes, in_proj, gain_up),
+        4,
+        1000,
+        [pltpu.VMEM(codes.shape, jnp.int32), pltpu.SemaphoreType.DMA((3,))],
+        in_specs=[hbm] * 3,
     )
     cut = GROUPS[SPLIT][0]
-    own_early, own_first = call(
-        functools.partial(own_early_kernel, rows * cols),
-        "own_early",
-        (pltpu.VMEM((2 * rows * cols, 9 * share), F32), pltpu.VMEM((2 * rows * cols, cut * share), F32)),
+    own_rows = 2 * rows * cols
+    (own_first,) = call(
+        functools.partial(own_first_kernel, rows * cols),
+        "own_first",
+        (pltpu.VMEM((own_rows, cut * share), F32),),
         (act, w),
         4,
         1000,
     )
 
-    near, own_early = lax.optimization_barrier((near, own_early))
+    near, own_first = lax.optimization_barrier((near, own_first))
     far = lax.ppermute(near, "section", swap)
     near, far = in_space(pltpu.VMEM, near, far)
-    (own_rest,) = call(
-        functools.partial(own_late_kernel, rows * cols),
-        "own_late",
-        (pltpu.VMEM((2 * rows * cols, (9 - cut) * share), F32),),
+    own_rest, own_late = call(
+        functools.partial(own_rest_kernel, rows * cols),
+        "own_rest",
+        (pltpu.VMEM((own_rows, (9 - cut) * share), F32), pltpu.VMEM((own_rows, 9 * share), F32)),
         (act, w, near),
         4,
         1000,
     )
-    far, own_rest = lax.optimization_barrier((far, own_rest))
+    far, own_rest, own_late = lax.optimization_barrier((far, own_rest, own_late))
 
     early, halo = call(
         early_hidden_kernel,
         "hidden_early",
         (hidden_shape, pltpu.VMEM((2 * frames * cols, width), BF16)),
-        (near, far, proj, gain, w, own_early),
+        (near, far, proj, gain, w, own_first, own_rest),
         8,
         1000,
     )
@@ -361,7 +361,7 @@
         functools.partial(late_hidden_kernel, rows, cols),
         "hidden_late",
         (hidden_shape,),
-        (halo, w, own_first, own_rest),
+        (halo, w, own_late),
         8,
         1000,
     )

time: 14.6 us -> 14.4 us (0.986)
  the two profiles are of different devices: /device:TPU:0 before, /device:TPU:25 now
where the time goes in v8:
time: 14.4 us; the launch traced here: 14.2 us
  Pallas kernels  7.46 us (52%)
  starting transfers between devices  6.46 us (45%)
    pallas_call x7, Pallas kernels, call(): pl.pallas_call(kernel, out_shape=outs, in_specs=in_specs or [vmem()] * le...  7.46 us
    ppermute x1, starting transfers between devices, body(): near = lax.ppermute(codes, ('rows', 'section'), joint)  3.26 us
    ppermute x1, starting transfers between devices, body(): far = lax.ppermute(near, 'section', swap)  2.56 us
    ppermute x1, starting transfers between devices, body(): late_other = lax.ppermute(late, 'section', swap)  0.55 us
  transfers between devices with their start and end apart: 4, of which 1 were waited for; matrix products, arithmetic and copies ran while one was open for 0% of the time, Pallas kernels for 35%

profile of v8, /device:TPU:25, one launch (start us, length us, event | category | flops | bytes accessed | tf_op | source)
XLA Modules:
  0.0 14.2 jit_solution(12938223513341987380)
XLA Ops:
  0.0 0.0 copy-start
  0.0 3.3 %collective-permute-start = (s32[4,4,24]{2,1,0:T(4,128)}, s32[4,4,24]{2,1,0:T(4,128)S(1)}, u32[]{:S(2)}, u32[]{:S(2)}) collective-permute-start(s32[4,4,24]{2,1,0:T(4,128)} %codes_hbm.1), channel_id=1, source_target_pairs={{0,2},{2,4},{4,6},{6,8},{8,10},{10,12},{12,14},{3,1},{5,3},{7,5},{... | collective-permute-start | bytes 4616 | tf_op jit(solution)/shard_map/ppermute | solution.py:306
  3.3 1.3 %latent.1 = (bf16[384,512]{1,0:T(8,128)(2,1)S(1)}, bf16[18,512]{1,0:T(8,128)(2,1)S(1)}, f32[1,512]{1,0:T(1,128)S(1)}) custom-call(s32[4,4,24]{2,1,0:T(4,128)} %codes_hbm.1, bf16[18,512]{1,0:T(8,128)(2,1)} %proj_hbm.1, f32[1,512]{1,0:T(1,128)} %bitcast.4), custom_call_target="tpu_custom_call" | custom-call | flops 1000000000 | bytes 10000000 | tf_op jit(solution)/shard_map/latent/pallas_call | solution.py:283
  4.5 0.0 copy-done
  4.6 0.5 %own_first.1.first_ref = f32[192,768]{1,0:T(8,128)S(1)} custom-call(bf16[384,512]{1,0:T(8,128)(2,1)S(1)} %get-tuple-element.19.act_ref, bf16[27,512,128]{2,1,0:T(8,128)(2,1)S(1)} %copy-done), custom_call_target="tpu_custom_call" | custom-call | flops 1000000000 | bytes 10000000 | tf_op jit(solution)/shard_map/own_first/pallas_call | solution.py:283
  5.0 0.0 collective-permute-done.after_ref.near_ref
  5.0 2.6 %collective-permute-start.1 = (s32[4,4,24]{2,1,0:T(4,128)S(1)}, s32[4,4,24]{2,1,0:T(4,128)S(1)}, u32[]{:S(2)}, u32[]{:S(2)}) collective-permute-start(s32[4,4,24]{2,1,0:T(4,128)S(1)} %collective-permute-done.after_ref.near_ref), channel_id=1, source_target_pairs={{0,1},{1,0},{2,3},{3,2},{4,5},{5,4},{6,7},{7,6},{8,9},{9,8},{10,11... | collective-permute-start | bytes 4616 | tf_op jit(solution)/shard_map/ppermute | solution.py:339
  7.6 1.1 %own_rest.1 = (f32[192,384]{1,0:T(8,128)S(1)}, f32[192,1152]{1,0:T(8,128)S(1)}) custom-call(bf16[384,512]{1,0:T(8,128)(2,1)S(1)} %get-tuple-element.19.act_ref, bf16[27,512,128]{2,1,0:T(8,128)(2,1)S(1)} %copy-done, s32[4,4,24]{2,1,0:T(4,128)S(1)} %collective-permute-done.after_ref.near_ref), custom_call_target="tpu_custom_call" | custom-call | flops 1000000000 | bytes 10000000 | tf_op jit(solution)/shard_map/own_rest/pallas_call | solution.py:283
  8.7 0.0 collective-permute-done.1.far_ref
  8.7 0.9 %hidden_early.1 = (bf16[240,512]{1,0:T(8,128)(2,1)S(1)}, bf16[192,512]{1,0:T(8,128)(2,1)S(1)}) custom-call(s32[4,4,24]{2,1,0:T(4,128)S(1)} %collective-permute-done.after_ref.near_ref, s32[4,4,24]{2,1,0:T(4,128)S(1)} %collective-permute-done.1.far_ref, bf16[18,512]{1,0:T(8,128)(2,1)S(1)} %get-tuple-element.24.proj_ref, ...), custom_call_target="tpu_custom_call" | custom-call | flops 1000000000 | bytes 10000000 | tf_op jit(solution)/shard_map/hidden_early/pallas_call | solution.py:283
  9.7 0.0 copy-start.1
  9.7 0.0 copy-start.2
  9.7 0.1 collective-permute-start.3
  9.8 0.8 %hidden_late.1.own_ref = bf16[240,512]{1,0:T(8,128)(2,1)S(1)} custom-call(bf16[192,512]{1,0:T(8,128)(2,1)S(1)} %get-tuple-element.28.act_ref, bf16[27,512,128]{2,1,0:T(8,128)(2,1)S(1)} %copy-done, f32[192,1152]{1,0:T(8,128)S(1)} %get-tuple-element.29.own_ref), custom_call_target="tpu_custom_call" | custom-call | flops 1000000000 | bytes 10000000 | tf_op jit(solution)/shard_map/hidden_late/pallas_call | solution.py:283
  10.6 0.6 %collective-permute-start.2 = (bf16[240,512]{1,0:T(8,128)(2,1)S(1)}, bf16[240,512]{1,0:T(8,128)(2,1)S(1)}, u32[]{:S(2)}, u32[]{:S(2)}) collective-permute-start(bf16[240,512]{1,0:T(8,128)(2,1)S(1)} %hidden_late.1.own_ref), channel_id=1, source_target_pairs={{0,1},{1,0},{2,3},{3,2},{4,5},{5,4},{6,7},{7,6},{8,9},{9,8},{10,11... | collective-permute-start | bytes 737288 | tf_op jit(solution)/shard_map/ppermute | solution.py:368
  11.1 0.1 collective-permute-done.3.other_ref
  11.3 0.0 copy-done.1
  11.3 0.0 copy-done.2
  11.3 1.3 %out_early.1 = (bf16[2,8,48,64]{3,2,1,0:T(8,128)(2,1)S(1)}, f32[8,48,256]{2,1,0:T(8,128)S(1)}) custom-call(bf16[240,512]{1,0:T(8,128)(2,1)S(1)} %get-tuple-element.30.own_ref, bf16[240,512]{1,0:T(8,128)(2,1)S(1)} %collective-permute-done.3.other_ref, f32[1,256]{1,0:T(1,128)S(1)} %bitcast.2, bf16[27,64,256]{2,1,0:T(8,128)(2,1)S(1)} %copy-done.1), custom_call_target="tpu_custom_call" | custom-call | flops 2000000000 | bytes 10000000 | tf_op jit(solution)/shard_map/out_early/pallas_call | solution.py:283
  12.5 0.0 collective-permute-done.2.other_ref
  12.5 1.6 %out_late.1 = bf16[4,8,48,64]{3,2,1,0:T(8,128)(2,1)} custom-call(bf16[240,512]{1,0:T(8,128)(2,1)S(1)} %hidden_late.1.own_ref, bf16[240,512]{1,0:T(8,128)(2,1)S(1)} %collective-permute-done.2.other_ref, f32[1,256]{1,0:T(1,128)S(1)} %bitcast.3, bf16[27,64,256]{2,1,0:T(8,128)(2,1)S(1)} %copy-done.1, bf16[2,8,48,64]{3,2,1,0:T(8,128)(2,1)S(1)} %get-tuple-element.31.early_ref, ...), custom_call_target="tpu_custom_call" | custom-call | flops 1000000000 | bytes 10000000 | tf_op jit(solution)/shard_map/out_late/pallas_call | solution.py:283
Async XLA Ops:
  0.0 4.6 %copy-start = (bf16[27,512,128]{2,1,0:T(8,128)(2,1)S(1)}, bf16[27,512,128]{2,1,0:T(8,128)(2,1)}, u32[]{:S(2)}) copy-start(bf16[27,512,128]{2,1,0:T(8,128)(2,1)} %w_ref.7) | copy-start | bytes 10616836
  0.0 5.0 %collective-permute-start = (s32[4,4,24]{2,1,0:T(4,128)}, s32[4,4,24]{2,1,0:T(4,128)S(1)}, u32[]{:S(2)}, u32[]{:S(2)}) collective-permute-start(s32[4,4,24]{2,1,0:T(4,128)} %codes_hbm.1), channel_id=1, source_target_pairs={{0,2},{2,4},{4,6},{6,8},{8,10},{10,12},{12,14},{3,1},{5,3},{7,5},{... | collective-permute-start | bytes 4616 | tf_op jit(solution)/shard_map/ppermute | solution.py:306
  5.0 3.7 %collective-permute-start.1 = (s32[4,4,24]{2,1,0:T(4,128)S(1)}, s32[4,4,24]{2,1,0:T(4,128)S(1)}, u32[]{:S(2)}, u32[]{:S(2)}) collective-permute-start(s32[4,4,24]{2,1,0:T(4,128)S(1)} %collective-permute-done.after_ref.near_ref), channel_id=1, source_target_pairs={{0,1},{1,0},{2,3},{3,2},{4,5},{5,4},{6,7},{7,6},{8,9},{9,8},{10,11... | collective-permute-start | bytes 4616 | tf_op jit(solution)/shard_map/ppermute | solution.py:339
  9.7 1.6 %copy-start.1 = (bf16[27,64,256]{2,1,0:T(8,128)(2,1)S(1)}, bf16[27,64,256]{2,1,0:T(8,128)(2,1)}, u32[]{:S(2)}) copy-start(bf16[27,64,256]{2,1,0:T(8,128)(2,1)} %tap_ref.3) | copy-start | bytes 2654212
  9.7 1.6 %copy-start.2 = (f32[256]{0:T(256)S(1)}, f32[256]{0:T(256)}, u32[]{:S(2)}) copy-start(f32[256]{0:T(256)} %param.10) | copy-start | bytes 3076
  9.7 1.6 %collective-permute-start.3 = (bf16[240,512]{1,0:T(8,128)(2,1)S(1)}, bf16[240,512]{1,0:T(8,128)(2,1)S(1)}, u32[]{:S(2)}, u32[]{:S(2)}) collective-permute-start(bf16[240,512]{1,0:T(8,128)(2,1)S(1)} %get-tuple-element.30.own_ref), channel_id=1, source_target_pairs={{0,1},{1,0},{2,3},{3,2},{4,5},{5,4},{6,7},{7,6},{8,9},{9,8},{10,11... | collective-permute-start | bytes 737288 | tf_op jit(solution)/shard_map/ppermute | solution.py:359
  10.6 2.0 %collective-permute-start.2 = (bf16[240,512]{1,0:T(8,128)(2,1)S(1)}, bf16[240,512]{1,0:T(8,128)(2,1)S(1)}, u32[]{:S(2)}, u32[]{:S(2)}) collective-permute-start(bf16[240,512]{1,0:T(8,128)(2,1)S(1)} %hidden_late.1.own_ref), channel_id=1, source_target_pairs={{0,1},{1,0},{2,3},{3,2},{4,5},{5,4},{6,7},{7,6},{8,9},{9,8},{10,11... | collective-permute-start | bytes 737288 | tf_op jit(solution)/shard_map/ppermute | solution.py:368

commit v9 on v8

--- a/solution.py
+++ b/solution.py
@@ -301,7 +301,7 @@
     pairs = rows + 1
     height = 2 * rows
     count = lax.axis_size("rows")
-    joint = [(2 * i, 2 * i + 2) for i in range(count - 1)] + [(2 * i + 3, 2 * i + 1) for i in range(count - 1)]
+    joint = [pair for i in range(count - 1) for pair in ((2 * i + 1, 2 * i + 2), (2 * i + 2, 2 * i + 1))]
     swap = [(0, 1), (1, 0)]
     near = lax.ppermute(codes, ("rows", "section"), joint)
     gain_res = gain_res.reshape(1, -1)

time: 14.4 us -> 13.9 us (0.965)
  the two profiles are of different devices: /device:TPU:25 before, /device:TPU:0 now
where the time goes in v9:
time: 13.9 us; the launch traced here: 13.6 us
  Pallas kernels  7.74 us (56%)
  starting transfers between devices  5.65 us (41%)
  waiting for transfers between devices  0.14 us (1%)
    pallas_call x7, Pallas kernels, call(): pl.pallas_call(kernel, out_shape=outs, in_specs=in_specs or [vmem()] * le...  7.74 us
    ppermute x1, starting transfers between devices, body(): far = lax.ppermute(near, 'section', swap)  4.23 us
    ppermute x1, starting transfers between devices, body(): near = lax.ppermute(codes, ('rows', 'section'), joint)  0.78 us
    ppermute x1, starting transfers between devices, body(): late_other = lax.ppermute(late, 'section', swap)  0.55 us
  transfers between devices with their start and end apart: 4, of which 1 were waited for; matrix products, arithmetic and copies ran while one was open for 0% of the time, Pallas kernels for 38%

profile of v9, /device:TPU:0, one launch (start us, length us, event | category | flops | bytes accessed | tf_op | source)
XLA Modules:
  0.0 13.6 jit_solution(2808378157762306119)
XLA Ops:
  0.0 0.0 copy-start
  0.0 0.8 %collective-permute-start = (s32[4,4,24]{2,1,0:T(4,128)}, s32[4,4,24]{2,1,0:T(4,128)S(1)}, u32[]{:S(2)}, u32[]{:S(2)}) collective-permute-start(s32[4,4,24]{2,1,0:T(4,128)} %codes_hbm.1), channel_id=1, source_target_pairs={{1,2},{2,1},{3,4},{4,3},{5,6},{6,5},{7,8},{8,7},{9,10},{10,9},{11,... | collective-permute-start | bytes 4616 | tf_op jit(solution)/shard_map/ppermute | solution.py:306
  0.8 1.5 %latent.1 = (bf16[384,512]{1,0:T(8,128)(2,1)S(1)}, bf16[18,512]{1,0:T(8,128)(2,1)S(1)}, f32[1,512]{1,0:T(1,128)S(1)}) custom-call(s32[4,4,24]{2,1,0:T(4,128)} %codes_hbm.1, bf16[18,512]{1,0:T(8,128)(2,1)} %proj_hbm.1, f32[1,512]{1,0:T(1,128)} %bitcast.4), custom_call_target="tpu_custom_call" | custom-call | flops 1000000000 | bytes 10000000 | tf_op jit(solution)/shard_map/latent/pallas_call | solution.py:283
  2.3 0.0 copy-done
  2.4 0.5 %own_first.1.first_ref = f32[192,768]{1,0:T(8,128)S(1)} custom-call(bf16[384,512]{1,0:T(8,128)(2,1)S(1)} %get-tuple-element.19.act_ref, bf16[27,512,128]{2,1,0:T(8,128)(2,1)S(1)} %copy-done), custom_call_target="tpu_custom_call" | custom-call | flops 1000000000 | bytes 10000000 | tf_op jit(solution)/shard_map/own_first/pallas_call | solution.py:283
  2.8 0.0 collective-permute-done.after_ref.near_ref
  2.8 4.2 %collective-permute-start.1 = (s32[4,4,24]{2,1,0:T(4,128)S(1)}, s32[4,4,24]{2,1,0:T(4,128)S(1)}, u32[]{:S(2)}, u32[]{:S(2)}) collective-permute-start(s32[4,4,24]{2,1,0:T(4,128)S(1)} %collective-permute-done.after_ref.near_ref), channel_id=1, source_target_pairs={{0,1},{1,0},{2,3},{3,2},{4,5},{5,4},{6,7},{7,6},{8,9},{9,8},{10,11... | collective-permute-start | bytes 4616 | tf_op jit(solution)/shard_map/ppermute | solution.py:339
  7.0 1.1 %own_rest.1 = (f32[192,384]{1,0:T(8,128)S(1)}, f32[192,1152]{1,0:T(8,128)S(1)}) custom-call(bf16[384,512]{1,0:T(8,128)(2,1)S(1)} %get-tuple-element.19.act_ref, bf16[27,512,128]{2,1,0:T(8,128)(2,1)S(1)} %copy-done, s32[4,4,24]{2,1,0:T(4,128)S(1)} %collective-permute-done.after_ref.near_ref), custom_call_target="tpu_custom_call" | custom-call | flops 1000000000 | bytes 10000000 | tf_op jit(solution)/shard_map/own_rest/pallas_call | solution.py:283
  8.2 0.0 collective-permute-done.1.far_ref
  8.2 0.9 %hidden_early.1 = (bf16[240,512]{1,0:T(8,128)(2,1)S(1)}, bf16[192,512]{1,0:T(8,128)(2,1)S(1)}) custom-call(s32[4,4,24]{2,1,0:T(4,128)S(1)} %collective-permute-done.after_ref.near_ref, s32[4,4,24]{2,1,0:T(4,128)S(1)} %collective-permute-done.1.far_ref, bf16[18,512]{1,0:T(8,128)(2,1)S(1)} %get-tuple-element.24.proj_ref, ...), custom_call_target="tpu_custom_call" | custom-call | flops 1000000000 | bytes 10000000 | tf_op jit(solution)/shard_map/hidden_early/pallas_call | solution.py:283
  9.1 0.0 copy-start.1
  9.1 0.0 copy-start.2
  9.1 0.1 collective-permute-start.3
  9.2 0.8 %hidden_late.1.own_ref = bf16[240,512]{1,0:T(8,128)(2,1)S(1)} custom-call(bf16[192,512]{1,0:T(8,128)(2,1)S(1)} %get-tuple-element.28.act_ref, bf16[27,512,128]{2,1,0:T(8,128)(2,1)S(1)} %copy-done, f32[192,1152]{1,0:T(8,128)S(1)} %get-tuple-element.29.own_ref), custom_call_target="tpu_custom_call" | custom-call | flops 1000000000 | bytes 10000000 | tf_op jit(solution)/shard_map/hidden_late/pallas_call | solution.py:283
  10.0 0.5 %collective-permute-start.2 = (bf16[240,512]{1,0:T(8,128)(2,1)S(1)}, bf16[240,512]{1,0:T(8,128)(2,1)S(1)}, u32[]{:S(2)}, u32[]{:S(2)}) collective-permute-start(bf16[240,512]{1,0:T(8,128)(2,1)S(1)} %hidden_late.1.own_ref), channel_id=1, source_target_pairs={{0,1},{1,0},{2,3},{3,2},{4,5},{5,4},{6,7},{7,6},{8,9},{9,8},{10,11... | collective-permute-start | bytes 737288 | tf_op jit(solution)/shard_map/ppermute | solution.py:368
  10.6 0.1 collective-permute-done.3.other_ref
  10.7 0.0 copy-done.1
  10.7 0.0 copy-done.2
  10.7 1.3 %out_early.1 = (bf16[2,8,48,64]{3,2,1,0:T(8,128)(2,1)S(1)}, f32[8,48,256]{2,1,0:T(8,128)S(1)}) custom-call(bf16[240,512]{1,0:T(8,128)(2,1)S(1)} %get-tuple-element.30.own_ref, bf16[240,512]{1,0:T(8,128)(2,1)S(1)} %collective-permute-done.3.other_ref, f32[1,256]{1,0:T(1,128)S(1)} %bitcast.2, bf16[27,64,256]{2,1,0:T(8,128)(2,1)S(1)} %copy-done.1), custom_call_target="tpu_custom_call" | custom-call | flops 2000000000 | bytes 10000000 | tf_op jit(solution)/shard_map/out_early/pallas_call | solution.py:283
  12.0 0.0 collective-permute-done.2.other_ref
  12.0 1.6 %out_late.1 = bf16[4,8,48,64]{3,2,1,0:T(8,128)(2,1)} custom-call(bf16[240,512]{1,0:T(8,128)(2,1)S(1)} %hidden_late.1.own_ref, bf16[240,512]{1,0:T(8,128)(2,1)S(1)} %collective-permute-done.2.other_ref, f32[1,256]{1,0:T(1,128)S(1)} %bitcast.3, bf16[27,64,256]{2,1,0:T(8,128)(2,1)S(1)} %copy-done.1, bf16[2,8,48,64]{3,2,1,0:T(8,128)(2,1)S(1)} %get-tuple-element.31.early_ref, ...), custom_call_target="tpu_custom_call" | custom-call | flops 1000000000 | bytes 10000000 | tf_op jit(solution)/shard_map/out_late/pallas_call | solution.py:283
Async XLA Ops:
  0.0 2.3 %copy-start = (bf16[27,512,128]{2,1,0:T(8,128)(2,1)S(1)}, bf16[27,512,128]{2,1,0:T(8,128)(2,1)}, u32[]{:S(2)}) copy-start(bf16[27,512,128]{2,1,0:T(8,128)(2,1)} %w_ref.7) | copy-start | bytes 10616836
  0.0 2.8 %collective-permute-start = (s32[4,4,24]{2,1,0:T(4,128)}, s32[4,4,24]{2,1,0:T(4,128)S(1)}, u32[]{:S(2)}, u32[]{:S(2)}) collective-permute-start(s32[4,4,24]{2,1,0:T(4,128)} %codes_hbm.1), channel_id=1, source_target_pairs={{1,2},{2,1},{3,4},{4,3},{5,6},{6,5},{7,8},{8,7},{9,10},{10,9},{11,... | collective-permute-start | bytes 4616 | tf_op jit(solution)/shard_map/ppermute | solution.py:306
  2.8 5.4 %collective-permute-start.1 = (s32[4,4,24]{2,1,0:T(4,128)S(1)}, s32[4,4,24]{2,1,0:T(4,128)S(1)}, u32[]{:S(2)}, u32[]{:S(2)}) collective-permute-start(s32[4,4,24]{2,1,0:T(4,128)S(1)} %collective-permute-done.after_ref.near_ref), channel_id=1, source_target_pairs={{0,1},{1,0},{2,3},{3,2},{4,5},{5,4},{6,7},{7,6},{8,9},{9,8},{10,11... | collective-permute-start | bytes 4616 | tf_op jit(solution)/shard_map/ppermute | solution.py:339
  9.1 1.6 %copy-start.1 = (bf16[27,64,256]{2,1,0:T(8,128)(2,1)S(1)}, bf16[27,64,256]{2,1,0:T(8,128)(2,1)}, u32[]{:S(2)}) copy-start(bf16[27,64,256]{2,1,0:T(8,128)(2,1)} %tap_ref.3) | copy-start | bytes 2654212
  9.1 1.6 %copy-start.2 = (f32[256]{0:T(256)S(1)}, f32[256]{0:T(256)}, u32[]{:S(2)}) copy-start(f32[256]{0:T(256)} %param.10) | copy-start | bytes 3076
  9.1 1.6 %collective-permute-start.3 = (bf16[240,512]{1,0:T(8,128)(2,1)S(1)}, bf16[240,512]{1,0:T(8,128)(2,1)S(1)}, u32[]{:S(2)}, u32[]{:S(2)}) collective-permute-start(bf16[240,512]{1,0:T(8,128)(2,1)S(1)} %get-tuple-element.30.own_ref), channel_id=1, source_target_pairs={{0,1},{1,0},{2,3},{3,2},{4,5},{5,4},{6,7},{7,6},{8,9},{9,8},{10,11... | collective-permute-start | bytes 737288 | tf_op jit(solution)/shard_map/ppermute | solution.py:359
  10.0 2.0 %collective-permute-start.2 = (bf16[240,512]{1,0:T(8,128)(2,1)S(1)}, bf16[240,512]{1,0:T(8,128)(2,1)S(1)}, u32[]{:S(2)}, u32[]{:S(2)}) collective-permute-start(bf16[240,512]{1,0:T(8,128)(2,1)S(1)} %hidden_late.1.own_ref), channel_id=1, source_target_pairs={{0,1},{1,0},{2,3},{3,2},{4,5},{5,4},{6,7},{7,6},{8,9},{9,8},{10,11... | collective-permute-start | bytes 737288 | tf_op jit(solution)/shard_map/ppermute | solution.py:368

commit v10 on v9

v10 whole, which is shorter than its diff:
```python
import functools

import jax
import jax.numpy as jnp
from jax import lax
from jax.experimental import pallas as pl
from jax.experimental.pallas import tpu as pltpu
from jax.sharding import PartitionSpec as P

BITS = 18
EPS = 1e-06
F32 = jnp.float32
BF16 = jnp.bfloat16
MIB = 1024 * 1024
GROUPS = ((0, 2), (2, 2), (4, 2), (6, 2), (8, 1))
SPLIT = 2


def silu_of_half(h):
    return h + h * jnp.tanh(h)


def latent_rows(rows, in_proj, gain):
    cols = rows[0].shape[1]
    count = len(rows)
    wide = jnp.concatenate([jnp.broadcast_to(row, (cols, cols)) for row in rows], axis=0)
    sub = lax.broadcasted_iota(jnp.int32, (count, cols, cols), 1).reshape(count * cols, cols)
    lane = lax.broadcasted_iota(jnp.int32, (count * cols, cols), 1)
    picked = jnp.where(sub == lane, wide, 0).astype(F32)
    column = jnp.sum(picked, axis=1, keepdims=True).astype(jnp.int32)
    spread = jnp.broadcast_to(column, (count * cols, BITS))
    shift = lax.broadcasted_iota(jnp.int32, (count * cols, BITS), 1)
    bits = ((jnp.right_shift(spread, shift) & 1) * 2 - 1).astype(F32).astype(BF16)
    latent = jnp.dot(bits, in_proj, preferred_element_type=F32)
    mean = jnp.mean(latent * latent, axis=1, keepdims=True)
    return silu_of_half(latent * lax.rsqrt(mean + EPS) * (0.5 * gain))


def shifted(x, cols, amount):
    rows, lanes = x.shape
    place = lax.broadcasted_iota(jnp.int32, (rows // cols, cols, lanes), 1).reshape(rows, lanes)
    moved = pltpu.roll(x, amount % rows, 0)
    return jnp.where(place == (0 if amount == 1 else cols - 1), 0.0, moved)


def weights(w_ref, a, group):
    return jnp.concatenate([w_ref[9 * a + group[0] + k] for k in range(group[1])], axis=1)


def products(act, n, w_ref, group):
    share = w_ref.shape[2]
    if group[1] == 1:
        both = jnp.concatenate([weights(w_ref, 2, group), weights(w_ref, 1, group)], axis=1)
        now = jnp.dot(act, both, preferred_element_type=F32)
        now, back = now[:, :share], now[: 3 * n, share:]
    else:
        now = jnp.dot(act, weights(w_ref, 2, group), preferred_element_type=F32)
        back = jnp.dot(act[: 3 * n], weights(w_ref, 1, group), preferred_element_type=F32)
    oldest = jnp.dot(act[: 2 * n], weights(w_ref, 0, group), preferred_element_type=F32)
    return jnp.concatenate([now[:n], now[n : 2 * n] + back[:n], now[2 * n :] + back[n:] + oldest], axis=0)


def latent_kernel(codes_hbm, proj_hbm, gain_hbm, act_ref, proj_ref, gain_ref, codes_ref, sems):
    pairs = ((codes_hbm, codes_ref), (proj_hbm, proj_ref), (gain_hbm, gain_ref))
    copies = [pltpu.make_async_copy(src, dst, sems.at[n]) for n, (src, dst) in enumerate(pairs)]
    for copy in copies:
        copy.start()
    for copy in copies:
        copy.wait()
    frames, rows, cols = codes_ref.shape
    codes = [codes_ref[t, r : r + 1, :] for t in range(frames) for r in range(rows)]
    act_ref[...] = latent_rows(codes, proj_ref[...], gain_ref[...]).astype(BF16)


def lanes_of(group, share, start=0):
    return pl.ds((group[0] - start) * share, group[1] * share)


def own_first_kernel(n, act_ref, w_ref, first_ref):
    for group in GROUPS[:SPLIT]:
        first_ref[:, lanes_of(group, w_ref.shape[2])] = products(act_ref[...], n, w_ref, group)


def of_row(part, frames, stride, start, cols):
    return jnp.concatenate([part[t * stride + start : t * stride + start + cols] for t in range(frames)], axis=0)


def put_hidden(upper, lower, cols, share, q, h_ref):
    size = upper(0).shape[0]
    sums = [[], []]
    for c in range(3):
        x = upper(c) + lower(6 + c)
        sums[0].append(x + upper(3 + c))
        sums[1].append(x + lower(3 + c))
    out = pl.ds(q * size, size)
    for py, (left, mid, right) in enumerate(sums):
        even = shifted(left, cols, 1) + (mid + right)
        odd = (left + mid) + shifted(right, cols, -1)
        h_ref[out, pl.ds(2 * py * share, share)] = even.astype(BF16)
        h_ref[out, pl.ds((2 * py + 1) * share, share)] = odd.astype(BF16)


def own_rest_kernel(frames, cols, act_ref, w_ref, first_ref, after_ref, h_ref, edge_ref):
    share = w_ref.shape[2]
    n = act_ref.shape[0] // frames
    rows = n // cols
    act = act_ref[...]
    done = [first_ref[...]] + [products(act, n, w_ref, group) for group in GROUPS[SPLIT:]]
    taken = []
    for part in done:
        taken += [part[:, k * share : (k + 1) * share] for k in range(part.shape[1] // share)]

    def row(r):
        return lambda tap: of_row(taken[tap], frames, n, r * cols, cols)

    for q in range(rows - 1):
        put_hidden(row(q), row(q + 1), cols, share, q, h_ref)
    for k in range(6):
        edge_ref[0, :, pl.ds(k * share, share)] = row(0)(3 + k)
        edge_ref[1, :, pl.ds(k * share, share)] = row(rows - 1)(k)


def halo_kernel(near_ref, far_ref, proj_ref, gain_ref, w_ref, edge_ref, h_ref):
    frames, rows, cols = near_ref.shape
    share = w_ref.shape[2]
    first = lax.axis_index("section") == 0
    place = lax.axis_index("rows")
    last = lax.axis_size("rows") - 1
    codes = []
    for t in range(frames):
        low = [ref[t, rows - 1 : rows, :] for ref in (near_ref, far_ref)]
        high = [ref[t, 0:1, :] for ref in (near_ref, far_ref)]
        codes += [jnp.where(first, low[0], low[1]), jnp.where(first, high[1], high[0])]
    act = latent_rows(codes, proj_ref[...], gain_ref[...])
    side = lax.broadcasted_iota(jnp.int32, (frames, 2, cols, act.shape[1]), 1).reshape(act.shape)
    keep = jnp.where(side == 0, (place > 0).astype(F32), (place < last).astype(F32))
    act = (act * keep).astype(BF16)
    halo = jnp.concatenate([products(act, 2 * cols, w_ref, group) for group in GROUPS], axis=1)

    def outer(e):
        return lambda tap: of_row(halo[:, tap * share : (tap + 1) * share], frames, 2 * cols, e * cols, cols)

    put_hidden(outer(0), lambda tap: edge_ref[0, :, pl.ds((tap - 3) * share, share)], cols, share, 0, h_ref)
    put_hidden(lambda tap: edge_ref[1, :, pl.ds(tap * share, share)], outer(1), cols, share, 1, h_ref)


def part_starts(part):
    section = lax.axis_index("section")
    return [pl.multiple_of(k * part, part) for k in (section, 1 - section)]


def normalise(size, own_ref, other_ref, gain_ref, keeps):
    part = own_ref.shape[1] // 4
    gains = [0.5 * gain_ref[:, pl.ds(start, part)] for start in part_starts(part)]
    rows = []
    for j, keep in enumerate(keeps):
        cells = []
        for px in range(2):
            lanes = pl.ds((2 * (j % 2) + px) * part, part)
            x = [ref[pl.ds(j // 2 * size, size), lanes].astype(F32) for ref in (own_ref, other_ref)]
            mean = jnp.sum(x[0] * x[0] + x[1] * x[1], axis=1, keepdims=True) / (2 * part)
            scale = lax.rsqrt(mean + EPS)
            if keep is not None:
                scale = jnp.where(keep, scale, 0.0)
            cells += [silu_of_half(x[s] * scale * gains[s]).astype(BF16) for s in range(2)]
        rows.append(jnp.concatenate(cells, axis=1))
    return rows


def out_products(windows, tap_ref, a, m):
    left = jnp.concatenate([jnp.concatenate([row[:m] for row in window], axis=1) for window in windows], axis=0)
    part = tap_ref.shape[2] // 2
    starts = part_starts(part)
    lines = [[], [], [], []]
    for b in range(3):
        w = [
            jnp.concatenate([tap_ref[9 * a + 3 * b + c, :, pl.ds(start, part)] for start in starts], axis=1)
            for c in range(3)
        ]
        zero = jnp.zeros_like(w[0])
        for line, cells in zip(lines, ((w[1], w[2]), (w[0], w[1]), (zero, w[0]), (w[2], zero))):
            line += cells
    right = jnp.concatenate([jnp.concatenate(line, axis=1) for line in lines], axis=0)
    total = lax.dot_general(left, right, (((1,), (1,)), ((), ())), preferred_element_type=F32)
    return total.reshape(len(windows), m, right.shape[0])


def out_rows(windows, tap_ref, frames, cols, mix_ref, o_ref):
    size = frames * cols
    height = len(windows)
    rows, ow = o_ref.shape[2:]
    now, back, oldest = [out_products(windows, tap_ref, a, -(-(frames - 2 + a) * cols // 16) * 16) for a in (2, 1, 0)]
    for y in range(height):
        full = jnp.concatenate(
            [
                now[y, :cols],
                now[y, cols : 2 * cols] + back[y, :cols],
                now[y, 2 * cols :] + back[y, cols : size - cols] + oldest[y, : size - 2 * cols],
            ],
            axis=0,
        )
        side = full[:, 2 * ow :]
        lane = lax.broadcasted_iota(jnp.int32, side.shape, 1)
        both = full[:, : 2 * ow] + jnp.where(lane < ow, shifted(side, cols, 1), shifted(side, cols, -1))
        mix_ref[y, pl.ds(0, size, stride=2), :] = both
        mix_ref[y, pl.ds(1, size, stride=2), :] = pltpu.roll(both, ow, 1)
    for y in range(height):
        result = mix_ref[y][:, :ow].astype(BF16)
        for t in range(frames):
            o_ref[t, y] = result[rows * t : rows * (t + 1)]


def inner_out_kernel(frames, cols, own_ref, other_ref, gain_ref, tap_ref, o_ref, norm_ref, mix_ref):
    size = frames * cols
    count = own_ref.shape[0] // size * 2
    rows = normalise(size, own_ref, other_ref, gain_ref, [None] * count)
    for k, j in enumerate((0, 1, count - 2, count - 1)):
        norm_ref[k] = rows[j]
    out_rows([rows[y : y + 3] for y in range(count - 2)], tap_ref, frames, cols, mix_ref, o_ref)


def edge_out_kernel(frames, cols, own_ref, other_ref, gain_ref, tap_ref, norm_ref, inner_ref, o_hbm, o_ref, mix_ref, sems):
    size = frames * cols
    inner = inner_ref.shape[1]
    copies = [pltpu.make_async_copy(inner_ref, o_hbm.at[:, pl.ds(2, inner)], sems.at[0])]
    copies[0].start()
    place = lax.axis_index("rows")
    last = lax.axis_size("rows") - 1
    edge = normalise(size, own_ref, other_ref, gain_ref, (place > 0, None, None, place < last))
    top = edge[:2] + [norm_ref[0], norm_ref[1]]
    bottom = [norm_ref[2], norm_ref[3]] + edge[2:]
    windows = [side[y : y + 3] for side in (top, bottom) for y in range(2)]
    out_rows(windows, tap_ref, frames, cols, mix_ref, o_ref)
    for k, start in enumerate((0, inner + 2)):
        copies.append(
            pltpu.make_async_copy(o_ref.at[:, pl.ds(2 * k, 2)], o_hbm.at[:, pl.ds(start, 2)], sems.at[1 + k])
        )
        copies[-1].start()
    for copy in copies:
        copy.wait()


def params(mib):
    return pltpu.CompilerParams(vmem_limit_bytes=mib * MIB)


def cost(mflops):
    return pl.CostEstimate(flops=mflops * 10**6, bytes_accessed=10**7, transcendentals=0)


def vmem():
    return pl.BlockSpec(memory_space=pltpu.VMEM)


def in_space(space, *arrays):
    return tuple(pltpu.with_memory_space_constraint(x, space) for x in arrays)


def call(kernel, name, outs, ins, mib, mflops, scratch=(), in_specs=None, out_specs=None):
    results = pl.pallas_call(
        kernel,
        out_shape=outs,
        in_specs=in_specs or [vmem()] * len(ins),
        out_specs=out_specs or (vmem(),) * len(outs),
        scratch_shapes=list(scratch),
        compiler_params=params(mib),
        cost_estimate=cost(mflops),
        name=name,
    )(*ins)
    return results if out_specs else in_space(pltpu.VMEM, *results)


def body(codes, in_proj, gain_up, up_kernel, gain_res, out_kernel):
    frames, rows, cols = codes.shape
    size = frames * cols
    width, share = up_kernel.shape[1:]
    ow = out_kernel.shape[1]
    height = 2 * rows
    inner = height - 4
    count = lax.axis_size("rows")
    joint = [pair for i in range(count - 1) for pair in ((2 * i + 1, 2 * i + 2), (2 * i + 2, 2 * i + 1))]
    swap = [(0, 1), (1, 0)]
    near = lax.ppermute(codes, ("rows", "section"), joint)
    gain_res = gain_res.reshape(1, -1)
    w, tap = in_space(pltpu.VMEM, up_kernel, out_kernel)
    codes, in_proj, gain_up = in_space(pltpu.HBM, codes, in_proj, gain_up.reshape(1, -1))
    hbm = pl.BlockSpec(memory_space=pltpu.HBM)

    act, proj, gain = call(
        latent_kernel,
        "latent",
        (
            pltpu.VMEM((frames * rows * cols, width), BF16),
            pltpu.VMEM(in_proj.shape, BF16),
            pltpu.VMEM(gain_up.shape, F32),
        ),
        (codes, in_proj, gain_up),
        4,
        1000,
        [pltpu.VMEM(codes.shape, jnp.int32), pltpu.SemaphoreType.DMA((3,))],
        in_specs=[hbm] * 3,
    )
    cut = GROUPS[SPLIT][0]
    (own_first,) = call(
        functools.partial(own_first_kernel, rows * cols),
        "own_first",
        (pltpu.VMEM((rows * size, cut * share), F32),),
        (act, w),
        6,
        1000,
    )

    near, own_first = lax.optimization_barrier((near, own_first))
    far = lax.ppermute(near, "section", swap)
    near, far, own_first = in_space(pltpu.VMEM, near, far, own_first)
    inner_own, edge = call(
        functools.partial(own_rest_kernel, frames, cols),
        "own_rest",
        (pltpu.VMEM(((rows - 1) * size, 4 * share), BF16), pltpu.VMEM((2, size, 6 * share), F32)),
        (act, w, own_first, near),
        8,
        1000,
    )
    far, inner_own, edge = lax.optimization_barrier((far, inner_own, edge))
    inner_other = lax.ppermute(inner_own, "section", swap)
    far, inner_own, edge = in_space(pltpu.VMEM, far, inner_own, edge)
    (edge_own,) = call(
        halo_kernel,
        "halo",
        (pltpu.VMEM((2 * size, 4 * share), BF16),),
        (near, far, proj, gain, w, edge),
        8,
        3000,
    )
    edge_other = lax.ppermute(edge_own, "section", swap)
    inner_other, edge_other = in_space(pltpu.VMEM, inner_other, edge_other)

    mixed = pltpu.VMEM((max(inner, 4), 2 * size, 2 * ow), F32)
    out_inner, norm = call(
        functools.partial(inner_out_kernel, frames, cols),
        "out_inner",
        (pltpu.VMEM((frames, inner, 2 * cols, ow), BF16), pltpu.VMEM((4, size, 4 * share), BF16)),
        (inner_own, inner_other, gain_res, tap),
        12,
        2000,
        [mixed],
    )
    return call(
        functools.partial(edge_out_kernel, frames, cols),
        "out_edge",
        jax.ShapeDtypeStruct((frames, height, 2 * cols, ow), BF16),
        (edge_own, edge_other, gain_res, tap, norm, out_inner),
        12,
        1000,
        [pltpu.VMEM((frames, 4, 2 * cols, ow), BF16), mixed, pltpu.SemaphoreType.DMA((3,))],
        out_specs=hbm,
    )


def solution(mesh):
    in_specs = (
        P("clip", "rows", None),
        P(),
        P(),
        P(None, None, "section"),
        P(),
        P(None, "section", None),
    )
    out_specs = P("clip", "rows", None, "section")
    return jax.shard_map(body, mesh=mesh, in_specs=in_specs, out_specs=out_specs, check_vma=False)
```

time: 13.9 us -> 13.1 us (0.942)
  Pallas kernels: 7.74 us -> 7.11 us
    pallas_call x7 -> x6, Pallas kernels: 7.74 us -> 7.11 us  [call(): pl.pallas_call(kernel, out_shape=outs, in_specs=in_specs or [vmem()] * le...]
  transfers between devices with their start and end apart: 4 -> 4, of which waited for: 1 -> 0; matrix products, arithmetic and copies ran while one was open for 0% -> 0% of each run, Pallas kernels for 38% -> 41%
where the time goes in v10:
time: 13.1 us; the launch traced here: 12.9 us
  Pallas kernels  7.11 us (54%)
  starting transfers between devices  5.65 us (43%)
    pallas_call x6, Pallas kernels, call(): pl.pallas_call(kernel, out_shape=outs, in_specs=in_specs or [vmem()] * le...  7.11 us
    ppermute x1, starting transfers between devices, body(): far = lax.ppermute(near, 'section', swap)  4.22 us
    ppermute x1, starting transfers between devices, body(): near = lax.ppermute(codes, ('rows', 'section'), joint)  0.78 us
    ppermute x1, starting transfers between devices, body(): inner_other = lax.ppermute(inner_own, 'section', swap)  0.33 us
    ppermute x1, starting transfers between devices, body(): edge_other = lax.ppermute(edge_own, 'section', swap)  0.31 us
  transfers between devices with their start and end apart: 4, of which 0 were waited for; matrix products, arithmetic and copies ran while one was open for 0% of the time, Pallas kernels for 41%

profile of v10, /device:TPU:0, one launch (start us, length us, event | category | flops | bytes accessed | tf_op | source)
XLA Modules:
  0.0 12.9 jit_solution(9614123777377269494)
XLA Ops:
  0.0 0.0 copy-start
  0.0 0.8 %collective-permute-start = (s32[4,4,24]{2,1,0:T(4,128)}, s32[4,4,24]{2,1,0:T(4,128)S(1)}, u32[]{:S(2)}, u32[]{:S(2)}) collective-permute-start(s32[4,4,24]{2,1,0:T(4,128)} %codes_hbm.1), channel_id=1, source_target_pairs={{1,2},{2,1},{3,4},{4,3},{5,6},{6,5},{7,8},{8,7},{9,10},{10,9},{11,... | collective-permute-start | bytes 4616 | tf_op jit(solution)/shard_map/ppermute | solution.py:283
  0.8 1.5 %latent.1 = (bf16[384,512]{1,0:T(8,128)(2,1)S(1)}, bf16[18,512]{1,0:T(8,128)(2,1)S(1)}, f32[1,512]{1,0:T(1,128)S(1)}) custom-call(s32[4,4,24]{2,1,0:T(4,128)} %codes_hbm.1, bf16[18,512]{1,0:T(8,128)(2,1)} %proj_hbm.1, f32[1,512]{1,0:T(1,128)} %bitcast.4), custom_call_target="tpu_custom_call" | custom-call | flops 1000000000 | bytes 10000000 | tf_op jit(solution)/shard_map/latent/pallas_call | solution.py:260
  2.3 0.0 copy-done
  2.4 0.6 %own_first.1.first_ref = f32[384,512]{1,0:T(8,128)S(1)} custom-call(bf16[384,512]{1,0:T(8,128)(2,1)S(1)} %get-tuple-element.17.act_ref, bf16[27,512,128]{2,1,0:T(8,128)(2,1)S(1)} %copy-done), custom_call_target="tpu_custom_call" | custom-call | flops 1000000000 | bytes 10000000 | tf_op jit(solution)/shard_map/own_first/pallas_call | solution.py:260
  3.0 0.0 collective-permute-done.after_ref.near_ref
  3.0 4.2 %collective-permute-start.1 = (s32[4,4,24]{2,1,0:T(4,128)S(1)}, s32[4,4,24]{2,1,0:T(4,128)S(1)}, u32[]{:S(2)}, u32[]{:S(2)}) collective-permute-start(s32[4,4,24]{2,1,0:T(4,128)S(1)} %collective-permute-done.after_ref.near_ref), channel_id=1, source_target_pairs={{0,1},{1,0},{2,3},{3,2},{4,5},{5,4},{6,7},{7,6},{8,9},{9,8},{10,11... | collective-permute-start | bytes 4616 | tf_op jit(solution)/shard_map/ppermute | solution.py:314
  7.2 0.8 %own_rest.1 = (bf16[288,512]{1,0:T(8,128)(2,1)S(1)}, f32[2,96,768]{2,1,0:T(8,128)S(1)}) custom-call(bf16[384,512]{1,0:T(8,128)(2,1)S(1)} %get-tuple-element.17.act_ref, bf16[27,512,128]{2,1,0:T(8,128)(2,1)S(1)} %copy-done, f32[384,512]{1,0:T(8,128)S(1)} %own_first.1.first_ref, s32[4,4,24]{2,1,0:T(4,128)S(1)} %collective-permute-done.after_ref.near_ref), custom_call_target="tpu_custom_call" | custom-call | flops 1000000000 | bytes 10000000 | tf_op jit(solution)/shard_map/own_rest/pallas_call | solution.py:260
  8.1 0.0 collective-permute-done.1.far_ref
  8.1 0.3 %collective-permute-start.3 = (bf16[288,512]{1,0:T(8,128)(2,1)S(1)}, bf16[288,512]{1,0:T(8,128)(2,1)S(1)}, u32[]{:S(2)}, u32[]{:S(2)}) collective-permute-start(bf16[288,512]{1,0:T(8,128)(2,1)S(1)} %get-tuple-element.26.own_ref), channel_id=1, source_target_pairs={{0,1},{1,0},{2,3},{3,2},{4,5},{5,4},{6,7},{7,6},{8,9},{9,8},{10,11... | collective-permute-start | bytes 884744 | tf_op jit(solution)/shard_map/ppermute | solution.py:325
  8.4 0.0 copy-start.1
  8.4 0.0 copy-start.2
  8.4 1.1 %halo.1.own_ref = bf16[192,512]{1,0:T(8,128)(2,1)S(1)} custom-call(s32[4,4,24]{2,1,0:T(4,128)S(1)} %collective-permute-done.after_ref.near_ref, s32[4,4,24]{2,1,0:T(4,128)S(1)} %collective-permute-done.1.far_ref, bf16[18,512]{1,0:T(8,128)(2,1)S(1)} %get-tuple-element.23.proj_ref, f32[1,512]{1,0:T(1,128)S(1)} %get-tuple-element.24.gain_ref, ...), custom_call_target="tpu_custom_call" | custom-call | flops 3000000000 | bytes 10000000 | tf_op jit(solution)/shard_map/halo/pallas_call | solution.py:260
  9.5 0.3 %collective-permute-start.2 = (bf16[192,512]{1,0:T(8,128)(2,1)S(1)}, bf16[192,512]{1,0:T(8,128)(2,1)S(1)}, u32[]{:S(2)}, u32[]{:S(2)}) collective-permute-start(bf16[192,512]{1,0:T(8,128)(2,1)S(1)} %halo.1.own_ref), channel_id=1, source_target_pairs={{0,1},{1,0},{2,3},{3,2},{4,5},{5,4},{6,7},{7,6},{8,9},{9,8},{10,11... | collective-permute-start | bytes 589832 | tf_op jit(solution)/shard_map/ppermute | solution.py:335
  9.8 0.0 collective-permute-done.3.other_ref
  9.8 0.0 copy-done.1
  9.8 0.0 copy-done.2
  9.8 1.2 %out_inner.1 = (bf16[4,4,48,64]{3,2,1,0:T(8,128)(2,1)S(1)}, bf16[4,96,512]{2,1,0:T(8,128)(2,1)S(1)}) custom-call(bf16[288,512]{1,0:T(8,128)(2,1)S(1)} %get-tuple-element.26.own_ref, bf16[288,512]{1,0:T(8,128)(2,1)S(1)} %collective-permute-done.3.other_ref, f32[1,256]{1,0:T(1,128)S(1)} %bitcast.2, bf16[27,64,256]{2,1,0:T(8,128)(2,1)S(1)} %copy-done.1), custom_call_target="tpu_custom_call" | custom-call | flops 2000000000 | bytes 10000000 | tf_op jit(solution)/shard_map/out_inner/pallas_call | solution.py:260
  11.0 0.0 collective-permute-done.2.other_ref
  11.0 1.8 %out_edge.1 = bf16[4,8,48,64]{3,2,1,0:T(8,128)(2,1)} custom-call(bf16[192,512]{1,0:T(8,128)(2,1)S(1)} %halo.1.own_ref, bf16[192,512]{1,0:T(8,128)(2,1)S(1)} %collective-permute-done.2.other_ref, f32[1,256]{1,0:T(1,128)S(1)} %bitcast.3, bf16[27,64,256]{2,1,0:T(8,128)(2,1)S(1)} %copy-done.1, bf16[4,96,512]{2,1,0:T(8,128)(2,1)S(1)} %get-tuple-element.27.norm_ref, ...), custom_call_target="tpu_custom_call" | custom-call | flops 1000000000 | bytes 10000000 | tf_op jit(solution)/shard_map/out_edge/pallas_call | solution.py:260
Async XLA Ops:
  0.0 2.3 %copy-start = (bf16[27,512,128]{2,1,0:T(8,128)(2,1)S(1)}, bf16[27,512,128]{2,1,0:T(8,128)(2,1)}, u32[]{:S(2)}) copy-start(bf16[27,512,128]{2,1,0:T(8,128)(2,1)} %w_ref.5) | copy-start | bytes 10616836
  0.0 3.0 %collective-permute-start = (s32[4,4,24]{2,1,0:T(4,128)}, s32[4,4,24]{2,1,0:T(4,128)S(1)}, u32[]{:S(2)}, u32[]{:S(2)}) collective-permute-start(s32[4,4,24]{2,1,0:T(4,128)} %codes_hbm.1), channel_id=1, source_target_pairs={{1,2},{2,1},{3,4},{4,3},{5,6},{6,5},{7,8},{8,7},{9,10},{10,9},{11,... | collective-permute-start | bytes 4616 | tf_op jit(solution)/shard_map/ppermute | solution.py:283
  3.0 5.1 %collective-permute-start.1 = (s32[4,4,24]{2,1,0:T(4,128)S(1)}, s32[4,4,24]{2,1,0:T(4,128)S(1)}, u32[]{:S(2)}, u32[]{:S(2)}) collective-permute-start(s32[4,4,24]{2,1,0:T(4,128)S(1)} %collective-permute-done.after_ref.near_ref), channel_id=1, source_target_pairs={{0,1},{1,0},{2,3},{3,2},{4,5},{5,4},{6,7},{7,6},{8,9},{9,8},{10,11... | collective-permute-start | bytes 4616 | tf_op jit(solution)/shard_map/ppermute | solution.py:314
  8.1 1.7 %collective-permute-start.3 = (bf16[288,512]{1,0:T(8,128)(2,1)S(1)}, bf16[288,512]{1,0:T(8,128)(2,1)S(1)}, u32[]{:S(2)}, u32[]{:S(2)}) collective-permute-start(bf16[288,512]{1,0:T(8,128)(2,1)S(1)} %get-tuple-element.26.own_ref), channel_id=1, source_target_pairs={{0,1},{1,0},{2,3},{3,2},{4,5},{5,4},{6,7},{7,6},{8,9},{9,8},{10,11... | collective-permute-start | bytes 884744 | tf_op jit(solution)/shard_map/ppermute | solution.py:325
  8.4 1.4 %copy-start.1 = (bf16[27,64,256]{2,1,0:T(8,128)(2,1)S(1)}, bf16[27,64,256]{2,1,0:T(8,128)(2,1)}, u32[]{:S(2)}) copy-start(bf16[27,64,256]{2,1,0:T(8,128)(2,1)} %tap_ref.3) | copy-start | bytes 2654212
  8.4 1.4 %copy-start.2 = (f32[256]{0:T(256)S(1)}, f32[256]{0:T(256)}, u32[]{:S(2)}) copy-start(f32[256]{0:T(256)} %param.10) | copy-start | bytes 3076
  9.5 1.5 %collective-permute-start.2 = (bf16[192,512]{1,0:T(8,128)(2,1)S(1)}, bf16[192,512]{1,0:T(8,128)(2,1)S(1)}, u32[]{:S(2)}, u32[]{:S(2)}) collective-permute-start(bf16[192,512]{1,0:T(8,128)(2,1)S(1)} %halo.1.own_ref), channel_id=1, source_target_pairs={{0,1},{1,0},{2,3},{3,2},{4,5},{5,4},{6,7},{7,6},{8,9},{9,8},{10,11... | collective-permute-start | bytes 589832 | tf_op jit(solution)/shard_map/ppermute | solution.py:335

commit v11 on v10

--- a/solution.py
+++ b/solution.py
@@ -321,16 +321,16 @@
         8,
         1000,
     )
-    far, inner_own, edge = lax.optimization_barrier((far, inner_own, edge))
     inner_other = lax.ppermute(inner_own, "section", swap)
-    far, inner_own, edge = in_space(pltpu.VMEM, far, inner_own, edge)
+    far, edge = lax.optimization_barrier((far, edge))
+    far, edge = in_space(pltpu.VMEM, far, edge)
     (edge_own,) = call(
         halo_kernel,
         "halo",
         (pltpu.VMEM((2 * size, 4 * share), BF16),),
         (near, far, proj, gain, w, edge),
         8,
-        3000,
+        20000,
     )
     edge_other = lax.ppermute(edge_own, "section", swap)
     inner_other, edge_other = in_space(pltpu.VMEM, inner_other, edge_other)

time: 13.1 us -> 13.1 us (level)
    ppermute x1, starting transfers between devices: 0.33 us -> 0.08 us  [body(): inner_other = lax.ppermute(inner_own, 'section', swap)]
    ppermute x1, starting transfers between devices: 0.31 us -> 0.53 us  [body(): edge_other = lax.ppermute(edge_own, 'section', swap)]
where the time goes in v11:
time: 13.1 us; the launch traced here: 12.9 us
  Pallas kernels  7.12 us (54%)
  starting transfers between devices  5.61 us (43%)
    pallas_call x6, Pallas kernels, call(): pl.pallas_call(kernel, out_shape=outs, in_specs=in_specs or [vmem()] * le...  7.12 us
    ppermute x1, starting transfers between devices, body(): far = lax.ppermute(near, 'section', swap)  4.22 us
    ppermute x1, starting transfers between devices, body(): near = lax.ppermute(codes, ('rows', 'section'), joint)  0.78 us
    ppermute x1, starting transfers between devices, body(): edge_other = lax.ppermute(edge_own, 'section', swap)  0.53 us
  transfers between devices with their start and end apart: 4, of which 0 were waited for; matrix products, arithmetic and copies ran while one was open for 0% of the time, Pallas kernels for 41%

profile of v11, /device:TPU:0, one launch (start us, length us, event | category | flops | bytes accessed | tf_op | source)
XLA Modules:
  0.0 12.9 jit_solution(13829819229332943944)
XLA Ops:
  0.0 0.0 copy-start
  0.0 0.8 %collective-permute-start = (s32[4,4,24]{2,1,0:T(4,128)}, s32[4,4,24]{2,1,0:T(4,128)S(1)}, u32[]{:S(2)}, u32[]{:S(2)}) collective-permute-start(s32[4,4,24]{2,1,0:T(4,128)} %codes_hbm.1), channel_id=1, source_target_pairs={{1,2},{2,1},{3,4},{4,3},{5,6},{6,5},{7,8},{8,7},{9,10},{10,9},{11,... | collective-permute-start | bytes 4616 | tf_op jit(solution)/shard_map/ppermute | solution.py:283
  0.8 1.5 %latent.1 = (bf16[384,512]{1,0:T(8,128)(2,1)S(1)}, bf16[18,512]{1,0:T(8,128)(2,1)S(1)}, f32[1,512]{1,0:T(1,128)S(1)}) custom-call(s32[4,4,24]{2,1,0:T(4,128)} %codes_hbm.1, bf16[18,512]{1,0:T(8,128)(2,1)} %proj_hbm.1, f32[1,512]{1,0:T(1,128)} %bitcast.4), custom_call_target="tpu_custom_call" | custom-call | flops 1000000000 | bytes 10000000 | tf_op jit(solution)/shard_map/latent/pallas_call | solution.py:260
  2.3 0.0 copy-done
  2.4 0.6 %own_first.1.first_ref = f32[384,512]{1,0:T(8,128)S(1)} custom-call(bf16[384,512]{1,0:T(8,128)(2,1)S(1)} %get-tuple-element.16.act_ref, bf16[27,512,128]{2,1,0:T(8,128)(2,1)S(1)} %copy-done), custom_call_target="tpu_custom_call" | custom-call | flops 1000000000 | bytes 10000000 | tf_op jit(solution)/shard_map/own_first/pallas_call | solution.py:260
  3.0 0.0 collective-permute-done.after_ref.near_ref
  3.0 4.2 %collective-permute-start.1 = (s32[4,4,24]{2,1,0:T(4,128)S(1)}, s32[4,4,24]{2,1,0:T(4,128)S(1)}, u32[]{:S(2)}, u32[]{:S(2)}) collective-permute-start(s32[4,4,24]{2,1,0:T(4,128)S(1)} %collective-permute-done.after_ref.near_ref), channel_id=1, source_target_pairs={{0,1},{1,0},{2,3},{3,2},{4,5},{5,4},{6,7},{7,6},{8,9},{9,8},{10,11... | collective-permute-start | bytes 4616 | tf_op jit(solution)/shard_map/ppermute | solution.py:314
  7.2 0.8 %own_rest.1 = (bf16[288,512]{1,0:T(8,128)(2,1)S(1)}, f32[2,96,768]{2,1,0:T(8,128)S(1)}) custom-call(bf16[384,512]{1,0:T(8,128)(2,1)S(1)} %get-tuple-element.16.act_ref, bf16[27,512,128]{2,1,0:T(8,128)(2,1)S(1)} %copy-done, f32[384,512]{1,0:T(8,128)S(1)} %own_first.1.first_ref, s32[4,4,24]{2,1,0:T(4,128)S(1)} %collective-permute-done.after_ref.near_ref), custom_call_target="tpu_custom_call" | custom-call | flops 1000000000 | bytes 10000000 | tf_op jit(solution)/shard_map/own_rest/pallas_call | solution.py:260
  8.1 0.1 collective-permute-start.3
  8.1 0.0 collective-permute-done.1.far_ref
  8.1 0.0 copy-start.1
  8.2 0.0 copy-start.2
  8.2 1.1 %halo.1.own_ref = bf16[192,512]{1,0:T(8,128)(2,1)S(1)} custom-call(s32[4,4,24]{2,1,0:T(4,128)S(1)} %collective-permute-done.after_ref.near_ref, s32[4,4,24]{2,1,0:T(4,128)S(1)} %collective-permute-done.1.far_ref, bf16[18,512]{1,0:T(8,128)(2,1)S(1)} %get-tuple-element.21.proj_ref, f32[1,512]{1,0:T(1,128)S(1)} %get-tuple-element.22.gain_ref, ...), custom_call_target="tpu_custom_call" | custom-call | flops 20000000000 | bytes 10000000 | tf_op jit(solution)/shard_map/halo/pallas_call | solution.py:260
  9.3 0.5 %collective-permute-start.2 = (bf16[192,512]{1,0:T(8,128)(2,1)S(1)}, bf16[192,512]{1,0:T(8,128)(2,1)S(1)}, u32[]{:S(2)}, u32[]{:S(2)}) collective-permute-start(bf16[192,512]{1,0:T(8,128)(2,1)S(1)} %halo.1.own_ref), channel_id=1, source_target_pairs={{0,1},{1,0},{2,3},{3,2},{4,5},{5,4},{6,7},{7,6},{8,9},{9,8},{10,11... | collective-permute-start | bytes 589832 | tf_op jit(solution)/shard_map/ppermute | solution.py:335
  9.8 0.0 collective-permute-done.3.other_ref
  9.8 0.0 copy-done.1
  9.8 0.0 copy-done.2
  9.8 1.2 %out_inner.1 = (bf16[4,4,48,64]{3,2,1,0:T(8,128)(2,1)S(1)}, bf16[4,96,512]{2,1,0:T(8,128)(2,1)S(1)}) custom-call(bf16[288,512]{1,0:T(8,128)(2,1)S(1)} %get-tuple-element.24.own_ref, bf16[288,512]{1,0:T(8,128)(2,1)S(1)} %collective-permute-done.3.other_ref, f32[1,256]{1,0:T(1,128)S(1)} %bitcast.2, bf16[27,64,256]{2,1,0:T(8,128)(2,1)S(1)} %copy-done.1), custom_call_target="tpu_custom_call" | custom-call | flops 2000000000 | bytes 10000000 | tf_op jit(solution)/shard_map/out_inner/pallas_call | solution.py:260
  11.0 0.0 collective-permute-done.2.other_ref
  11.0 1.8 %out_edge.1 = bf16[4,8,48,64]{3,2,1,0:T(8,128)(2,1)} custom-call(bf16[192,512]{1,0:T(8,128)(2,1)S(1)} %halo.1.own_ref, bf16[192,512]{1,0:T(8,128)(2,1)S(1)} %collective-permute-done.2.other_ref, f32[1,256]{1,0:T(1,128)S(1)} %bitcast.3, bf16[27,64,256]{2,1,0:T(8,128)(2,1)S(1)} %copy-done.1, bf16[4,96,512]{2,1,0:T(8,128)(2,1)S(1)} %get-tuple-element.25.norm_ref, ...), custom_call_target="tpu_custom_call" | custom-call | flops 1000000000 | bytes 10000000 | tf_op jit(solution)/shard_map/out_edge/pallas_call | solution.py:260
Async XLA Ops:
  0.0 2.3 %copy-start = (bf16[27,512,128]{2,1,0:T(8,128)(2,1)S(1)}, bf16[27,512,128]{2,1,0:T(8,128)(2,1)}, u32[]{:S(2)}) copy-start(bf16[27,512,128]{2,1,0:T(8,128)(2,1)} %w_ref.5) | copy-start | bytes 10616836
  0.0 3.0 %collective-permute-start = (s32[4,4,24]{2,1,0:T(4,128)}, s32[4,4,24]{2,1,0:T(4,128)S(1)}, u32[]{:S(2)}, u32[]{:S(2)}) collective-permute-start(s32[4,4,24]{2,1,0:T(4,128)} %codes_hbm.1), channel_id=1, source_target_pairs={{1,2},{2,1},{3,4},{4,3},{5,6},{6,5},{7,8},{8,7},{9,10},{10,9},{11,... | collective-permute-start | bytes 4616 | tf_op jit(solution)/shard_map/ppermute | solution.py:283
  3.0 5.1 %collective-permute-start.1 = (s32[4,4,24]{2,1,0:T(4,128)S(1)}, s32[4,4,24]{2,1,0:T(4,128)S(1)}, u32[]{:S(2)}, u32[]{:S(2)}) collective-permute-start(s32[4,4,24]{2,1,0:T(4,128)S(1)} %collective-permute-done.after_ref.near_ref), channel_id=1, source_target_pairs={{0,1},{1,0},{2,3},{3,2},{4,5},{5,4},{6,7},{7,6},{8,9},{9,8},{10,11... | collective-permute-start | bytes 4616 | tf_op jit(solution)/shard_map/ppermute | solution.py:314
  8.1 1.7 %collective-permute-start.3 = (bf16[288,512]{1,0:T(8,128)(2,1)S(1)}, bf16[288,512]{1,0:T(8,128)(2,1)S(1)}, u32[]{:S(2)}, u32[]{:S(2)}) collective-permute-start(bf16[288,512]{1,0:T(8,128)(2,1)S(1)} %get-tuple-element.24.own_ref), channel_id=1, source_target_pairs={{0,1},{1,0},{2,3},{3,2},{4,5},{5,4},{6,7},{7,6},{8,9},{9,8},{10,11... | collective-permute-start | bytes 884744 | tf_op jit(solution)/shard_map/ppermute | solution.py:324
  8.1 1.7 %copy-start.1 = (bf16[27,64,256]{2,1,0:T(8,128)(2,1)S(1)}, bf16[27,64,256]{2,1,0:T(8,128)(2,1)}, u32[]{:S(2)}) copy-start(bf16[27,64,256]{2,1,0:T(8,128)(2,1)} %tap_ref.3) | copy-start | bytes 2654212
  8.2 1.6 %copy-start.2 = (f32[256]{0:T(256)S(1)}, f32[256]{0:T(256)}, u32[]{:S(2)}) copy-start(f32[256]{0:T(256)} %param.10) | copy-start | bytes 3076
  9.3 1.7 %collective-permute-start.2 = (bf16[192,512]{1,0:T(8,128)(2,1)S(1)}, bf16[192,512]{1,0:T(8,128)(2,1)S(1)}, u32[]{:S(2)}, u32[]{:S(2)}) collective-permute-start(bf16[192,512]{1,0:T(8,128)(2,1)S(1)} %halo.1.own_ref), channel_id=1, source_target_pairs={{0,1},{1,0},{2,3},{3,2},{4,5},{5,4},{6,7},{7,6},{8,9},{9,8},{10,11... | collective-permute-start | bytes 589832 | tf_op jit(solution)/shard_map/ppermute | solution.py:335

commit v12 on v11

--- a/solution.py
+++ b/solution.py
@@ -13,7 +13,7 @@
 BF16 = jnp.bfloat16
 MIB = 1024 * 1024
 GROUPS = ((0, 2), (2, 2), (4, 2), (6, 2), (8, 1))
-SPLIT = 2
+SPLIT = 3
 
 
 def silu_of_half(h):
@@ -60,13 +60,11 @@
     return jnp.concatenate([now[:n], now[n : 2 * n] + back[:n], now[2 * n :] + back[n:] + oldest], axis=0)
 
 
-def latent_kernel(codes_hbm, proj_hbm, gain_hbm, act_ref, proj_ref, gain_ref, codes_ref, sems):
-    pairs = ((codes_hbm, codes_ref), (proj_hbm, proj_ref), (gain_hbm, gain_ref))
-    copies = [pltpu.make_async_copy(src, dst, sems.at[n]) for n, (src, dst) in enumerate(pairs)]
-    for copy in copies:
-        copy.start()
-    for copy in copies:
-        copy.wait()
+def open_kernel(mark_ref):
+    mark_ref[...] = jnp.zeros_like(mark_ref)
+
+
+def latent_kernel(codes_ref, proj_ref, gain_ref, mark_ref, act_ref):
     frames, rows, cols = codes_ref.shape
     codes = [codes_ref[t, r : r + 1, :] for t in range(frames) for r in range(rows)]
     act_ref[...] = latent_rows(codes, proj_ref[...], gain_ref[...]).astype(BF16)
@@ -280,25 +278,22 @@
     count = lax.axis_size("rows")
     joint = [pair for i in range(count - 1) for pair in ((2 * i + 1, 2 * i + 2), (2 * i + 2, 2 * i + 1))]
     swap = [(0, 1), (1, 0)]
-    near = lax.ppermute(codes, ("rows", "section"), joint)
+    (mark,) = call(open_kernel, "open", (pltpu.VMEM((8, 128), F32),), (), 1, 1000)
+    sent, mark = lax.optimization_barrier((codes, mark))
+    (mark,) = in_space(pltpu.VMEM, mark)
+    near = lax.ppermute(sent, ("rows", "section"), joint)
     gain_res = gain_res.reshape(1, -1)
-    w, tap = in_space(pltpu.VMEM, up_kernel, out_kernel)
-    codes, in_proj, gain_up = in_space(pltpu.HBM, codes, in_proj, gain_up.reshape(1, -1))
+    w, tap, proj, gain = in_space(pltpu.VMEM, up_kernel, out_kernel, in_proj, gain_up.reshape(1, -1))
+    (codes,) = in_space(pltpu.VMEM, codes)
     hbm = pl.BlockSpec(memory_space=pltpu.HBM)
 
-    act, proj, gain = call(
+    (act,) = call(
         latent_kernel,
         "latent",
-        (
-            pltpu.VMEM((frames * rows * cols, width), BF16),
-            pltpu.VMEM(in_proj.shape, BF16),
-            pltpu.VMEM(gain_up.shape, F32),
-        ),
-        (codes, in_proj, gain_up),
+        (pltpu.VMEM((frames * rows * cols, width), BF16),),
+        (codes, proj, gain, mark),
         4,
         1000,
-        [pltpu.VMEM(codes.shape, jnp.int32), pltpu.SemaphoreType.DMA((3,))],
-        in_specs=[hbm] * 3,
     )
     cut = GROUPS[SPLIT][0]
     (own_first,) = call(

time: 13.1 us -> 13 us (level)
  the two profiles are of different devices: /device:TPU:0 before, /device:TPU:25 now
where the time goes in v12:
time: 13 us; the launch traced here: 12.8 us
  Pallas kernels  6.12 us (47%)
  starting transfers between devices  5.78 us (44%)
  local copies, waits for them, and re-layouts  0.69 us (5%)
    pallas_call x7, Pallas kernels, call(): pl.pallas_call(kernel, out_shape=outs, in_specs=in_specs or [vmem()] * le...  6.12 us
    ppermute x1, starting transfers between devices, body(): near = lax.ppermute(sent, ('rows', 'section'), joint)  3.8 us
    ppermute x1, starting transfers between devices, body(): far = lax.ppermute(near, 'section', swap)  1.46 us
    unnamed x12, local copies, waits for them, and re-layouts  0.69 us
    ppermute x1, starting transfers between devices, body(): edge_other = lax.ppermute(edge_own, 'section', swap)  0.46 us
  transfers between devices with their start and end apart: 4, of which 1 were waited for; matrix products, arithmetic and copies ran while one was open for 0% of the time, Pallas kernels for 33%

profile of v12, /device:TPU:25, one launch (start us, length us, event | category | flops | bytes accessed | tf_op | source)
XLA Modules:
  0.0 12.8 jit_solution(2932017547888034285)
XLA Ops:
  0.0 0.0 copy-start.3
  0.0 0.0 copy-start.2
  0.0 0.0 copy-start.4
  0.0 0.0 copy-start
  0.0 0.7 %copy-done.3 = s32[4,4,24]{2,1,0:T(4,128)S(1)} copy-done((s32[4,4,24]{2,1,0:T(4,128)S(1)}, s32[4,4,24]{2,1,0:T(4,128)}, u32[]{:S(2)}) %copy-start.3) | copy-done | bytes 1560
  0.7 3.8 %collective-permute-start = (s32[4,4,24]{2,1,0:T(4,128)S(1)}, s32[4,4,24]{2,1,0:T(4,128)S(1)}, u32[]{:S(2)}, u32[]{:S(2)}) collective-permute-start(s32[4,4,24]{2,1,0:T(4,128)S(1)} %copy-done.3), channel_id=1, source_target_pairs={{1,2},{2,1},{3,4},{4,3},{5,6},{6,5},{7,8},{8,7},{9,10},{10,9},{11,... | collective-permute-start | bytes 4616 | tf_op jit(solution)/shard_map/ppermute | solution.py:284
  4.5 0.0 copy-done.2
  4.5 0.0 copy-done.4
  4.5 0.5 %latent.1.act_ref = bf16[384,512]{1,0:T(8,128)(2,1)S(1)} custom-call(s32[4,4,24]{2,1,0:T(4,128)S(1)} %copy-done.3, bf16[18,512]{1,0:T(8,128)(2,1)S(1)} %copy-done.2, f32[1,512]{1,0:T(1,128)S(1)} %bitcast.2, f32[8,128]{1,0:T(8,128)S(1)} %open.1.mark_ref), custom_call_target="tpu_custom_call" | custom-call | flops 1000000000 | bytes 10000000 | tf_op jit(solution)/shard_map/latent/pallas_call | solution.py:258
  5.0 0.0 copy-done
  5.0 0.9 %own_first.1.first_ref = f32[384,768]{1,0:T(8,128)S(1)} custom-call(bf16[384,512]{1,0:T(8,128)(2,1)S(1)} %latent.1.act_ref, bf16[27,512,128]{2,1,0:T(8,128)(2,1)S(1)} %copy-done), custom_call_target="tpu_custom_call" | custom-call | flops 1000000000 | bytes 10000000 | tf_op jit(solution)/shard_map/own_first/pallas_call | solution.py:258
  5.9 0.0 collective-permute-done.after_ref.near_ref
  5.9 1.5 %collective-permute-start.1 = (s32[4,4,24]{2,1,0:T(4,128)S(1)}, s32[4,4,24]{2,1,0:T(4,128)S(1)}, u32[]{:S(2)}, u32[]{:S(2)}) collective-permute-start(s32[4,4,24]{2,1,0:T(4,128)S(1)} %collective-permute-done.after_ref.near_ref), channel_id=1, source_target_pairs={{0,1},{1,0},{2,3},{3,2},{4,5},{5,4},{6,7},{7,6},{8,9},{9,8},{10,11... | collective-permute-start | bytes 4616 | tf_op jit(solution)/shard_map/ppermute | solution.py:309
  7.4 0.6 %own_rest.1 = (bf16[288,512]{1,0:T(8,128)(2,1)S(1)}, f32[2,96,768]{2,1,0:T(8,128)S(1)}) custom-call(bf16[384,512]{1,0:T(8,128)(2,1)S(1)} %latent.1.act_ref, bf16[27,512,128]{2,1,0:T(8,128)(2,1)S(1)} %copy-done, f32[384,768]{1,0:T(8,128)S(1)} %own_first.1.first_ref, s32[4,4,24]{2,1,0:T(4,128)S(1)} %collective-permute-done.after_ref.near_ref), custom_call_target="tpu_custom_call" | custom-call | flops 1000000000 | bytes 10000000 | tf_op jit(solution)/shard_map/own_rest/pallas_call | solution.py:258
  8.0 0.1 collective-permute-start.3
  8.1 0.1 collective-permute-done.1.far_ref
  8.2 0.0 copy-start.1
  8.2 0.0 copy-start.5
  8.2 1.1 %halo.1.own_ref = bf16[192,512]{1,0:T(8,128)(2,1)S(1)} custom-call(s32[4,4,24]{2,1,0:T(4,128)S(1)} %collective-permute-done.after_ref.near_ref, s32[4,4,24]{2,1,0:T(4,128)S(1)} %collective-permute-done.1.far_ref, bf16[18,512]{1,0:T(8,128)(2,1)S(1)} %copy-done.2, f32[1,512]{1,0:T(1,128)S(1)} %bitcast.3, bf16[27,512,128]{2,1,0:T(8,128)(2,1)S(1)} %copy-done, ...), custom_call_target="tpu_custom_call" | custom-call | flops 20000000000 | bytes 10000000 | tf_op jit(solution)/shard_map/halo/pallas_call | solution.py:258
  9.3 0.5 %collective-permute-start.2 = (bf16[192,512]{1,0:T(8,128)(2,1)S(1)}, bf16[192,512]{1,0:T(8,128)(2,1)S(1)}, u32[]{:S(2)}, u32[]{:S(2)}) collective-permute-start(bf16[192,512]{1,0:T(8,128)(2,1)S(1)} %halo.1.own_ref), channel_id=1, source_target_pairs={{0,1},{1,0},{2,3},{3,2},{4,5},{5,4},{6,7},{7,6},{8,9},{9,8},{10,11... | collective-permute-start | bytes 589832 | tf_op jit(solution)/shard_map/ppermute | solution.py:330
  9.8 0.0 collective-permute-done.3.other_ref
  9.8 0.0 copy-done.1
  9.8 0.0 copy-done.5
  9.8 1.2 %out_inner.1 = (bf16[4,4,48,64]{3,2,1,0:T(8,128)(2,1)S(1)}, bf16[4,96,512]{2,1,0:T(8,128)(2,1)S(1)}) custom-call(bf16[288,512]{1,0:T(8,128)(2,1)S(1)} %get-tuple-element.22.own_ref, bf16[288,512]{1,0:T(8,128)(2,1)S(1)} %collective-permute-done.3.other_ref, f32[1,256]{1,0:T(1,128)S(1)} %bitcast.4, bf16[27,64,256]{2,1,0:T(8,128)(2,1)S(1)} %copy-done.1), custom_call_target="tpu_custom_call" | custom-call | flops 2000000000 | bytes 10000000 | tf_op jit(solution)/shard_map/out_inner/pallas_call | solution.py:258
  11.0 0.0 collective-permute-done.2.other_ref
  11.0 1.9 %out_edge.1 = bf16[4,8,48,64]{3,2,1,0:T(8,128)(2,1)} custom-call(bf16[192,512]{1,0:T(8,128)(2,1)S(1)} %halo.1.own_ref, bf16[192,512]{1,0:T(8,128)(2,1)S(1)} %collective-permute-done.2.other_ref, f32[1,256]{1,0:T(1,128)S(1)} %bitcast.5, bf16[27,64,256]{2,1,0:T(8,128)(2,1)S(1)} %copy-done.1, bf16[4,96,512]{2,1,0:T(8,128)(2,1)S(1)} %get-tuple-element.23.norm_ref, ...), custom_call_target="tpu_custom_call" | custom-call | flops 1000000000 | bytes 10000000 | tf_op jit(solution)/shard_map/out_edge/pallas_call | solution.py:258
  (1 shorter events, 0.0 us)
Async XLA Ops:
  0.0 0.7 %copy-start.3 = (s32[4,4,24]{2,1,0:T(4,128)S(1)}, s32[4,4,24]{2,1,0:T(4,128)}, u32[]{:S(2)}) copy-start(s32[4,4,24]{2,1,0:T(4,128)} %codes_ref.1) | copy-start | bytes 4612
  0.0 4.5 %copy-start.2 = (bf16[18,512]{1,0:T(8,128)(2,1)S(1)}, bf16[18,512]{1,0:T(8,128)(2,1)}, u32[]{:S(2)}) copy-start(bf16[18,512]{1,0:T(8,128)(2,1)} %proj_ref.3) | copy-start | bytes 55300
  0.0 4.5 %copy-start.4 = (f32[512]{0:T(512)S(1)}, f32[512]{0:T(512)}, u32[]{:S(2)}) copy-start(f32[512]{0:T(512)} %param.8) | copy-start | bytes 6148
  0.0 5.0 %copy-start = (bf16[27,512,128]{2,1,0:T(8,128)(2,1)S(1)}, bf16[27,512,128]{2,1,0:T(8,128)(2,1)}, u32[]{:S(2)}) copy-start(bf16[27,512,128]{2,1,0:T(8,128)(2,1)} %w_ref.5) | copy-start | bytes 10616836
  0.7 5.2 %collective-permute-start = (s32[4,4,24]{2,1,0:T(4,128)S(1)}, s32[4,4,24]{2,1,0:T(4,128)S(1)}, u32[]{:S(2)}, u32[]{:S(2)}) collective-permute-start(s32[4,4,24]{2,1,0:T(4,128)S(1)} %copy-done.3), channel_id=1, source_target_pairs={{1,2},{2,1},{3,4},{4,3},{5,6},{6,5},{7,8},{8,7},{9,10},{10,9},{11,... | collective-permute-start | bytes 4616 | tf_op jit(solution)/shard_map/ppermute | solution.py:284
  5.9 2.3 %collective-permute-start.1 = (s32[4,4,24]{2,1,0:T(4,128)S(1)}, s32[4,4,24]{2,1,0:T(4,128)S(1)}, u32[]{:S(2)}, u32[]{:S(2)}) collective-permute-start(s32[4,4,24]{2,1,0:T(4,128)S(1)} %collective-permute-done.after_ref.near_ref), channel_id=1, source_target_pairs={{0,1},{1,0},{2,3},{3,2},{4,5},{5,4},{6,7},{7,6},{8,9},{9,8},{10,11... | collective-permute-start | bytes 4616 | tf_op jit(solution)/shard_map/ppermute | solution.py:309
  8.0 1.8 %collective-permute-start.3 = (bf16[288,512]{1,0:T(8,128)(2,1)S(1)}, bf16[288,512]{1,0:T(8,128)(2,1)S(1)}, u32[]{:S(2)}, u32[]{:S(2)}) collective-permute-start(bf16[288,512]{1,0:T(8,128)(2,1)S(1)} %get-tuple-element.22.own_ref), channel_id=1, source_target_pairs={{0,1},{1,0},{2,3},{3,2},{4,5},{5,4},{6,7},{7,6},{8,9},{9,8},{10,11... | collective-permute-start | bytes 884744 | tf_op jit(solution)/shard_map/ppermute | solution.py:319
  8.2 1.6 %copy-start.1 = (bf16[27,64,256]{2,1,0:T(8,128)(2,1)S(1)}, bf16[27,64,256]{2,1,0:T(8,128)(2,1)}, u32[]{:S(2)}) copy-start(bf16[27,64,256]{2,1,0:T(8,128)(2,1)} %tap_ref.3) | copy-start | bytes 2654212
  8.2 1.6 %copy-start.5 = (f32[256]{0:T(256)S(1)}, f32[256]{0:T(256)}, u32[]{:S(2)}) copy-start(f32[256]{0:T(256)} %param.10) | copy-start | bytes 3076
  9.3 1.7 %collective-permute-start.2 = (bf16[192,512]{1,0:T(8,128)(2,1)S(1)}, bf16[192,512]{1,0:T(8,128)(2,1)S(1)}, u32[]{:S(2)}, u32[]{:S(2)}) collective-permute-start(bf16[192,512]{1,0:T(8,128)(2,1)S(1)} %halo.1.own_ref), channel_id=1, source_target_pairs={{0,1},{1,0},{2,3},{3,2},{4,5},{5,4},{6,7},{7,6},{8,9},{9,8},{10,11... | collective-permute-start | bytes 589832 | tf_op jit(solution)/shard_map/ppermute | solution.py:330

commit v13 on v12

--- a/solution.py
+++ b/solution.py
@@ -279,9 +279,7 @@
     joint = [pair for i in range(count - 1) for pair in ((2 * i + 1, 2 * i + 2), (2 * i + 2, 2 * i + 1))]
     swap = [(0, 1), (1, 0)]
     (mark,) = call(open_kernel, "open", (pltpu.VMEM((8, 128), F32),), (), 1, 1000)
-    sent, mark = lax.optimization_barrier((codes, mark))
-    (mark,) = in_space(pltpu.VMEM, mark)
-    near = lax.ppermute(sent, ("rows", "section"), joint)
+    near = lax.ppermute(codes, ("rows", "section"), joint)
     gain_res = gain_res.reshape(1, -1)
     w, tap, proj, gain = in_space(pltpu.VMEM, up_kernel, out_kernel, in_proj, gain_up.reshape(1, -1))
     (codes,) = in_space(pltpu.VMEM, codes)

time: 13 us -> 12.7 us (0.977)
  the two profiles are of different devices: /device:TPU:25 before, /device:TPU:17 now
where the time goes in v13:
time: 12.7 us; the launch traced here: 12.5 us
  Pallas kernels  6.11 us (48%)
  starting transfers between devices  6.02 us (47%)
  waiting for transfers between devices  0.23 us (2%)
    pallas_call x7, Pallas kernels, call(): pl.pallas_call(kernel, out_shape=outs, in_specs=in_specs or [vmem()] * le...  6.11 us
    ppermute x1, starting transfers between devices, body(): near = lax.ppermute(codes, ('rows', 'section'), joint)  3.94 us
    ppermute x1, starting transfers between devices, body(): far = lax.ppermute(near, 'section', swap)  1.54 us
    ppermute x1, starting transfers between devices, body(): edge_other = lax.ppermute(edge_own, 'section', swap)  0.47 us
  transfers between devices with their start and end apart: 4, of which 2 were waited for; matrix products, arithmetic and copies ran while one was open for 0% of the time, Pallas kernels for 34%

profile of v13, /device:TPU:17, one launch (start us, length us, event | category | flops | bytes accessed | tf_op | source)
XLA Modules:
  0.0 12.5 jit_solution(7949365692091223144)
XLA Ops:
  0.0 0.0 copy-start.3
  0.0 0.0 copy-start.2
  0.0 0.0 copy-start.4
  0.0 0.0 copy-start
  0.0 3.9 %collective-permute-start = (s32[4,4,24]{2,1,0:T(4,128)}, s32[4,4,24]{2,1,0:T(4,128)S(1)}, u32[]{:S(2)}, u32[]{:S(2)}) collective-permute-start(s32[4,4,24]{2,1,0:T(4,128)} %codes_ref.1), channel_id=1, source_target_pairs={{1,2},{2,1},{3,4},{4,3},{5,6},{6,5},{7,8},{8,7},{9,10},{10,9},{11,... | collective-permute-start | bytes 4616 | tf_op jit(solution)/shard_map/ppermute | solution.py:282
  4.0 0.0 copy-done.3
  4.0 0.0 copy-done.2
  4.0 0.0 copy-done.4
  4.0 0.5 %latent.1.act_ref = bf16[384,512]{1,0:T(8,128)(2,1)S(1)} custom-call(s32[4,4,24]{2,1,0:T(4,128)S(1)} %copy-done.3, bf16[18,512]{1,0:T(8,128)(2,1)S(1)} %copy-done.2, f32[1,512]{1,0:T(1,128)S(1)} %bitcast.2, f32[8,128]{1,0:T(8,128)S(1)} %open.1.mark_ref), custom_call_target="tpu_custom_call" | custom-call | flops 1000000000 | bytes 10000000 | tf_op jit(solution)/shard_map/latent/pallas_call | solution.py:258
  4.5 0.0 copy-done
  4.5 0.9 %own_first.1.first_ref = f32[384,768]{1,0:T(8,128)S(1)} custom-call(bf16[384,512]{1,0:T(8,128)(2,1)S(1)} %latent.1.act_ref, bf16[27,512,128]{2,1,0:T(8,128)(2,1)S(1)} %copy-done), custom_call_target="tpu_custom_call" | custom-call | flops 1000000000 | bytes 10000000 | tf_op jit(solution)/shard_map/own_first/pallas_call | solution.py:258
  5.4 0.1 collective-permute-done.after_ref.near_ref
  5.5 1.5 %collective-permute-start.1 = (s32[4,4,24]{2,1,0:T(4,128)S(1)}, s32[4,4,24]{2,1,0:T(4,128)S(1)}, u32[]{:S(2)}, u32[]{:S(2)}) collective-permute-start(s32[4,4,24]{2,1,0:T(4,128)S(1)} %collective-permute-done.after_ref.near_ref), channel_id=1, source_target_pairs={{0,1},{1,0},{2,3},{3,2},{4,5},{5,4},{6,7},{7,6},{8,9},{9,8},{10,11... | collective-permute-start | bytes 4616 | tf_op jit(solution)/shard_map/ppermute | solution.py:307
  7.0 0.6 %own_rest.1 = (bf16[288,512]{1,0:T(8,128)(2,1)S(1)}, f32[2,96,768]{2,1,0:T(8,128)S(1)}) custom-call(bf16[384,512]{1,0:T(8,128)(2,1)S(1)} %latent.1.act_ref, bf16[27,512,128]{2,1,0:T(8,128)(2,1)S(1)} %copy-done, f32[384,768]{1,0:T(8,128)S(1)} %own_first.1.first_ref, s32[4,4,24]{2,1,0:T(4,128)S(1)} %collective-permute-done.after_ref.near_ref), custom_call_target="tpu_custom_call" | custom-call | flops 1000000000 | bytes 10000000 | tf_op jit(solution)/shard_map/own_rest/pallas_call | solution.py:258
  7.7 0.1 collective-permute-start.3
  7.8 0.1 collective-permute-done.1.far_ref
  7.9 0.0 copy-start.1
  7.9 0.0 copy-start.5
  7.9 1.1 %halo.1.own_ref = bf16[192,512]{1,0:T(8,128)(2,1)S(1)} custom-call(s32[4,4,24]{2,1,0:T(4,128)S(1)} %collective-permute-done.after_ref.near_ref, s32[4,4,24]{2,1,0:T(4,128)S(1)} %collective-permute-done.1.far_ref, bf16[18,512]{1,0:T(8,128)(2,1)S(1)} %copy-done.2, f32[1,512]{1,0:T(1,128)S(1)} %bitcast.3, bf16[27,512,128]{2,1,0:T(8,128)(2,1)S(1)} %copy-done, ...), custom_call_target="tpu_custom_call" | custom-call | flops 20000000000 | bytes 10000000 | tf_op jit(solution)/shard_map/halo/pallas_call | solution.py:258
  9.0 0.5 %collective-permute-start.2 = (bf16[192,512]{1,0:T(8,128)(2,1)S(1)}, bf16[192,512]{1,0:T(8,128)(2,1)S(1)}, u32[]{:S(2)}, u32[]{:S(2)}) collective-permute-start(bf16[192,512]{1,0:T(8,128)(2,1)S(1)} %halo.1.own_ref), channel_id=1, source_target_pairs={{0,1},{1,0},{2,3},{3,2},{4,5},{5,4},{6,7},{7,6},{8,9},{9,8},{10,11... | collective-permute-start | bytes 589832 | tf_op jit(solution)/shard_map/ppermute | solution.py:328
  9.4 0.0 collective-permute-done.3.other_ref
  9.4 0.0 copy-done.1
  9.4 0.0 copy-done.5
  9.4 1.2 %out_inner.1 = (bf16[4,4,48,64]{3,2,1,0:T(8,128)(2,1)S(1)}, bf16[4,96,512]{2,1,0:T(8,128)(2,1)S(1)}) custom-call(bf16[288,512]{1,0:T(8,128)(2,1)S(1)} %get-tuple-element.18.own_ref, bf16[288,512]{1,0:T(8,128)(2,1)S(1)} %collective-permute-done.3.other_ref, f32[1,256]{1,0:T(1,128)S(1)} %bitcast.4, bf16[27,64,256]{2,1,0:T(8,128)(2,1)S(1)} %copy-done.1), custom_call_target="tpu_custom_call" | custom-call | flops 2000000000 | bytes 10000000 | tf_op jit(solution)/shard_map/out_inner/pallas_call | solution.py:258
  10.6 0.0 collective-permute-done.2.other_ref
  10.7 1.9 %out_edge.1 = bf16[4,8,48,64]{3,2,1,0:T(8,128)(2,1)} custom-call(bf16[192,512]{1,0:T(8,128)(2,1)S(1)} %halo.1.own_ref, bf16[192,512]{1,0:T(8,128)(2,1)S(1)} %collective-permute-done.2.other_ref, f32[1,256]{1,0:T(1,128)S(1)} %bitcast.5, bf16[27,64,256]{2,1,0:T(8,128)(2,1)S(1)} %copy-done.1, bf16[4,96,512]{2,1,0:T(8,128)(2,1)S(1)} %get-tuple-element.19.norm_ref, ...), custom_call_target="tpu_custom_call" | custom-call | flops 1000000000 | bytes 10000000 | tf_op jit(solution)/shard_map/out_edge/pallas_call | solution.py:258
  (1 shorter events, 0.0 us)
Async XLA Ops:
  0.0 4.0 %copy-start.3 = (s32[4,4,24]{2,1,0:T(4,128)S(1)}, s32[4,4,24]{2,1,0:T(4,128)}, u32[]{:S(2)}) copy-start(s32[4,4,24]{2,1,0:T(4,128)} %codes_ref.1) | copy-start | bytes 4612
  0.0 4.0 %copy-start.2 = (bf16[18,512]{1,0:T(8,128)(2,1)S(1)}, bf16[18,512]{1,0:T(8,128)(2,1)}, u32[]{:S(2)}) copy-start(bf16[18,512]{1,0:T(8,128)(2,1)} %proj_ref.3) | copy-start | bytes 55300
  0.0 4.0 %copy-start.4 = (f32[512]{0:T(512)S(1)}, f32[512]{0:T(512)}, u32[]{:S(2)}) copy-start(f32[512]{0:T(512)} %param.8) | copy-start | bytes 6148
  0.0 4.5 %copy-start = (bf16[27,512,128]{2,1,0:T(8,128)(2,1)S(1)}, bf16[27,512,128]{2,1,0:T(8,128)(2,1)}, u32[]{:S(2)}) copy-start(bf16[27,512,128]{2,1,0:T(8,128)(2,1)} %w_ref.5) | copy-start | bytes 10616836
  0.0 5.5 %collective-permute-start = (s32[4,4,24]{2,1,0:T(4,128)}, s32[4,4,24]{2,1,0:T(4,128)S(1)}, u32[]{:S(2)}, u32[]{:S(2)}) collective-permute-start(s32[4,4,24]{2,1,0:T(4,128)} %codes_ref.1), channel_id=1, source_target_pairs={{1,2},{2,1},{3,4},{4,3},{5,6},{6,5},{7,8},{8,7},{9,10},{10,9},{11,... | collective-permute-start | bytes 4616 | tf_op jit(solution)/shard_map/ppermute | solution.py:282
  5.5 2.4 %collective-permute-start.1 = (s32[4,4,24]{2,1,0:T(4,128)S(1)}, s32[4,4,24]{2,1,0:T(4,128)S(1)}, u32[]{:S(2)}, u32[]{:S(2)}) collective-permute-start(s32[4,4,24]{2,1,0:T(4,128)S(1)} %collective-permute-done.after_ref.near_ref), channel_id=1, source_target_pairs={{0,1},{1,0},{2,3},{3,2},{4,5},{5,4},{6,7},{7,6},{8,9},{9,8},{10,11... | collective-permute-start | bytes 4616 | tf_op jit(solution)/shard_map/ppermute | solution.py:307
  7.7 1.8 %collective-permute-start.3 = (bf16[288,512]{1,0:T(8,128)(2,1)S(1)}, bf16[288,512]{1,0:T(8,128)(2,1)S(1)}, u32[]{:S(2)}, u32[]{:S(2)}) collective-permute-start(bf16[288,512]{1,0:T(8,128)(2,1)S(1)} %get-tuple-element.18.own_ref), channel_id=1, source_target_pairs={{0,1},{1,0},{2,3},{3,2},{4,5},{5,4},{6,7},{7,6},{8,9},{9,8},{10,11... | collective-permute-start | bytes 884744 | tf_op jit(solution)/shard_map/ppermute | solution.py:317
  7.9 1.6 %copy-start.1 = (bf16[27,64,256]{2,1,0:T(8,128)(2,1)S(1)}, bf16[27,64,256]{2,1,0:T(8,128)(2,1)}, u32[]{:S(2)}) copy-start(bf16[27,64,256]{2,1,0:T(8,128)(2,1)} %tap_ref.3) | copy-start | bytes 2654212
  7.9 1.6 %copy-start.5 = (f32[256]{0:T(256)S(1)}, f32[256]{0:T(256)}, u32[]{:S(2)}) copy-start(f32[256]{0:T(256)} %param.10) | copy-start | bytes 3076
  9.0 1.7 %collective-permute-start.2 = (bf16[192,512]{1,0:T(8,128)(2,1)S(1)}, bf16[192,512]{1,0:T(8,128)(2,1)S(1)}, u32[]{:S(2)}, u32[]{:S(2)}) collective-permute-start(bf16[192,512]{1,0:T(8,128)(2,1)S(1)} %halo.1.own_ref), channel_id=1, source_target_pairs={{0,1},{1,0},{2,3},{3,2},{4,5},{5,4},{6,7},{7,6},{8,9},{9,8},{10,11... | collective-permute-start | bytes 589832 | tf_op jit(solution)/shard_map/ppermute | solution.py:328

commit v14 on v13

--- a/solution.py
+++ b/solution.py
@@ -13,7 +13,7 @@
 BF16 = jnp.bfloat16
 MIB = 1024 * 1024
 GROUPS = ((0, 2), (2, 2), (4, 2), (6, 2), (8, 1))
-SPLIT = 3
+SPLIT = 4
 
 
 def silu_of_half(h):

time: 12.7 us -> 12.6 us (level)
  the two profiles are of different devices: /device:TPU:17 before, /device:TPU:0 now
where the time goes in v14:
time: 12.6 us; the launch traced here: 12.4 us
  Pallas kernels  6.09 us (48%)
  starting transfers between devices  5.09 us (40%)
  local copies, waits for them, and re-layouts  0.73 us (6%)
  waiting for transfers between devices  0.36 us (3%)
    pallas_call x7, Pallas kernels, call(): pl.pallas_call(kernel, out_shape=outs, in_specs=in_specs or [vmem()] * le...  6.09 us
    ppermute x1, starting transfers between devices, body(): far = lax.ppermute(near, 'section', swap)  3.81 us
    ppermute x1, starting transfers between devices, body(): near = lax.ppermute(codes, ('rows', 'section'), joint)  0.79 us
    unnamed x12, local copies, waits for them, and re-layouts  0.73 us
    ppermute x1, starting transfers between devices, body(): edge_other = lax.ppermute(edge_own, 'section', swap)  0.41 us
    ppermute x1, waiting for transfers between devices, body(): far = lax.ppermute(near, 'section', swap)  0.35 us
  transfers between devices with their start and end apart: 4, of which 1 were waited for; matrix products, arithmetic and copies ran while one was open for 0% of the time, Pallas kernels for 34%

profile of v14, /device:TPU:0, one launch (start us, length us, event | category | flops | bytes accessed | tf_op | source)
XLA Modules:
  0.0 12.4 jit_solution(18216134248311258892)
XLA Ops:
  0.0 0.0 copy-start.3
  0.0 0.0 copy-start.2
  0.0 0.0 copy-start.4
  0.0 0.0 copy-start
  0.0 0.8 %collective-permute-start = (s32[4,4,24]{2,1,0:T(4,128)}, s32[4,4,24]{2,1,0:T(4,128)S(1)}, u32[]{:S(2)}, u32[]{:S(2)}) collective-permute-start(s32[4,4,24]{2,1,0:T(4,128)} %codes_ref.1), channel_id=1, source_target_pairs={{1,2},{2,1},{3,4},{4,3},{5,6},{6,5},{7,8},{8,7},{9,10},{10,9},{11,... | collective-permute-start | bytes 4616 | tf_op jit(solution)/shard_map/ppermute | solution.py:282
  0.8 0.0 copy-done.3
  0.8 0.0 copy-done.2
  0.8 0.0 copy-done.4
  0.8 0.5 %latent.1.act_ref = bf16[384,512]{1,0:T(8,128)(2,1)S(1)} custom-call(s32[4,4,24]{2,1,0:T(4,128)S(1)} %copy-done.3, bf16[18,512]{1,0:T(8,128)(2,1)S(1)} %copy-done.2, f32[1,512]{1,0:T(1,128)S(1)} %bitcast.2, f32[8,128]{1,0:T(8,128)S(1)} %open.1.mark_ref), custom_call_target="tpu_custom_call" | custom-call | flops 1000000000 | bytes 10000000 | tf_op jit(solution)/shard_map/latent/pallas_call | solution.py:258
  1.3 0.7 %copy-done = bf16[27,512,128]{2,1,0:T(8,128)(2,1)S(1)} copy-done((bf16[27,512,128]{2,1,0:T(8,128)(2,1)S(1)}, bf16[27,512,128]{2,1,0:T(8,128)(2,1)}, u32[]{:S(2)}) %copy-start) | copy-done | bytes 3538968
  2.1 1.1 %own_first.1.first_ref = f32[384,1024]{1,0:T(8,128)S(1)} custom-call(bf16[384,512]{1,0:T(8,128)(2,1)S(1)} %latent.1.act_ref, bf16[27,512,128]{2,1,0:T(8,128)(2,1)S(1)} %copy-done), custom_call_target="tpu_custom_call" | custom-call | flops 1000000000 | bytes 10000000 | tf_op jit(solution)/shard_map/own_first/pallas_call | solution.py:258
  3.1 0.0 collective-permute-done.after_ref.near_ref
  3.1 3.8 %collective-permute-start.1 = (s32[4,4,24]{2,1,0:T(4,128)S(1)}, s32[4,4,24]{2,1,0:T(4,128)S(1)}, u32[]{:S(2)}, u32[]{:S(2)}) collective-permute-start(s32[4,4,24]{2,1,0:T(4,128)S(1)} %collective-permute-done.after_ref.near_ref), channel_id=1, source_target_pairs={{0,1},{1,0},{2,3},{3,2},{4,5},{5,4},{6,7},{7,6},{8,9},{9,8},{10,11... | collective-permute-start | bytes 4616 | tf_op jit(solution)/shard_map/ppermute | solution.py:307
  7.0 0.4 %own_rest.1 = (bf16[288,512]{1,0:T(8,128)(2,1)S(1)}, f32[2,96,768]{2,1,0:T(8,128)S(1)}) custom-call(bf16[384,512]{1,0:T(8,128)(2,1)S(1)} %latent.1.act_ref, bf16[27,512,128]{2,1,0:T(8,128)(2,1)S(1)} %copy-done, f32[384,1024]{1,0:T(8,128)S(1)} %own_first.1.first_ref, s32[4,4,24]{2,1,0:T(4,128)S(1)} %collective-permute-done.after_ref.near_ref), custom_call_target="tpu_custom_call" | custom-call | flops 1000000000 | bytes 10000000 | tf_op jit(solution)/shard_map/own_rest/pallas_call | solution.py:258
  7.4 0.1 collective-permute-start.3
  7.4 0.4 %collective-permute-done.1.far_ref = s32[4,4,24]{2,1,0:T(4,128)S(1)} collective-permute-done((s32[4,4,24]{2,1,0:T(4,128)S(1)}, s32[4,4,24]{2,1,0:T(4,128)S(1)}, u32[]{:S(2)}, u32[]{:S(2)}) %collective-permute-start.1) | collective-permute-done | bytes 1568 | tf_op jit(solution)/shard_map/ppermute | solution.py:307
  7.8 0.0 copy-start.1
  7.8 0.0 copy-start.5
  7.8 1.1 %halo.1.own_ref = bf16[192,512]{1,0:T(8,128)(2,1)S(1)} custom-call(s32[4,4,24]{2,1,0:T(4,128)S(1)} %collective-permute-done.after_ref.near_ref, s32[4,4,24]{2,1,0:T(4,128)S(1)} %collective-permute-done.1.far_ref, bf16[18,512]{1,0:T(8,128)(2,1)S(1)} %copy-done.2, f32[1,512]{1,0:T(1,128)S(1)} %bitcast.3, bf16[27,512,128]{2,1,0:T(8,128)(2,1)S(1)} %copy-done, ...), custom_call_target="tpu_custom_call" | custom-call | flops 20000000000 | bytes 10000000 | tf_op jit(solution)/shard_map/halo/pallas_call | solution.py:258
  8.9 0.4 %collective-permute-start.2 = (bf16[192,512]{1,0:T(8,128)(2,1)S(1)}, bf16[192,512]{1,0:T(8,128)(2,1)S(1)}, u32[]{:S(2)}, u32[]{:S(2)}) collective-permute-start(bf16[192,512]{1,0:T(8,128)(2,1)S(1)} %halo.1.own_ref), channel_id=1, source_target_pairs={{0,1},{1,0},{2,3},{3,2},{4,5},{5,4},{6,7},{7,6},{8,9},{9,8},{10,11... | collective-permute-start | bytes 589832 | tf_op jit(solution)/shard_map/ppermute | solution.py:328
  9.3 0.0 collective-permute-done.3.other_ref
  9.3 0.0 copy-done.1
  9.3 0.0 copy-done.5
  9.3 1.2 %out_inner.1 = (bf16[4,4,48,64]{3,2,1,0:T(8,128)(2,1)S(1)}, bf16[4,96,512]{2,1,0:T(8,128)(2,1)S(1)}) custom-call(bf16[288,512]{1,0:T(8,128)(2,1)S(1)} %get-tuple-element.18.own_ref, bf16[288,512]{1,0:T(8,128)(2,1)S(1)} %collective-permute-done.3.other_ref, f32[1,256]{1,0:T(1,128)S(1)} %bitcast.4, bf16[27,64,256]{2,1,0:T(8,128)(2,1)S(1)} %copy-done.1), custom_call_target="tpu_custom_call" | custom-call | flops 2000000000 | bytes 10000000 | tf_op jit(solution)/shard_map/out_inner/pallas_call | solution.py:258
  10.5 0.0 collective-permute-done.2.other_ref
  10.5 1.9 %out_edge.1 = bf16[4,8,48,64]{3,2,1,0:T(8,128)(2,1)} custom-call(bf16[192,512]{1,0:T(8,128)(2,1)S(1)} %halo.1.own_ref, bf16[192,512]{1,0:T(8,128)(2,1)S(1)} %collective-permute-done.2.other_ref, f32[1,256]{1,0:T(1,128)S(1)} %bitcast.5, bf16[27,64,256]{2,1,0:T(8,128)(2,1)S(1)} %copy-done.1, bf16[4,96,512]{2,1,0:T(8,128)(2,1)S(1)} %get-tuple-element.19.norm_ref, ...), custom_call_target="tpu_custom_call" | custom-call | flops 1000000000 | bytes 10000000 | tf_op jit(solution)/shard_map/out_edge/pallas_call | solution.py:258
  (1 shorter events, 0.0 us)
Async XLA Ops:
  0.0 0.8 %copy-start.3 = (s32[4,4,24]{2,1,0:T(4,128)S(1)}, s32[4,4,24]{2,1,0:T(4,128)}, u32[]{:S(2)}) copy-start(s32[4,4,24]{2,1,0:T(4,128)} %codes_ref.1) | copy-start | bytes 4612
  0.0 0.8 %copy-start.2 = (bf16[18,512]{1,0:T(8,128)(2,1)S(1)}, bf16[18,512]{1,0:T(8,128)(2,1)}, u32[]{:S(2)}) copy-start(bf16[18,512]{1,0:T(8,128)(2,1)} %proj_ref.3) | copy-start | bytes 55300
  0.0 0.8 %copy-start.4 = (f32[512]{0:T(512)S(1)}, f32[512]{0:T(512)}, u32[]{:S(2)}) copy-start(f32[512]{0:T(512)} %param.8) | copy-start | bytes 6148
  0.0 2.0 %copy-start = (bf16[27,512,128]{2,1,0:T(8,128)(2,1)S(1)}, bf16[27,512,128]{2,1,0:T(8,128)(2,1)}, u32[]{:S(2)}) copy-start(bf16[27,512,128]{2,1,0:T(8,128)(2,1)} %w_ref.5) | copy-start | bytes 10616836
  0.0 3.1 %collective-permute-start = (s32[4,4,24]{2,1,0:T(4,128)}, s32[4,4,24]{2,1,0:T(4,128)S(1)}, u32[]{:S(2)}, u32[]{:S(2)}) collective-permute-start(s32[4,4,24]{2,1,0:T(4,128)} %codes_ref.1), channel_id=1, source_target_pairs={{1,2},{2,1},{3,4},{4,3},{5,6},{6,5},{7,8},{8,7},{9,10},{10,9},{11,... | collective-permute-start | bytes 4616 | tf_op jit(solution)/shard_map/ppermute | solution.py:282
  3.1 4.6 %collective-permute-start.1 = (s32[4,4,24]{2,1,0:T(4,128)S(1)}, s32[4,4,24]{2,1,0:T(4,128)S(1)}, u32[]{:S(2)}, u32[]{:S(2)}) collective-permute-start(s32[4,4,24]{2,1,0:T(4,128)S(1)} %collective-permute-done.after_ref.near_ref), channel_id=1, source_target_pairs={{0,1},{1,0},{2,3},{3,2},{4,5},{5,4},{6,7},{7,6},{8,9},{9,8},{10,11... | collective-permute-start | bytes 4616 | tf_op jit(solution)/shard_map/ppermute | solution.py:307
  7.4 1.9 %collective-permute-start.3 = (bf16[288,512]{1,0:T(8,128)(2,1)S(1)}, bf16[288,512]{1,0:T(8,128)(2,1)S(1)}, u32[]{:S(2)}, u32[]{:S(2)}) collective-permute-start(bf16[288,512]{1,0:T(8,128)(2,1)S(1)} %get-tuple-element.18.own_ref), channel_id=1, source_target_pairs={{0,1},{1,0},{2,3},{3,2},{4,5},{5,4},{6,7},{7,6},{8,9},{9,8},{10,11... | collective-permute-start | bytes 884744 | tf_op jit(solution)/shard_map/ppermute | solution.py:317
  7.8 1.5 %copy-start.1 = (bf16[27,64,256]{2,1,0:T(8,128)(2,1)S(1)}, bf16[27,64,256]{2,1,0:T(8,128)(2,1)}, u32[]{:S(2)}) copy-start(bf16[27,64,256]{2,1,0:T(8,128)(2,1)} %tap_ref.3) | copy-start | bytes 2654212
  7.8 1.5 %copy-start.5 = (f32[256]{0:T(256)S(1)}, f32[256]{0:T(256)}, u32[]{:S(2)}) copy-start(f32[256]{0:T(256)} %param.10) | copy-start | bytes 3076
  8.9 1.6 %collective-permute-start.2 = (bf16[192,512]{1,0:T(8,128)(2,1)S(1)}, bf16[192,512]{1,0:T(8,128)(2,1)S(1)}, u32[]{:S(2)}, u32[]{:S(2)}) collective-permute-start(bf16[192,512]{1,0:T(8,128)(2,1)S(1)} %halo.1.own_ref), channel_id=1, source_target_pairs={{0,1},{1,0},{2,3},{3,2},{4,5},{5,4},{6,7},{7,6},{8,9},{9,8},{10,11... | collective-permute-start | bytes 589832 | tf_op jit(solution)/shard_map/ppermute | solution.py:328

commit v15 on v14

--- a/solution.py
+++ b/solution.py
@@ -121,7 +121,7 @@
 def halo_kernel(near_ref, far_ref, proj_ref, gain_ref, w_ref, edge_ref, h_ref):
     frames, rows, cols = near_ref.shape
     share = w_ref.shape[2]
-    first = lax.axis_index("section") == 0
+    first = lax.axis_index("section") == 1
     place = lax.axis_index("rows")
     last = lax.axis_size("rows") - 1
     codes = []
@@ -276,7 +276,7 @@
     height = 2 * rows
     inner = height - 4
     count = lax.axis_size("rows")
-    joint = [pair for i in range(count - 1) for pair in ((2 * i + 1, 2 * i + 2), (2 * i + 2, 2 * i + 1))]
+    joint = [pair for i in range(count - 1) for pair in ((2 * i, 2 * i + 3), (2 * i + 3, 2 * i))]
     swap = [(0, 1), (1, 0)]
     (mark,) = call(open_kernel, "open", (pltpu.VMEM((8, 128), F32),), (), 1, 1000)
     near = lax.ppermute(codes, ("rows", "section"), joint)

time: 12.6 us -> 12.6 us (level)
  the two profiles are of different devices: /device:TPU:0 before, /device:TPU:7 now
where the time goes in v15:
time: 12.6 us; the launch traced here: 12.5 us
  Pallas kernels  6.1 us (48%)
  starting transfers between devices  5.05 us (40%)
  waiting for transfers between devices  1.18 us (9%)
    pallas_call x7, Pallas kernels, call(): pl.pallas_call(kernel, out_shape=outs, in_specs=in_specs or [vmem()] * le...  6.1 us
    ppermute x1, starting transfers between devices, body(): near = lax.ppermute(codes, ('rows', 'section'), joint)  2.99 us
    ppermute x1, starting transfers between devices, body(): far = lax.ppermute(near, 'section', swap)  1.57 us
    ppermute x1, waiting for transfers between devices, body(): near = lax.ppermute(codes, ('rows', 'section'), joint)  0.81 us
    ppermute x1, starting transfers between devices, body(): edge_other = lax.ppermute(edge_own, 'section', swap)  0.42 us
    ppermute x1, waiting for transfers between devices, body(): far = lax.ppermute(near, 'section', swap)  0.36 us
  transfers between devices with their start and end apart: 4, of which 2 were waited for; matrix products, arithmetic and copies ran while one was open for 0% of the time, Pallas kernels for 34%

profile of v15, /device:TPU:7, one launch (start us, length us, event | category | flops | bytes accessed | tf_op | source)
XLA Modules:
  0.0 12.5 jit_solution(3400102204206119425)
XLA Ops:
  0.0 0.0 copy-start.3
  0.0 0.0 copy-start.2
  0.0 0.0 copy-start.4
  0.0 0.0 copy-start
  0.0 3.0 %collective-permute-start = (s32[4,4,24]{2,1,0:T(4,128)}, s32[4,4,24]{2,1,0:T(4,128)S(1)}, u32[]{:S(2)}, u32[]{:S(2)}) collective-permute-start(s32[4,4,24]{2,1,0:T(4,128)} %codes_ref.1), channel_id=1, source_target_pairs={{0,3},{3,0},{2,5},{5,2},{4,7},{7,4},{6,9},{9,6},{8,11},{11,8},{10,... | collective-permute-start | bytes 4616 | tf_op jit(solution)/shard_map/ppermute | solution.py:282
  3.0 0.0 copy-done.3
  3.0 0.0 copy-done.2
  3.0 0.0 copy-done.4
  3.1 0.5 %latent.1.act_ref = bf16[384,512]{1,0:T(8,128)(2,1)S(1)} custom-call(s32[4,4,24]{2,1,0:T(4,128)S(1)} %copy-done.3, bf16[18,512]{1,0:T(8,128)(2,1)S(1)} %copy-done.2, f32[1,512]{1,0:T(1,128)S(1)} %bitcast.2, f32[8,128]{1,0:T(8,128)S(1)} %open.1.mark_ref), custom_call_target="tpu_custom_call" | custom-call | flops 1000000000 | bytes 10000000 | tf_op jit(solution)/shard_map/latent/pallas_call | solution.py:258
  3.5 0.0 copy-done
  3.6 1.1 %own_first.1.first_ref = f32[384,1024]{1,0:T(8,128)S(1)} custom-call(bf16[384,512]{1,0:T(8,128)(2,1)S(1)} %latent.1.act_ref, bf16[27,512,128]{2,1,0:T(8,128)(2,1)S(1)} %copy-done), custom_call_target="tpu_custom_call" | custom-call | flops 1000000000 | bytes 10000000 | tf_op jit(solution)/shard_map/own_first/pallas_call | solution.py:258
  4.6 0.8 %collective-permute-done.after_ref.near_ref = s32[4,4,24]{2,1,0:T(4,128)S(1)} collective-permute-done((s32[4,4,24]{2,1,0:T(4,128)}, s32[4,4,24]{2,1,0:T(4,128)S(1)}, u32[]{:S(2)}, u32[]{:S(2)}) %collective-permute-start) | collective-permute-done | bytes 1568 | tf_op jit(solution)/shard_map/ppermute | solution.py:282
  5.5 1.6 %collective-permute-start.1 = (s32[4,4,24]{2,1,0:T(4,128)S(1)}, s32[4,4,24]{2,1,0:T(4,128)S(1)}, u32[]{:S(2)}, u32[]{:S(2)}) collective-permute-start(s32[4,4,24]{2,1,0:T(4,128)S(1)} %collective-permute-done.after_ref.near_ref), channel_id=1, source_target_pairs={{0,1},{1,0},{2,3},{3,2},{4,5},{5,4},{6,7},{7,6},{8,9},{9,8},{10,11... | collective-permute-start | bytes 4616 | tf_op jit(solution)/shard_map/ppermute | solution.py:307
  7.0 0.4 %own_rest.1 = (bf16[288,512]{1,0:T(8,128)(2,1)S(1)}, f32[2,96,768]{2,1,0:T(8,128)S(1)}) custom-call(bf16[384,512]{1,0:T(8,128)(2,1)S(1)} %latent.1.act_ref, bf16[27,512,128]{2,1,0:T(8,128)(2,1)S(1)} %copy-done, f32[384,1024]{1,0:T(8,128)S(1)} %own_first.1.first_ref, s32[4,4,24]{2,1,0:T(4,128)S(1)} %collective-permute-done.after_ref.near_ref), custom_call_target="tpu_custom_call" | custom-call | flops 1000000000 | bytes 10000000 | tf_op jit(solution)/shard_map/own_rest/pallas_call | solution.py:258
  7.4 0.1 collective-permute-start.3
  7.5 0.4 %collective-permute-done.1.far_ref = s32[4,4,24]{2,1,0:T(4,128)S(1)} collective-permute-done((s32[4,4,24]{2,1,0:T(4,128)S(1)}, s32[4,4,24]{2,1,0:T(4,128)S(1)}, u32[]{:S(2)}, u32[]{:S(2)}) %collective-permute-start.1) | collective-permute-done | bytes 1568 | tf_op jit(solution)/shard_map/ppermute | solution.py:307
  7.9 0.0 copy-start.1
  7.9 0.0 copy-start.5
  7.9 1.1 %halo.1.own_ref = bf16[192,512]{1,0:T(8,128)(2,1)S(1)} custom-call(s32[4,4,24]{2,1,0:T(4,128)S(1)} %collective-permute-done.after_ref.near_ref, s32[4,4,24]{2,1,0:T(4,128)S(1)} %collective-permute-done.1.far_ref, bf16[18,512]{1,0:T(8,128)(2,1)S(1)} %copy-done.2, f32[1,512]{1,0:T(1,128)S(1)} %bitcast.3, bf16[27,512,128]{2,1,0:T(8,128)(2,1)S(1)} %copy-done, ...), custom_call_target="tpu_custom_call" | custom-call | flops 20000000000 | bytes 10000000 | tf_op jit(solution)/shard_map/halo/pallas_call | solution.py:258
  9.0 0.4 %collective-permute-start.2 = (bf16[192,512]{1,0:T(8,128)(2,1)S(1)}, bf16[192,512]{1,0:T(8,128)(2,1)S(1)}, u32[]{:S(2)}, u32[]{:S(2)}) collective-permute-start(bf16[192,512]{1,0:T(8,128)(2,1)S(1)} %halo.1.own_ref), channel_id=1, source_target_pairs={{0,1},{1,0},{2,3},{3,2},{4,5},{5,4},{6,7},{7,6},{8,9},{9,8},{10,11... | collective-permute-start | bytes 589832 | tf_op jit(solution)/shard_map/ppermute | solution.py:328
  9.4 0.0 collective-permute-done.3.other_ref
  9.4 0.0 copy-done.1
  9.4 0.0 copy-done.5
  9.4 1.2 %out_inner.1 = (bf16[4,4,48,64]{3,2,1,0:T(8,128)(2,1)S(1)}, bf16[4,96,512]{2,1,0:T(8,128)(2,1)S(1)}) custom-call(bf16[288,512]{1,0:T(8,128)(2,1)S(1)} %get-tuple-element.18.own_ref, bf16[288,512]{1,0:T(8,128)(2,1)S(1)} %collective-permute-done.3.other_ref, f32[1,256]{1,0:T(1,128)S(1)} %bitcast.4, bf16[27,64,256]{2,1,0:T(8,128)(2,1)S(1)} %copy-done.1), custom_call_target="tpu_custom_call" | custom-call | flops 2000000000 | bytes 10000000 | tf_op jit(solution)/shard_map/out_inner/pallas_call | solution.py:258
  10.6 0.0 collective-permute-done.2.other_ref
  10.6 1.9 %out_edge.1 = bf16[4,8,48,64]{3,2,1,0:T(8,128)(2,1)} custom-call(bf16[192,512]{1,0:T(8,128)(2,1)S(1)} %halo.1.own_ref, bf16[192,512]{1,0:T(8,128)(2,1)S(1)} %collective-permute-done.2.other_ref, f32[1,256]{1,0:T(1,128)S(1)} %bitcast.5, bf16[27,64,256]{2,1,0:T(8,128)(2,1)S(1)} %copy-done.1, bf16[4,96,512]{2,1,0:T(8,128)(2,1)S(1)} %get-tuple-element.19.norm_ref, ...), custom_call_target="tpu_custom_call" | custom-call | flops 1000000000 | bytes 10000000 | tf_op jit(solution)/shard_map/out_edge/pallas_call | solution.py:258
  (1 shorter events, 0.0 us)
Async XLA Ops:
  0.0 3.0 %copy-start.3 = (s32[4,4,24]{2,1,0:T(4,128)S(1)}, s32[4,4,24]{2,1,0:T(4,128)}, u32[]{:S(2)}) copy-start(s32[4,4,24]{2,1,0:T(4,128)} %codes_ref.1) | copy-start | bytes 4612
  0.0 3.0 %copy-start.2 = (bf16[18,512]{1,0:T(8,128)(2,1)S(1)}, bf16[18,512]{1,0:T(8,128)(2,1)}, u32[]{:S(2)}) copy-start(bf16[18,512]{1,0:T(8,128)(2,1)} %proj_ref.3) | copy-start | bytes 55300
  0.0 3.0 %copy-start.4 = (f32[512]{0:T(512)S(1)}, f32[512]{0:T(512)}, u32[]{:S(2)}) copy-start(f32[512]{0:T(512)} %param.8) | copy-start | bytes 6148
  0.0 3.5 %copy-start = (bf16[27,512,128]{2,1,0:T(8,128)(2,1)S(1)}, bf16[27,512,128]{2,1,0:T(8,128)(2,1)}, u32[]{:S(2)}) copy-start(bf16[27,512,128]{2,1,0:T(8,128)(2,1)} %w_ref.5) | copy-start | bytes 10616836
  0.0 5.4 %collective-permute-start = (s32[4,4,24]{2,1,0:T(4,128)}, s32[4,4,24]{2,1,0:T(4,128)S(1)}, u32[]{:S(2)}, u32[]{:S(2)}) collective-permute-start(s32[4,4,24]{2,1,0:T(4,128)} %codes_ref.1), channel_id=1, source_target_pairs={{0,3},{3,0},{2,5},{5,2},{4,7},{7,4},{6,9},{9,6},{8,11},{11,8},{10,... | collective-permute-start | bytes 4616 | tf_op jit(solution)/shard_map/ppermute | solution.py:282
  5.5 2.4 %collective-permute-start.1 = (s32[4,4,24]{2,1,0:T(4,128)S(1)}, s32[4,4,24]{2,1,0:T(4,128)S(1)}, u32[]{:S(2)}, u32[]{:S(2)}) collective-permute-start(s32[4,4,24]{2,1,0:T(4,128)S(1)} %collective-permute-done.after_ref.near_ref), channel_id=1, source_target_pairs={{0,1},{1,0},{2,3},{3,2},{4,5},{5,4},{6,7},{7,6},{8,9},{9,8},{10,11... | collective-permute-start | bytes 4616 | tf_op jit(solution)/shard_map/ppermute | solution.py:307
  7.4 2.0 %collective-permute-start.3 = (bf16[288,512]{1,0:T(8,128)(2,1)S(1)}, bf16[288,512]{1,0:T(8,128)(2,1)S(1)}, u32[]{:S(2)}, u32[]{:S(2)}) collective-permute-start(bf16[288,512]{1,0:T(8,128)(2,1)S(1)} %get-tuple-element.18.own_ref), channel_id=1, source_target_pairs={{0,1},{1,0},{2,3},{3,2},{4,5},{5,4},{6,7},{7,6},{8,9},{9,8},{10,11... | collective-permute-start | bytes 884744 | tf_op jit(solution)/shard_map/ppermute | solution.py:317
  7.9 1.5 %copy-start.1 = (bf16[27,64,256]{2,1,0:T(8,128)(2,1)S(1)}, bf16[27,64,256]{2,1,0:T(8,128)(2,1)}, u32[]{:S(2)}) copy-start(bf16[27,64,256]{2,1,0:T(8,128)(2,1)} %tap_ref.3) | copy-start | bytes 2654212
  7.9 1.5 %copy-start.5 = (f32[256]{0:T(256)S(1)}, f32[256]{0:T(256)}, u32[]{:S(2)}) copy-start(f32[256]{0:T(256)} %param.10) | copy-start | bytes 3076
  9.0 1.6 %collective-permute-start.2 = (bf16[192,512]{1,0:T(8,128)(2,1)S(1)}, bf16[192,512]{1,0:T(8,128)(2,1)S(1)}, u32[]{:S(2)}, u32[]{:S(2)}) collective-permute-start(bf16[192,512]{1,0:T(8,128)(2,1)S(1)} %halo.1.own_ref), channel_id=1, source_target_pairs={{0,1},{1,0},{2,3},{3,2},{4,5},{5,4},{6,7},{7,6},{8,9},{9,8},{10,11... | collective-permute-start | bytes 589832 | tf_op jit(solution)/shard_map/ppermute | solution.py:328

commit v16 on v15

--- a/solution.py
+++ b/solution.py
@@ -13,7 +13,6 @@
 BF16 = jnp.bfloat16
 MIB = 1024 * 1024
 GROUPS = ((0, 2), (2, 2), (4, 2), (6, 2), (8, 1))
-SPLIT = 4
 
 
 def silu_of_half(h):
@@ -70,13 +69,21 @@
     act_ref[...] = latent_rows(codes, proj_ref[...], gain_ref[...]).astype(BF16)
 
 
-def lanes_of(group, share, start=0):
-    return pl.ds((group[0] - start) * share, group[1] * share)
-
-
-def own_first_kernel(n, act_ref, w_ref, first_ref):
-    for group in GROUPS[:SPLIT]:
-        first_ref[:, lanes_of(group, w_ref.shape[2])] = products(act_ref[...], n, w_ref, group)
+def row_products(act, n, w_ref, base):
+    parts = []
+    for first in range(0, 6, 2):
+        total = []
+        for a in range(3):
+            m = -(-(2 + a) * n // 16) * 16
+            pair = jnp.concatenate([w_ref[9 * a + base + first + k] for k in range(2)], axis=1)
+            total.append(jnp.dot(act[:m], pair, preferred_element_type=F32))
+        oldest, back, now = total
+        parts.append(
+            jnp.concatenate(
+                [now[:n], now[n : 2 * n] + back[:n], now[2 * n :] + back[n : 3 * n] + oldest[: 2 * n]], axis=0
+            )
+        )
+    return jnp.concatenate(parts, axis=1)
 
 
 def of_row(part, frames, stride, start, cols):
@@ -98,15 +105,15 @@
         h_ref[out, pl.ds((2 * py + 1) * share, share)] = odd.astype(BF16)
 
 
-def own_rest_kernel(frames, cols, act_ref, w_ref, first_ref, after_ref, h_ref, edge_ref):
+def own_kernel(frames, cols, act_ref, w_ref, h_ref, edge_ref):
     share = w_ref.shape[2]
     n = act_ref.shape[0] // frames
     rows = n // cols
     act = act_ref[...]
-    done = [first_ref[...]] + [products(act, n, w_ref, group) for group in GROUPS[SPLIT:]]
     taken = []
-    for part in done:
-        taken += [part[:, k * share : (k + 1) * share] for k in range(part.shape[1] // share)]
+    for group in GROUPS:
+        part = products(act, n, w_ref, group)
+        taken += [part[:, k * share : (k + 1) * share] for k in range(group[1])]
 
     def row(r):
         return lambda tap: of_row(taken[tap], frames, n, r * cols, cols)
@@ -118,28 +125,39 @@
         edge_ref[1, :, pl.ds(k * share, share)] = row(rows - 1)(k)
 
 
-def halo_kernel(near_ref, far_ref, proj_ref, gain_ref, w_ref, edge_ref, h_ref):
-    frames, rows, cols = near_ref.shape
-    share = w_ref.shape[2]
-    first = lax.axis_index("section") == 1
+def halo_products(codes_ref, below, proj_ref, gain_ref, w_ref):
+    frames, rows, cols = codes_ref.shape
     place = lax.axis_index("rows")
     last = lax.axis_size("rows") - 1
-    codes = []
-    for t in range(frames):
-        low = [ref[t, rows - 1 : rows, :] for ref in (near_ref, far_ref)]
-        high = [ref[t, 0:1, :] for ref in (near_ref, far_ref)]
-        codes += [jnp.where(first, low[0], low[1]), jnp.where(first, high[1], high[0])]
+    codes = [jnp.where(below, codes_ref[t, rows - 1 : rows, :], codes_ref[t, 0:1, :]) for t in range(frames)]
     act = latent_rows(codes, proj_ref[...], gain_ref[...])
-    side = lax.broadcasted_iota(jnp.int32, (frames, 2, cols, act.shape[1]), 1).reshape(act.shape)
-    keep = jnp.where(side == 0, (place > 0).astype(F32), (place < last).astype(F32))
-    act = (act * keep).astype(BF16)
-    halo = jnp.concatenate([products(act, 2 * cols, w_ref, group) for group in GROUPS], axis=1)
-
-    def outer(e):
-        return lambda tap: of_row(halo[:, tap * share : (tap + 1) * share], frames, 2 * cols, e * cols, cols)
-
-    put_hidden(outer(0), lambda tap: edge_ref[0, :, pl.ds((tap - 3) * share, share)], cols, share, 0, h_ref)
-    put_hidden(lambda tap: edge_ref[1, :, pl.ds(tap * share, share)], outer(1), cols, share, 1, h_ref)
+    inside = jnp.where(below, place > 0, place < last)
+    act = jnp.where(inside, act, 0.0).astype(BF16)
+    return row_products(act, cols, w_ref, jnp.where(below, 0, 3))
+
+
+def near_kernel(near_ref, proj_ref, gain_ref, w_ref, part_ref):
+    below = lax.axis_index("section") == 1
+    part_ref[...] = halo_products(near_ref, below, proj_ref, gain_ref, w_ref)
+
+
+def halo_kernel(far_ref, proj_ref, gain_ref, w_ref, near_ref, edge_ref, h_ref):
+    share = w_ref.shape[2]
+    cols = far_ref.shape[2]
+    below = lax.axis_index("section") == 0
+    far = halo_products(far_ref, below, proj_ref, gain_ref, w_ref)
+
+    def of(part, k):
+        return part[:, k * share : (k + 1) * share]
+
+    def lower_row(tap):
+        return jnp.where(below, of(far, tap), near_ref[:, pl.ds(tap * share, share)])
+
+    def upper_row(tap):
+        return jnp.where(below, near_ref[:, pl.ds((tap - 3) * share, share)], of(far, tap - 3))
+
+    put_hidden(lower_row, lambda tap: edge_ref[0, :, pl.ds((tap - 3) * share, share)], cols, share, 0, h_ref)
+    put_hidden(lambda tap: edge_ref[1, :, pl.ds(tap * share, share)], upper_row, cols, share, 1, h_ref)
 
 
 def part_starts(part):
@@ -293,35 +311,34 @@
         4,
         1000,
     )
-    cut = GROUPS[SPLIT][0]
-    (own_first,) = call(
-        functools.partial(own_first_kernel, rows * cols),
-        "own_first",
-        (pltpu.VMEM((rows * size, cut * share), F32),),
+    inner_own, edge = call(
+        functools.partial(own_kernel, frames, cols),
+        "own",
+        (pltpu.VMEM(((rows - 1) * size, 4 * share), BF16), pltpu.VMEM((2, size, 6 * share), F32)),
         (act, w),
-        6,
-        1000,
-    )
-
-    near, own_first = lax.optimization_barrier((near, own_first))
-    far = lax.ppermute(near, "section", swap)
-    near, far, own_first = in_space(pltpu.VMEM, near, far, own_first)
-    inner_own, edge = call(
-        functools.partial(own_rest_kernel, frames, cols),
-        "own_rest",
-        (pltpu.VMEM(((rows - 1) * size, 4 * share), BF16), pltpu.VMEM((2, size, 6 * share), F32)),
-        (act, w, own_first, near),
         8,
         1000,
     )
     inner_other = lax.ppermute(inner_own, "section", swap)
-    far, edge = lax.optimization_barrier((far, edge))
-    far, edge = in_space(pltpu.VMEM, far, edge)
+
+    near, edge = lax.optimization_barrier((near, edge))
+    far = lax.ppermute(near, "section", swap)
+    near, far, edge = in_space(pltpu.VMEM, near, far, edge)
+    (near_part,) = call(
+        near_kernel,
+        "near",
+        (pltpu.VMEM((size, 6 * share), F32),),
+        (near, proj, gain, w),
+        6,
+        3000,
+    )
+    far, near_part = lax.optimization_barrier((far, near_part))
+    far, near_part = in_space(pltpu.VMEM, far, near_part)
     (edge_own,) = call(
         halo_kernel,
         "halo",
         (pltpu.VMEM((2 * size, 4 * share), BF16),),
-        (near, far, proj, gain, w, edge),
+        (far, proj, gain, w, near_part, edge),
         8,
         20000,
     )

time: 12.6 us -> 12.4 us (0.984)
  the two profiles are of different devices: /device:TPU:7 before, /device:TPU:0 now
where the time goes in v16:
time: 12.4 us; the launch traced here: 12.3 us
  Pallas kernels  6.42 us (52%)
  starting transfers between devices  5.32 us (43%)
  waiting for transfers between devices  0.37 us (3%)
    pallas_call x7, Pallas kernels, call(): pl.pallas_call(kernel, out_shape=outs, in_specs=in_specs or [vmem()] * le...  6.42 us
    ppermute x1, starting transfers between devices, body(): near = lax.ppermute(codes, ('rows', 'section'), joint)  4.56 us
    ppermute x1, starting transfers between devices, body(): far = lax.ppermute(near, 'section', swap)  0.49 us
    ppermute x1, waiting for transfers between devices, body(): far = lax.ppermute(near, 'section', swap)  0.25 us
  transfers between devices with their start and end apart: 4, of which 2 were waited for; matrix products, arithmetic and copies ran while one was open for 0% of the time, Pallas kernels for 37%

profile of v16, /device:TPU:0, one launch (start us, length us, event | category | flops | bytes accessed | tf_op | source)
XLA Modules:
  0.0 12.3 jit_solution(4164715622540384759)
XLA Ops:
  0.0 0.0 copy-start.3
  0.0 0.0 copy-start.2
  0.0 0.0 copy-start.4
  0.0 0.0 copy-start
  0.0 4.6 %collective-permute-start = (s32[4,4,24]{2,1,0:T(4,128)}, s32[4,4,24]{2,1,0:T(4,128)S(1)}, u32[]{:S(2)}, u32[]{:S(2)}) collective-permute-start(s32[4,4,24]{2,1,0:T(4,128)} %codes_ref.1), channel_id=1, source_target_pairs={{0,3},{3,0},{2,5},{5,2},{4,7},{7,4},{6,9},{9,6},{8,11},{11,8},{10,... | collective-permute-start | bytes 4616 | tf_op jit(solution)/shard_map/ppermute | solution.py:300
  4.6 0.0 copy-done.3
  4.6 0.0 copy-done.2
  4.6 0.0 copy-done.4
  4.6 0.5 %latent.1.act_ref = bf16[384,512]{1,0:T(8,128)(2,1)S(1)} custom-call(s32[4,4,24]{2,1,0:T(4,128)S(1)} %copy-done.3, bf16[18,512]{1,0:T(8,128)(2,1)S(1)} %copy-done.2, f32[1,512]{1,0:T(1,128)S(1)} %bitcast.2, f32[8,128]{1,0:T(8,128)S(1)} %open.1.mark_ref), custom_call_target="tpu_custom_call" | custom-call | flops 1000000000 | bytes 10000000 | tf_op jit(solution)/shard_map/latent/pallas_call | solution.py:276
  5.1 0.0 copy-done
  5.1 1.3 %own.1 = (bf16[288,512]{1,0:T(8,128)(2,1)S(1)}, f32[2,96,768]{2,1,0:T(8,128)S(1)}) custom-call(bf16[384,512]{1,0:T(8,128)(2,1)S(1)} %latent.1.act_ref, bf16[27,512,128]{2,1,0:T(8,128)(2,1)S(1)} %copy-done), custom_call_target="tpu_custom_call" | custom-call | flops 1000000000 | bytes 10000000 | tf_op jit(solution)/shard_map/own/pallas_call | solution.py:276
  6.4 0.1 collective-permute-start.3
  6.5 0.0 collective-permute-done.near_ref
  6.5 0.5 %collective-permute-start.1 = (s32[4,4,24]{2,1,0:T(4,128)S(1)}, s32[4,4,24]{2,1,0:T(4,128)S(1)}, u32[]{:S(2)}, u32[]{:S(2)}) collective-permute-start(s32[4,4,24]{2,1,0:T(4,128)S(1)} %collective-permute-done.near_ref), channel_id=1, source_target_pairs={{0,1},{1,0},{2,3},{3,2},{4,5},{5,4},{6,7},{7,6},{8,9},{9,8},{10,11... | collective-permute-start | bytes 4616 | tf_op jit(solution)/shard_map/ppermute | solution.py:325
  7.0 0.8 %near.1.near_ref = f32[96,768]{1,0:T(8,128)S(1)} custom-call(s32[4,4,24]{2,1,0:T(4,128)S(1)} %collective-permute-done.near_ref, bf16[18,512]{1,0:T(8,128)(2,1)S(1)} %copy-done.2, f32[1,512]{1,0:T(1,128)S(1)} %bitcast.3, bf16[27,512,128]{2,1,0:T(8,128)(2,1)S(1)} %copy-done), custom_call_target="tpu_custom_call" | custom-call | flops 3000000000 | bytes 10000000 | tf_op jit(solution)/shard_map/near/pallas_call | solution.py:276
  7.8 0.0 copy-start.1
  7.8 0.0 copy-start.5
  7.8 0.2 %collective-permute-done.1.far_ref = s32[4,4,24]{2,1,0:T(4,128)S(1)} collective-permute-done((s32[4,4,24]{2,1,0:T(4,128)S(1)}, s32[4,4,24]{2,1,0:T(4,128)S(1)}, u32[]{:S(2)}, u32[]{:S(2)}) %collective-permute-start.1) | collective-permute-done | bytes 1568 | tf_op jit(solution)/shard_map/ppermute | solution.py:325
  8.1 0.9 %halo.1.own_ref = bf16[192,512]{1,0:T(8,128)(2,1)S(1)} custom-call(s32[4,4,24]{2,1,0:T(4,128)S(1)} %collective-permute-done.1.far_ref, bf16[18,512]{1,0:T(8,128)(2,1)S(1)} %copy-done.2, f32[1,512]{1,0:T(1,128)S(1)} %bitcast.4, bf16[27,512,128]{2,1,0:T(8,128)(2,1)S(1)} %copy-done, f32[96,768]{1,0:T(8,128)S(1)} %near.1.near_ref, ...), custom_call_target="tpu_custom_call" | custom-call | flops 20000000000 | bytes 10000000 | tf_op jit(solution)/shard_map/halo/pallas_call | solution.py:276
  8.9 0.2 %collective-permute-start.2 = (bf16[192,512]{1,0:T(8,128)(2,1)S(1)}, bf16[192,512]{1,0:T(8,128)(2,1)S(1)}, u32[]{:S(2)}, u32[]{:S(2)}) collective-permute-start(bf16[192,512]{1,0:T(8,128)(2,1)S(1)} %halo.1.own_ref), channel_id=1, source_target_pairs={{0,1},{1,0},{2,3},{3,2},{4,5},{5,4},{6,7},{7,6},{8,9},{9,8},{10,11... | collective-permute-start | bytes 589832 | tf_op jit(solution)/shard_map/ppermute | solution.py:345
  9.1 0.0 collective-permute-done.3.other_ref
  9.1 0.0 copy-done.1
  9.1 0.0 copy-done.5
  9.1 1.2 %out_inner.1 = (bf16[4,4,48,64]{3,2,1,0:T(8,128)(2,1)S(1)}, bf16[4,96,512]{2,1,0:T(8,128)(2,1)S(1)}) custom-call(bf16[288,512]{1,0:T(8,128)(2,1)S(1)} %get-tuple-element.18.own_ref, bf16[288,512]{1,0:T(8,128)(2,1)S(1)} %collective-permute-done.3.other_ref, f32[1,256]{1,0:T(1,128)S(1)} %bitcast.5, bf16[27,64,256]{2,1,0:T(8,128)(2,1)S(1)} %copy-done.1), custom_call_target="tpu_custom_call" | custom-call | flops 2000000000 | bytes 10000000 | tf_op jit(solution)/shard_map/out_inner/pallas_call | solution.py:276
  10.3 0.1 collective-permute-done.2.other_ref
  10.4 1.8 %out_edge.1 = bf16[4,8,48,64]{3,2,1,0:T(8,128)(2,1)} custom-call(bf16[192,512]{1,0:T(8,128)(2,1)S(1)} %halo.1.own_ref, bf16[192,512]{1,0:T(8,128)(2,1)S(1)} %collective-permute-done.2.other_ref, f32[1,256]{1,0:T(1,128)S(1)} %bitcast.6, bf16[27,64,256]{2,1,0:T(8,128)(2,1)S(1)} %copy-done.1, bf16[4,96,512]{2,1,0:T(8,128)(2,1)S(1)} %get-tuple-element.19.norm_ref, ...), custom_call_target="tpu_custom_call" | custom-call | flops 1000000000 | bytes 10000000 | tf_op jit(solution)/shard_map/out_edge/pallas_call | solution.py:276
  (1 shorter events, 0.0 us)
Async XLA Ops:
  0.0 4.6 %copy-start.3 = (s32[4,4,24]{2,1,0:T(4,128)S(1)}, s32[4,4,24]{2,1,0:T(4,128)}, u32[]{:S(2)}) copy-start(s32[4,4,24]{2,1,0:T(4,128)} %codes_ref.1) | copy-start | bytes 4612
  0.0 4.6 %copy-start.2 = (bf16[18,512]{1,0:T(8,128)(2,1)S(1)}, bf16[18,512]{1,0:T(8,128)(2,1)}, u32[]{:S(2)}) copy-start(bf16[18,512]{1,0:T(8,128)(2,1)} %proj_ref.5) | copy-start | bytes 55300
  0.0 4.6 %copy-start.4 = (f32[512]{0:T(512)S(1)}, f32[512]{0:T(512)}, u32[]{:S(2)}) copy-start(f32[512]{0:T(512)} %param.8) | copy-start | bytes 6148
  0.0 5.1 %copy-start = (bf16[27,512,128]{2,1,0:T(8,128)(2,1)S(1)}, bf16[27,512,128]{2,1,0:T(8,128)(2,1)}, u32[]{:S(2)}) copy-start(bf16[27,512,128]{2,1,0:T(8,128)(2,1)} %w_ref.5) | copy-start | bytes 10616836
  0.0 6.5 %collective-permute-start = (s32[4,4,24]{2,1,0:T(4,128)}, s32[4,4,24]{2,1,0:T(4,128)S(1)}, u32[]{:S(2)}, u32[]{:S(2)}) collective-permute-start(s32[4,4,24]{2,1,0:T(4,128)} %codes_ref.1), channel_id=1, source_target_pairs={{0,3},{3,0},{2,5},{5,2},{4,7},{7,4},{6,9},{9,6},{8,11},{11,8},{10,... | collective-permute-start | bytes 4616 | tf_op jit(solution)/shard_map/ppermute | solution.py:300
  6.4 2.7 %collective-permute-start.3 = (bf16[288,512]{1,0:T(8,128)(2,1)S(1)}, bf16[288,512]{1,0:T(8,128)(2,1)S(1)}, u32[]{:S(2)}, u32[]{:S(2)}) collective-permute-start(bf16[288,512]{1,0:T(8,128)(2,1)S(1)} %get-tuple-element.18.own_ref), channel_id=1, source_target_pairs={{0,1},{1,0},{2,3},{3,2},{4,5},{5,4},{6,7},{7,6},{8,9},{9,8},{10,11... | collective-permute-start | bytes 884744 | tf_op jit(solution)/shard_map/ppermute | solution.py:322
  6.5 1.6 %collective-permute-start.1 = (s32[4,4,24]{2,1,0:T(4,128)S(1)}, s32[4,4,24]{2,1,0:T(4,128)S(1)}, u32[]{:S(2)}, u32[]{:S(2)}) collective-permute-start(s32[4,4,24]{2,1,0:T(4,128)S(1)} %collective-permute-done.near_ref), channel_id=1, source_target_pairs={{0,1},{1,0},{2,3},{3,2},{4,5},{5,4},{6,7},{7,6},{8,9},{9,8},{10,11... | collective-permute-start | bytes 4616 | tf_op jit(solution)/shard_map/ppermute | solution.py:325
  7.8 1.3 %copy-start.1 = (bf16[27,64,256]{2,1,0:T(8,128)(2,1)S(1)}, bf16[27,64,256]{2,1,0:T(8,128)(2,1)}, u32[]{:S(2)}) copy-start(bf16[27,64,256]{2,1,0:T(8,128)(2,1)} %tap_ref.3) | copy-start | bytes 2654212
  7.8 1.3 %copy-start.5 = (f32[256]{0:T(256)S(1)}, f32[256]{0:T(256)}, u32[]{:S(2)}) copy-start(f32[256]{0:T(256)} %param.10) | copy-start | bytes 3076
  8.9 1.5 %collective-permute-start.2 = (bf16[192,512]{1,0:T(8,128)(2,1)S(1)}, bf16[192,512]{1,0:T(8,128)(2,1)S(1)}, u32[]{:S(2)}, u32[]{:S(2)}) collective-permute-start(bf16[192,512]{1,0:T(8,128)(2,1)S(1)} %halo.1.own_ref), channel_id=1, source_target_pairs={{0,1},{1,0},{2,3},{3,2},{4,5},{5,4},{6,7},{7,6},{8,9},{9,8},{10,11... | collective-permute-start | bytes 589832 | tf_op jit(solution)/shard_map/ppermute | solution.py:345

commit v17 on v16

--- a/solution.py
+++ b/solution.py
@@ -183,59 +183,96 @@
     return rows
 
 
-def out_products(windows, tap_ref, a, m):
-    left = jnp.concatenate([jnp.concatenate([row[:m] for row in window], axis=1) for window in windows], axis=0)
+def table(tap_ref, a, b):
     part = tap_ref.shape[2] // 2
-    starts = part_starts(part)
-    lines = [[], [], [], []]
-    for b in range(3):
-        w = [
-            jnp.concatenate([tap_ref[9 * a + 3 * b + c, :, pl.ds(start, part)] for start in starts], axis=1)
-            for c in range(3)
-        ]
-        zero = jnp.zeros_like(w[0])
-        for line, cells in zip(lines, ((w[1], w[2]), (w[0], w[1]), (zero, w[0]), (w[2], zero))):
-            line += cells
-    right = jnp.concatenate([jnp.concatenate(line, axis=1) for line in lines], axis=0)
+    w = [
+        jnp.concatenate([tap_ref[9 * a + 3 * b + c, :, pl.ds(start, part)] for start in part_starts(part)], axis=1)
+        for c in range(3)
+    ]
+    zero = jnp.zeros_like(w[0])
+    lines = ((w[1], w[2]), (w[0], w[1]), (zero, w[0]), (w[2], zero))
+    return jnp.concatenate([jnp.concatenate(line, axis=1) for line in lines], axis=0)
+
+
+def times(left, right, count):
     total = lax.dot_general(left, right, (((1,), (1,)), ((), ())), preferred_element_type=F32)
-    return total.reshape(len(windows), m, right.shape[0])
-
-
-def out_rows(windows, tap_ref, frames, cols, mix_ref, o_ref):
+    return total.reshape(count, left.shape[0] // count, right.shape[0])
+
+
+def reach(frames, cols, a):
+    return -(-(frames - 2 + a) * cols // 16) * 16
+
+
+def in_time(now, back, oldest, cols):
+    size = now.shape[0]
+    return jnp.concatenate(
+        [
+            now[:cols],
+            now[cols : 2 * cols] + back[:cols],
+            now[2 * cols :] + back[cols : size - cols] + oldest[: size - 2 * cols],
+        ],
+        axis=0,
+    )
+
+
+def window_sums(windows, tap_ref, frames, cols):
+    sums = []
+    for a in (2, 1, 0):
+        m = reach(frames, cols, a)
+        left = jnp.concatenate([jnp.concatenate([row[:m] for row in window], axis=1) for window in windows], axis=0)
+        right = jnp.concatenate([table(tap_ref, a, b) for b in range(3)], axis=1)
+        sums.append(times(left, right, len(windows)))
+    return [in_time(*[part[y] for part in sums], cols) for y in range(len(windows))]
+
+
+def partial_sums(terms, tap_ref, frames, cols):
+    sums = []
+    for a in (2, 1, 0):
+        m = reach(frames, cols, a)
+        share = {}
+        for b, pairs in enumerate(terms):
+            part = times(jnp.concatenate([row[:m] for _, row in pairs], axis=0), table(tap_ref, a, b), len(pairs))
+            for k, (y, _) in enumerate(pairs):
+                share[y] = share[y] + part[k] if y in share else part[k]
+        sums.append(share)
+    return [in_time(*[share[y] for share in sums], cols) for y in sorted(sums[0])]
+
+
+def put_rows(fulls, frames, cols, mix_ref, o_ref):
     size = frames * cols
-    height = len(windows)
     rows, ow = o_ref.shape[2:]
-    now, back, oldest = [out_products(windows, tap_ref, a, -(-(frames - 2 + a) * cols // 16) * 16) for a in (2, 1, 0)]
-    for y in range(height):
-        full = jnp.concatenate(
-            [
-                now[y, :cols],
-                now[y, cols : 2 * cols] + back[y, :cols],
-                now[y, 2 * cols :] + back[y, cols : size - cols] + oldest[y, : size - 2 * cols],
-            ],
-            axis=0,
-        )
+    for y, full in enumerate(fulls):
         side = full[:, 2 * ow :]
         lane = lax.broadcasted_iota(jnp.int32, side.shape, 1)
         both = full[:, : 2 * ow] + jnp.where(lane < ow, shifted(side, cols, 1), shifted(side, cols, -1))
         mix_ref[y, pl.ds(0, size, stride=2), :] = both
         mix_ref[y, pl.ds(1, size, stride=2), :] = pltpu.roll(both, ow, 1)
-    for y in range(height):
+    for y in range(len(fulls)):
         result = mix_ref[y][:, :ow].astype(BF16)
         for t in range(frames):
             o_ref[t, y] = result[rows * t : rows * (t + 1)]
 
 
-def inner_out_kernel(frames, cols, own_ref, other_ref, gain_ref, tap_ref, o_ref, norm_ref, mix_ref):
-    size = frames * cols
-    count = own_ref.shape[0] // size * 2
-    rows = normalise(size, own_ref, other_ref, gain_ref, [None] * count)
-    for k, j in enumerate((0, 1, count - 2, count - 1)):
-        norm_ref[k] = rows[j]
-    out_rows([rows[y : y + 3] for y in range(count - 2)], tap_ref, frames, cols, mix_ref, o_ref)
-
-
-def edge_out_kernel(frames, cols, own_ref, other_ref, gain_ref, tap_ref, norm_ref, inner_ref, o_hbm, o_ref, mix_ref, sems):
+def norm_kernel(size, own_ref, other_ref, gain_ref, norm_ref):
+    for j, row in enumerate(normalise(size, own_ref, other_ref, gain_ref, [None] * norm_ref.shape[0])):
+        norm_ref[j] = row
+
+
+def inner_out_kernel(frames, cols, norm_ref, tap_ref, o_ref, held_ref, mix_ref):
+    count = norm_ref.shape[0]
+    rows = [norm_ref[j] for j in range(count)]
+    fulls = window_sums([rows[y : y + 3] for y in range(count - 2)], tap_ref, frames, cols)
+    terms = (
+        ((2, rows[-2]), (3, rows[-1])),
+        ((1, rows[0]), (2, rows[-1])),
+        ((0, rows[0]), (1, rows[1])),
+    )
+    for y, full in enumerate(partial_sums(terms, tap_ref, frames, cols)):
+        held_ref[y] = full
+    put_rows(fulls, frames, cols, mix_ref, o_ref)
+
+
+def edge_out_kernel(frames, cols, own_ref, other_ref, gain_ref, tap_ref, held_ref, inner_ref, o_hbm, o_ref, mix_ref, sems):
     size = frames * cols
     inner = inner_ref.shape[1]
     copies = [pltpu.make_async_copy(inner_ref, o_hbm.at[:, pl.ds(2, inner)], sems.at[0])]
@@ -243,10 +280,13 @@
     place = lax.axis_index("rows")
     last = lax.axis_size("rows") - 1
     edge = normalise(size, own_ref, other_ref, gain_ref, (place > 0, None, None, place < last))
-    top = edge[:2] + [norm_ref[0], norm_ref[1]]
-    bottom = [norm_ref[2], norm_ref[3]] + edge[2:]
-    windows = [side[y : y + 3] for side in (top, bottom) for y in range(2)]
-    out_rows(windows, tap_ref, frames, cols, mix_ref, o_ref)
+    terms = (
+        ((0, edge[0]), (1, edge[1])),
+        ((0, edge[1]), (3, edge[2])),
+        ((2, edge[2]), (3, edge[3])),
+    )
+    fulls = [held_ref[y] + full for y, full in enumerate(partial_sums(terms, tap_ref, frames, cols))]
+    put_rows(fulls, frames, cols, mix_ref, o_ref)
     for k, start in enumerate((0, inner + 2)):
         copies.append(
             pltpu.make_async_copy(o_ref.at[:, pl.ds(2 * k, 2)], o_hbm.at[:, pl.ds(start, 2)], sems.at[1 + k])
@@ -330,10 +370,20 @@
         (pltpu.VMEM((size, 6 * share), F32),),
         (near, proj, gain, w),
         6,
-        3000,
-    )
-    far, near_part = lax.optimization_barrier((far, near_part))
-    far, near_part = in_space(pltpu.VMEM, far, near_part)
+        20000,
+    )
+    inner_other, near_part = lax.optimization_barrier((inner_other, near_part))
+    inner_own, inner_other = in_space(pltpu.VMEM, inner_own, inner_other)
+    (norm,) = call(
+        functools.partial(norm_kernel, size),
+        "norm",
+        (pltpu.VMEM((height - 2, size, 4 * share), BF16),),
+        (inner_own, inner_other, gain_res),
+        6,
+        1000,
+    )
+    far, near_part, norm = lax.optimization_barrier((far, near_part, norm))
+    far, near_part, norm = in_space(pltpu.VMEM, far, near_part, norm)
     (edge_own,) = call(
         halo_kernel,
         "halo",
@@ -343,14 +393,14 @@
         20000,
     )
     edge_other = lax.ppermute(edge_own, "section", swap)
-    inner_other, edge_other = in_space(pltpu.VMEM, inner_other, edge_other)
+    (edge_other,) = in_space(pltpu.VMEM, edge_other)
 
     mixed = pltpu.VMEM((max(inner, 4), 2 * size, 2 * ow), F32)
-    out_inner, norm = call(
+    out_inner, held = call(
         functools.partial(inner_out_kernel, frames, cols),
         "out_inner",
-        (pltpu.VMEM((frames, inner, 2 * cols, ow), BF16), pltpu.VMEM((4, size, 4 * share), BF16)),
-        (inner_own, inner_other, gain_res, tap),
+        (pltpu.VMEM((frames, inner, 2 * cols, ow), BF16), pltpu.VMEM((4, size, 4 * ow), F32)),
+        (norm, tap),
         12,
         2000,
         [mixed],
@@ -359,7 +409,7 @@
         functools.partial(edge_out_kernel, frames, cols),
         "out_edge",
         jax.ShapeDtypeStruct((frames, height, 2 * cols, ow), BF16),
-        (edge_own, edge_other, gain_res, tap, norm, out_inner),
+        (edge_own, edge_other, gain_res, tap, held, out_inner),
         12,
         1000,
         [pltpu.VMEM((frames, 4, 2 * cols, ow), BF16), mixed, pltpu.SemaphoreType.DMA((3,))],

time: 12.4 us -> 13 us (1.048)
  Pallas kernels: 6.42 us -> 6.98 us
    pallas_call x7 -> x8, Pallas kernels: 6.42 us -> 6.98 us  [call(): pl.pallas_call(kernel, out_shape=outs, in_specs=in_specs or [vmem()] * le...]
    ppermute x1, waiting for transfers between devices: 0.01 us -> 0.26 us  [body(): inner_other = lax.ppermute(inner_own, 'section', swap)]
    ppermute x1, waiting for transfers between devices: 0.25 us -> 0.01 us  [body(): far = lax.ppermute(near, 'section', swap)]
  transfers between devices with their start and end apart: 4 -> 4, of which waited for: 2 -> 1; matrix products, arithmetic and copies ran while one was open for 0% -> 0% of each run, Pallas kernels for 37% -> 35%
where the time goes in v17:
time: 13 us; the launch traced here: 12.8 us
  Pallas kernels  6.98 us (54%)
  starting transfers between devices  5.31 us (41%)
  waiting for transfers between devices  0.27 us (2%)
  between operations  0.13 us (1%)
    pallas_call x8, Pallas kernels, call(): pl.pallas_call(kernel, out_shape=outs, in_specs=in_specs or [vmem()] * le...  6.98 us
    ppermute x1, starting transfers between devices, body(): near = lax.ppermute(codes, ('rows', 'section'), joint)  4.56 us
    ppermute x1, starting transfers between devices, body(): far = lax.ppermute(near, 'section', swap)  0.48 us
  transfers between devices with their start and end apart: 4, of which 1 were waited for; matrix products, arithmetic and copies ran while one was open for 0% of the time, Pallas kernels for 35%

profile of v17, /device:TPU:0, one launch (start us, length us, event | category | flops | bytes accessed | tf_op | source)
XLA Modules:
  0.0 12.8 jit_solution(8847159910476516201)
XLA Ops:
  0.0 0.0 copy-start.3
  0.0 0.0 copy-start.2
  0.0 0.0 copy-start.4
  0.0 0.0 copy-start
  0.0 4.6 %collective-permute-start = (s32[4,4,24]{2,1,0:T(4,128)}, s32[4,4,24]{2,1,0:T(4,128)S(1)}, u32[]{:S(2)}, u32[]{:S(2)}) collective-permute-start(s32[4,4,24]{2,1,0:T(4,128)} %codes_ref.1), channel_id=1, source_target_pairs={{0,3},{3,0},{2,5},{5,2},{4,7},{7,4},{6,9},{9,6},{8,11},{11,8},{10,... | collective-permute-start | bytes 4616 | tf_op jit(solution)/shard_map/ppermute | solution.py:340
  4.6 0.0 copy-done.3
  4.6 0.0 copy-done.2
  4.6 0.0 copy-done.4
  4.6 0.5 %latent.1.act_ref = bf16[384,512]{1,0:T(8,128)(2,1)S(1)} custom-call(s32[4,4,24]{2,1,0:T(4,128)S(1)} %copy-done.3, bf16[18,512]{1,0:T(8,128)(2,1)S(1)} %copy-done.2, f32[1,512]{1,0:T(1,128)S(1)} %bitcast.2, f32[8,128]{1,0:T(8,128)S(1)} %open.1.mark_ref), custom_call_target="tpu_custom_call" | custom-call | flops 1000000000 | bytes 10000000 | tf_op jit(solution)/shard_map/latent/pallas_call | solution.py:316
  5.1 0.0 copy-done
  5.1 1.3 %own.1 = (bf16[288,512]{1,0:T(8,128)(2,1)S(1)}, f32[2,96,768]{2,1,0:T(8,128)S(1)}) custom-call(bf16[384,512]{1,0:T(8,128)(2,1)S(1)} %latent.1.act_ref, bf16[27,512,128]{2,1,0:T(8,128)(2,1)S(1)} %copy-done), custom_call_target="tpu_custom_call" | custom-call | flops 1000000000 | bytes 10000000 | tf_op jit(solution)/shard_map/own/pallas_call | solution.py:316
  6.4 0.1 collective-permute-start.2
  6.5 0.0 collective-permute-done.near_ref
  6.5 0.0 copy-start.5
  6.5 0.5 %collective-permute-start.1 = (s32[4,4,24]{2,1,0:T(4,128)S(1)}, s32[4,4,24]{2,1,0:T(4,128)S(1)}, u32[]{:S(2)}, u32[]{:S(2)}) collective-permute-start(s32[4,4,24]{2,1,0:T(4,128)S(1)} %collective-permute-done.near_ref), channel_id=1, source_target_pairs={{0,1},{1,0},{2,3},{3,2},{4,5},{5,4},{6,7},{7,6},{8,9},{9,8},{10,11... | collective-permute-start | bytes 4616 | tf_op jit(solution)/shard_map/ppermute | solution.py:365
  7.0 0.8 %near.1.near_ref = f32[96,768]{1,0:T(8,128)S(1)} custom-call(s32[4,4,24]{2,1,0:T(4,128)S(1)} %collective-permute-done.near_ref, bf16[18,512]{1,0:T(8,128)(2,1)S(1)} %copy-done.2, f32[1,512]{1,0:T(1,128)S(1)} %bitcast.3, bf16[27,512,128]{2,1,0:T(8,128)(2,1)S(1)} %copy-done), custom_call_target="tpu_custom_call" | custom-call | flops 20000000000 | bytes 10000000 | tf_op jit(solution)/shard_map/near/pallas_call | solution.py:316
  7.8 0.3 %collective-permute-done.2.other_ref = bf16[288,512]{1,0:T(8,128)(2,1)S(1)} collective-permute-done((bf16[288,512]{1,0:T(8,128)(2,1)S(1)}, bf16[288,512]{1,0:T(8,128)(2,1)S(1)}, u32[]{:S(2)}, u32[]{:S(2)}) %collective-permute-start.2) | collective-permute-done | bytes 294944 | tf_op jit(solution)/shard_map/ppermute | solution.py:362
  8.1 0.0 copy-done.5
  8.1 0.4 %norm.1.norm_ref = bf16[6,96,512]{2,1,0:T(8,128)(2,1)S(1)} custom-call(bf16[288,512]{1,0:T(8,128)(2,1)S(1)} %get-tuple-element.18.own_ref, bf16[288,512]{1,0:T(8,128)(2,1)S(1)} %collective-permute-done.2.other_ref, f32[1,256]{1,0:T(1,128)S(1)} %bitcast.5), custom_call_target="tpu_custom_call" | custom-call | flops 1000000000 | bytes 10000000 | tf_op jit(solution)/shard_map/norm/pallas_call | solution.py:316
  8.4 0.0 copy-start.1
  8.5 0.0 collective-permute-done.1.far_ref
  8.5 0.9 %halo.1.own_ref = bf16[192,512]{1,0:T(8,128)(2,1)S(1)} custom-call(s32[4,4,24]{2,1,0:T(4,128)S(1)} %collective-permute-done.1.far_ref, bf16[18,512]{1,0:T(8,128)(2,1)S(1)} %copy-done.2, f32[1,512]{1,0:T(1,128)S(1)} %bitcast.4, bf16[27,512,128]{2,1,0:T(8,128)(2,1)S(1)} %copy-done, f32[96,768]{1,0:T(8,128)S(1)} %near.1.near_ref, ...), custom_call_target="tpu_custom_call" | custom-call | flops 20000000000 | bytes 10000000 | tf_op jit(solution)/shard_map/halo/pallas_call | solution.py:316
  9.3 0.2 %collective-permute-start.3 = (bf16[192,512]{1,0:T(8,128)(2,1)S(1)}, bf16[192,512]{1,0:T(8,128)(2,1)S(1)}, u32[]{:S(2)}, u32[]{:S(2)}) collective-permute-start(bf16[192,512]{1,0:T(8,128)(2,1)S(1)} %halo.1.own_ref), channel_id=1, source_target_pairs={{0,1},{1,0},{2,3},{3,2},{4,5},{5,4},{6,7},{7,6},{8,9},{9,8},{10,11... | collective-permute-start | bytes 589832 | tf_op jit(solution)/shard_map/ppermute | solution.py:395
  9.5 0.1 copy-done.1
  9.6 1.5 %out_inner.1 = (bf16[4,4,48,64]{3,2,1,0:T(8,128)(2,1)S(1)}, f32[4,96,256]{2,1,0:T(8,128)S(1)}) custom-call(bf16[6,96,512]{2,1,0:T(8,128)(2,1)S(1)} %norm.1.norm_ref, bf16[27,64,256]{2,1,0:T(8,128)(2,1)S(1)} %copy-done.1), custom_call_target="tpu_custom_call" | custom-call | flops 2000000000 | bytes 10000000 | tf_op jit(solution)/shard_map/out_inner/pallas_call | solution.py:316
  11.1 0.0 collective-permute-done.3.other_ref
  11.1 1.7 %out_edge.1 = bf16[4,8,48,64]{3,2,1,0:T(8,128)(2,1)} custom-call(bf16[192,512]{1,0:T(8,128)(2,1)S(1)} %halo.1.own_ref, bf16[192,512]{1,0:T(8,128)(2,1)S(1)} %collective-permute-done.3.other_ref, f32[1,256]{1,0:T(1,128)S(1)} %bitcast.6, bf16[27,64,256]{2,1,0:T(8,128)(2,1)S(1)} %copy-done.1, f32[4,96,256]{2,1,0:T(8,128)S(1)} %get-tuple-element.25.held_ref, ...), custom_call_target="tpu_custom_call" | custom-call | flops 1000000000 | bytes 10000000 | tf_op jit(solution)/shard_map/out_edge/pallas_call | solution.py:316
  (1 shorter events, 0.0 us)
Async XLA Ops:
  0.0 4.6 %copy-start.3 = (s32[4,4,24]{2,1,0:T(4,128)S(1)}, s32[4,4,24]{2,1,0:T(4,128)}, u32[]{:S(2)}) copy-start(s32[4,4,24]{2,1,0:T(4,128)} %codes_ref.1) | copy-start | bytes 4612
  0.0 4.6 %copy-start.2 = (bf16[18,512]{1,0:T(8,128)(2,1)S(1)}, bf16[18,512]{1,0:T(8,128)(2,1)}, u32[]{:S(2)}) copy-start(bf16[18,512]{1,0:T(8,128)(2,1)} %proj_ref.5) | copy-start | bytes 55300
  0.0 4.6 %copy-start.4 = (f32[512]{0:T(512)S(1)}, f32[512]{0:T(512)}, u32[]{:S(2)}) copy-start(f32[512]{0:T(512)} %param.8) | copy-start | bytes 6148
  0.0 5.1 %copy-start = (bf16[27,512,128]{2,1,0:T(8,128)(2,1)S(1)}, bf16[27,512,128]{2,1,0:T(8,128)(2,1)}, u32[]{:S(2)}) copy-start(bf16[27,512,128]{2,1,0:T(8,128)(2,1)} %w_ref.5) | copy-start | bytes 10616836
  0.0 6.5 %collective-permute-start = (s32[4,4,24]{2,1,0:T(4,128)}, s32[4,4,24]{2,1,0:T(4,128)S(1)}, u32[]{:S(2)}, u32[]{:S(2)}) collective-permute-start(s32[4,4,24]{2,1,0:T(4,128)} %codes_ref.1), channel_id=1, source_target_pairs={{0,3},{3,0},{2,5},{5,2},{4,7},{7,4},{6,9},{9,6},{8,11},{11,8},{10,... | collective-permute-start | bytes 4616 | tf_op jit(solution)/shard_map/ppermute | solution.py:340
  6.4 1.6 %collective-permute-start.2 = (bf16[288,512]{1,0:T(8,128)(2,1)S(1)}, bf16[288,512]{1,0:T(8,128)(2,1)S(1)}, u32[]{:S(2)}, u32[]{:S(2)}) collective-permute-start(bf16[288,512]{1,0:T(8,128)(2,1)S(1)} %get-tuple-element.18.own_ref), channel_id=1, source_target_pairs={{0,1},{1,0},{2,3},{3,2},{4,5},{5,4},{6,7},{7,6},{8,9},{9,8},{10,11... | collective-permute-start | bytes 884744 | tf_op jit(solution)/shard_map/ppermute | solution.py:362
  6.5 1.6 %copy-start.5 = (f32[256]{0:T(256)S(1)}, f32[256]{0:T(256)}, u32[]{:S(2)}) copy-start(f32[256]{0:T(256)} %param.10) | copy-start | bytes 3076
  6.5 1.9 %collective-permute-start.1 = (s32[4,4,24]{2,1,0:T(4,128)S(1)}, s32[4,4,24]{2,1,0:T(4,128)S(1)}, u32[]{:S(2)}, u32[]{:S(2)}) collective-permute-start(s32[4,4,24]{2,1,0:T(4,128)S(1)} %collective-permute-done.near_ref), channel_id=1, source_target_pairs={{0,1},{1,0},{2,3},{3,2},{4,5},{5,4},{6,7},{7,6},{8,9},{9,8},{10,11... | collective-permute-start | bytes 4616 | tf_op jit(solution)/shard_map/ppermute | solution.py:365
  8.4 1.2 %copy-start.1 = (bf16[27,64,256]{2,1,0:T(8,128)(2,1)S(1)}, bf16[27,64,256]{2,1,0:T(8,128)(2,1)}, u32[]{:S(2)}) copy-start(bf16[27,64,256]{2,1,0:T(8,128)(2,1)} %tap_ref.3) | copy-start | bytes 2654212
  9.3 1.8 %collective-permute-start.3 = (bf16[192,512]{1,0:T(8,128)(2,1)S(1)}, bf16[192,512]{1,0:T(8,128)(2,1)S(1)}, u32[]{:S(2)}, u32[]{:S(2)}) collective-permute-start(bf16[192,512]{1,0:T(8,128)(2,1)S(1)} %halo.1.own_ref), channel_id=1, source_target_pairs={{0,1},{1,0},{2,3},{3,2},{4,5},{5,4},{6,7},{7,6},{8,9},{9,8},{10,11... | collective-permute-start | bytes 589832 | tf_op jit(solution)/shard_map/ppermute | solution.py:395

commit v18 on v16

--- a/solution.py
+++ b/solution.py
@@ -201,7 +201,7 @@
     return total.reshape(len(windows), m, right.shape[0])
 
 
-def out_rows(windows, tap_ref, frames, cols, mix_ref, o_ref):
+def out_rows(windows, tap_ref, frames, cols, mix_ref, o_ref, after_half=None):
     size = frames * cols
     height = len(windows)
     rows, ow = o_ref.shape[2:]
@@ -224,6 +224,8 @@
         result = mix_ref[y][:, :ow].astype(BF16)
         for t in range(frames):
             o_ref[t, y] = result[rows * t : rows * (t + 1)]
+        if after_half is not None and 2 * (y + 1) == height:
+            after_half()
 
 
 def inner_out_kernel(frames, cols, own_ref, other_ref, gain_ref, tap_ref, o_ref, norm_ref, mix_ref):
@@ -246,12 +248,12 @@
     top = edge[:2] + [norm_ref[0], norm_ref[1]]
     bottom = [norm_ref[2], norm_ref[3]] + edge[2:]
     windows = [side[y : y + 3] for side in (top, bottom) for y in range(2)]
-    out_rows(windows, tap_ref, frames, cols, mix_ref, o_ref)
     for k, start in enumerate((0, inner + 2)):
         copies.append(
             pltpu.make_async_copy(o_ref.at[:, pl.ds(2 * k, 2)], o_hbm.at[:, pl.ds(start, 2)], sems.at[1 + k])
         )
-        copies[-1].start()
+    out_rows(windows, tap_ref, frames, cols, mix_ref, o_ref, copies[1].start)
+    copies[2].start()
     for copy in copies:
         copy.wait()
 

time: 12.4 us -> 12.4 us (level)
  transfers between devices with their start and end apart: 4 -> 4, of which waited for: 2 -> 2; matrix products, arithmetic and copies ran while one was open for 0% -> 0% of each run, Pallas kernels for 37% -> 38%
where the time goes in v18:
time: 12.4 us; the launch traced here: 12.2 us
  Pallas kernels  6.41 us (52%)
  starting transfers between devices  5.32 us (43%)
  waiting for transfers between devices  0.37 us (3%)
    pallas_call x7, Pallas kernels, call(): pl.pallas_call(kernel, out_shape=outs, in_specs=in_specs or [vmem()] * le...  6.41 us
    ppermute x1, starting transfers between devices, body(): near = lax.ppermute(codes, ('rows', 'section'), joint)  4.56 us
    ppermute x1, starting transfers between devices, body(): far = lax.ppermute(near, 'section', swap)  0.49 us
    ppermute x1, waiting for transfers between devices, body(): far = lax.ppermute(near, 'section', swap)  0.25 us
  transfers between devices with their start and end apart: 4, of which 2 were waited for; matrix products, arithmetic and copies ran while one was open for 0% of the time, Pallas kernels for 38%

profile of v18, /device:TPU:0, one launch (start us, length us, event | category | flops | bytes accessed | tf_op | source)
XLA Modules:
  0.0 12.2 jit_solution(15170460866051486711)
XLA Ops:
  0.0 0.0 copy-start.3
  0.0 0.0 copy-start.2
  0.0 0.0 copy-start.4
  0.0 0.0 copy-start
  0.0 4.6 %collective-permute-start = (s32[4,4,24]{2,1,0:T(4,128)}, s32[4,4,24]{2,1,0:T(4,128)S(1)}, u32[]{:S(2)}, u32[]{:S(2)}) collective-permute-start(s32[4,4,24]{2,1,0:T(4,128)} %codes_ref.1), channel_id=1, source_target_pairs={{0,3},{3,0},{2,5},{5,2},{4,7},{7,4},{6,9},{9,6},{8,11},{11,8},{10,... | collective-permute-start | bytes 4616 | tf_op jit(solution)/shard_map/ppermute | solution.py:302
  4.6 0.0 copy-done.3
  4.6 0.0 copy-done.2
  4.6 0.0 copy-done.4
  4.6 0.5 %latent.1.act_ref = bf16[384,512]{1,0:T(8,128)(2,1)S(1)} custom-call(s32[4,4,24]{2,1,0:T(4,128)S(1)} %copy-done.3, bf16[18,512]{1,0:T(8,128)(2,1)S(1)} %copy-done.2, f32[1,512]{1,0:T(1,128)S(1)} %bitcast.2, f32[8,128]{1,0:T(8,128)S(1)} %open.1.mark_ref), custom_call_target="tpu_custom_call" | custom-call | flops 1000000000 | bytes 10000000 | tf_op jit(solution)/shard_map/latent/pallas_call | solution.py:278
  5.1 0.0 copy-done
  5.1 1.3 %own.1 = (bf16[288,512]{1,0:T(8,128)(2,1)S(1)}, f32[2,96,768]{2,1,0:T(8,128)S(1)}) custom-call(bf16[384,512]{1,0:T(8,128)(2,1)S(1)} %latent.1.act_ref, bf16[27,512,128]{2,1,0:T(8,128)(2,1)S(1)} %copy-done), custom_call_target="tpu_custom_call" | custom-call | flops 1000000000 | bytes 10000000 | tf_op jit(solution)/shard_map/own/pallas_call | solution.py:278
  6.4 0.1 collective-permute-start.3
  6.5 0.0 collective-permute-done.near_ref
  6.5 0.5 %collective-permute-start.1 = (s32[4,4,24]{2,1,0:T(4,128)S(1)}, s32[4,4,24]{2,1,0:T(4,128)S(1)}, u32[]{:S(2)}, u32[]{:S(2)}) collective-permute-start(s32[4,4,24]{2,1,0:T(4,128)S(1)} %collective-permute-done.near_ref), channel_id=1, source_target_pairs={{0,1},{1,0},{2,3},{3,2},{4,5},{5,4},{6,7},{7,6},{8,9},{9,8},{10,11... | collective-permute-start | bytes 4616 | tf_op jit(solution)/shard_map/ppermute | solution.py:327
  7.0 0.8 %near.1.near_ref = f32[96,768]{1,0:T(8,128)S(1)} custom-call(s32[4,4,24]{2,1,0:T(4,128)S(1)} %collective-permute-done.near_ref, bf16[18,512]{1,0:T(8,128)(2,1)S(1)} %copy-done.2, f32[1,512]{1,0:T(1,128)S(1)} %bitcast.3, bf16[27,512,128]{2,1,0:T(8,128)(2,1)S(1)} %copy-done), custom_call_target="tpu_custom_call" | custom-call | flops 3000000000 | bytes 10000000 | tf_op jit(solution)/shard_map/near/pallas_call | solution.py:278
  7.8 0.0 copy-start.1
  7.8 0.0 copy-start.5
  7.8 0.2 %collective-permute-done.1.far_ref = s32[4,4,24]{2,1,0:T(4,128)S(1)} collective-permute-done((s32[4,4,24]{2,1,0:T(4,128)S(1)}, s32[4,4,24]{2,1,0:T(4,128)S(1)}, u32[]{:S(2)}, u32[]{:S(2)}) %collective-permute-start.1) | collective-permute-done | bytes 1568 | tf_op jit(solution)/shard_map/ppermute | solution.py:327
  8.1 0.9 %halo.1.own_ref = bf16[192,512]{1,0:T(8,128)(2,1)S(1)} custom-call(s32[4,4,24]{2,1,0:T(4,128)S(1)} %collective-permute-done.1.far_ref, bf16[18,512]{1,0:T(8,128)(2,1)S(1)} %copy-done.2, f32[1,512]{1,0:T(1,128)S(1)} %bitcast.4, bf16[27,512,128]{2,1,0:T(8,128)(2,1)S(1)} %copy-done, f32[96,768]{1,0:T(8,128)S(1)} %near.1.near_ref, ...), custom_call_target="tpu_custom_call" | custom-call | flops 20000000000 | bytes 10000000 | tf_op jit(solution)/shard_map/halo/pallas_call | solution.py:278
  8.9 0.2 %collective-permute-start.2 = (bf16[192,512]{1,0:T(8,128)(2,1)S(1)}, bf16[192,512]{1,0:T(8,128)(2,1)S(1)}, u32[]{:S(2)}, u32[]{:S(2)}) collective-permute-start(bf16[192,512]{1,0:T(8,128)(2,1)S(1)} %halo.1.own_ref), channel_id=1, source_target_pairs={{0,1},{1,0},{2,3},{3,2},{4,5},{5,4},{6,7},{7,6},{8,9},{9,8},{10,11... | collective-permute-start | bytes 589832 | tf_op jit(solution)/shard_map/ppermute | solution.py:347
  9.1 0.0 collective-permute-done.3.other_ref
  9.1 0.0 copy-done.1
  9.1 0.0 copy-done.5
  9.1 1.2 %out_inner.1 = (bf16[4,4,48,64]{3,2,1,0:T(8,128)(2,1)S(1)}, bf16[4,96,512]{2,1,0:T(8,128)(2,1)S(1)}) custom-call(bf16[288,512]{1,0:T(8,128)(2,1)S(1)} %get-tuple-element.18.own_ref, bf16[288,512]{1,0:T(8,128)(2,1)S(1)} %collective-permute-done.3.other_ref, f32[1,256]{1,0:T(1,128)S(1)} %bitcast.5, bf16[27,64,256]{2,1,0:T(8,128)(2,1)S(1)} %copy-done.1), custom_call_target="tpu_custom_call" | custom-call | flops 2000000000 | bytes 10000000 | tf_op jit(solution)/shard_map/out_inner/pallas_call | solution.py:278
  10.3 0.1 collective-permute-done.2.other_ref
  10.4 1.8 %out_edge.1 = bf16[4,8,48,64]{3,2,1,0:T(8,128)(2,1)} custom-call(bf16[192,512]{1,0:T(8,128)(2,1)S(1)} %halo.1.own_ref, bf16[192,512]{1,0:T(8,128)(2,1)S(1)} %collective-permute-done.2.other_ref, f32[1,256]{1,0:T(1,128)S(1)} %bitcast.6, bf16[27,64,256]{2,1,0:T(8,128)(2,1)S(1)} %copy-done.1, bf16[4,96,512]{2,1,0:T(8,128)(2,1)S(1)} %get-tuple-element.19.norm_ref, ...), custom_call_target="tpu_custom_call" | custom-call | flops 1000000000 | bytes 10000000 | tf_op jit(solution)/shard_map/out_edge/pallas_call | solution.py:278
  (1 shorter events, 0.0 us)
Async XLA Ops:
  0.0 4.6 %copy-start.3 = (s32[4,4,24]{2,1,0:T(4,128)S(1)}, s32[4,4,24]{2,1,0:T(4,128)}, u32[]{:S(2)}) copy-start(s32[4,4,24]{2,1,0:T(4,128)} %codes_ref.1) | copy-start | bytes 4612
  0.0 4.6 %copy-start.2 = (bf16[18,512]{1,0:T(8,128)(2,1)S(1)}, bf16[18,512]{1,0:T(8,128)(2,1)}, u32[]{:S(2)}) copy-start(bf16[18,512]{1,0:T(8,128)(2,1)} %proj_ref.5) | copy-start | bytes 55300
  0.0 4.6 %copy-start.4 = (f32[512]{0:T(512)S(1)}, f32[512]{0:T(512)}, u32[]{:S(2)}) copy-start(f32[512]{0:T(512)} %param.8) | copy-start | bytes 6148
  0.0 5.1 %copy-start = (bf16[27,512,128]{2,1,0:T(8,128)(2,1)S(1)}, bf16[27,512,128]{2,1,0:T(8,128)(2,1)}, u32[]{:S(2)}) copy-start(bf16[27,512,128]{2,1,0:T(8,128)(2,1)} %w_ref.5) | copy-start | bytes 10616836
  0.0 6.5 %collective-permute-start = (s32[4,4,24]{2,1,0:T(4,128)}, s32[4,4,24]{2,1,0:T(4,128)S(1)}, u32[]{:S(2)}, u32[]{:S(2)}) collective-permute-start(s32[4,4,24]{2,1,0:T(4,128)} %codes_ref.1), channel_id=1, source_target_pairs={{0,3},{3,0},{2,5},{5,2},{4,7},{7,4},{6,9},{9,6},{8,11},{11,8},{10,... | collective-permute-start | bytes 4616 | tf_op jit(solution)/shard_map/ppermute | solution.py:302
  6.4 2.7 %collective-permute-start.3 = (bf16[288,512]{1,0:T(8,128)(2,1)S(1)}, bf16[288,512]{1,0:T(8,128)(2,1)S(1)}, u32[]{:S(2)}, u32[]{:S(2)}) collective-permute-start(bf16[288,512]{1,0:T(8,128)(2,1)S(1)} %get-tuple-element.18.own_ref), channel_id=1, source_target_pairs={{0,1},{1,0},{2,3},{3,2},{4,5},{5,4},{6,7},{7,6},{8,9},{9,8},{10,11... | collective-permute-start | bytes 884744 | tf_op jit(solution)/shard_map/ppermute | solution.py:324
  6.5 1.6 %collective-permute-start.1 = (s32[4,4,24]{2,1,0:T(4,128)S(1)}, s32[4,4,24]{2,1,0:T(4,128)S(1)}, u32[]{:S(2)}, u32[]{:S(2)}) collective-permute-start(s32[4,4,24]{2,1,0:T(4,128)S(1)} %collective-permute-done.near_ref), channel_id=1, source_target_pairs={{0,1},{1,0},{2,3},{3,2},{4,5},{5,4},{6,7},{7,6},{8,9},{9,8},{10,11... | collective-permute-start | bytes 4616 | tf_op jit(solution)/shard_map/ppermute | solution.py:327
  7.8 1.3 %copy-start.1 = (bf16[27,64,256]{2,1,0:T(8,128)(2,1)S(1)}, bf16[27,64,256]{2,1,0:T(8,128)(2,1)}, u32[]{:S(2)}) copy-start(bf16[27,64,256]{2,1,0:T(8,128)(2,1)} %tap_ref.3) | copy-start | bytes 2654212
  7.8 1.3 %copy-start.5 = (f32[256]{0:T(256)S(1)}, f32[256]{0:T(256)}, u32[]{:S(2)}) copy-start(f32[256]{0:T(256)} %param.10) | copy-start | bytes 3076
  8.9 1.5 %collective-permute-start.2 = (bf16[192,512]{1,0:T(8,128)(2,1)S(1)}, bf16[192,512]{1,0:T(8,128)(2,1)S(1)}, u32[]{:S(2)}, u32[]{:S(2)}) collective-permute-start(bf16[192,512]{1,0:T(8,128)(2,1)S(1)} %halo.1.own_ref), channel_id=1, source_target_pairs={{0,1},{1,0},{2,3},{3,2},{4,5},{5,4},{6,7},{7,6},{8,9},{9,8},{10,11... | collective-permute-start | bytes 589832 | tf_op jit(solution)/shard_map/ppermute | solution.py:347

commit v19 on v18

--- a/solution.py
+++ b/solution.py
@@ -206,25 +206,27 @@
     height = len(windows)
     rows, ow = o_ref.shape[2:]
     now, back, oldest = [out_products(windows, tap_ref, a, -(-(frames - 2 + a) * cols // 16) * 16) for a in (2, 1, 0)]
-    for y in range(height):
-        full = jnp.concatenate(
-            [
-                now[y, :cols],
-                now[y, cols : 2 * cols] + back[y, :cols],
-                now[y, 2 * cols :] + back[y, cols : size - cols] + oldest[y, : size - 2 * cols],
-            ],
-            axis=0,
-        )
-        side = full[:, 2 * ow :]
-        lane = lax.broadcasted_iota(jnp.int32, side.shape, 1)
-        both = full[:, : 2 * ow] + jnp.where(lane < ow, shifted(side, cols, 1), shifted(side, cols, -1))
-        mix_ref[y, pl.ds(0, size, stride=2), :] = both
-        mix_ref[y, pl.ds(1, size, stride=2), :] = pltpu.roll(both, ow, 1)
-    for y in range(height):
-        result = mix_ref[y][:, :ow].astype(BF16)
-        for t in range(frames):
-            o_ref[t, y] = result[rows * t : rows * (t + 1)]
-        if after_half is not None and 2 * (y + 1) == height:
+    half = height // 2
+    for part in (range(half), range(half, height)):
+        for y in part:
+            full = jnp.concatenate(
+                [
+                    now[y, :cols],
+                    now[y, cols : 2 * cols] + back[y, :cols],
+                    now[y, 2 * cols :] + back[y, cols : size - cols] + oldest[y, : size - 2 * cols],
+                ],
+                axis=0,
+            )
+            side = full[:, 2 * ow :]
+            lane = lax.broadcasted_iota(jnp.int32, side.shape, 1)
+            both = full[:, : 2 * ow] + jnp.where(lane < ow, shifted(side, cols, 1), shifted(side, cols, -1))
+            mix_ref[y, pl.ds(0, size, stride=2), :] = both
+            mix_ref[y, pl.ds(1, size, stride=2), :] = pltpu.roll(both, ow, 1)
+        for y in part:
+            result = mix_ref[y][:, :ow].astype(BF16)
+            for t in range(frames):
+                o_ref[t, y] = result[rows * t : rows * (t + 1)]
+        if after_half is not None and part.start == 0:
             after_half()
 
 

time: 12.4 us -> 12.4 us (level)
  no operation moved by 1% of the time
where the time goes in v19:
time: 12.4 us; the launch traced here: 12.2 us
  Pallas kernels  6.41 us (52%)
  starting transfers between devices  5.32 us (43%)
  waiting for transfers between devices  0.37 us (3%)
    pallas_call x7, Pallas kernels, call(): pl.pallas_call(kernel, out_shape=outs, in_specs=in_specs or [vmem()] * le...  6.41 us
    ppermute x1, starting transfers between devices, body(): near = lax.ppermute(codes, ('rows', 'section'), joint)  4.56 us
    ppermute x1, starting transfers between devices, body(): far = lax.ppermute(near, 'section', swap)  0.49 us
    ppermute x1, waiting for transfers between devices, body(): far = lax.ppermute(near, 'section', swap)  0.25 us
  transfers between devices with their start and end apart: 4, of which 2 were waited for; matrix products, arithmetic and copies ran while one was open for 0% of the time, Pallas kernels for 38%

profile of v19, /device:TPU:0, one launch (start us, length us, event | category | flops | bytes accessed | tf_op | source)
XLA Modules:
  0.0 12.2 jit_solution(15170460866051486711)
XLA Ops:
  0.0 0.0 copy-start.3
  0.0 0.0 copy-start.2
  0.0 0.0 copy-start.4
  0.0 0.0 copy-start
  0.0 4.6 %collective-permute-start = (s32[4,4,24]{2,1,0:T(4,128)}, s32[4,4,24]{2,1,0:T(4,128)S(1)}, u32[]{:S(2)}, u32[]{:S(2)}) collective-permute-start(s32[4,4,24]{2,1,0:T(4,128)} %codes_ref.1), channel_id=1, source_target_pairs={{0,3},{3,0},{2,5},{5,2},{4,7},{7,4},{6,9},{9,6},{8,11},{11,8},{10,... | collective-permute-start | bytes 4616 | tf_op jit(solution)/shard_map/ppermute | solution.py:304
  4.6 0.0 copy-done.3
  4.6 0.0 copy-done.2
  4.6 0.0 copy-done.4
  4.6 0.5 %latent.1.act_ref = bf16[384,512]{1,0:T(8,128)(2,1)S(1)} custom-call(s32[4,4,24]{2,1,0:T(4,128)S(1)} %copy-done.3, bf16[18,512]{1,0:T(8,128)(2,1)S(1)} %copy-done.2, f32[1,512]{1,0:T(1,128)S(1)} %bitcast.2, f32[8,128]{1,0:T(8,128)S(1)} %open.1.mark_ref), custom_call_target="tpu_custom_call" | custom-call | flops 1000000000 | bytes 10000000 | tf_op jit(solution)/shard_map/latent/pallas_call | solution.py:280
  5.1 0.0 copy-done
  5.1 1.3 %own.1 = (bf16[288,512]{1,0:T(8,128)(2,1)S(1)}, f32[2,96,768]{2,1,0:T(8,128)S(1)}) custom-call(bf16[384,512]{1,0:T(8,128)(2,1)S(1)} %latent.1.act_ref, bf16[27,512,128]{2,1,0:T(8,128)(2,1)S(1)} %copy-done), custom_call_target="tpu_custom_call" | custom-call | flops 1000000000 | bytes 10000000 | tf_op jit(solution)/shard_map/own/pallas_call | solution.py:280
  6.4 0.1 collective-permute-start.3
  6.5 0.0 collective-permute-done.near_ref
  6.5 0.5 %collective-permute-start.1 = (s32[4,4,24]{2,1,0:T(4,128)S(1)}, s32[4,4,24]{2,1,0:T(4,128)S(1)}, u32[]{:S(2)}, u32[]{:S(2)}) collective-permute-start(s32[4,4,24]{2,1,0:T(4,128)S(1)} %collective-permute-done.near_ref), channel_id=1, source_target_pairs={{0,1},{1,0},{2,3},{3,2},{4,5},{5,4},{6,7},{7,6},{8,9},{9,8},{10,11... | collective-permute-start | bytes 4616 | tf_op jit(solution)/shard_map/ppermute | solution.py:329
  7.0 0.8 %near.1.near_ref = f32[96,768]{1,0:T(8,128)S(1)} custom-call(s32[4,4,24]{2,1,0:T(4,128)S(1)} %collective-permute-done.near_ref, bf16[18,512]{1,0:T(8,128)(2,1)S(1)} %copy-done.2, f32[1,512]{1,0:T(1,128)S(1)} %bitcast.3, bf16[27,512,128]{2,1,0:T(8,128)(2,1)S(1)} %copy-done), custom_call_target="tpu_custom_call" | custom-call | flops 3000000000 | bytes 10000000 | tf_op jit(solution)/shard_map/near/pallas_call | solution.py:280
  7.8 0.0 copy-start.1
  7.8 0.0 copy-start.5
  7.8 0.2 %collective-permute-done.1.far_ref = s32[4,4,24]{2,1,0:T(4,128)S(1)} collective-permute-done((s32[4,4,24]{2,1,0:T(4,128)S(1)}, s32[4,4,24]{2,1,0:T(4,128)S(1)}, u32[]{:S(2)}, u32[]{:S(2)}) %collective-permute-start.1) | collective-permute-done | bytes 1568 | tf_op jit(solution)/shard_map/ppermute | solution.py:329
  8.1 0.9 %halo.1.own_ref = bf16[192,512]{1,0:T(8,128)(2,1)S(1)} custom-call(s32[4,4,24]{2,1,0:T(4,128)S(1)} %collective-permute-done.1.far_ref, bf16[18,512]{1,0:T(8,128)(2,1)S(1)} %copy-done.2, f32[1,512]{1,0:T(1,128)S(1)} %bitcast.4, bf16[27,512,128]{2,1,0:T(8,128)(2,1)S(1)} %copy-done, f32[96,768]{1,0:T(8,128)S(1)} %near.1.near_ref, ...), custom_call_target="tpu_custom_call" | custom-call | flops 20000000000 | bytes 10000000 | tf_op jit(solution)/shard_map/halo/pallas_call | solution.py:280
  8.9 0.2 %collective-permute-start.2 = (bf16[192,512]{1,0:T(8,128)(2,1)S(1)}, bf16[192,512]{1,0:T(8,128)(2,1)S(1)}, u32[]{:S(2)}, u32[]{:S(2)}) collective-permute-start(bf16[192,512]{1,0:T(8,128)(2,1)S(1)} %halo.1.own_ref), channel_id=1, source_target_pairs={{0,1},{1,0},{2,3},{3,2},{4,5},{5,4},{6,7},{7,6},{8,9},{9,8},{10,11... | collective-permute-start | bytes 589832 | tf_op jit(solution)/shard_map/ppermute | solution.py:349
  9.1 0.0 collective-permute-done.3.other_ref
  9.1 0.0 copy-done.1
  9.1 0.0 copy-done.5
  9.1 1.2 %out_inner.1 = (bf16[4,4,48,64]{3,2,1,0:T(8,128)(2,1)S(1)}, bf16[4,96,512]{2,1,0:T(8,128)(2,1)S(1)}) custom-call(bf16[288,512]{1,0:T(8,128)(2,1)S(1)} %get-tuple-element.18.own_ref, bf16[288,512]{1,0:T(8,128)(2,1)S(1)} %collective-permute-done.3.other_ref, f32[1,256]{1,0:T(1,128)S(1)} %bitcast.5, bf16[27,64,256]{2,1,0:T(8,128)(2,1)S(1)} %copy-done.1), custom_call_target="tpu_custom_call" | custom-call | flops 2000000000 | bytes 10000000 | tf_op jit(solution)/shard_map/out_inner/pallas_call | solution.py:280
  10.3 0.1 collective-permute-done.2.other_ref
  10.4 1.8 %out_edge.1 = bf16[4,8,48,64]{3,2,1,0:T(8,128)(2,1)} custom-call(bf16[192,512]{1,0:T(8,128)(2,1)S(1)} %halo.1.own_ref, bf16[192,512]{1,0:T(8,128)(2,1)S(1)} %collective-permute-done.2.other_ref, f32[1,256]{1,0:T(1,128)S(1)} %bitcast.6, bf16[27,64,256]{2,1,0:T(8,128)(2,1)S(1)} %copy-done.1, bf16[4,96,512]{2,1,0:T(8,128)(2,1)S(1)} %get-tuple-element.19.norm_ref, ...), custom_call_target="tpu_custom_call" | custom-call | flops 1000000000 | bytes 10000000 | tf_op jit(solution)/shard_map/out_edge/pallas_call | solution.py:280
  (1 shorter events, 0.0 us)
Async XLA Ops:
  0.0 4.6 %copy-start.3 = (s32[4,4,24]{2,1,0:T(4,128)S(1)}, s32[4,4,24]{2,1,0:T(4,128)}, u32[]{:S(2)}) copy-start(s32[4,4,24]{2,1,0:T(4,128)} %codes_ref.1) | copy-start | bytes 4612
  0.0 4.6 %copy-start.2 = (bf16[18,512]{1,0:T(8,128)(2,1)S(1)}, bf16[18,512]{1,0:T(8,128)(2,1)}, u32[]{:S(2)}) copy-start(bf16[18,512]{1,0:T(8,128)(2,1)} %proj_ref.5) | copy-start | bytes 55300
  0.0 4.6 %copy-start.4 = (f32[512]{0:T(512)S(1)}, f32[512]{0:T(512)}, u32[]{:S(2)}) copy-start(f32[512]{0:T(512)} %param.8) | copy-start | bytes 6148
  0.0 5.1 %copy-start = (bf16[27,512,128]{2,1,0:T(8,128)(2,1)S(1)}, bf16[27,512,128]{2,1,0:T(8,128)(2,1)}, u32[]{:S(2)}) copy-start(bf16[27,512,128]{2,1,0:T(8,128)(2,1)} %w_ref.5) | copy-start | bytes 10616836
  0.0 6.5 %collective-permute-start = (s32[4,4,24]{2,1,0:T(4,128)}, s32[4,4,24]{2,1,0:T(4,128)S(1)}, u32[]{:S(2)}, u32[]{:S(2)}) collective-permute-start(s32[4,4,24]{2,1,0:T(4,128)} %codes_ref.1), channel_id=1, source_target_pairs={{0,3},{3,0},{2,5},{5,2},{4,7},{7,4},{6,9},{9,6},{8,11},{11,8},{10,... | collective-permute-start | bytes 4616 | tf_op jit(solution)/shard_map/ppermute | solution.py:304
  6.4 2.7 %collective-permute-start.3 = (bf16[288,512]{1,0:T(8,128)(2,1)S(1)}, bf16[288,512]{1,0:T(8,128)(2,1)S(1)}, u32[]{:S(2)}, u32[]{:S(2)}) collective-permute-start(bf16[288,512]{1,0:T(8,128)(2,1)S(1)} %get-tuple-element.18.own_ref), channel_id=1, source_target_pairs={{0,1},{1,0},{2,3},{3,2},{4,5},{5,4},{6,7},{7,6},{8,9},{9,8},{10,11... | collective-permute-start | bytes 884744 | tf_op jit(solution)/shard_map/ppermute | solution.py:326
  6.5 1.6 %collective-permute-start.1 = (s32[4,4,24]{2,1,0:T(4,128)S(1)}, s32[4,4,24]{2,1,0:T(4,128)S(1)}, u32[]{:S(2)}, u32[]{:S(2)}) collective-permute-start(s32[4,4,24]{2,1,0:T(4,128)S(1)} %collective-permute-done.near_ref), channel_id=1, source_target_pairs={{0,1},{1,0},{2,3},{3,2},{4,5},{5,4},{6,7},{7,6},{8,9},{9,8},{10,11... | collective-permute-start | bytes 4616 | tf_op jit(solution)/shard_map/ppermute | solution.py:329
  7.8 1.3 %copy-start.1 = (bf16[27,64,256]{2,1,0:T(8,128)(2,1)S(1)}, bf16[27,64,256]{2,1,0:T(8,128)(2,1)}, u32[]{:S(2)}) copy-start(bf16[27,64,256]{2,1,0:T(8,128)(2,1)} %tap_ref.3) | copy-start | bytes 2654212
  7.8 1.3 %copy-start.5 = (f32[256]{0:T(256)S(1)}, f32[256]{0:T(256)}, u32[]{:S(2)}) copy-start(f32[256]{0:T(256)} %param.10) | copy-start | bytes 3076
  8.9 1.5 %collective-permute-start.2 = (bf16[192,512]{1,0:T(8,128)(2,1)S(1)}, bf16[192,512]{1,0:T(8,128)(2,1)S(1)}, u32[]{:S(2)}, u32[]{:S(2)}) collective-permute-start(bf16[192,512]{1,0:T(8,128)(2,1)S(1)} %halo.1.own_ref), channel_id=1, source_target_pairs={{0,1},{1,0},{2,3},{3,2},{4,5},{5,4},{6,7},{7,6},{8,9},{9,8},{10,11... | collective-permute-start | bytes 589832 | tf_op jit(solution)/shard_map/ppermute | solution.py:349

commit v20 on v18

--- a/solution.py
+++ b/solution.py
@@ -232,9 +232,9 @@
     size = frames * cols
     count = own_ref.shape[0] // size * 2
     rows = normalise(size, own_ref, other_ref, gain_ref, [None] * count)
+    out_rows([rows[y : y + 3] for y in range(count - 2)], tap_ref, frames, cols, mix_ref, o_ref)
     for k, j in enumerate((0, 1, count - 2, count - 1)):
         norm_ref[k] = rows[j]
-    out_rows([rows[y : y + 3] for y in range(count - 2)], tap_ref, frames, cols, mix_ref, o_ref)
 
 
 def edge_out_kernel(frames, cols, own_ref, other_ref, gain_ref, tap_ref, norm_ref, inner_ref, o_hbm, o_ref, mix_ref, sems):

time: 12.4 us -> 12.4 us (level)
  no operation moved by 1% of the time
where the time goes in v20:
time: 12.4 us; the launch traced here: 12.2 us
  Pallas kernels  6.41 us (52%)
  starting transfers between devices  5.32 us (43%)
  waiting for transfers between devices  0.37 us (3%)
    pallas_call x7, Pallas kernels, call(): pl.pallas_call(kernel, out_shape=outs, in_specs=in_specs or [vmem()] * le...  6.41 us
    ppermute x1, starting transfers between devices, body(): near = lax.ppermute(codes, ('rows', 'section'), joint)  4.56 us
    ppermute x1, starting transfers between devices, body(): far = lax.ppermute(near, 'section', swap)  0.49 us
    ppermute x1, waiting for transfers between devices, body(): far = lax.ppermute(near, 'section', swap)  0.25 us
  transfers between devices with their start and end apart: 4, of which 2 were waited for; matrix products, arithmetic and copies ran while one was open for 0% of the time, Pallas kernels for 38%

profile of v20, /device:TPU:0, one launch (start us, length us, event | category | flops | bytes accessed | tf_op | source)
XLA Modules:
  0.0 12.2 jit_solution(15437876998940987652)
XLA Ops:
  0.0 0.0 copy-start.3
  0.0 0.0 copy-start.2
  0.0 0.0 copy-start.4
  0.0 0.0 copy-start
  0.0 4.6 %collective-permute-start = (s32[4,4,24]{2,1,0:T(4,128)}, s32[4,4,24]{2,1,0:T(4,128)S(1)}, u32[]{:S(2)}, u32[]{:S(2)}) collective-permute-start(s32[4,4,24]{2,1,0:T(4,128)} %codes_ref.1), channel_id=1, source_target_pairs={{0,3},{3,0},{2,5},{5,2},{4,7},{7,4},{6,9},{9,6},{8,11},{11,8},{10,... | collective-permute-start | bytes 4616 | tf_op jit(solution)/shard_map/ppermute | solution.py:302
  4.6 0.0 copy-done.3
  4.6 0.0 copy-done.2
  4.6 0.0 copy-done.4
  4.6 0.5 %latent.1.act_ref = bf16[384,512]{1,0:T(8,128)(2,1)S(1)} custom-call(s32[4,4,24]{2,1,0:T(4,128)S(1)} %copy-done.3, bf16[18,512]{1,0:T(8,128)(2,1)S(1)} %copy-done.2, f32[1,512]{1,0:T(1,128)S(1)} %bitcast.2, f32[8,128]{1,0:T(8,128)S(1)} %open.1.mark_ref), custom_call_target="tpu_custom_call" | custom-call | flops 1000000000 | bytes 10000000 | tf_op jit(solution)/shard_map/latent/pallas_call | solution.py:278
  5.1 0.0 copy-done
  5.1 1.3 %own.1 = (bf16[288,512]{1,0:T(8,128)(2,1)S(1)}, f32[2,96,768]{2,1,0:T(8,128)S(1)}) custom-call(bf16[384,512]{1,0:T(8,128)(2,1)S(1)} %latent.1.act_ref, bf16[27,512,128]{2,1,0:T(8,128)(2,1)S(1)} %copy-done), custom_call_target="tpu_custom_call" | custom-call | flops 1000000000 | bytes 10000000 | tf_op jit(solution)/shard_map/own/pallas_call | solution.py:278
  6.4 0.1 collective-permute-start.3
  6.5 0.0 collective-permute-done.near_ref
  6.5 0.5 %collective-permute-start.1 = (s32[4,4,24]{2,1,0:T(4,128)S(1)}, s32[4,4,24]{2,1,0:T(4,128)S(1)}, u32[]{:S(2)}, u32[]{:S(2)}) collective-permute-start(s32[4,4,24]{2,1,0:T(4,128)S(1)} %collective-permute-done.near_ref), channel_id=1, source_target_pairs={{0,1},{1,0},{2,3},{3,2},{4,5},{5,4},{6,7},{7,6},{8,9},{9,8},{10,11... | collective-permute-start | bytes 4616 | tf_op jit(solution)/shard_map/ppermute | solution.py:327
  7.0 0.8 %near.1.near_ref = f32[96,768]{1,0:T(8,128)S(1)} custom-call(s32[4,4,24]{2,1,0:T(4,128)S(1)} %collective-permute-done.near_ref, bf16[18,512]{1,0:T(8,128)(2,1)S(1)} %copy-done.2, f32[1,512]{1,0:T(1,128)S(1)} %bitcast.3, bf16[27,512,128]{2,1,0:T(8,128)(2,1)S(1)} %copy-done), custom_call_target="tpu_custom_call" | custom-call | flops 3000000000 | bytes 10000000 | tf_op jit(solution)/shard_map/near/pallas_call | solution.py:278
  7.8 0.0 copy-start.1
  7.8 0.0 copy-start.5
  7.8 0.2 %collective-permute-done.1.far_ref = s32[4,4,24]{2,1,0:T(4,128)S(1)} collective-permute-done((s32[4,4,24]{2,1,0:T(4,128)S(1)}, s32[4,4,24]{2,1,0:T(4,128)S(1)}, u32[]{:S(2)}, u32[]{:S(2)}) %collective-permute-start.1) | collective-permute-done | bytes 1568 | tf_op jit(solution)/shard_map/ppermute | solution.py:327
  8.1 0.9 %halo.1.own_ref = bf16[192,512]{1,0:T(8,128)(2,1)S(1)} custom-call(s32[4,4,24]{2,1,0:T(4,128)S(1)} %collective-permute-done.1.far_ref, bf16[18,512]{1,0:T(8,128)(2,1)S(1)} %copy-done.2, f32[1,512]{1,0:T(1,128)S(1)} %bitcast.4, bf16[27,512,128]{2,1,0:T(8,128)(2,1)S(1)} %copy-done, f32[96,768]{1,0:T(8,128)S(1)} %near.1.near_ref, ...), custom_call_target="tpu_custom_call" | custom-call | flops 20000000000 | bytes 10000000 | tf_op jit(solution)/shard_map/halo/pallas_call | solution.py:278
  8.9 0.2 %collective-permute-start.2 = (bf16[192,512]{1,0:T(8,128)(2,1)S(1)}, bf16[192,512]{1,0:T(8,128)(2,1)S(1)}, u32[]{:S(2)}, u32[]{:S(2)}) collective-permute-start(bf16[192,512]{1,0:T(8,128)(2,1)S(1)} %halo.1.own_ref), channel_id=1, source_target_pairs={{0,1},{1,0},{2,3},{3,2},{4,5},{5,4},{6,7},{7,6},{8,9},{9,8},{10,11... | collective-permute-start | bytes 589832 | tf_op jit(solution)/shard_map/ppermute | solution.py:347
  9.1 0.0 collective-permute-done.3.other_ref
  9.1 0.0 copy-done.1
  9.1 0.0 copy-done.5
  9.1 1.2 %out_inner.1 = (bf16[4,4,48,64]{3,2,1,0:T(8,128)(2,1)S(1)}, bf16[4,96,512]{2,1,0:T(8,128)(2,1)S(1)}) custom-call(bf16[288,512]{1,0:T(8,128)(2,1)S(1)} %get-tuple-element.18.own_ref, bf16[288,512]{1,0:T(8,128)(2,1)S(1)} %collective-permute-done.3.other_ref, f32[1,256]{1,0:T(1,128)S(1)} %bitcast.5, bf16[27,64,256]{2,1,0:T(8,128)(2,1)S(1)} %copy-done.1), custom_call_target="tpu_custom_call" | custom-call | flops 2000000000 | bytes 10000000 | tf_op jit(solution)/shard_map/out_inner/pallas_call | solution.py:278
  10.3 0.1 collective-permute-done.2.other_ref
  10.4 1.8 %out_edge.1 = bf16[4,8,48,64]{3,2,1,0:T(8,128)(2,1)} custom-call(bf16[192,512]{1,0:T(8,128)(2,1)S(1)} %halo.1.own_ref, bf16[192,512]{1,0:T(8,128)(2,1)S(1)} %collective-permute-done.2.other_ref, f32[1,256]{1,0:T(1,128)S(1)} %bitcast.6, bf16[27,64,256]{2,1,0:T(8,128)(2,1)S(1)} %copy-done.1, bf16[4,96,512]{2,1,0:T(8,128)(2,1)S(1)} %get-tuple-element.19.norm_ref, ...), custom_call_target="tpu_custom_call" | custom-call | flops 1000000000 | bytes 10000000 | tf_op jit(solution)/shard_map/out_edge/pallas_call | solution.py:278
  (1 shorter events, 0.0 us)
Async XLA Ops:
  0.0 4.6 %copy-start.3 = (s32[4,4,24]{2,1,0:T(4,128)S(1)}, s32[4,4,24]{2,1,0:T(4,128)}, u32[]{:S(2)}) copy-start(s32[4,4,24]{2,1,0:T(4,128)} %codes_ref.1) | copy-start | bytes 4612
  0.0 4.6 %copy-start.2 = (bf16[18,512]{1,0:T(8,128)(2,1)S(1)}, bf16[18,512]{1,0:T(8,128)(2,1)}, u32[]{:S(2)}) copy-start(bf16[18,512]{1,0:T(8,128)(2,1)} %proj_ref.5) | copy-start | bytes 55300
  0.0 4.6 %copy-start.4 = (f32[512]{0:T(512)S(1)}, f32[512]{0:T(512)}, u32[]{:S(2)}) copy-start(f32[512]{0:T(512)} %param.8) | copy-start | bytes 6148
  0.0 5.1 %copy-start = (bf16[27,512,128]{2,1,0:T(8,128)(2,1)S(1)}, bf16[27,512,128]{2,1,0:T(8,128)(2,1)}, u32[]{:S(2)}) copy-start(bf16[27,512,128]{2,1,0:T(8,128)(2,1)} %w_ref.5) | copy-start | bytes 10616836
  0.0 6.5 %collective-permute-start = (s32[4,4,24]{2,1,0:T(4,128)}, s32[4,4,24]{2,1,0:T(4,128)S(1)}, u32[]{:S(2)}, u32[]{:S(2)}) collective-permute-start(s32[4,4,24]{2,1,0:T(4,128)} %codes_ref.1), channel_id=1, source_target_pairs={{0,3},{3,0},{2,5},{5,2},{4,7},{7,4},{6,9},{9,6},{8,11},{11,8},{10,... | collective-permute-start | bytes 4616 | tf_op jit(solution)/shard_map/ppermute | solution.py:302
  6.4 2.7 %collective-permute-start.3 = (bf16[288,512]{1,0:T(8,128)(2,1)S(1)}, bf16[288,512]{1,0:T(8,128)(2,1)S(1)}, u32[]{:S(2)}, u32[]{:S(2)}) collective-permute-start(bf16[288,512]{1,0:T(8,128)(2,1)S(1)} %get-tuple-element.18.own_ref), channel_id=1, source_target_pairs={{0,1},{1,0},{2,3},{3,2},{4,5},{5,4},{6,7},{7,6},{8,9},{9,8},{10,11... | collective-permute-start | bytes 884744 | tf_op jit(solution)/shard_map/ppermute | solution.py:324
  6.5 1.6 %collective-permute-start.1 = (s32[4,4,24]{2,1,0:T(4,128)S(1)}, s32[4,4,24]{2,1,0:T(4,128)S(1)}, u32[]{:S(2)}, u32[]{:S(2)}) collective-permute-start(s32[4,4,24]{2,1,0:T(4,128)S(1)} %collective-permute-done.near_ref), channel_id=1, source_target_pairs={{0,1},{1,0},{2,3},{3,2},{4,5},{5,4},{6,7},{7,6},{8,9},{9,8},{10,11... | collective-permute-start | bytes 4616 | tf_op jit(solution)/shard_map/ppermute | solution.py:327
  7.8 1.3 %copy-start.1 = (bf16[27,64,256]{2,1,0:T(8,128)(2,1)S(1)}, bf16[27,64,256]{2,1,0:T(8,128)(2,1)}, u32[]{:S(2)}) copy-start(bf16[27,64,256]{2,1,0:T(8,128)(2,1)} %tap_ref.3) | copy-start | bytes 2654212
  7.8 1.3 %copy-start.5 = (f32[256]{0:T(256)S(1)}, f32[256]{0:T(256)}, u32[]{:S(2)}) copy-start(f32[256]{0:T(256)} %param.10) | copy-start | bytes 3076
  8.9 1.5 %collective-permute-start.2 = (bf16[192,512]{1,0:T(8,128)(2,1)S(1)}, bf16[192,512]{1,0:T(8,128)(2,1)S(1)}, u32[]{:S(2)}, u32[]{:S(2)}) collective-permute-start(bf16[192,512]{1,0:T(8,128)(2,1)S(1)} %halo.1.own_ref), channel_id=1, source_target_pairs={{0,1},{1,0},{2,3},{3,2},{4,5},{5,4},{6,7},{7,6},{8,9},{9,8},{10,11... | collective-permute-start | bytes 589832 | tf_op jit(solution)/shard_map/ppermute | solution.py:347
